TPU v7x, 128 devices: a whole 4x4x4 slice. The times are simulated.
128 devices in a mesh: mesh: 16 (over y, x), src: 8 (over z, core).
Axes of the slice: x: 4, y: 4, z: 4, core: 2. Of those that a mesh axis runs over, the one named last changes fastest.
Arguments:
- right_side: float32 [262144, 256], P(('mesh', 'src')), may hold values from -6 to 6
- tile_stiff: float32 [32768, 32, 32], P(('mesh', 'src')), as said below
- tile_nodes: int32 [32768, 32], P(('mesh', 'src')), may hold values from 0 to 2304, as said below
- node_shift: float32 [262144], P(('mesh', 'src')), may hold values from 0.5 to 2
- slot_nodes: int32 [16, 32768], P(None, ('mesh', 'src')), may hold values from 0 to 2047
- slot_load: float32 [16, 98304], P(None, ('mesh', 'src')), may hold values from -6 to 6
- dipole_slot: int32 [16384], P(('mesh', 'src')), may hold values from 0 to 255, as said below
Outputs:
- solution: float32 [262144, 256], P(('mesh', 'src'))
- leadfield: float32 [3, 16384, 256], P(None, ('mesh', 'src'))
Inputs may be any that keep to these rules, and one draw needn't show every extreme that they name: `tile_stiff`: every tile is symmetric positive definite. `tile_nodes`: the largest value marks a padded slot; every other value is a row of the partition's extended nodes. The live slots of one tile lie within 64 consecutive rows. `dipole_slot`: the 128 entries of one owner are distinct; at most 2 of one owner's entries name one source partition, and each owner has a source partition with exactly 2.
All inputs are finite; a program needn't handle non-finite values.
Results may differ from a plain program's by a relative error of at most 0.00018.
Values sent between devices are 32-bit elements; how exact they have to be, the bound alone decides.
No kernel may reach another device: no remote copies, remote signals or barrier semaphores. Data moves between devices by JAX's collectives and lax.ppermute only.
A program may use at most 128 MiB of HBM per device.

v0:
```python
import jax
import jax.numpy as jnp
from jax import lax
from jax.experimental import pallas as pl
from jax.experimental.pallas import tpu as pltpu
from jax.sharding import Mesh
from jax.sharding import PartitionSpec as P


F32 = jnp.float32
BF16 = jnp.bfloat16
AXES = ("row", "column", "depth", "core")
CHIPS = ("row", "column", "depth")
ITERS = 3
HALO = 128
REACH = 64
WIN = 256
STEP = WIN - REACH
SHIFT = 4.5
ROUNDS = 8
GUARD = 0.01
SMALL = 128
SPAN = 80
BATCH = 8
EDGE = 192


def dot(a, b, dims=((1,), (0,))):
    return lax.dot_general(a, b, (dims, ((), ())), preferred_element_type=F32)


def halves(x):
    high = x.astype(BF16)
    return high, (x - high.astype(F32)).astype(BF16)


def dot3(ah, al, bh, bl, dims=((1,), (0,))):
    return dot(ah, bh, dims) + (dot(ah, bl, dims) + dot(al, bh, dims))


def full_dot(a, b):
    return lax.dot_general(
        a, b, (((1,), (0,)), ((), ())), preferred_element_type=F32, precision=lax.Precision.HIGHEST
    )


def iota(shape, dim):
    return lax.broadcasted_iota(jnp.int32, shape, dim)


def in_vmem(count):
    return [pl.BlockSpec(memory_space=pltpu.VMEM)] * count


def assemble_kernel(
    group_ref, first_ref, stiff_ref, place_ref, offset_ref, diag_ref, out_ref,
    rows_ref, small_ref, block_ref, lane_ref,
):
    slots, _, tiles = stiff_ref.shape
    windows = out_ref.shape[0]
    lanes = BATCH * slots
    one = lambda mask: jnp.where(mask, 1.0, 0.0).astype(BF16)
    block_ref[...] = one(iota((lanes, lanes), 0) // slots == iota((lanes, lanes), 1) // slots)
    for t in range(BATCH):
        lane_ref[t * SPAN : (t + 1) * SPAN] = one(iota((SPAN, lanes), 1) // slots == t)

    def clear(g, carry):
        small_ref[g] = jnp.zeros((SMALL, SMALL), F32)
        return carry

    lax.fori_loop(0, small_ref.shape[0], clear, 0)
    for i in range(slots):
        plane = stiff_ref[i]
        stacked = jnp.concatenate([plane] * (128 // slots), axis=0)
        rows_ref[pl.ds(i, tiles, stride=slots), :] = stacked.T

    row_in_window = iota((SMALL, lanes), 0)
    row_in_span = iota((SPAN, lanes), 0)

    def batch(b, carry):
        base = pl.multiple_of(b * lanes, lanes)
        parts = halves(rows_ref[pl.ds(base, lanes), :])
        block = block_ref[...]
        wide = [jnp.concatenate([part] * (lanes // 128), axis=1) * block for part in parts]
        hot = one(row_in_window == place_ref[pl.ds(b, 1), :])
        both = dot(jnp.concatenate(wide, axis=0), hot, ((1,), (1,)))
        uh, ul = halves(both[:lanes] + both[lanes:])
        match = one(row_in_span == offset_ref[pl.ds(b, 1), :])
        pick = jnp.concatenate([match] * BATCH, axis=0) * lane_ref[...]
        full = dot(pick, jnp.concatenate([uh, ul], axis=1))
        full = full[:, :SMALL] + full[:, SMALL:]
        for t in range(BATCH):
            g = group_ref[b * BATCH + t]
            r = pl.multiple_of(first_ref[b * BATCH + t], 16)
            small_ref[g, pl.ds(r, SPAN), :] += full[t * SPAN : (t + 1) * SPAN]
        return carry

    lax.fori_loop(0, tiles // BATCH, batch, 0)

    eye = iota((WIN, WIN), 0) == iota((WIN, WIN), 1)
    gap = jnp.zeros((SMALL, REACH), F32)

    def gather(g, carry):
        out_ref[g] = jnp.where(eye, diag_ref[pl.ds(g, 1), :], 0.0)
        out_ref[g, :SMALL, :SMALL] += small_ref[3 * g]
        middle = jnp.concatenate([gap, small_ref[3 * g + 1], gap], axis=1)
        out_ref[g, REACH : REACH + SMALL, :] += middle
        out_ref[g, SMALL:, SMALL:] += small_ref[3 * g + 2]
        return carry

    lax.fori_loop(0, windows, gather, 0)


def assemble(tile_stiff, tile_nodes, node_shift):
    tiles, slots = tile_nodes.shape
    ext = node_shift.shape[0] + 2 * HALO
    windows = ext // STEP
    smalls = ext // REACH
    lowest = jnp.min(tile_nodes, axis=1)
    group = jnp.minimum(lowest // REACH, smalls - 1)
    first = jnp.minimum((lowest - group * REACH) // 16 * 16, REACH - 16)
    place = jnp.where(tile_nodes == ext, -1, tile_nodes - group[:, None] * REACH)
    offset = jnp.where(tile_nodes == ext, -1, place - first[:, None])
    diag = jnp.pad(node_shift - SHIFT, (HALO, HALO)).reshape(windows, STEP)
    diag = jnp.pad(diag, ((0, 0), (0, WIN - STEP)))
    lanes = BATCH * slots
    smem = pl.BlockSpec(memory_space=pltpu.SMEM)
    return pl.pallas_call(
        assemble_kernel,
        out_shape=jax.ShapeDtypeStruct((windows, WIN, WIN), F32),
        in_specs=[smem, smem] + in_vmem(4),
        out_specs=pl.BlockSpec(memory_space=pltpu.VMEM),
        scratch_shapes=[
            pltpu.VMEM((tiles * slots, 128), F32),
            pltpu.VMEM((smalls, SMALL, SMALL), F32),
            pltpu.VMEM((lanes, lanes), BF16),
            pltpu.VMEM((BATCH * SPAN, lanes), BF16),
        ],
        compiler_params=pltpu.CompilerParams(vmem_limit_bytes=28 << 20),
        name="assemble",
    )(
        group,
        first,
        jnp.transpose(tile_stiff, (1, 2, 0)),
        place.reshape(-1, lanes),
        offset.reshape(-1, lanes),
        diag,
    )


LOW = 2 * HALO


def powers_kernel(
    valid_ref, own_ref, left_ref, right_ref, band_ref, lband_ref, rband_ref,
    k1_ref, k2_ref, mine_ref, theirs_ref,
    bh_ref, bl_ref, lh_ref, ll_ref, rh_ref, rl_ref,
    vh_ref, vl_ref, wh_ref, wl_ref, y_ref,
):
    own, cols = own_ref.shape
    windows = band_ref.shape[0]
    frame = vh_ref.shape[0]
    high = LOW + own

    def split_band(g, carry):
        bh_ref[g], bl_ref[g] = halves(band_ref[g])
        return carry

    lax.fori_loop(0, windows, split_band, 0)
    lh_ref[...], ll_ref[...] = halves(lband_ref[...])
    rh_ref[...], rl_ref[...] = halves(rband_ref[...])

    zero = jnp.zeros((LOW - EDGE, cols), BF16)
    tail = jnp.zeros((frame - high - EDGE, cols), BF16)
    for ref in (vh_ref, vl_ref):
        ref[: LOW - EDGE] = zero
        ref[high + EDGE :] = tail
    vh_ref[LOW - EDGE : LOW], vl_ref[LOW - EDGE : LOW] = halves(left_ref[...])
    vh_ref[high : high + EDGE], vl_ref[high : high + EDGE] = halves(right_ref[...])
    chunk = 256

    def split_own(i, carry):
        at = pl.multiple_of(i * chunk, chunk)
        h, l = halves(own_ref[pl.ds(at, chunk), :])
        vh_ref[pl.ds(LOW + at, chunk), :] = h
        vl_ref[pl.ds(LOW + at, chunk), :] = l
        return carry

    lax.fori_loop(0, own // chunk, split_own, 0)

    def apply(xh_ref, xl_ref):
        y_ref[...] = jnp.zeros_like(y_ref)

        def window(g, carry):
            at = pl.multiple_of(HALO + g * STEP, 64)
            xh = xh_ref[pl.ds(at, WIN), :]
            xl = xl_ref[pl.ds(at, WIN), :]
            y_ref[pl.ds(at, WIN), :] += dot3(bh_ref[g], bl_ref[g], xh, xl)
            return carry

        lax.fori_loop(0, windows, window, 0)

        def extra(h_ref, l_ref, lo, rows, out, at):
            y_ref[out : out + rows] += dot3(
                h_ref[lo : lo + rows], l_ref[lo : lo + rows],
                xh_ref[at : at + WIN], xl_ref[at : at + WIN],
            )

        extra(lh_ref, ll_ref, 0, 128, HALO, 0)
        extra(lh_ref, ll_ref, 128, 192, HALO + 64, HALO + 64)
        extra(rh_ref, rl_ref, 0, 256, own + HALO, own + HALO)
        extra(rh_ref, rl_ref, 256, 64, own + HALO + STEP, own + HALO + STEP)

    def keep(oh_ref, ol_ref):
        oh_ref[:HALO] = jnp.zeros((HALO, cols), BF16)
        ol_ref[:HALO] = jnp.zeros((HALO, cols), BF16)
        oh_ref[high + HALO :] = jnp.zeros((frame - high - HALO, cols), BF16)
        ol_ref[high + HALO :] = jnp.zeros((frame - high - HALO, cols), BF16)
        lower = jnp.where(valid_ref[0] > 0, y_ref[HALO:LOW], 0.0)
        upper = jnp.where(valid_ref[1] > 0, y_ref[high : high + HALO], 0.0)
        oh_ref[HALO:LOW], ol_ref[HALO:LOW] = halves(lower)
        oh_ref[high : high + HALO], ol_ref[high : high + HALO] = halves(upper)

        def split(i, carry):
            at = pl.multiple_of(LOW + i * chunk, chunk)
            h, l = halves(y_ref[pl.ds(at, chunk), :])
            oh_ref[pl.ds(at, chunk), :] = h
            ol_ref[pl.ds(at, chunk), :] = l
            return carry

        lax.fori_loop(0, own // chunk, split, 0)

    tn = ((0,), (0,))

    def put(n, value):
        here = valid_ref[2] == n // ITERS

        @pl.when(here)
        def _():
            for c in range(cols // 128):
                mine_ref[n % ITERS, c] = value[:, c * 128 : (c + 1) * 128]

        @pl.when(jnp.logical_not(here))
        def _():
            for c in range(cols // 128):
                theirs_ref[n % ITERS, c] = value[:, c * 128 : (c + 1) * 128]

    def square(n, xh_ref, xl_ref):
        xh = xh_ref[LOW:high]
        cross = dot(xh, xl_ref[LOW:high], tn)
        put(n, dot(xh, xh, tn) + (cross + cross.T))

    def product(n, xh_ref, xl_ref, zh_ref, zl_ref):
        put(n, dot3(xh_ref[LOW:high], xl_ref[LOW:high], zh_ref[LOW:high], zl_ref[LOW:high], tn))

    square(0, vh_ref, vl_ref)
    apply(vh_ref, vl_ref)
    k1_ref[...] = y_ref[LOW:high]
    keep(wh_ref, wl_ref)
    product(1, vh_ref, vl_ref, wh_ref, wl_ref)
    square(2, wh_ref, wl_ref)
    apply(wh_ref, wl_ref)
    k2_ref[...] = y_ref[LOW:high]
    keep(vh_ref, vl_ref)
    product(3, wh_ref, wl_ref, vh_ref, vl_ref)
    square(4, vh_ref, vl_ref)
    apply(vh_ref, vl_ref)
    keep(wh_ref, wl_ref)
    product(5, vh_ref, vl_ref, wh_ref, wl_ref)


def powers(vector, left, right, valid, bands):
    band, lband, rband = bands
    own, cols = vector.shape
    frame = own + 2 * LOW + 64
    full = jax.ShapeDtypeStruct((own, cols), F32)
    half = jax.ShapeDtypeStruct((ITERS, cols // 128, cols, 128), F32)
    wide = pltpu.VMEM((frame, cols), BF16)
    edge = pltpu.VMEM(lband.shape, BF16)
    return pl.pallas_call(
        powers_kernel,
        out_shape=(full, full, half, half),
        in_specs=[pl.BlockSpec(memory_space=pltpu.SMEM)] + in_vmem(6),
        out_specs=tuple(in_vmem(4)),
        compiler_params=pltpu.CompilerParams(vmem_limit_bytes=44 << 20),
        scratch_shapes=[pltpu.VMEM(band.shape, BF16)] * 2 + [edge] * 4 + [wide] * 4
        + [pltpu.VMEM((frame, cols), F32)],
        name="powers",
    )(valid, vector, left, right, band, lband, rband)


def diagonals(matrix):
    size = matrix.shape[0]
    on = jnp.where(iota((size, size), 0) == iota((size, size), 1), matrix, 0.0)
    return jnp.sum(on, axis=0, keepdims=True), jnp.sum(on, axis=1, keepdims=True)


def split_dot(a, b):
    return dot3(*halves(a), *halves(b))


def inverse_spd(matrix, mul):
    size = matrix.shape[0]
    unit = (iota((size, size), 0) == iota((size, size), 1)).astype(F32)
    along, down = diagonals(matrix)
    scale = lax.rsqrt(along) * lax.rsqrt(down)
    scaled = matrix * scale
    norm = jnp.max(jnp.sum(jnp.abs(scaled), axis=1, keepdims=True))
    factor = jnp.where(norm < 1.9, 1.0, 1.9 / norm)
    rest = unit - factor * scaled

    def going(state):
        k, worst, _, _ = state
        return (k < 40) & (worst > 1e-8)

    def step(state):
        k, _, total, power = state
        both = mul(jnp.concatenate([total, power], axis=0), power)
        total = total + both[:size]
        power = both[size:]
        return k + 1, jnp.max(jnp.abs(power)), total, power

    rounds, worst, total, _ = lax.while_loop(
        going, step, (0, jnp.max(jnp.abs(rest)), unit * factor, rest)
    )
    return total * scale, worst, rounds


def ratio(left, whole):
    return jnp.min(diagonals(left)[0] / diagonals(whole)[0])


def galerkin_kernel(core_ref, mine_ref, theirs_ref, out_ref, good_ref, mom_ref):
    parts = mine_ref.shape[1]

    def unpack(source_ref, start):
        for n in range(ITERS):
            mom_ref[start + n] = jnp.concatenate([source_ref[n, c] for c in range(parts)], axis=1)

    @pl.when(core_ref[0] == 0)
    def _():
        unpack(mine_ref, 0)
        unpack(theirs_ref, ITERS)

    @pl.when(core_ref[0] != 0)
    def _():
        unpack(theirs_ref, 0)
        unpack(mine_ref, ITERS)

    m = [mom_ref[n] for n in range(2 * ITERS)]
    m = [0.5 * (x + x.T) for x in m]
    h = [m[n + 1] + SHIFT * m[n] for n in range(2 * ITERS - 1)]
    size = m[0].shape[0]

    def right_of(inverse, *targets):
        wide = split_dot(inverse, jnp.concatenate(targets, axis=1))
        return [wide[:, n * size : (n + 1) * size] for n in range(len(targets))]

    s0, w0, k0 = inverse_spd(h[0], split_dot)
    z01, z02, z0m = right_of(s0, h[1], h[2], m[0])
    lower = split_dot(
        jnp.concatenate([h[1], h[2]], axis=0), jnp.concatenate([z01, z02, z0m], axis=1)
    )
    first = h[2] - lower[:size, :size]
    cross = h[3] - lower[:size, size : 2 * size]
    m1 = m[1] - lower[:size, 2 * size :]
    last = h[4] - lower[size:, size : 2 * size]
    m2 = m[2] - lower[size:, 2 * size :]
    first = 0.5 * (first + first.T)
    s1, w1, k1 = inverse_spd(first, split_dot)
    z12, z1m = right_of(s1, cross, m1)
    lower = split_dot(cross.T, jnp.concatenate([z12, z1m], axis=1))
    rest = last - lower[:, :size]
    rest = 0.5 * (rest + rest.T)
    m2 = m2 - lower[:, size:]
    s2, w2, k2 = inverse_spd(rest, split_dot)
    y2 = split_dot(s2, m2)
    y1 = z1m - split_dot(z12, y2)
    y0 = z0m - split_dot(jnp.concatenate([z01, z02], axis=1), jnp.concatenate([y1, y2], axis=0))
    out_ref[:size] = y0
    out_ref[size : 2 * size] = y1
    out_ref[2 * size :] = y2
    share = jnp.minimum(ratio(first, h[2]), ratio(rest, h[4]))
    rounds = jnp.maximum(k0, jnp.maximum(k1, k2))
    worst = jnp.maximum(w0, jnp.maximum(w1, w2))
    good_ref[0] = jnp.where((share > GUARD) & (worst <= 1e-8) & (rounds <= ROUNDS), 1, 0)


def galerkin(core, mine, theirs):
    size = mine.shape[2]
    smem = pl.BlockSpec(memory_space=pltpu.SMEM)
    return pl.pallas_call(
        galerkin_kernel,
        out_shape=(jax.ShapeDtypeStruct((ITERS * size, size), F32), jax.ShapeDtypeStruct((1,), jnp.int32)),
        in_specs=[smem] + in_vmem(2),
        out_specs=(pl.BlockSpec(memory_space=pltpu.VMEM), smem),
        scratch_shapes=[pltpu.VMEM((2 * ITERS, size, size), F32)],
        compiler_params=pltpu.CompilerParams(vmem_limit_bytes=32 << 20),
        name="galerkin",
    )(core, mine, theirs)


def solve_kernel(matrix_ref, target_ref, out_ref):
    matrix = matrix_ref[...]
    matrix = 0.5 * (matrix + matrix.T)
    inverse, _, _ = inverse_spd(matrix, full_dot)
    guess = full_dot(inverse, target_ref[...])
    out_ref[...] = guess + full_dot(inverse, target_ref[...] - full_dot(matrix, guess))


def solve(matrix, target):
    return pl.pallas_call(
        solve_kernel,
        out_shape=jax.ShapeDtypeStruct(target.shape, F32),
        in_specs=in_vmem(2),
        out_specs=in_vmem(1)[0],
        name="solve",
    )(matrix, target)


def total_of(mine, theirs):
    shape = mine.shape
    chips = lax.axis_size(CHIPS)
    other = [(0, 1), (1, 0)]
    pair = mine + lax.ppermute(theirs, "core", other)
    pair = pair.reshape(chips, -1, 128)
    own = lax.all_to_all(pair, CHIPS, 0, 0, tiled=True).sum(axis=0)
    gathered = lax.all_to_all(jnp.broadcast_to(own[None], pair.shape), CHIPS, 0, 0, tiled=True)
    gathered = gathered.reshape(shape)
    return gathered, lax.ppermute(gathered, "core", other)


def both_ways(to_right, to_left):
    count = lax.axis_size(AXES)
    up = [(i, i + 1) for i in range(count - 1)]
    return lax.ppermute(to_right, AXES, up), lax.ppermute(to_left, AXES, [(b, a) for a, b in up])


def halo_of(vector):
    return both_ways(vector[-EDGE:], vector[:EDGE])


def plain_cg(right_side, valid, bands):
    def times(a, b):
        return jnp.dot(a, b, preferred_element_type=F32, precision=lax.Precision.HIGHEST)

    def gram_of(parts):
        return jnp.concatenate([parts[0], parts[1]], axis=1)

    def step(k, state):
        answer, residual, direction, gram = state
        on_direction = k % 2 == 0
        vector = jnp.where(on_direction, direction, residual)
        image, _, mine, theirs = powers(vector, *halo_of(vector), valid, bands)
        low, high = total_of(mine, theirs)
        low = jnp.where(valid[2] == 0, low, high)
        square = gram_of(low[0])
        gram = jnp.where(k == 0, square, gram)
        dir_gram = gram_of(low[1]) + SHIFT * square
        factor = solve(
            jnp.where(on_direction, dir_gram, gram), jnp.where(on_direction, gram, square)
        )
        along = times(direction, factor)
        applied = times(image + SHIFT * vector, factor)
        answer = jnp.where(on_direction, answer + along, answer)
        direction = jnp.where(on_direction, direction, residual + along)
        residual = jnp.where(on_direction, residual - applied, residual)
        return answer, residual, direction, jnp.where(on_direction, gram, square)

    state = (jnp.zeros_like(right_side), right_side, right_side, jnp.zeros((right_side.shape[1],) * 2, F32))
    return lax.fori_loop(0, 2 * ITERS - 1, step, state)[0]


def loads_kernel(nodes_ref, load_ref, high_ref, low_ref):
    groups, pairs = nodes_ref.shape
    slots = 8
    support = pairs // slots
    blocks = high_ref.shape[1] // 128
    own_lane = iota((slots, pairs), 1) // support == iota((slots, pairs), 0)
    row = iota((128, pairs), 0)

    def half_group(g):
        nodes = nodes_ref[pl.ds(g, 1), :]
        hot = jnp.where(row == nodes % 128, 1.0, 0.0).astype(BF16)
        block = jnp.broadcast_to(nodes // 128, (slots, pairs))
        terms = []
        for k in range(3):
            spread = jnp.where(own_lane, load_ref[k, pl.ds(g, 1), :], 0.0)
            high = spread.astype(BF16).astype(F32)
            terms.append((high, spread - high))
        rows = []
        for c in range(blocks):
            hit = block == c
            for high, low in terms:
                rows.append(
                    jnp.concatenate([jnp.where(hit, high, 0.0), jnp.where(hit, low, 0.0)], axis=1)
                )
        left = jnp.concatenate(rows, axis=0).astype(BF16)
        return dot(left, jnp.concatenate([hot, hot], axis=1), ((1,), (1,)))

    def group(g, carry):
        first = half_group(2 * g)
        second = half_group(2 * g + 1)
        total = groups * slots
        for c in range(blocks):
            for k in range(3):
                at = (c * 3 + k) * slots
                value = jnp.concatenate([first[at : at + slots], second[at : at + slots]], axis=0)
                high, low = halves(value)
                to = pl.multiple_of(k * total + g * 2 * slots, 16)
                high_ref[pl.ds(to, 2 * slots), c * 128 : (c + 1) * 128] = high
                low_ref[pl.ds(to, 2 * slots), c * 128 : (c + 1) * 128] = low
        return carry

    lax.fori_loop(0, groups // 2, group, 0)


def load_matrix(slot_nodes, slot_load, rows):
    support, slots = slot_nodes.shape
    groups = slots * support // 128
    nodes = slot_nodes.T.reshape(groups, 128)
    loads = slot_load.reshape(support, slots, 3).transpose(2, 1, 0).reshape(3, groups, 128)
    out = jax.ShapeDtypeStruct((3 * slots, rows), BF16)
    return pl.pallas_call(
        loads_kernel,
        out_shape=(out, out),
        in_specs=in_vmem(2),
        out_specs=tuple(in_vmem(2)),
        compiler_params=pltpu.CompilerParams(vmem_limit_bytes=20 << 20),
        name="loads",
    )(nodes, loads)


def rows_of(wh, wl, xh, xl, out_ref):
    full = dot3(wh, wl, xh, xl)
    cols = full.shape[1]
    slots = full.shape[0] // 3
    for k in range(3):
        out_ref[:, k * cols : (k + 1) * cols] += full[k * slots : (k + 1) * slots]


def combine_kernel(k0_ref, k1_ref, k2_ref, c_ref, wh_ref, wl_ref, x_ref, out_ref, ch_ref, cl_ref):
    size = c_ref.shape[1]

    @pl.when(pl.program_id(0) == 0)
    def _():
        ch_ref[...], cl_ref[...] = halves(c_ref[...])
        out_ref[...] = jnp.zeros_like(out_ref)

    total = jnp.zeros(x_ref.shape, F32)
    for n, ref in enumerate((k0_ref, k1_ref, k2_ref)):
        ah, al = halves(ref[...])
        at = n * size
        total = total + dot3(ah, al, ch_ref[at : at + size], cl_ref[at : at + size])
    x_ref[...] = total
    rows_of(wh_ref[...], wl_ref[...], *halves(total), out_ref)


def leading_kernel(x_ref, wh_ref, wl_ref, out_ref):
    @pl.when(pl.program_id(0) == 0)
    def _():
        out_ref[...] = jnp.zeros_like(out_ref)

    rows_of(wh_ref[...], wl_ref[...], *halves(x_ref[...]), out_ref)


CHUNK = 512


def combine(k0, k1, k2, coef, weights):
    rows, cols = k0.shape
    loads = weights[0].shape[0]
    block = pl.BlockSpec((CHUNK, cols), lambda i: (i, 0))
    weight = pl.BlockSpec((loads, CHUNK), lambda i: (0, i))
    out = (loads // 3, 3 * cols)
    return pl.pallas_call(
        combine_kernel,
        grid=(rows // CHUNK,),
        out_shape=(jax.ShapeDtypeStruct((rows, cols), F32), jax.ShapeDtypeStruct(out, F32)),
        in_specs=[block] * 3 + [pl.BlockSpec(coef.shape, lambda i: (0, 0)), weight, weight],
        out_specs=(block, pl.BlockSpec(out, lambda i: (0, 0))),
        scratch_shapes=[pltpu.VMEM(coef.shape, BF16)] * 2,
        compiler_params=pltpu.CompilerParams(vmem_limit_bytes=32 << 20),
        name="combine",
    )(k0, k1, k2, coef, *weights)


def leading(x, weights):
    rows, cols = x.shape
    loads = weights[0].shape[0]
    weight = pl.BlockSpec((loads, CHUNK), lambda i: (0, i))
    out = (loads // 3, 3 * cols)
    return pl.pallas_call(
        leading_kernel,
        grid=(rows // CHUNK,),
        out_shape=jax.ShapeDtypeStruct(out, F32),
        in_specs=[pl.BlockSpec((CHUNK, cols), lambda i: (i, 0)), weight, weight],
        out_specs=pl.BlockSpec(out, lambda i: (0, 0)),
        name="leading",
    )(x, *weights)


def exact_path(right_side, valid, bands, weights):
    answer = plain_cg(right_side, valid, bands)
    return answer, leading(answer, weights)


def one_device(right_side, tile_stiff, tile_nodes, node_shift, slot_nodes, slot_load, dipole_slot):
    count = lax.axis_size(AXES)
    index = lax.axis_index(AXES)
    core = lax.axis_index("core")
    valid = jnp.stack([index > 0, index < count - 1, core]).astype(jnp.int32)
    left, right = halo_of(right_side)
    band = assemble(tile_stiff, tile_nodes, node_shift)
    to_right = jnp.concatenate([band[-2, 128:], band[-1, :192]], axis=0)
    to_left = jnp.concatenate([band[0], band[1, :64]], axis=0)
    bands = (band, *both_ways(to_right, to_left))
    weights = load_matrix(slot_nodes, slot_load, right_side.shape[0])
    k1, k2, mine, theirs = powers(right_side, left, right, valid, bands)
    coef, good = galerkin(core[None], *total_of(mine, theirs))
    answer, rows = lax.cond(
        good[0] > 0,
        lambda: combine(right_side, k1, k2, coef, weights),
        lambda: exact_path(right_side, valid, bands, weights),
    )
    slots, wide = rows.shape
    received = lax.all_to_all(rows.reshape(count, slots // count, wide), AXES, 0, 0, tiled=True)
    picked = received.reshape(slots, wide)[dipole_slot]
    leadfield = picked.reshape(-1, 3, wide // 3).transpose(1, 0, 2)
    return answer, leadfield


def solution(mesh):
    rows, depth = mesh.devices.shape
    outer = 4 if rows % 4 == 0 else 1
    flat = Mesh(mesh.devices.reshape(outer, rows // outer, depth // 2, 2), AXES)
    return jax.shard_map(
        one_device,
        mesh=flat,
        in_specs=(
            P(AXES, None),
            P(AXES, None, None),
            P(AXES, None),
            P(AXES),
            P(None, AXES),
            P(None, AXES),
            P(AXES),
        ),
        out_specs=(P(AXES, None), P(None, AXES, None)),
        check_vma=False,
    )
```

profile of v0, /device:TPU:1, one launch (start us, length us, event | category | flops | bytes accessed | tf_op | source)
XLA Modules:
  0.0 758.0 jit_solution(9736310199571398155)
XLA Ops:
  2.9 24.3 %assemble.1.band_ref = f32[12,256,256]{2,1,0:T(8,128)S(1)} custom-call(s32[256]{0:T(256)S(1)} %get-tuple-element.363.group_ref, s32[256]{0:T(256)S(1)} %multiply_minimum_fusion.first_ref, f32[32,32,256]{2,1,0:T(8,128)S(1)} %bitcast.51, s32[32,256]{1,0:T(8,128)S(1)} %reshape.111.place_ref, s32[32,256]{1,0:T(8,128)S(1)} %reshape.112.offset_ref, ...), custom_call_target="tpu_custom_call" | custom-call | tf_op jit(solution)/shard_map/assemble/pallas_call | solution.py:128
  27.3 3.3 collective-permute-start.7
  31.4 3.5 collective-permute-start.6
  41.4 4.0 collective-permute-done.5.right_ref
  45.3 25.2 %powers.9 = (f32[2048,256]{1,0:T(8,128)}, f32[2048,256]{1,0:T(8,128)}, f32[3,2,256,128]{3,2,1,0:T(8,128)S(1)}, f32[3,2,256,128]{3,2,1,0:T(8,128)S(1)}) custom-call(s32[3]{0:T(128)S(1)} %pad_add_fusion.valid_ref, f32[2048,256]{1,0:T(8,128)S(1)} %copy.45.own_ref, f32[192,256]{1,0:T(8,128)S(1)} %collective-permute-done.4.left_ref, ...), custom_call_target="tpu_custom_call" | custom-call | tf_op jit(solution)/shard_map/powers/pallas_call | solution.py:280
  73.1 33.5 %all_to_all.43 = f32[64,24,128]{2,1,0:T(8,128)S(1)} all-to-all(f32[64,24,128]{2,1,0:T(8,128)S(1)} %bitcast.55), channel_id=1, replica_groups=mesh['row'=4,'column'=4,'depth'=4,'core'=2] {'row','column','depth'}, dimensions={0} | all-to-all | bytes 1572864 | tf_op jit(solution)/shard_map/all_to_all | solution.py:427
  106.7 18.4 %all_to_all.44 = f32[64,24,128]{2,1,0:T(8,128)S(1)} all-to-all(f32[64,24,128]{2,1,0:T(8,128)S(1)} %broadcast_in_dim.40), channel_id=1, replica_groups=mesh['row'=4,'column'=4,'depth'=4,'core'=2] {'row','column','depth'}, dimensions={0} | all-to-all | bytes 1572864 | tf_op jit(solution)/shard_map/all_to_all | solution.py:428
  125.1 3.1 collective-permute-start.9
  128.9 7.1 loads.1
  136.0 21.7 %galerkin.1 = (f32[768,256]{1,0:T(8,128)}, s32[1]{0:T(128)}) custom-call(s32[1]{0:T(128)} %bitcast.core_ref, f32[3,2,256,128]{3,2,1,0:T(8,128)S(1)} %bitcast.50, f32[3,2,256,128]{3,2,1,0:T(8,128)S(1)} %collective-permute-done.9.theirs_ref), custom_call_target="tpu_custom_call" | custom-call | tf_op jit(solution)/shard_map/galerkin/pallas_call | solution.py:392
  158.3 575.7 %conditional.1 = ((f32[2048,256]{1,0:T(8,128)}, f32[256,768]{1,0:T(8,128)S(1)})) conditional(s32[]{:T(128)} %bitcast.10, (s32[]{:T(128)}, s32[3]{0:T(128)S(1)}, f32[12,256,256]{2,1,0:T(8,128)}, f32[320,256]{1,0:T(8,128)S(1)}, f32[320,256]{1,0:T(8,128)S(1)}, /*index=5*/f32[2048,256]{1,0:T(8,128)}, bf16[768,2048]{1,0:T(8,128)(2,1)}, ...), branch_computations={%region_2.6_spmd, %region_6.7_spmd} | conditional | flops 3228103680 | bytes 125330232 | solution.py:621
  158.4 3.2 copy.27
  161.6 566.5 %while.21 = (s32[]{:T(128)}, f32[2048,256]{1,0:T(8,128)}, f32[2048,256]{1,0:T(8,128)S(1)}, f32[2048,256]{1,0:T(8,128)}, f32[256,256]{1,0:T(8,128)S(1)}, /*index=...) while((s32[]{:T(128)}, f32[2048,256]{1,0:T(8,128)}, ...), condition=%wide.region_5.5_spmd.clone, body=%wide.region_3.4_spmd.clone.sunk | while | flops 3228103680 | bytes 112747136 | solution.py:471
  161.8 2.5 copy.46
  170.6 4.4 collective-permute-done.1.right_ref
  175.0 23.2 %powers.10 = (f32[2048,256]{1,0:T(8,128)S(1)}, f32[2048,256]{1,0:T(8,128)}, f32[3,2,256,128]{3,2,1,0:T(8,128)S(1)}, f32[3,2,256,128]{3,2,1,0:T(8,128)S(1)}) custom-call(s32[3]{0:T(128)S(1)} %get-tuple-element.499.valid_ref, f32[2048,256]{1,0:T(8,128)S(1)} %broadcast_select_fusion.5.own_ref, f32[192,256]{1,0:T(8,128)S(1)} %collective-permute-done.left_ref, ...), custom_call_target="tpu_custom_call" | custom-call | tf_op jit(solution)/shard_map/cond/branch_0_fun/while/body/eval_jaxpr/powers/pallas_call | solution.py:280
  200.5 26.9 %all_to_all.45 = f32[64,24,128]{2,1,0:T(8,128)S(1)} all-to-all(f32[64,24,128]{2,1,0:T(8,128)S(1)} %bitcast.54), channel_id=1, replica_groups=mesh['row'=4,'column'=4,'depth'=4,'core'=2] {'row','column','depth'}, dimensions={0} | all-to-all | bytes 1572864 | tf_op jit(solution)/shard_map/cond/branch_0_fun/while/body/eval_jaxpr/all_to_all | solution.py:427
  227.6 18.4 %all_to_all.46 = f32[64,24,128]{2,1,0:T(8,128)S(1)} all-to-all(f32[64,24,128]{2,1,0:T(8,128)S(1)} %broadcast_in_dim.48), channel_id=1, replica_groups=mesh['row'=4,'column'=4,'depth'=4,'core'=2] {'row','column','depth'}, dimensions={0} | all-to-all | bytes 1572864 | tf_op jit(solution)/shard_map/cond/branch_0_fun/while/body/eval_jaxpr/all_to_all | solution.py:428
  246.0 3.1 collective-permute-start.3
  253.2 11.0 %solve.8 = f32[256,256]{1,0:T(8,128)} custom-call(f32[256,256]{1,0:T(8,128)} %get-tuple-element.460.matrix_ref, f32[256,256]{1,0:T(8,128)S(1)} %get-tuple-element.497.target_ref), custom_call_target="tpu_custom_call" | custom-call | tf_op jit(solution)/shard_map/cond/branch_0_fun/while/body/eval_jaxpr/solve/pallas_call | solution.py:412
  264.2 4.4 subtract_select_fusion.4
  268.6 5.7 add_select_fusion.3
  275.7 2.5 copy.46
  281.5 2.4 collective-permute-start.1
  284.1 4.4 collective-permute-done.1.right_ref
  288.5 23.2 %powers.10 = (f32[2048,256]{1,0:T(8,128)S(1)}, f32[2048,256]{1,0:T(8,128)}, f32[3,2,256,128]{3,2,1,0:T(8,128)S(1)}, f32[3,2,256,128]{3,2,1,0:T(8,128)S(1)}) custom-call(s32[3]{0:T(128)S(1)} %get-tuple-element.499.valid_ref, f32[2048,256]{1,0:T(8,128)S(1)} %broadcast_select_fusion.5.own_ref, f32[192,256]{1,0:T(8,128)S(1)} %collective-permute-done.left_ref, ...), custom_call_target="tpu_custom_call" | custom-call | tf_op jit(solution)/shard_map/cond/branch_0_fun/while/body/eval_jaxpr/powers/pallas_call | solution.py:280
  314.1 26.5 %all_to_all.45 = f32[64,24,128]{2,1,0:T(8,128)S(1)} all-to-all(f32[64,24,128]{2,1,0:T(8,128)S(1)} %bitcast.54), channel_id=1, replica_groups=mesh['row'=4,'column'=4,'depth'=4,'core'=2] {'row','column','depth'}, dimensions={0} | all-to-all | bytes 1572864 | tf_op jit(solution)/shard_map/cond/branch_0_fun/while/body/eval_jaxpr/all_to_all | solution.py:427
  340.7 18.4 %all_to_all.46 = f32[64,24,128]{2,1,0:T(8,128)S(1)} all-to-all(f32[64,24,128]{2,1,0:T(8,128)S(1)} %broadcast_in_dim.48), channel_id=1, replica_groups=mesh['row'=4,'column'=4,'depth'=4,'core'=2] {'row','column','depth'}, dimensions={0} | all-to-all | bytes 1572864 | tf_op jit(solution)/shard_map/cond/branch_0_fun/while/body/eval_jaxpr/all_to_all | solution.py:428
  359.1 3.1 collective-permute-start.3
  366.3 11.0 %solve.8 = f32[256,256]{1,0:T(8,128)} custom-call(f32[256,256]{1,0:T(8,128)} %get-tuple-element.460.matrix_ref, f32[256,256]{1,0:T(8,128)S(1)} %get-tuple-element.497.target_ref), custom_call_target="tpu_custom_call" | custom-call | tf_op jit(solution)/shard_map/cond/branch_0_fun/while/body/eval_jaxpr/solve/pallas_call | solution.py:412
  377.3 4.4 subtract_select_fusion.4
  381.8 5.7 add_select_fusion.3
  388.8 2.5 copy.46
  394.7 2.4 collective-permute-start.1
  397.2 4.4 collective-permute-done.1.right_ref
  401.6 23.2 %powers.10 = (f32[2048,256]{1,0:T(8,128)S(1)}, f32[2048,256]{1,0:T(8,128)}, f32[3,2,256,128]{3,2,1,0:T(8,128)S(1)}, f32[3,2,256,128]{3,2,1,0:T(8,128)S(1)}) custom-call(s32[3]{0:T(128)S(1)} %get-tuple-element.499.valid_ref, f32[2048,256]{1,0:T(8,128)S(1)} %broadcast_select_fusion.5.own_ref, f32[192,256]{1,0:T(8,128)S(1)} %collective-permute-done.left_ref, ...), custom_call_target="tpu_custom_call" | custom-call | tf_op jit(solution)/shard_map/cond/branch_0_fun/while/body/eval_jaxpr/powers/pallas_call | solution.py:280
  427.2 26.5 %all_to_all.45 = f32[64,24,128]{2,1,0:T(8,128)S(1)} all-to-all(f32[64,24,128]{2,1,0:T(8,128)S(1)} %bitcast.54), channel_id=1, replica_groups=mesh['row'=4,'column'=4,'depth'=4,'core'=2] {'row','column','depth'}, dimensions={0} | all-to-all | bytes 1572864 | tf_op jit(solution)/shard_map/cond/branch_0_fun/while/body/eval_jaxpr/all_to_all | solution.py:427
  453.8 18.4 %all_to_all.46 = f32[64,24,128]{2,1,0:T(8,128)S(1)} all-to-all(f32[64,24,128]{2,1,0:T(8,128)S(1)} %broadcast_in_dim.48), channel_id=1, replica_groups=mesh['row'=4,'column'=4,'depth'=4,'core'=2] {'row','column','depth'}, dimensions={0} | all-to-all | bytes 1572864 | tf_op jit(solution)/shard_map/cond/branch_0_fun/while/body/eval_jaxpr/all_to_all | solution.py:428
  472.2 3.1 collective-permute-start.3
  479.4 11.0 %solve.8 = f32[256,256]{1,0:T(8,128)} custom-call(f32[256,256]{1,0:T(8,128)} %get-tuple-element.460.matrix_ref, f32[256,256]{1,0:T(8,128)S(1)} %get-tuple-element.497.target_ref), custom_call_target="tpu_custom_call" | custom-call | tf_op jit(solution)/shard_map/cond/branch_0_fun/while/body/eval_jaxpr/solve/pallas_call | solution.py:412
  490.4 4.4 subtract_select_fusion.4
  494.9 5.7 add_select_fusion.3
  501.9 2.5 copy.46
  510.4 4.4 collective-permute-done.1.right_ref
  514.8 23.2 %powers.10 = (f32[2048,256]{1,0:T(8,128)S(1)}, f32[2048,256]{1,0:T(8,128)}, f32[3,2,256,128]{3,2,1,0:T(8,128)S(1)}, f32[3,2,256,128]{3,2,1,0:T(8,128)S(1)}) custom-call(s32[3]{0:T(128)S(1)} %get-tuple-element.499.valid_ref, f32[2048,256]{1,0:T(8,128)S(1)} %broadcast_select_fusion.5.own_ref, f32[192,256]{1,0:T(8,128)S(1)} %collective-permute-done.left_ref, ...), custom_call_target="tpu_custom_call" | custom-call | tf_op jit(solution)/shard_map/cond/branch_0_fun/while/body/eval_jaxpr/powers/pallas_call | solution.py:280
  540.3 26.5 %all_to_all.45 = f32[64,24,128]{2,1,0:T(8,128)S(1)} all-to-all(f32[64,24,128]{2,1,0:T(8,128)S(1)} %bitcast.54), channel_id=1, replica_groups=mesh['row'=4,'column'=4,'depth'=4,'core'=2] {'row','column','depth'}, dimensions={0} | all-to-all | bytes 1572864 | tf_op jit(solution)/shard_map/cond/branch_0_fun/while/body/eval_jaxpr/all_to_all | solution.py:427
  566.9 18.4 %all_to_all.46 = f32[64,24,128]{2,1,0:T(8,128)S(1)} all-to-all(f32[64,24,128]{2,1,0:T(8,128)S(1)} %broadcast_in_dim.48), channel_id=1, replica_groups=mesh['row'=4,'column'=4,'depth'=4,'core'=2] {'row','column','depth'}, dimensions={0} | all-to-all | bytes 1572864 | tf_op jit(solution)/shard_map/cond/branch_0_fun/while/body/eval_jaxpr/all_to_all | solution.py:428
  585.3 3.1 collective-permute-start.3
  592.5 11.0 %solve.8 = f32[256,256]{1,0:T(8,128)} custom-call(f32[256,256]{1,0:T(8,128)} %get-tuple-element.460.matrix_ref, f32[256,256]{1,0:T(8,128)S(1)} %get-tuple-element.497.target_ref), custom_call_target="tpu_custom_call" | custom-call | tf_op jit(solution)/shard_map/cond/branch_0_fun/while/body/eval_jaxpr/solve/pallas_call | solution.py:412
  603.5 4.4 subtract_select_fusion.4
  608.0 5.7 add_select_fusion.3
  615.0 2.5 copy.46
  620.9 2.4 collective-permute-start.1
  623.5 4.4 collective-permute-done.1.right_ref
  627.9 23.2 %powers.10 = (f32[2048,256]{1,0:T(8,128)S(1)}, f32[2048,256]{1,0:T(8,128)}, f32[3,2,256,128]{3,2,1,0:T(8,128)S(1)}, f32[3,2,256,128]{3,2,1,0:T(8,128)S(1)}) custom-call(s32[3]{0:T(128)S(1)} %get-tuple-element.499.valid_ref, f32[2048,256]{1,0:T(8,128)S(1)} %broadcast_select_fusion.5.own_ref, f32[192,256]{1,0:T(8,128)S(1)} %collective-permute-done.left_ref, ...), custom_call_target="tpu_custom_call" | custom-call | tf_op jit(solution)/shard_map/cond/branch_0_fun/while/body/eval_jaxpr/powers/pallas_call | solution.py:280
  653.4 26.5 %all_to_all.45 = f32[64,24,128]{2,1,0:T(8,128)S(1)} all-to-all(f32[64,24,128]{2,1,0:T(8,128)S(1)} %bitcast.54), channel_id=1, replica_groups=mesh['row'=4,'column'=4,'depth'=4,'core'=2] {'row','column','depth'}, dimensions={0} | all-to-all | bytes 1572864 | tf_op jit(solution)/shard_map/cond/branch_0_fun/while/body/eval_jaxpr/all_to_all | solution.py:427
  680.1 18.4 %all_to_all.46 = f32[64,24,128]{2,1,0:T(8,128)S(1)} all-to-all(f32[64,24,128]{2,1,0:T(8,128)S(1)} %broadcast_in_dim.48), channel_id=1, replica_groups=mesh['row'=4,'column'=4,'depth'=4,'core'=2] {'row','column','depth'}, dimensions={0} | all-to-all | bytes 1572864 | tf_op jit(solution)/shard_map/cond/branch_0_fun/while/body/eval_jaxpr/all_to_all | solution.py:428
  698.4 3.1 collective-permute-start.3
  705.7 11.0 %solve.8 = f32[256,256]{1,0:T(8,128)} custom-call(f32[256,256]{1,0:T(8,128)} %get-tuple-element.460.matrix_ref, f32[256,256]{1,0:T(8,128)S(1)} %get-tuple-element.497.target_ref), custom_call_target="tpu_custom_call" | custom-call | tf_op jit(solution)/shard_map/cond/branch_0_fun/while/body/eval_jaxpr/solve/pallas_call | solution.py:412
  716.7 4.4 subtract_select_fusion.4
  721.1 5.7 add_select_fusion.3
  728.1 5.7 leading.1
  735.4 3.6 all-to-all-start.4
  739.0 16.1 %all-to-all-done.4 = f32[128,2,768]{2,1,0:T(2,128)S(1)} async-done(((f32[128,2,768]{2,1,0:T(2,128)}), f32[128,2,768]{2,1,0:T(2,128)S(1)}, u32[]{:S(2)}, u32[]{:S(2)}) %all-to-all-start.4) | async-done | bytes 786464 | tf_op jit(solution)/shard_map/all_to_all | solution.py:627
  (227 shorter events, 79.4 us)
Async XLA Ops:
  0.6 2.3 copy-start
  2.3 43.0 %copy-start.3 = (f32[2048,256]{1,0:T(8,128)}, f32[2048,256]{1,0:T(8,128)S(1)}, u32[]{:S(2)}) copy-start(f32[2048,256]{1,0:T(8,128)S(1)} %copy.45.own_ref) | copy-start | bytes 6291460
  27.2 10.9 %copy-start.6 = (f32[12,256,256]{2,1,0:T(8,128)}, f32[12,256,256]{2,1,0:T(8,128)S(1)}, u32[]{:S(2)}) copy-start(f32[12,256,256]{2,1,0:T(8,128)S(1)} %assemble.1.band_ref) | copy-start | bytes 9437188
  27.3 18.0 %collective-permute-start.7 = (f32[320,256]{1,0:T(8,128)S(1)}, f32[320,256]{1,0:T(8,128)S(1)}, u32[]{:S(2)}, u32[]{:S(2)}) collective-permute-start(f32[320,256]{1,0:T(8,128)S(1)} %pad_maximum_fusion.2), channel_id=1, source_target_pairs={{1,0},{2,1},{3,2},{4,3},{5,4},{6,5},{7,6},{8,7},{9,8},{10,9},{11,1... | collective-permute-start | bytes 983048 | tf_op jit(solution)/shard_map/ppermute | solution.py:436
  31.4 13.9 %collective-permute-start.6 = (f32[320,256]{1,0:T(8,128)}, f32[320,256]{1,0:T(8,128)S(1)}, u32[]{:S(2)}, u32[]{:S(2)}) collective-permute-start(f32[320,256]{1,0:T(8,128)} %pad_maximum_fusion.1), channel_id=1, source_target_pairs={{0,1},{1,2},{2,3},{3,4},{4,5},{5,6},{6,7},{7,8},{8,9},{9,10},{10,1... | collective-permute-start | bytes 983048 | tf_op jit(solution)/shard_map/ppermute | solution.py:436
  35.7 5.7 collective-permute-start.4
  38.1 7.2 collective-permute-start.5
  70.5 2.4 collective-permute-start.8
  73.0 55.1 %copy-start.14 = (f32[16,768]{1,0:T(8,128)S(1)}, f32[16,768]{1,0:T(8,128)}, u32[]{:S(2)}) copy-start(f32[16,768]{1,0:T(8,128)} %param.16) | copy-start | bytes 147460
  106.7 22.0 %copy-start.15 = (s32[16,256]{1,0:T(8,128)S(1)}, s32[16,256]{1,0:T(8,128)}, u32[]{:S(2)}) copy-start(s32[16,256]{1,0:T(8,128)} %param.15) | copy-start | bytes 49156
  125.1 10.9 %collective-permute-start.9 = (f32[3,2,256,128]{3,2,1,0:T(8,128)S(1)}, f32[3,2,256,128]{3,2,1,0:T(8,128)S(1)}, u32[]{:S(2)}, u32[]{:S(2)}) collective-permute-start(f32[3,2,256,128]{3,2,1,0:T(8,128)S(1)} %bitcast.49), channel_id=1, source_target_pairs={{0,1},{1,0},{2,3},{3,2},{4,5},{5,4},{6,7},{7,6},{8,9},{9,8},{10,11... | collective-permute-start | bytes 2359304 | tf_op jit(solution)/shard_map/ppermute | solution.py:430
  158.4 3.2 copy-start.4
  161.8 2.5 copy-start.5
  161.8 13.2 %copy-start.11 = (f32[320,256]{1,0:T(8,128)}, f32[320,256]{1,0:T(8,128)S(1)}, u32[]{:S(2)}) copy-start(f32[320,256]{1,0:T(8,128)S(1)} %get-tuple-element.501.lband_ref) | copy-start | bytes 983044 | tf_op jit(solution)/shard_map/cond/branch_0_fun/while
  164.3 10.7 %copy-start.7 = (f32[12,256,256]{2,1,0:T(8,128)S(1)}, f32[12,256,256]{2,1,0:T(8,128)}, u32[]{:S(2)}) copy-start(f32[12,256,256]{2,1,0:T(8,128)} %get-tuple-element.500.band_ref) | copy-start | bytes 9437188 | tf_op jit(solution)/shard_map/cond/branch_0_fun/while
  165.6 4.9 collective-permute-start
  168.0 7.0 collective-permute-start.1
  198.2 2.3 collective-permute-start.2
  246.0 5.1 collective-permute-start.3
  264.2 4.4 copy-start.2
  264.2 4.4 copy-start.8
  264.2 4.4 copy-start.10
  275.6 2.5 copy-start.5
  275.6 12.9 %copy-start.11 = (f32[320,256]{1,0:T(8,128)}, f32[320,256]{1,0:T(8,128)S(1)}, u32[]{:S(2)}) copy-start(f32[320,256]{1,0:T(8,128)S(1)} %get-tuple-element.501.lband_ref) | copy-start | bytes 983044 | tf_op jit(solution)/shard_map/cond/branch_0_fun/while
  278.1 10.4 %copy-start.7 = (f32[12,256,256]{2,1,0:T(8,128)S(1)}, f32[12,256,256]{2,1,0:T(8,128)}, u32[]{:S(2)}) copy-start(f32[12,256,256]{2,1,0:T(8,128)} %get-tuple-element.500.band_ref) | copy-start | bytes 9437188 | tf_op jit(solution)/shard_map/cond/branch_0_fun/while
  279.5 4.7 collective-permute-start
  281.5 7.0 collective-permute-start.1
  311.7 2.3 collective-permute-start.2
  359.1 5.1 collective-permute-start.3
  377.3 4.4 copy-start.2
  377.3 4.4 copy-start.8
  377.3 4.4 copy-start.10
  388.8 2.5 copy-start.5
  388.8 12.9 %copy-start.11 = (f32[320,256]{1,0:T(8,128)}, f32[320,256]{1,0:T(8,128)S(1)}, u32[]{:S(2)}) copy-start(f32[320,256]{1,0:T(8,128)S(1)} %get-tuple-element.501.lband_ref) | copy-start | bytes 983044 | tf_op jit(solution)/shard_map/cond/branch_0_fun/while
  391.2 10.4 %copy-start.7 = (f32[12,256,256]{2,1,0:T(8,128)S(1)}, f32[12,256,256]{2,1,0:T(8,128)}, u32[]{:S(2)}) copy-start(f32[12,256,256]{2,1,0:T(8,128)} %get-tuple-element.500.band_ref) | copy-start | bytes 9437188 | tf_op jit(solution)/shard_map/cond/branch_0_fun/while
  392.6 4.7 collective-permute-start
  394.7 7.0 collective-permute-start.1
  424.8 2.3 collective-permute-start.2
  472.2 5.1 collective-permute-start.3
  490.4 4.4 copy-start.2
  490.4 4.4 copy-start.8
  490.4 4.4 copy-start.10
  501.9 2.5 copy-start.5
  501.9 12.9 %copy-start.11 = (f32[320,256]{1,0:T(8,128)}, f32[320,256]{1,0:T(8,128)S(1)}, u32[]{:S(2)}) copy-start(f32[320,256]{1,0:T(8,128)S(1)} %get-tuple-element.501.lband_ref) | copy-start | bytes 983044 | tf_op jit(solution)/shard_map/cond/branch_0_fun/while
  504.4 10.4 %copy-start.7 = (f32[12,256,256]{2,1,0:T(8,128)S(1)}, f32[12,256,256]{2,1,0:T(8,128)}, u32[]{:S(2)}) copy-start(f32[12,256,256]{2,1,0:T(8,128)} %get-tuple-element.500.band_ref) | copy-start | bytes 9437188 | tf_op jit(solution)/shard_map/cond/branch_0_fun/while
  505.7 4.7 collective-permute-start
  507.8 7.0 collective-permute-start.1
  538.0 2.3 collective-permute-start.2
  585.3 5.1 collective-permute-start.3
  603.5 4.4 copy-start.2
  603.5 4.4 copy-start.8
  603.5 4.4 copy-start.10
  615.0 2.5 copy-start.5
  615.0 12.9 %copy-start.11 = (f32[320,256]{1,0:T(8,128)}, f32[320,256]{1,0:T(8,128)S(1)}, u32[]{:S(2)}) copy-start(f32[320,256]{1,0:T(8,128)S(1)} %get-tuple-element.501.lband_ref) | copy-start | bytes 983044 | tf_op jit(solution)/shard_map/cond/branch_0_fun/while
  617.5 10.4 %copy-start.7 = (f32[12,256,256]{2,1,0:T(8,128)S(1)}, f32[12,256,256]{2,1,0:T(8,128)}, u32[]{:S(2)}) copy-start(f32[12,256,256]{2,1,0:T(8,128)} %get-tuple-element.500.band_ref) | copy-start | bytes 9437188 | tf_op jit(solution)/shard_map/cond/branch_0_fun/while
  618.8 4.7 collective-permute-start
  620.9 7.0 collective-permute-start.1
  651.1 2.3 collective-permute-start.2
  698.4 5.1 collective-permute-start.3
  716.7 4.4 copy-start.2
  716.7 4.4 copy-start.8
  716.7 4.4 copy-start.10
  734.1 4.9 copy-start.17
  735.4 19.7 %all-to-all-start.4 = ((f32[128,2,768]{2,1,0:T(2,128)}), f32[128,2,768]{2,1,0:T(2,128)S(1)}, u32[]{:S(2)}, u32[]{:S(2)}) async-start(f32[128,2,768]{2,1,0:T(2,128)} %reshape.119), calls=%async_computation.4 | async-start | bytes 1572864 | tf_op jit(solution)/shard_map/all_to_all | solution.py:627
  (17 other events, 23.7 us)
where the time goes:
time: 768 us; the launch traced here: 758 us
  blocking collectives  277 us (36%)
  Pallas kernels  255 us (33%)
  waiting for transfers between devices  68.3 us (9%)
  starting transfers between devices  55.6 us (7%)
  matrix products  50.5 us (7%)
  local copies, waits for them, and re-layouts  35.6 us (5%)
  other arithmetic  13.5 us (2%)
    all_to_all x6, blocking collectives, total_of(): own = lax.all_to_all(pair, CHIPS, 0, 0, tiled=True).sum(axis=0)  166 us
    pallas_call x6, Pallas kernels, powers(): pl.pallas_call(powers_kernel, out_shape=(full, full, half, half), in_spec...  141 us
    all_to_all x6, blocking collectives, total_of(): lax.all_to_all(jnp.broadcast_to(own[None], pair.shape), CHIPS, 0, 0, tile...  110 us
    pallas_call x5, Pallas kernels, solve(): pl.pallas_call(solve_kernel, out_shape=jax.ShapeDtypeStruct(target.shape,...  55 us
    dot_general x10, matrix products, times(): jnp.dot(a, b, preferred_element_type=F32, precision=lax.Precision.HIGHEST)  50.5 us
    ppermute x7, waiting for transfers between devices, both_ways(): lax.ppermute(to_left, AXES, [(b, a) for a, b in up])  25.9 us
    pallas_call x1, Pallas kernels, assemble(): pl.pallas_call(assemble_kernel, out_shape=jax.ShapeDtypeStruct((windows,...  24.3 us
    while x100, local copies, waits for them, and re-layouts  24.2 us
  transfers between devices with their start and end apart: 27, of which 24 were waited for; matrix products, arithmetic and copies ran while one was open for 0% of the time, Pallas kernels for 1%

commit v1 on v0

--- a/solution.py
+++ b/solution.py
@@ -18,10 +18,12 @@
 STEP = WIN - REACH
 SHIFT = 4.5
 ROUNDS = 8
+CLOSE = 1e-7
 GUARD = 0.01
 SMALL = 128
 SPAN = 80
 BATCH = 8
+TOGETHER = 2
 EDGE = 192
 
 
@@ -77,7 +79,7 @@
     row_in_window = iota((SMALL, lanes), 0)
     row_in_span = iota((SPAN, lanes), 0)
 
-    def batch(b, carry):
+    def product_of(b):
         base = pl.multiple_of(b * lanes, lanes)
         parts = halves(rows_ref[pl.ds(base, lanes), :])
         block = block_ref[...]
@@ -88,14 +90,18 @@
         match = one(row_in_span == offset_ref[pl.ds(b, 1), :])
         pick = jnp.concatenate([match] * BATCH, axis=0) * lane_ref[...]
         full = dot(pick, jnp.concatenate([uh, ul], axis=1))
-        full = full[:, :SMALL] + full[:, SMALL:]
-        for t in range(BATCH):
-            g = group_ref[b * BATCH + t]
-            r = pl.multiple_of(first_ref[b * BATCH + t], 16)
-            small_ref[g, pl.ds(r, SPAN), :] += full[t * SPAN : (t + 1) * SPAN]
+        return full[:, :SMALL] + full[:, SMALL:]
+
+    def batch(i, carry):
+        full = [product_of(TOGETHER * i + n) for n in range(TOGETHER)]
+        for n in range(TOGETHER):
+            for t in range(BATCH):
+                tile = (TOGETHER * i + n) * BATCH + t
+                r = pl.multiple_of(first_ref[tile], 16)
+                small_ref[group_ref[tile], pl.ds(r, SPAN), :] += full[n][t * SPAN : (t + 1) * SPAN]
         return carry
 
-    lax.fori_loop(0, tiles // BATCH, batch, 0)
+    lax.fori_loop(0, tiles // (BATCH * TOGETHER), batch, 0)
 
     eye = iota((WIN, WIN), 0) == iota((WIN, WIN), 1)
     gap = jnp.zeros((SMALL, REACH), F32)
@@ -191,14 +197,18 @@
     def apply(xh_ref, xl_ref):
         y_ref[...] = jnp.zeros_like(y_ref)
 
-        def window(g, carry):
-            at = pl.multiple_of(HALO + g * STEP, 64)
-            xh = xh_ref[pl.ds(at, WIN), :]
-            xl = xl_ref[pl.ds(at, WIN), :]
-            y_ref[pl.ds(at, WIN), :] += dot3(bh_ref[g], bl_ref[g], xh, xl)
+        def window(i, carry):
+            values = []
+            for n in range(3):
+                at = pl.multiple_of(HALO + (3 * i + n) * STEP, 64)
+                xh = xh_ref[pl.ds(at, WIN), :]
+                xl = xl_ref[pl.ds(at, WIN), :]
+                values.append((at, dot3(bh_ref[3 * i + n], bl_ref[3 * i + n], xh, xl)))
+            for at, value in values:
+                y_ref[pl.ds(at, WIN), :] += value
             return carry
 
-        lax.fori_loop(0, windows, window, 0)
+        lax.fori_loop(0, windows // 3, window, 0)
 
         def extra(h_ref, l_ref, lo, rows, out, at):
             y_ref[out : out + rows] += dot3(
@@ -245,28 +255,25 @@
             for c in range(cols // 128):
                 theirs_ref[n % ITERS, c] = value[:, c * 128 : (c + 1) * 128]
 
-    def square(n, xh_ref, xl_ref):
-        xh = xh_ref[LOW:high]
-        cross = dot(xh, xl_ref[LOW:high], tn)
-        put(n, dot(xh, xh, tn) + (cross + cross.T))
-
-    def product(n, xh_ref, xl_ref, zh_ref, zl_ref):
-        put(n, dot3(xh_ref[LOW:high], xl_ref[LOW:high], zh_ref[LOW:high], zl_ref[LOW:high], tn))
-
-    square(0, vh_ref, vl_ref)
+    def moments(n, xh_ref, xl_ref, zh_ref, zl_ref):
+        xh, zh = xh_ref[LOW:high], zh_ref[LOW:high]
+        by_high = dot(xh, jnp.concatenate([xh, xl_ref[LOW:high], zh, zl_ref[LOW:high]], axis=1), tn)
+        by_low = dot(xl_ref[LOW:high], zh, tn)
+        cross = by_high[:, cols : 2 * cols]
+        put(n, by_high[:, :cols] + (cross + cross.T))
+        put(n + 1, by_high[:, 2 * cols : 3 * cols] + (by_high[:, 3 * cols :] + by_low))
+
     apply(vh_ref, vl_ref)
     k1_ref[...] = y_ref[LOW:high]
     keep(wh_ref, wl_ref)
-    product(1, vh_ref, vl_ref, wh_ref, wl_ref)
-    square(2, wh_ref, wl_ref)
+    moments(0, vh_ref, vl_ref, wh_ref, wl_ref)
     apply(wh_ref, wl_ref)
     k2_ref[...] = y_ref[LOW:high]
     keep(vh_ref, vl_ref)
-    product(3, wh_ref, wl_ref, vh_ref, vl_ref)
-    square(4, vh_ref, vl_ref)
+    moments(2, wh_ref, wl_ref, vh_ref, vl_ref)
     apply(vh_ref, vl_ref)
     keep(wh_ref, wl_ref)
-    product(5, vh_ref, vl_ref, wh_ref, wl_ref)
+    moments(4, vh_ref, vl_ref, wh_ref, wl_ref)
 
 
 def powers(vector, left, right, valid, bands):
@@ -282,7 +289,7 @@
         out_shape=(full, full, half, half),
         in_specs=[pl.BlockSpec(memory_space=pltpu.SMEM)] + in_vmem(6),
         out_specs=tuple(in_vmem(4)),
-        compiler_params=pltpu.CompilerParams(vmem_limit_bytes=44 << 20),
+        compiler_params=pltpu.CompilerParams(vmem_limit_bytes=32 << 20),
         scratch_shapes=[pltpu.VMEM(band.shape, BF16)] * 2 + [edge] * 4 + [wide] * 4
         + [pltpu.VMEM((frame, cols), F32)],
         name="powers",
@@ -299,7 +306,7 @@
     return dot3(*halves(a), *halves(b))
 
 
-def inverse_spd(matrix, mul):
+def inverse_spd(matrix, mul, limit):
     size = matrix.shape[0]
     unit = (iota((size, size), 0) == iota((size, size), 1)).astype(F32)
     along, down = diagonals(matrix)
@@ -311,7 +318,7 @@
 
     def going(state):
         k, worst, _, _ = state
-        return (k < 40) & (worst > 1e-8)
+        return (k < 40) & (worst > limit)
 
     def step(state):
         k, _, total, power = state
@@ -320,8 +327,10 @@
         power = both[size:]
         return k + 1, jnp.max(jnp.abs(power)), total, power
 
+    total = factor * (unit + rest)
+    power = mul(rest, rest)
     rounds, worst, total, _ = lax.while_loop(
-        going, step, (0, jnp.max(jnp.abs(rest)), unit * factor, rest)
+        going, step, (1, jnp.max(jnp.abs(power)), total, power)
     )
     return total * scale, worst, rounds
 
@@ -348,7 +357,7 @@
         unpack(mine_ref, ITERS)
 
     m = [mom_ref[n] for n in range(2 * ITERS)]
-    m = [0.5 * (x + x.T) for x in m]
+    m = [x if n % 2 == 0 else 0.5 * (x + x.T) for n, x in enumerate(m)]
     h = [m[n + 1] + SHIFT * m[n] for n in range(2 * ITERS - 1)]
     size = m[0].shape[0]
 
@@ -356,7 +365,7 @@
         wide = split_dot(inverse, jnp.concatenate(targets, axis=1))
         return [wide[:, n * size : (n + 1) * size] for n in range(len(targets))]
 
-    s0, w0, k0 = inverse_spd(h[0], split_dot)
+    s0, w0, k0 = inverse_spd(h[0], split_dot, CLOSE)
     z01, z02, z0m = right_of(s0, h[1], h[2], m[0])
     lower = split_dot(
         jnp.concatenate([h[1], h[2]], axis=0), jnp.concatenate([z01, z02, z0m], axis=1)
@@ -367,13 +376,13 @@
     last = h[4] - lower[size:, size : 2 * size]
     m2 = m[2] - lower[size:, 2 * size :]
     first = 0.5 * (first + first.T)
-    s1, w1, k1 = inverse_spd(first, split_dot)
+    s1, w1, k1 = inverse_spd(first, split_dot, CLOSE)
     z12, z1m = right_of(s1, cross, m1)
     lower = split_dot(cross.T, jnp.concatenate([z12, z1m], axis=1))
     rest = last - lower[:, :size]
     rest = 0.5 * (rest + rest.T)
     m2 = m2 - lower[:, size:]
-    s2, w2, k2 = inverse_spd(rest, split_dot)
+    s2, w2, k2 = inverse_spd(rest, split_dot, CLOSE)
     y2 = split_dot(s2, m2)
     y1 = z1m - split_dot(z12, y2)
     y0 = z0m - split_dot(jnp.concatenate([z01, z02], axis=1), jnp.concatenate([y1, y2], axis=0))
@@ -383,7 +392,7 @@
     share = jnp.minimum(ratio(first, h[2]), ratio(rest, h[4]))
     rounds = jnp.maximum(k0, jnp.maximum(k1, k2))
     worst = jnp.maximum(w0, jnp.maximum(w1, w2))
-    good_ref[0] = jnp.where((share > GUARD) & (worst <= 1e-8) & (rounds <= ROUNDS), 1, 0)
+    good_ref[0] = jnp.where((share > GUARD) & (worst <= CLOSE) & (rounds <= ROUNDS), 1, 0)
 
 
 def galerkin(core, mine, theirs):
@@ -403,7 +412,7 @@
 def solve_kernel(matrix_ref, target_ref, out_ref):
     matrix = matrix_ref[...]
     matrix = 0.5 * (matrix + matrix.T)
-    inverse, _, _ = inverse_spd(matrix, full_dot)
+    inverse, _, _ = inverse_spd(matrix, full_dot, 1e-9)
     guess = full_dot(inverse, target_ref[...])
     out_ref[...] = guess + full_dot(inverse, target_ref[...] - full_dot(matrix, guess))
 
@@ -424,8 +433,9 @@
     other = [(0, 1), (1, 0)]
     pair = mine + lax.ppermute(theirs, "core", other)
     pair = pair.reshape(chips, -1, 128)
-    own = lax.all_to_all(pair, CHIPS, 0, 0, tiled=True).sum(axis=0)
-    gathered = lax.all_to_all(jnp.broadcast_to(own[None], pair.shape), CHIPS, 0, 0, tiled=True)
+    arrived = lax.all_to_all(pair, CHIPS, 0, 0, tiled=True)
+    own = jnp.broadcast_to(arrived.sum(axis=0)[None], pair.shape)
+    gathered = lax.all_to_all(own, CHIPS, 0, 0, tiled=True)
     gathered = gathered.reshape(shape)
     return gathered, lax.ppermute(gathered, "core", other)
 
@@ -531,21 +541,58 @@
     )(nodes, loads)
 
 
-def rows_of(wh, wl, xh, xl, out_ref):
-    full = dot3(wh, wl, xh, xl)
-    cols = full.shape[1]
-    slots = full.shape[0] // 3
-    for k in range(3):
-        out_ref[:, k * cols : (k + 1) * cols] += full[k * slots : (k + 1) * slots]
-
-
-def combine_kernel(k0_ref, k1_ref, k2_ref, c_ref, wh_ref, wl_ref, x_ref, out_ref, ch_ref, cl_ref):
+CHUNK = 512
+
+
+def basis_kernel(*refs):
+    *vector_refs, wh_ref, wl_ref, out_ref = refs
+
+    @pl.when(pl.program_id(0) == 0)
+    def _():
+        out_ref[...] = jnp.zeros_like(out_ref)
+
+    slots = out_ref.shape[0]
+    cols = vector_refs[0].shape[1]
+    count = len(vector_refs)
+    for n, ref in enumerate(vector_refs):
+        full = dot3(wh_ref[...], wl_ref[...], *halves(ref[...]))
+        for k in range(3):
+            at = (k * count + n) * cols
+            out_ref[:, at : at + cols] += full[k * slots : (k + 1) * slots]
+
+
+def basis(vectors, weights):
+    rows, cols = vectors[0].shape
+    loads = weights[0].shape[0]
+    weight = pl.BlockSpec((loads, CHUNK), lambda i: (0, i))
+    out = (loads // 3, 3 * len(vectors) * cols)
+    return pl.pallas_call(
+        basis_kernel,
+        grid=(rows // CHUNK,),
+        out_shape=jax.ShapeDtypeStruct(out, F32),
+        in_specs=[pl.BlockSpec((CHUNK, cols), lambda i: (i, 0))] * len(vectors) + [weight, weight],
+        out_specs=pl.BlockSpec(out, lambda i: (0, 0)),
+        compiler_params=pltpu.CompilerParams(vmem_limit_bytes=28 << 20),
+        name="basis",
+    )(*vectors, *weights)
+
+
+def to_owner(rows, dipole_slot):
+    slots, wide = rows.shape
+    count = lax.axis_size(AXES)
+    received = lax.all_to_all(rows.reshape(count, slots // count, wide), AXES, 0, 0, tiled=True)
+    return received.reshape(slots, wide)[dipole_slot]
+
+
+def combine_kernel(k0_ref, k1_ref, k2_ref, c_ref, picked_ref, x_ref, out_ref, ch_ref, cl_ref):
     size = c_ref.shape[1]
 
     @pl.when(pl.program_id(0) == 0)
     def _():
         ch_ref[...], cl_ref[...] = halves(c_ref[...])
-        out_ref[...] = jnp.zeros_like(out_ref)
+        wide = c_ref.shape[0]
+        for k in range(3):
+            out_ref[k] = dot3(*halves(picked_ref[:, k * wide : (k + 1) * wide]), ch_ref[...], cl_ref[...])
 
     total = jnp.zeros(x_ref.shape, F32)
     for n, ref in enumerate((k0_ref, k1_ref, k2_ref)):
@@ -553,56 +600,29 @@
         at = n * size
         total = total + dot3(ah, al, ch_ref[at : at + size], cl_ref[at : at + size])
     x_ref[...] = total
-    rows_of(wh_ref[...], wl_ref[...], *halves(total), out_ref)
-
-
-def leading_kernel(x_ref, wh_ref, wl_ref, out_ref):
-    @pl.when(pl.program_id(0) == 0)
-    def _():
-        out_ref[...] = jnp.zeros_like(out_ref)
-
-    rows_of(wh_ref[...], wl_ref[...], *halves(x_ref[...]), out_ref)
-
-
-CHUNK = 512
-
-
-def combine(k0, k1, k2, coef, weights):
+
+
+def combine(k0, k1, k2, coef, picked):
     rows, cols = k0.shape
-    loads = weights[0].shape[0]
     block = pl.BlockSpec((CHUNK, cols), lambda i: (i, 0))
-    weight = pl.BlockSpec((loads, CHUNK), lambda i: (0, i))
-    out = (loads // 3, 3 * cols)
+    whole = lambda shape: pl.BlockSpec(shape, lambda i: (0,) * len(shape))
+    out = (3, picked.shape[0], cols)
     return pl.pallas_call(
         combine_kernel,
         grid=(rows // CHUNK,),
         out_shape=(jax.ShapeDtypeStruct((rows, cols), F32), jax.ShapeDtypeStruct(out, F32)),
-        in_specs=[block] * 3 + [pl.BlockSpec(coef.shape, lambda i: (0, 0)), weight, weight],
-        out_specs=(block, pl.BlockSpec(out, lambda i: (0, 0))),
+        in_specs=[block] * 3 + [whole(coef.shape), whole(picked.shape)],
+        out_specs=(block, whole(out)),
         scratch_shapes=[pltpu.VMEM(coef.shape, BF16)] * 2,
-        compiler_params=pltpu.CompilerParams(vmem_limit_bytes=32 << 20),
+        compiler_params=pltpu.CompilerParams(vmem_limit_bytes=28 << 20),
         name="combine",
-    )(k0, k1, k2, coef, *weights)
-
-
-def leading(x, weights):
-    rows, cols = x.shape
-    loads = weights[0].shape[0]
-    weight = pl.BlockSpec((loads, CHUNK), lambda i: (0, i))
-    out = (loads // 3, 3 * cols)
-    return pl.pallas_call(
-        leading_kernel,
-        grid=(rows // CHUNK,),
-        out_shape=jax.ShapeDtypeStruct(out, F32),
-        in_specs=[pl.BlockSpec((CHUNK, cols), lambda i: (i, 0)), weight, weight],
-        out_specs=pl.BlockSpec(out, lambda i: (0, 0)),
-        name="leading",
-    )(x, *weights)
-
-
-def exact_path(right_side, valid, bands, weights):
+    )(k0, k1, k2, coef, picked)
+
+
+def exact_path(right_side, valid, bands, weights, dipole_slot):
     answer = plain_cg(right_side, valid, bands)
-    return answer, leading(answer, weights)
+    picked = to_owner(basis([answer], weights), dipole_slot)
+    return answer, picked.reshape(picked.shape[0], 3, -1).transpose(1, 0, 2)
 
 
 def one_device(right_side, tile_stiff, tile_nodes, node_shift, slot_nodes, slot_load, dipole_slot):
@@ -617,17 +637,14 @@
     bands = (band, *both_ways(to_right, to_left))
     weights = load_matrix(slot_nodes, slot_load, right_side.shape[0])
     k1, k2, mine, theirs = powers(right_side, left, right, valid, bands)
+    rows = basis([right_side, k1, k2], weights)
+    picked = to_owner(rows, dipole_slot)
     coef, good = galerkin(core[None], *total_of(mine, theirs))
-    answer, rows = lax.cond(
+    return lax.cond(
         good[0] > 0,
-        lambda: combine(right_side, k1, k2, coef, weights),
-        lambda: exact_path(right_side, valid, bands, weights),
+        lambda: combine(right_side, k1, k2, coef, picked),
+        lambda: exact_path(right_side, valid, bands, weights, dipole_slot),
     )
-    slots, wide = rows.shape
-    received = lax.all_to_all(rows.reshape(count, slots // count, wide), AXES, 0, 0, tiled=True)
-    picked = received.reshape(slots, wide)[dipole_slot]
-    leadfield = picked.reshape(-1, 3, wide // 3).transpose(1, 0, 2)
-    return answer, leadfield
 
 
 def solution(mesh):

time: 768 us -> 736 us (0.958)
  Pallas kernels: 255 us -> 218 us
  blocking collectives: 277 us -> 259 us
  starting transfers between devices: 55.6 us -> 71.1 us
  waiting for transfers between devices: 68.3 us -> 78.4 us
    pallas_call x6, Pallas kernels: 141 us -> 103 us  [powers(): pl.pallas_call(powers_kernel, out_shape=(full, full, half, half), in_spec...]
    all_to_all x12 -> x11, blocking collectives: 277 us -> 259 us  [the longest x6 167 us: total_of(): arrived = lax.all_to_all(pair, CHIPS, 0, 0, tiled=True)]
    all_to_all x1 -> x3, starting transfers between devices: 3.55 us -> 19.6 us  [the longest x2 14.7 us: to_owner(): lax.all_to_all(rows.reshape(count, slots // count, wide), AXES, 0, 0, til...]
    while x100 -> x70, local copies, waits for them, and re-layouts: 24.2 us -> 12.5 us
    pallas_call x1 -> x2, Pallas kernels: 5.68 us -> 15.5 us  [basis(): pl.pallas_call(basis_kernel, grid=(rows // CHUNK,), out_shape=jax.ShapeDt...]
    all_to_all x1 -> x3, waiting for transfers between devices: 16.1 us -> 24.1 us  [the longest x2 24.1 us: to_owner(): lax.all_to_all(rows.reshape(count, slots // count, wide), AXES, 0, 0, til...]
  transfers between devices with their start and end apart: 27 -> 29, of which waited for: 24 -> 26; matrix products, arithmetic and copies ran while one was open for 0% -> 1% of each run, Pallas kernels for 1% -> 5%
where the time goes in v1:
time: 736 us; the launch traced here: 726 us
  blocking collectives  259 us (35%)
  Pallas kernels  218 us (30%)
  waiting for transfers between devices  78.4 us (11%)
  starting transfers between devices  71.1 us (10%)
  matrix products  53.4 us (7%)
  local copies, waits for them, and re-layouts  28.1 us (4%)
  other arithmetic  13.6 us (2%)
    all_to_all x6, blocking collectives, total_of(): arrived = lax.all_to_all(pair, CHIPS, 0, 0, tiled=True)  167 us
    pallas_call x6, Pallas kernels, powers(): pl.pallas_call(powers_kernel, out_shape=(full, full, half, half), in_spec...  103 us
    all_to_all x5, blocking collectives, total_of(): gathered = lax.all_to_all(own, CHIPS, 0, 0, tiled=True)  91.9 us
    pallas_call x5, Pallas kernels, solve(): pl.pallas_call(solve_kernel, out_shape=jax.ShapeDtypeStruct(target.shape,...  53.4 us
    dot_general x10, matrix products, times(): jnp.dot(a, b, preferred_element_type=F32, precision=lax.Precision.HIGHEST)  53.4 us
    ppermute x7, waiting for transfers between devices, both_ways(): lax.ppermute(to_left, AXES, [(b, a) for a, b in up])  25.9 us
    all_to_all x2, waiting for transfers between devices, to_owner(): lax.all_to_all(rows.reshape(count, slots // count, wide), AXES, 0, 0, til...  24.1 us
    pallas_call x1, Pallas kernels, galerkin(): pl.pallas_call(galerkin_kernel, out_shape=(jax.ShapeDtypeStruct((ITERS *...  20.8 us
  transfers between devices with their start and end apart: 29, of which 26 were waited for; matrix products, arithmetic and copies ran while one was open for 1% of the time, Pallas kernels for 5%

profile of v1, /device:TPU:1, one launch (start us, length us, event | category | flops | bytes accessed | tf_op | source)
XLA Modules:
  0.0 725.5 jit_solution(16963792203441585425)
XLA Ops:
  2.9 20.4 %assemble.1.band_ref = f32[12,256,256]{2,1,0:T(8,128)S(1)} custom-call(s32[256]{0:T(256)S(1)} %get-tuple-element.382.group_ref, s32[256]{0:T(256)S(1)} %multiply_minimum_fusion.first_ref, f32[32,32,256]{2,1,0:T(8,128)S(1)} %bitcast.51, s32[32,256]{1,0:T(8,128)S(1)} %reshape.117.place_ref, s32[32,256]{1,0:T(8,128)S(1)} %reshape.118.offset_ref, ...), custom_call_target="tpu_custom_call" | custom-call | tf_op jit(solution)/shard_map/assemble/pallas_call | solution.py:134
  23.4 3.3 collective-permute-start.7
  27.5 3.5 collective-permute-start.6
  31.8 2.4 collective-permute-start.4
  37.4 4.0 collective-permute-done.5.right_ref
  41.4 18.9 %powers.9 = (f32[2048,256]{1,0:T(8,128)}, f32[2048,256]{1,0:T(8,128)}, f32[3,2,256,128]{3,2,1,0:T(8,128)S(1)}, f32[3,2,256,128]{3,2,1,0:T(8,128)S(1)}) custom-call(s32[3]{0:T(128)S(1)} %pad_add_fusion.valid_ref, f32[2048,256]{1,0:T(8,128)S(1)} %copy.51.own_ref.refs_0_, f32[192,256]{1,0:T(8,128)S(1)} %collective-permute-done.4.left_ref, ...), custom_call_target="tpu_custom_call" | custom-call | tf_op jit(solution)/shard_map/powers/pallas_call | solution.py:287
  62.9 33.4 %all_to_all.47 = f32[64,24,128]{2,1,0:T(8,128)S(1)} all-to-all(f32[64,24,128]{2,1,0:T(8,128)S(1)} %bitcast.55), channel_id=1, replica_groups=mesh['row'=4,'column'=4,'depth'=4,'core'=2] {'row','column','depth'}, dimensions={0} | all-to-all | bytes 1572864 | tf_op jit(solution)/shard_map/all_to_all | solution.py:436
  97.3 4.8 all-to-all-start.4
  102.9 4.5 loads.1
  110.1 9.8 %basis.3 = f32[256,2304]{1,0:T(8,128)S(1)} custom-call(f32[2048,256]{1,0:T(8,128)} %copy-done.1, f32[2048,256]{1,0:T(8,128)} %get-tuple-element.297.refs_1_, f32[2048,256]{1,0:T(8,128)} %get-tuple-element.298.refs_2_, bf16[768,2048]{1,0:T(8,128)(2,1)S(1)} %get-tuple-element.295.refs_3_, bf16[768,2048]{1,0:T(8,128)(2,1)S(1)} %get-tuple-element.296.refs_4_), custom_call_target="tpu_custom_call" | custom-call | tf_op jit(solution)/shard_map/basis/pallas_call | solution.py:569
  119.9 2.5 reshape.125
  122.4 11.2 %all-to-all-start.5 = ((f32[128,2,2304]{2,1,0:T(2,128)}), f32[128,2,2304]{2,1,0:T(2,128)}, u32[]{:S(2)}, u32[]{:S(2)}) async-start(f32[128,2,2304]{2,1,0:T(2,128)} %reshape.125), calls=%async_computation.5 | async-start | bytes 4718592 | tf_op jit(solution)/shard_map/all_to_all | solution.py:583
  136.7 20.8 %galerkin.1 = (f32[768,256]{1,0:T(8,128)}, s32[1]{0:T(128)}) custom-call(s32[1]{0:T(128)} %bitcast.2.core_ref, f32[3,2,256,128]{3,2,1,0:T(8,128)S(1)} %bitcast.50, f32[3,2,256,128]{3,2,1,0:T(8,128)S(1)} %collective-permute-done.9.theirs_ref), custom_call_target="tpu_custom_call" | custom-call | tf_op jit(solution)/shard_map/galerkin/pallas_call | solution.py:401
  158.2 8.0 %all-to-all-done.5 = f32[128,2,2304]{2,1,0:T(2,128)} async-done(((f32[128,2,2304]{2,1,0:T(2,128)}), f32[128,2,2304]{2,1,0:T(2,128)}, u32[]{:S(2)}, u32[]{:S(2)}) %all-to-all-start.5) | async-done | bytes 2359328 | tf_op jit(solution)/shard_map/all_to_all | solution.py:583
  166.1 558.0 %conditional.1 = ((f32[2048,256]{1,0:T(8,128)}, f32[3,128,256]{2,1,0:T(8,128)})) conditional(s32[]{:T(128)} %bitcast.12, (s32[]{:T(128)}, s32[3]{0:T(128)S(1)}, f32[12,256,256]{2,1,0:T(8,128)}, f32[320,256]{1,0:T(8,128)}, f32[320,256]{1,0:T(8,128)S(1)}, /*index=5*/f32[2048,256]{1,0:T(8,128)S(1)}, bf16[768,2048]{1,0:T(8,128)(2,1)}, ...), branch_computations={%region_2.6_spmd, %region_6.7_spmd} | conditional | flops 3228105216 | bytes 106724056 | solution.py:643
  167.5 527.2 %while.21 = (s32[]{:T(128)}, f32[2048,256]{1,0:T(8,128)}, f32[2048,256]{1,0:T(8,128)S(1)}, f32[2048,256]{1,0:T(8,128)}, f32[256,256]{1,0:T(8,128)S(1)}, /*index=...) while((s32[]{:T(128)}, f32[2048,256]{1,0:T(8,128)}, ...), condition=%wide.region_5.5_spmd.clone, body=%wide.region_3.4_spmd.clone.sunk | while | flops 3228103680 | bytes 94659104 | solution.py:481
  170.4 3.4 collective-permute-start
  176.4 4.4 collective-permute-done.1.right_ref
  180.8 16.8 %powers.10 = (f32[2048,256]{1,0:T(8,128)S(1)}, f32[2048,256]{1,0:T(8,128)}, f32[3,2,256,128]{3,2,1,0:T(8,128)S(1)}, f32[3,2,256,128]{3,2,1,0:T(8,128)S(1)}) custom-call(s32[3]{0:T(128)S(1)} %get-tuple-element.518.valid_ref, f32[2048,256]{1,0:T(8,128)S(1)} %broadcast_select_fusion.5.own_ref, f32[192,256]{1,0:T(8,128)S(1)} %collective-permute-done.left_ref, ...), custom_call_target="tpu_custom_call" | custom-call | tf_op jit(solution)/shard_map/cond/branch_0_fun/while/body/eval_jaxpr/powers/pallas_call | solution.py:287
  200.0 27.7 %all_to_all.48 = f32[64,24,128]{2,1,0:T(8,128)S(1)} all-to-all(f32[64,24,128]{2,1,0:T(8,128)S(1)} %bitcast.54), channel_id=1, replica_groups=mesh['row'=4,'column'=4,'depth'=4,'core'=2] {'row','column','depth'}, dimensions={0} | all-to-all | bytes 1572864 | tf_op jit(solution)/shard_map/cond/branch_0_fun/while/body/eval_jaxpr/all_to_all | solution.py:436
  227.9 18.4 %all_to_all.49 = f32[64,24,128]{2,1,0:T(8,128)S(1)} all-to-all(f32[64,24,128]{2,1,0:T(8,128)S(1)} %broadcast_in_dim.52), channel_id=1, replica_groups=mesh['row'=4,'column'=4,'depth'=4,'core'=2] {'row','column','depth'}, dimensions={0} | all-to-all | bytes 1572864 | tf_op jit(solution)/shard_map/cond/branch_0_fun/while/body/eval_jaxpr/all_to_all | solution.py:438
  246.2 3.1 collective-permute-start.3
  253.5 10.7 %solve.8 = f32[256,256]{1,0:T(8,128)} custom-call(f32[256,256]{1,0:T(8,128)} %get-tuple-element.479.matrix_ref, f32[256,256]{1,0:T(8,128)S(1)} %get-tuple-element.516.target_ref), custom_call_target="tpu_custom_call" | custom-call | tf_op jit(solution)/shard_map/cond/branch_0_fun/while/body/eval_jaxpr/solve/pallas_call | solution.py:421
  264.2 4.4 subtract_select_fusion.4
  268.6 5.8 add_select_fusion.3
  279.4 2.4 collective-permute-start.1
  282.0 4.4 collective-permute-done.1.right_ref
  286.4 16.8 %powers.10 = (f32[2048,256]{1,0:T(8,128)S(1)}, f32[2048,256]{1,0:T(8,128)}, f32[3,2,256,128]{3,2,1,0:T(8,128)S(1)}, f32[3,2,256,128]{3,2,1,0:T(8,128)S(1)}) custom-call(s32[3]{0:T(128)S(1)} %get-tuple-element.518.valid_ref, f32[2048,256]{1,0:T(8,128)S(1)} %broadcast_select_fusion.5.own_ref, f32[192,256]{1,0:T(8,128)S(1)} %collective-permute-done.left_ref, ...), custom_call_target="tpu_custom_call" | custom-call | tf_op jit(solution)/shard_map/cond/branch_0_fun/while/body/eval_jaxpr/powers/pallas_call | solution.py:287
  305.6 26.5 %all_to_all.48 = f32[64,24,128]{2,1,0:T(8,128)S(1)} all-to-all(f32[64,24,128]{2,1,0:T(8,128)S(1)} %bitcast.54), channel_id=1, replica_groups=mesh['row'=4,'column'=4,'depth'=4,'core'=2] {'row','column','depth'}, dimensions={0} | all-to-all | bytes 1572864 | tf_op jit(solution)/shard_map/cond/branch_0_fun/while/body/eval_jaxpr/all_to_all | solution.py:436
  332.2 18.4 %all_to_all.49 = f32[64,24,128]{2,1,0:T(8,128)S(1)} all-to-all(f32[64,24,128]{2,1,0:T(8,128)S(1)} %broadcast_in_dim.52), channel_id=1, replica_groups=mesh['row'=4,'column'=4,'depth'=4,'core'=2] {'row','column','depth'}, dimensions={0} | all-to-all | bytes 1572864 | tf_op jit(solution)/shard_map/cond/branch_0_fun/while/body/eval_jaxpr/all_to_all | solution.py:438
  350.6 3.1 collective-permute-start.3
  357.8 10.7 %solve.8 = f32[256,256]{1,0:T(8,128)} custom-call(f32[256,256]{1,0:T(8,128)} %get-tuple-element.479.matrix_ref, f32[256,256]{1,0:T(8,128)S(1)} %get-tuple-element.516.target_ref), custom_call_target="tpu_custom_call" | custom-call | tf_op jit(solution)/shard_map/cond/branch_0_fun/while/body/eval_jaxpr/solve/pallas_call | solution.py:421
  368.5 4.4 subtract_select_fusion.4
  373.0 6.4 add_select_fusion.3
  384.4 2.4 collective-permute-start.1
  387.0 4.4 collective-permute-done.1.right_ref
  391.4 16.8 %powers.10 = (f32[2048,256]{1,0:T(8,128)S(1)}, f32[2048,256]{1,0:T(8,128)}, f32[3,2,256,128]{3,2,1,0:T(8,128)S(1)}, f32[3,2,256,128]{3,2,1,0:T(8,128)S(1)}) custom-call(s32[3]{0:T(128)S(1)} %get-tuple-element.518.valid_ref, f32[2048,256]{1,0:T(8,128)S(1)} %broadcast_select_fusion.5.own_ref, f32[192,256]{1,0:T(8,128)S(1)} %collective-permute-done.left_ref, ...), custom_call_target="tpu_custom_call" | custom-call | tf_op jit(solution)/shard_map/cond/branch_0_fun/while/body/eval_jaxpr/powers/pallas_call | solution.py:287
  410.6 26.5 %all_to_all.48 = f32[64,24,128]{2,1,0:T(8,128)S(1)} all-to-all(f32[64,24,128]{2,1,0:T(8,128)S(1)} %bitcast.54), channel_id=1, replica_groups=mesh['row'=4,'column'=4,'depth'=4,'core'=2] {'row','column','depth'}, dimensions={0} | all-to-all | bytes 1572864 | tf_op jit(solution)/shard_map/cond/branch_0_fun/while/body/eval_jaxpr/all_to_all | solution.py:436
  437.2 18.4 %all_to_all.49 = f32[64,24,128]{2,1,0:T(8,128)S(1)} all-to-all(f32[64,24,128]{2,1,0:T(8,128)S(1)} %broadcast_in_dim.52), channel_id=1, replica_groups=mesh['row'=4,'column'=4,'depth'=4,'core'=2] {'row','column','depth'}, dimensions={0} | all-to-all | bytes 1572864 | tf_op jit(solution)/shard_map/cond/branch_0_fun/while/body/eval_jaxpr/all_to_all | solution.py:438
  455.6 3.1 collective-permute-start.3
  462.8 10.7 %solve.8 = f32[256,256]{1,0:T(8,128)} custom-call(f32[256,256]{1,0:T(8,128)} %get-tuple-element.479.matrix_ref, f32[256,256]{1,0:T(8,128)S(1)} %get-tuple-element.516.target_ref), custom_call_target="tpu_custom_call" | custom-call | tf_op jit(solution)/shard_map/cond/branch_0_fun/while/body/eval_jaxpr/solve/pallas_call | solution.py:421
  473.5 4.4 subtract_select_fusion.4
  477.9 6.4 add_select_fusion.3
  489.4 2.4 collective-permute-start.1
  492.0 4.4 collective-permute-done.1.right_ref
  496.4 16.8 %powers.10 = (f32[2048,256]{1,0:T(8,128)S(1)}, f32[2048,256]{1,0:T(8,128)}, f32[3,2,256,128]{3,2,1,0:T(8,128)S(1)}, f32[3,2,256,128]{3,2,1,0:T(8,128)S(1)}) custom-call(s32[3]{0:T(128)S(1)} %get-tuple-element.518.valid_ref, f32[2048,256]{1,0:T(8,128)S(1)} %broadcast_select_fusion.5.own_ref, f32[192,256]{1,0:T(8,128)S(1)} %collective-permute-done.left_ref, ...), custom_call_target="tpu_custom_call" | custom-call | tf_op jit(solution)/shard_map/cond/branch_0_fun/while/body/eval_jaxpr/powers/pallas_call | solution.py:287
  515.6 26.5 %all_to_all.48 = f32[64,24,128]{2,1,0:T(8,128)S(1)} all-to-all(f32[64,24,128]{2,1,0:T(8,128)S(1)} %bitcast.54), channel_id=1, replica_groups=mesh['row'=4,'column'=4,'depth'=4,'core'=2] {'row','column','depth'}, dimensions={0} | all-to-all | bytes 1572864 | tf_op jit(solution)/shard_map/cond/branch_0_fun/while/body/eval_jaxpr/all_to_all | solution.py:436
  542.2 18.4 %all_to_all.49 = f32[64,24,128]{2,1,0:T(8,128)S(1)} all-to-all(f32[64,24,128]{2,1,0:T(8,128)S(1)} %broadcast_in_dim.52), channel_id=1, replica_groups=mesh['row'=4,'column'=4,'depth'=4,'core'=2] {'row','column','depth'}, dimensions={0} | all-to-all | bytes 1572864 | tf_op jit(solution)/shard_map/cond/branch_0_fun/while/body/eval_jaxpr/all_to_all | solution.py:438
  560.6 3.1 collective-permute-start.3
  567.8 10.7 %solve.8 = f32[256,256]{1,0:T(8,128)} custom-call(f32[256,256]{1,0:T(8,128)} %get-tuple-element.479.matrix_ref, f32[256,256]{1,0:T(8,128)S(1)} %get-tuple-element.516.target_ref), custom_call_target="tpu_custom_call" | custom-call | tf_op jit(solution)/shard_map/cond/branch_0_fun/while/body/eval_jaxpr/solve/pallas_call | solution.py:421
  578.5 4.4 subtract_select_fusion.4
  582.9 6.4 add_select_fusion.3
  594.4 2.4 collective-permute-start.1
  597.0 4.4 collective-permute-done.1.right_ref
  601.4 16.8 %powers.10 = (f32[2048,256]{1,0:T(8,128)S(1)}, f32[2048,256]{1,0:T(8,128)}, f32[3,2,256,128]{3,2,1,0:T(8,128)S(1)}, f32[3,2,256,128]{3,2,1,0:T(8,128)S(1)}) custom-call(s32[3]{0:T(128)S(1)} %get-tuple-element.518.valid_ref, f32[2048,256]{1,0:T(8,128)S(1)} %broadcast_select_fusion.5.own_ref, f32[192,256]{1,0:T(8,128)S(1)} %collective-permute-done.left_ref, ...), custom_call_target="tpu_custom_call" | custom-call | tf_op jit(solution)/shard_map/cond/branch_0_fun/while/body/eval_jaxpr/powers/pallas_call | solution.py:287
  620.6 26.5 %all_to_all.48 = f32[64,24,128]{2,1,0:T(8,128)S(1)} all-to-all(f32[64,24,128]{2,1,0:T(8,128)S(1)} %bitcast.54), channel_id=1, replica_groups=mesh['row'=4,'column'=4,'depth'=4,'core'=2] {'row','column','depth'}, dimensions={0} | all-to-all | bytes 1572864 | tf_op jit(solution)/shard_map/cond/branch_0_fun/while/body/eval_jaxpr/all_to_all | solution.py:436
  647.2 18.4 %all_to_all.49 = f32[64,24,128]{2,1,0:T(8,128)S(1)} all-to-all(f32[64,24,128]{2,1,0:T(8,128)S(1)} %broadcast_in_dim.52), channel_id=1, replica_groups=mesh['row'=4,'column'=4,'depth'=4,'core'=2] {'row','column','depth'}, dimensions={0} | all-to-all | bytes 1572864 | tf_op jit(solution)/shard_map/cond/branch_0_fun/while/body/eval_jaxpr/all_to_all | solution.py:438
  665.6 3.1 collective-permute-start.3
  672.8 10.7 %solve.8 = f32[256,256]{1,0:T(8,128)} custom-call(f32[256,256]{1,0:T(8,128)} %get-tuple-element.479.matrix_ref, f32[256,256]{1,0:T(8,128)S(1)} %get-tuple-element.516.target_ref), custom_call_target="tpu_custom_call" | custom-call | tf_op jit(solution)/shard_map/cond/branch_0_fun/while/body/eval_jaxpr/solve/pallas_call | solution.py:421
  683.5 4.4 subtract_select_fusion.4
  687.9 6.4 add_select_fusion.3
  694.7 5.7 basis.2
  701.8 3.6 all-to-all-start.2
  705.4 16.1 %all-to-all-done.2 = f32[128,2,768]{2,1,0:T(2,128)S(1)} async-done(((f32[128,2,768]{2,1,0:T(2,128)}), f32[128,2,768]{2,1,0:T(2,128)S(1)}, u32[]{:S(2)}, u32[]{:S(2)}) %all-to-all-start.2) | async-done | bytes 786464 | tf_op jit(solution)/shard_map/cond/branch_0_fun/all_to_all | solution.py:583
  (208 shorter events, 81.6 us)
Async XLA Ops:
  2.3 39.1 %copy-start.1 = (f32[2048,256]{1,0:T(8,128)}, f32[2048,256]{1,0:T(8,128)S(1)}, u32[]{:S(2)}) copy-start(f32[2048,256]{1,0:T(8,128)S(1)} %copy.51.own_ref.refs_0_) | copy-start | bytes 6291460
  23.3 10.9 %copy-start.8 = (f32[12,256,256]{2,1,0:T(8,128)}, f32[12,256,256]{2,1,0:T(8,128)S(1)}, u32[]{:S(2)}) copy-start(f32[12,256,256]{2,1,0:T(8,128)S(1)} %assemble.1.band_ref) | copy-start | bytes 9437188
  23.4 18.0 %collective-permute-start.7 = (f32[320,256]{1,0:T(8,128)S(1)}, f32[320,256]{1,0:T(8,128)S(1)}, u32[]{:S(2)}, u32[]{:S(2)}) collective-permute-start(f32[320,256]{1,0:T(8,128)S(1)} %pad_maximum_fusion.2), channel_id=1, source_target_pairs={{1,0},{2,1},{3,2},{4,3},{5,4},{6,5},{7,6},{8,7},{9,8},{10,9},{11,1... | collective-permute-start | bytes 983048 | tf_op jit(solution)/shard_map/ppermute | solution.py:446
  27.5 13.9 %collective-permute-start.6 = (f32[320,256]{1,0:T(8,128)}, f32[320,256]{1,0:T(8,128)S(1)}, u32[]{:S(2)}, u32[]{:S(2)}) collective-permute-start(f32[320,256]{1,0:T(8,128)} %pad_maximum_fusion.1), channel_id=1, source_target_pairs={{0,1},{1,2},{2,3},{3,4},{4,5},{5,6},{6,7},{7,8},{8,9},{9,10},{10,1... | collective-permute-start | bytes 983048 | tf_op jit(solution)/shard_map/ppermute | solution.py:446
  31.8 5.6 collective-permute-start.4
  34.2 7.2 collective-permute-start.5
  41.4 18.9 %copy-start.13 = (f32[320,256]{1,0:T(8,128)}, f32[320,256]{1,0:T(8,128)S(1)}, u32[]{:S(2)}) copy-start(f32[320,256]{1,0:T(8,128)S(1)} %collective-permute-done.6.lband_ref) | copy-start | bytes 983044
  60.3 2.4 collective-permute-start.8
  62.9 39.3 %copy-start.16 = (f32[16,768]{1,0:T(8,128)S(1)}, f32[16,768]{1,0:T(8,128)}, u32[]{:S(2)}) copy-start(f32[16,768]{1,0:T(8,128)} %param.16) | copy-start | bytes 147460
  97.3 5.4 copy-start.17
  97.3 25.1 %all-to-all-start.4 = ((f32[64,24,128]{2,1,0:T(8,128)}), f32[64,24,128]{2,1,0:T(8,128)S(1)}, u32[]{:S(2)}, u32[]{:S(2)}) async-start(f32[64,24,128]{2,1,0:T(8,128)} %broadcast_in_dim.43), calls=%async_computation.4 | async-start | bytes 1572864 | tf_op jit(solution)/shard_map/all_to_all | solution.py:438
  107.4 2.7 copy-start.12
  122.4 43.8 %copy-start.2 = (f32[2048,256]{1,0:T(8,128)S(1)}, f32[2048,256]{1,0:T(8,128)}, u32[]{:S(2)}) copy-start(f32[2048,256]{1,0:T(8,128)} %copy-done.1) | copy-start | bytes 6291460
  122.4 43.8 %copy-start.19 = (s32[128]{0:T(128)S(1)}, s32[128]{0:T(128)}, u32[]{:S(2)}) copy-start(s32[128]{0:T(128)} %param.17) | copy-start | bytes 1540
  122.4 43.8 %all-to-all-start.5 = ((f32[128,2,2304]{2,1,0:T(2,128)}), f32[128,2,2304]{2,1,0:T(2,128)}, u32[]{:S(2)}, u32[]{:S(2)}) async-start(f32[128,2,2304]{2,1,0:T(2,128)} %reshape.125), calls=%async_computation.5 | async-start | bytes 4718592 | tf_op jit(solution)/shard_map/all_to_all | solution.py:583
  133.6 3.1 collective-permute-start.9
  167.7 2.4 copy-start.5
  170.1 10.7 %copy-start.6 = (f32[2048,256]{1,0:T(8,128)}, f32[2048,256]{1,0:T(8,128)S(1)}, u32[]{:S(2)}) copy-start(f32[2048,256]{1,0:T(8,128)S(1)} %copy.52) | copy-start | bytes 6291460 | tf_op jit(solution)/shard_map/cond/branch_0_fun/while
  170.1 10.7 %copy-start.9 = (f32[12,256,256]{2,1,0:T(8,128)S(1)}, f32[12,256,256]{2,1,0:T(8,128)}, u32[]{:S(2)}) copy-start(f32[12,256,256]{2,1,0:T(8,128)} %get-tuple-element.519.band_ref) | copy-start | bytes 9437188 | tf_op jit(solution)/shard_map/cond/branch_0_fun/while
  170.1 10.7 %copy-start.14 = (f32[320,256]{1,0:T(8,128)S(1)}, f32[320,256]{1,0:T(8,128)}, u32[]{:S(2)}) copy-start(f32[320,256]{1,0:T(8,128)} %get-tuple-element.520.lband_ref) | copy-start | bytes 983044 | tf_op jit(solution)/shard_map/cond/branch_0_fun/while
  170.4 6.0 collective-permute-start
  173.8 7.0 collective-permute-start.1
  197.6 2.3 collective-permute-start.2
  246.2 5.1 collective-permute-start.3
  264.2 4.4 copy-start.7
  264.2 4.4 copy-start.10
  276.9 9.5 %copy-start.6 = (f32[2048,256]{1,0:T(8,128)}, f32[2048,256]{1,0:T(8,128)S(1)}, u32[]{:S(2)}) copy-start(f32[2048,256]{1,0:T(8,128)S(1)} %copy.52) | copy-start | bytes 6291460 | tf_op jit(solution)/shard_map/cond/branch_0_fun/while
  276.9 9.5 %copy-start.9 = (f32[12,256,256]{2,1,0:T(8,128)S(1)}, f32[12,256,256]{2,1,0:T(8,128)}, u32[]{:S(2)}) copy-start(f32[12,256,256]{2,1,0:T(8,128)} %get-tuple-element.519.band_ref) | copy-start | bytes 9437188 | tf_op jit(solution)/shard_map/cond/branch_0_fun/while
  276.9 9.5 %copy-start.14 = (f32[320,256]{1,0:T(8,128)S(1)}, f32[320,256]{1,0:T(8,128)}, u32[]{:S(2)}) copy-start(f32[320,256]{1,0:T(8,128)} %get-tuple-element.520.lband_ref) | copy-start | bytes 983044 | tf_op jit(solution)/shard_map/cond/branch_0_fun/while
  277.2 4.8 collective-permute-start
  279.4 7.0 collective-permute-start.1
  303.2 2.3 collective-permute-start.2
  350.6 5.1 collective-permute-start.3
  368.5 4.4 copy-start.7
  368.5 4.4 copy-start.10
  381.9 9.5 %copy-start.6 = (f32[2048,256]{1,0:T(8,128)}, f32[2048,256]{1,0:T(8,128)S(1)}, u32[]{:S(2)}) copy-start(f32[2048,256]{1,0:T(8,128)S(1)} %copy.52) | copy-start | bytes 6291460 | tf_op jit(solution)/shard_map/cond/branch_0_fun/while
  381.9 9.5 %copy-start.9 = (f32[12,256,256]{2,1,0:T(8,128)S(1)}, f32[12,256,256]{2,1,0:T(8,128)}, u32[]{:S(2)}) copy-start(f32[12,256,256]{2,1,0:T(8,128)} %get-tuple-element.519.band_ref) | copy-start | bytes 9437188 | tf_op jit(solution)/shard_map/cond/branch_0_fun/while
  381.9 9.5 %copy-start.14 = (f32[320,256]{1,0:T(8,128)S(1)}, f32[320,256]{1,0:T(8,128)}, u32[]{:S(2)}) copy-start(f32[320,256]{1,0:T(8,128)} %get-tuple-element.520.lband_ref) | copy-start | bytes 983044 | tf_op jit(solution)/shard_map/cond/branch_0_fun/while
  382.2 4.8 collective-permute-start
  384.4 7.0 collective-permute-start.1
  408.2 2.3 collective-permute-start.2
  455.6 5.1 collective-permute-start.3
  473.5 4.4 copy-start.7
  473.5 4.4 copy-start.10
  486.9 9.5 %copy-start.6 = (f32[2048,256]{1,0:T(8,128)}, f32[2048,256]{1,0:T(8,128)S(1)}, u32[]{:S(2)}) copy-start(f32[2048,256]{1,0:T(8,128)S(1)} %copy.52) | copy-start | bytes 6291460 | tf_op jit(solution)/shard_map/cond/branch_0_fun/while
  486.9 9.5 %copy-start.9 = (f32[12,256,256]{2,1,0:T(8,128)S(1)}, f32[12,256,256]{2,1,0:T(8,128)}, u32[]{:S(2)}) copy-start(f32[12,256,256]{2,1,0:T(8,128)} %get-tuple-element.519.band_ref) | copy-start | bytes 9437188 | tf_op jit(solution)/shard_map/cond/branch_0_fun/while
  486.9 9.5 %copy-start.14 = (f32[320,256]{1,0:T(8,128)S(1)}, f32[320,256]{1,0:T(8,128)}, u32[]{:S(2)}) copy-start(f32[320,256]{1,0:T(8,128)} %get-tuple-element.520.lband_ref) | copy-start | bytes 983044 | tf_op jit(solution)/shard_map/cond/branch_0_fun/while
  487.2 4.8 collective-permute-start
  489.4 7.0 collective-permute-start.1
  513.2 2.3 collective-permute-start.2
  560.6 5.1 collective-permute-start.3
  578.5 4.4 copy-start.7
  578.5 4.4 copy-start.10
  589.5 2.4 copy-start.5
  591.9 9.5 %copy-start.6 = (f32[2048,256]{1,0:T(8,128)}, f32[2048,256]{1,0:T(8,128)S(1)}, u32[]{:S(2)}) copy-start(f32[2048,256]{1,0:T(8,128)S(1)} %copy.52) | copy-start | bytes 6291460 | tf_op jit(solution)/shard_map/cond/branch_0_fun/while
  591.9 9.5 %copy-start.9 = (f32[12,256,256]{2,1,0:T(8,128)S(1)}, f32[12,256,256]{2,1,0:T(8,128)}, u32[]{:S(2)}) copy-start(f32[12,256,256]{2,1,0:T(8,128)} %get-tuple-element.519.band_ref) | copy-start | bytes 9437188 | tf_op jit(solution)/shard_map/cond/branch_0_fun/while
  591.9 9.5 %copy-start.14 = (f32[320,256]{1,0:T(8,128)S(1)}, f32[320,256]{1,0:T(8,128)}, u32[]{:S(2)}) copy-start(f32[320,256]{1,0:T(8,128)} %get-tuple-element.520.lband_ref) | copy-start | bytes 983044 | tf_op jit(solution)/shard_map/cond/branch_0_fun/while
  592.2 4.8 collective-permute-start
  594.4 7.0 collective-permute-start.1
  618.2 2.3 collective-permute-start.2
  665.6 5.1 collective-permute-start.3
  683.5 4.4 copy-start.7
  683.5 4.4 copy-start.10
  701.8 19.7 %all-to-all-start.2 = ((f32[128,2,768]{2,1,0:T(2,128)}), f32[128,2,768]{2,1,0:T(2,128)S(1)}, u32[]{:S(2)}, u32[]{:S(2)}) async-start(f32[128,2,768]{2,1,0:T(2,128)} %reshape.104), calls=%async_computation.2 | async-start | bytes 1572864 | tf_op jit(solution)/shard_map/cond/branch_0_fun/all_to_all | solution.py:583
  (7 other events, 15.0 us)

commit v2 on v1

--- a/solution.py
+++ b/solution.py
@@ -55,53 +55,78 @@
 
 
 def assemble_kernel(
-    group_ref, first_ref, stiff_ref, place_ref, offset_ref, diag_ref, out_ref,
-    rows_ref, small_ref, block_ref, lane_ref,
+    group_ref, first_ref, stiff_ref, place_ref, offset_ref, diag_ref,
+    out_ref, up_ref, down_ref,
+    rows_ref, small_ref, block_ref, lane_ref, wait_ref,
 ):
     slots, _, tiles = stiff_ref.shape
     windows = out_ref.shape[0]
     lanes = BATCH * slots
     one = lambda mask: jnp.where(mask, 1.0, 0.0).astype(BF16)
-    block_ref[...] = one(iota((lanes, lanes), 0) // slots == iota((lanes, lanes), 1) // slots)
+    block_ref[...] = one(iota((lanes, lanes), 0) % BATCH == iota((lanes, lanes), 1) // slots)
     for t in range(BATCH):
-        lane_ref[t * SPAN : (t + 1) * SPAN] = one(iota((SPAN, lanes), 1) // slots == t)
+        lane_ref[t * SPAN : (t + 1) * SPAN] = one(iota((SPAN, lanes), 1) % BATCH == t)
 
     def clear(g, carry):
         small_ref[g] = jnp.zeros((SMALL, SMALL), F32)
         return carry
 
     lax.fori_loop(0, small_ref.shape[0], clear, 0)
-    for i in range(slots):
-        plane = stiff_ref[i]
-        stacked = jnp.concatenate([plane] * (128 // slots), axis=0)
-        rows_ref[pl.ds(i, tiles, stride=slots), :] = stacked.T
+
+    def turn(i, carry):
+        for n in range(4):
+            plane = stiff_ref[4 * i + n]
+            rows_ref[4 * i + n] = jnp.concatenate([plane] * (128 // slots), axis=0).T
+        return carry
+
+    lax.fori_loop(0, slots // 4, turn, 0)
 
     row_in_window = iota((SMALL, lanes), 0)
     row_in_span = iota((SPAN, lanes), 0)
 
-    def product_of(b):
-        base = pl.multiple_of(b * lanes, lanes)
-        parts = halves(rows_ref[pl.ds(base, lanes), :])
+    def first_side(b):
+        base = pl.multiple_of(b * BATCH, BATCH)
+        parts = halves(rows_ref[:, pl.ds(base, BATCH), :].reshape(lanes, 128))
         block = block_ref[...]
         wide = [jnp.concatenate([part] * (lanes // 128), axis=1) * block for part in parts]
         hot = one(row_in_window == place_ref[pl.ds(b, 1), :])
-        both = dot(jnp.concatenate(wide, axis=0), hot, ((1,), (1,)))
-        uh, ul = halves(both[:lanes] + both[lanes:])
+        return jnp.concatenate(wide, axis=0), hot
+
+    def second_side(b):
         match = one(row_in_span == offset_ref[pl.ds(b, 1), :])
-        pick = jnp.concatenate([match] * BATCH, axis=0) * lane_ref[...]
-        full = dot(pick, jnp.concatenate([uh, ul], axis=1))
-        return full[:, :SMALL] + full[:, SMALL:]
-
-    def batch(i, carry):
-        full = [product_of(TOGETHER * i + n) for n in range(TOGETHER)]
+        return jnp.concatenate([match] * BATCH, axis=0) * lane_ref[...]
+
+    def compute(i):
+        batches = [TOGETHER * i + n for n in range(TOGETHER)]
+        sides = [first_side(b) for b in batches]
+        both = [dot(wide, hot, ((1,), (1,))) for wide, hot in sides]
+        picks = [second_side(b) for b in batches]
+        rights = [jnp.concatenate(halves(x[:lanes] + x[lanes:]), axis=1) for x in both]
+        full = [dot(pick, right) for pick, right in zip(picks, rights)]
+        return [x[:, :SMALL] + x[:, SMALL:] for x in full]
+
+    def hold(full):
+        for n in range(TOGETHER):
+            wait_ref[n] = full[n]
+
+    def add_up(i):
         for n in range(TOGETHER):
             for t in range(BATCH):
                 tile = (TOGETHER * i + n) * BATCH + t
                 r = pl.multiple_of(first_ref[tile], 16)
-                small_ref[group_ref[tile], pl.ds(r, SPAN), :] += full[n][t * SPAN : (t + 1) * SPAN]
-        return carry
-
-    lax.fori_loop(0, tiles // (BATCH * TOGETHER), batch, 0)
+                small_ref[group_ref[tile], pl.ds(r, SPAN), :] += wait_ref[n, t * SPAN : (t + 1) * SPAN]
+
+    rounds = tiles // (BATCH * TOGETHER)
+    hold(compute(0))
+
+    def batch(i, carry):
+        full = compute(i)
+        add_up(i - 1)
+        hold(full)
+        return carry
+
+    lax.fori_loop(1, rounds, batch, 0)
+    add_up(rounds - 1)
 
     eye = iota((WIN, WIN), 0) == iota((WIN, WIN), 1)
     gap = jnp.zeros((SMALL, REACH), F32)
@@ -115,6 +140,10 @@
         return carry
 
     lax.fori_loop(0, windows, gather, 0)
+    up_ref[:128] = out_ref[windows - 2, 128:]
+    up_ref[128:] = out_ref[windows - 1, :192]
+    down_ref[:WIN] = out_ref[0]
+    down_ref[WIN:] = out_ref[1, :64]
 
 
 def assemble(tile_stiff, tile_nodes, node_shift):
@@ -131,16 +160,18 @@
     diag = jnp.pad(diag, ((0, 0), (0, WIN - STEP)))
     lanes = BATCH * slots
     smem = pl.BlockSpec(memory_space=pltpu.SMEM)
+    edge = jax.ShapeDtypeStruct((320, WIN), F32)
     return pl.pallas_call(
         assemble_kernel,
-        out_shape=jax.ShapeDtypeStruct((windows, WIN, WIN), F32),
+        out_shape=(jax.ShapeDtypeStruct((windows, WIN, WIN), F32), edge, edge),
         in_specs=[smem, smem] + in_vmem(4),
-        out_specs=pl.BlockSpec(memory_space=pltpu.VMEM),
+        out_specs=tuple(in_vmem(3)),
         scratch_shapes=[
-            pltpu.VMEM((tiles * slots, 128), F32),
+            pltpu.VMEM((slots, tiles, 128), F32),
             pltpu.VMEM((smalls, SMALL, SMALL), F32),
             pltpu.VMEM((lanes, lanes), BF16),
             pltpu.VMEM((BATCH * SPAN, lanes), BF16),
+            pltpu.VMEM((TOGETHER, BATCH * SPAN, SMALL), F32),
         ],
         compiler_params=pltpu.CompilerParams(vmem_limit_bytes=28 << 20),
         name="assemble",
@@ -149,7 +180,7 @@
         first,
         jnp.transpose(tile_stiff, (1, 2, 0)),
         place.reshape(-1, lanes),
-        offset.reshape(-1, lanes),
+        offset.reshape(-1, BATCH, slots).transpose(0, 2, 1).reshape(-1, lanes),
         diag,
     )
 
@@ -159,14 +190,14 @@
 
 def powers_kernel(
     valid_ref, own_ref, left_ref, right_ref, band_ref, lband_ref, rband_ref,
-    k1_ref, k2_ref, mine_ref, theirs_ref,
-    bh_ref, bl_ref, lh_ref, ll_ref, rh_ref, rl_ref,
-    vh_ref, vl_ref, wh_ref, wl_ref, y_ref,
+    image_ref, mine_ref, theirs_ref,
+    bh_ref, bl_ref, lh_ref, ll_ref, rh_ref, rl_ref, vh_ref, vl_ref, y_ref,
 ):
     own, cols = own_ref.shape
     windows = band_ref.shape[0]
-    frame = vh_ref.shape[0]
+    frame = y_ref.shape[0]
     high = LOW + own
+    chunk = 256
 
     def split_band(g, carry):
         bh_ref[g], bl_ref[g] = halves(band_ref[g])
@@ -175,122 +206,120 @@
     lax.fori_loop(0, windows, split_band, 0)
     lh_ref[...], ll_ref[...] = halves(lband_ref[...])
     rh_ref[...], rl_ref[...] = halves(rband_ref[...])
-
-    zero = jnp.zeros((LOW - EDGE, cols), BF16)
-    tail = jnp.zeros((frame - high - EDGE, cols), BF16)
     for ref in (vh_ref, vl_ref):
-        ref[: LOW - EDGE] = zero
-        ref[high + EDGE :] = tail
-    vh_ref[LOW - EDGE : LOW], vl_ref[LOW - EDGE : LOW] = halves(left_ref[...])
-    vh_ref[high : high + EDGE], vl_ref[high : high + EDGE] = halves(right_ref[...])
-    chunk = 256
+        for n, width in enumerate((EDGE, HALO)):
+            ref[n, : LOW - width] = jnp.zeros((LOW - width, cols), BF16)
+            ref[n, high + width :] = jnp.zeros((frame - high - width, cols), BF16)
+
+    def put(n, at, value):
+        vh_ref[n, at, :], vl_ref[n, at, :] = halves(value)
+
+    put(0, pl.ds(LOW - EDGE, EDGE), left_ref[...])
+    put(0, pl.ds(high, EDGE), right_ref[...])
 
     def split_own(i, carry):
         at = pl.multiple_of(i * chunk, chunk)
-        h, l = halves(own_ref[pl.ds(at, chunk), :])
-        vh_ref[pl.ds(LOW + at, chunk), :] = h
-        vl_ref[pl.ds(LOW + at, chunk), :] = l
+        put(0, pl.ds(LOW + at, chunk), own_ref[pl.ds(at, chunk), :])
         return carry
 
     lax.fori_loop(0, own // chunk, split_own, 0)
 
-    def apply(xh_ref, xl_ref):
-        y_ref[...] = jnp.zeros_like(y_ref)
+    def clear(i, carry):
+        y_ref[pl.ds(pl.multiple_of(i * 64, 64), 64), :] = jnp.zeros((64, cols), F32)
+        return carry
+
+    tn = ((0,), (0,))
+
+    def keep_moment(j, value):
+        here = valid_ref[2] == j // ITERS
+        for ref, chosen in ((mine_ref, here), (theirs_ref, jnp.logical_not(here))):
+            @pl.when(chosen)
+            def _(ref=ref):
+                for c in range(cols // 128):
+                    ref[j % ITERS, c] = value[:, c * 128 : (c + 1) * 128]
+
+    def power(n, carry):
+        now = n % 2
+        then = 1 - now
+        lax.fori_loop(0, frame // 64, clear, 0)
 
         def window(i, carry):
             values = []
-            for n in range(3):
-                at = pl.multiple_of(HALO + (3 * i + n) * STEP, 64)
-                xh = xh_ref[pl.ds(at, WIN), :]
-                xl = xl_ref[pl.ds(at, WIN), :]
-                values.append((at, dot3(bh_ref[3 * i + n], bl_ref[3 * i + n], xh, xl)))
+            for m in range(3):
+                at = pl.multiple_of(HALO + (3 * i + m) * STEP, 64)
+                xh = vh_ref[now, pl.ds(at, WIN), :]
+                xl = vl_ref[now, pl.ds(at, WIN), :]
+                values.append((at, dot3(bh_ref[3 * i + m], bl_ref[3 * i + m], xh, xl)))
             for at, value in values:
                 y_ref[pl.ds(at, WIN), :] += value
             return carry
 
         lax.fori_loop(0, windows // 3, window, 0)
 
-        def extra(h_ref, l_ref, lo, rows, out, at):
-            y_ref[out : out + rows] += dot3(
+        values = []
+        for h_ref, l_ref, lo, rows, out, at in (
+            (lh_ref, ll_ref, 0, 128, HALO, 0),
+            (lh_ref, ll_ref, 128, 192, HALO + 64, HALO + 64),
+            (rh_ref, rl_ref, 0, 256, own + HALO, own + HALO),
+            (rh_ref, rl_ref, 256, 64, own + HALO + STEP, own + HALO + STEP),
+        ):
+            value = dot3(
                 h_ref[lo : lo + rows], l_ref[lo : lo + rows],
-                xh_ref[at : at + WIN], xl_ref[at : at + WIN],
+                vh_ref[now, at : at + WIN], vl_ref[now, at : at + WIN],
             )
-
-        extra(lh_ref, ll_ref, 0, 128, HALO, 0)
-        extra(lh_ref, ll_ref, 128, 192, HALO + 64, HALO + 64)
-        extra(rh_ref, rl_ref, 0, 256, own + HALO, own + HALO)
-        extra(rh_ref, rl_ref, 256, 64, own + HALO + STEP, own + HALO + STEP)
-
-    def keep(oh_ref, ol_ref):
-        oh_ref[:HALO] = jnp.zeros((HALO, cols), BF16)
-        ol_ref[:HALO] = jnp.zeros((HALO, cols), BF16)
-        oh_ref[high + HALO :] = jnp.zeros((frame - high - HALO, cols), BF16)
-        ol_ref[high + HALO :] = jnp.zeros((frame - high - HALO, cols), BF16)
-        lower = jnp.where(valid_ref[0] > 0, y_ref[HALO:LOW], 0.0)
-        upper = jnp.where(valid_ref[1] > 0, y_ref[high : high + HALO], 0.0)
-        oh_ref[HALO:LOW], ol_ref[HALO:LOW] = halves(lower)
-        oh_ref[high : high + HALO], ol_ref[high : high + HALO] = halves(upper)
+            values.append((out, rows, value))
+        for out, rows, value in values:
+            y_ref[out : out + rows] += value
+
+        put(then, pl.ds(HALO, HALO), jnp.where(valid_ref[0] > 0, y_ref[HALO:LOW], 0.0))
+        put(then, pl.ds(high, HALO), jnp.where(valid_ref[1] > 0, y_ref[high : high + HALO], 0.0))
 
         def split(i, carry):
-            at = pl.multiple_of(LOW + i * chunk, chunk)
-            h, l = halves(y_ref[pl.ds(at, chunk), :])
-            oh_ref[pl.ds(at, chunk), :] = h
-            ol_ref[pl.ds(at, chunk), :] = l
+            at = pl.multiple_of(i * chunk, chunk)
+            value = y_ref[pl.ds(LOW + at, chunk), :]
+            put(then, pl.ds(LOW + at, chunk), value)
+
+            @pl.when(n + 1 < ITERS)
+            def _():
+                image_ref[jnp.minimum(n, ITERS - 2), pl.ds(at, chunk), :] = value
+
             return carry
 
         lax.fori_loop(0, own // chunk, split, 0)
 
-    tn = ((0,), (0,))
-
-    def put(n, value):
-        here = valid_ref[2] == n // ITERS
-
-        @pl.when(here)
+        xh, xl = vh_ref[now, LOW:high], vl_ref[now, LOW:high]
+        zh, zl = vh_ref[then, LOW:high], vl_ref[then, LOW:high]
+        by_high = dot(xh, jnp.concatenate([xh, xl, zh, zl], axis=1), tn)
+        by_low = dot(xl, zh, tn)
+        cross = by_high[:, cols : 2 * cols]
+        keep_moment(2 * n, by_high[:, :cols] + (cross + cross.T))
+        keep_moment(2 * n + 1, by_high[:, 2 * cols : 3 * cols] + (by_high[:, 3 * cols :] + by_low))
+
+        @pl.when(n == 0)
         def _():
-            for c in range(cols // 128):
-                mine_ref[n % ITERS, c] = value[:, c * 128 : (c + 1) * 128]
-
-        @pl.when(jnp.logical_not(here))
-        def _():
-            for c in range(cols // 128):
-                theirs_ref[n % ITERS, c] = value[:, c * 128 : (c + 1) * 128]
-
-    def moments(n, xh_ref, xl_ref, zh_ref, zl_ref):
-        xh, zh = xh_ref[LOW:high], zh_ref[LOW:high]
-        by_high = dot(xh, jnp.concatenate([xh, xl_ref[LOW:high], zh, zl_ref[LOW:high]], axis=1), tn)
-        by_low = dot(xl_ref[LOW:high], zh, tn)
-        cross = by_high[:, cols : 2 * cols]
-        put(n, by_high[:, :cols] + (cross + cross.T))
-        put(n + 1, by_high[:, 2 * cols : 3 * cols] + (by_high[:, 3 * cols :] + by_low))
-
-    apply(vh_ref, vl_ref)
-    k1_ref[...] = y_ref[LOW:high]
-    keep(wh_ref, wl_ref)
-    moments(0, vh_ref, vl_ref, wh_ref, wl_ref)
-    apply(wh_ref, wl_ref)
-    k2_ref[...] = y_ref[LOW:high]
-    keep(vh_ref, vl_ref)
-    moments(2, wh_ref, wl_ref, vh_ref, vl_ref)
-    apply(vh_ref, vl_ref)
-    keep(wh_ref, wl_ref)
-    moments(4, vh_ref, vl_ref, wh_ref, wl_ref)
+            for ref in (vh_ref, vl_ref):
+                ref[0, : HALO] = jnp.zeros((HALO, cols), BF16)
+                ref[0, high + HALO :] = jnp.zeros((frame - high - HALO, cols), BF16)
+
+        return carry
+
+    lax.fori_loop(0, ITERS, power, 0)
 
 
 def powers(vector, left, right, valid, bands):
     band, lband, rband = bands
     own, cols = vector.shape
     frame = own + 2 * LOW + 64
-    full = jax.ShapeDtypeStruct((own, cols), F32)
     half = jax.ShapeDtypeStruct((ITERS, cols // 128, cols, 128), F32)
-    wide = pltpu.VMEM((frame, cols), BF16)
+    wide = pltpu.VMEM((2, frame, cols), BF16)
     edge = pltpu.VMEM(lband.shape, BF16)
     return pl.pallas_call(
         powers_kernel,
-        out_shape=(full, full, half, half),
+        out_shape=(jax.ShapeDtypeStruct((ITERS - 1, own, cols), F32), half, half),
         in_specs=[pl.BlockSpec(memory_space=pltpu.SMEM)] + in_vmem(6),
-        out_specs=tuple(in_vmem(4)),
+        out_specs=tuple(in_vmem(3)),
         compiler_params=pltpu.CompilerParams(vmem_limit_bytes=32 << 20),
-        scratch_shapes=[pltpu.VMEM(band.shape, BF16)] * 2 + [edge] * 4 + [wide] * 4
+        scratch_shapes=[pltpu.VMEM(band.shape, BF16)] * 2 + [edge] * 4 + [wide] * 2
         + [pltpu.VMEM((frame, cols), F32)],
         name="powers",
     )(valid, vector, left, right, band, lband, rband)
@@ -461,7 +490,7 @@
         answer, residual, direction, gram = state
         on_direction = k % 2 == 0
         vector = jnp.where(on_direction, direction, residual)
-        image, _, mine, theirs = powers(vector, *halo_of(vector), valid, bands)
+        image, mine, theirs = powers(vector, *halo_of(vector), valid, bands)
         low, high = total_of(mine, theirs)
         low = jnp.where(valid[2] == 0, low, high)
         square = gram_of(low[0])
@@ -471,7 +500,7 @@
             jnp.where(on_direction, dir_gram, gram), jnp.where(on_direction, gram, square)
         )
         along = times(direction, factor)
-        applied = times(image + SHIFT * vector, factor)
+        applied = times(image[0] + SHIFT * vector, factor)
         answer = jnp.where(on_direction, answer + along, answer)
         direction = jnp.where(on_direction, direction, residual + along)
         residual = jnp.where(on_direction, residual - applied, residual)
@@ -562,7 +591,7 @@
 
 
 def basis(vectors, weights):
-    rows, cols = vectors[0].shape
+    rows, cols = vectors[0][0].shape[-2:]
     loads = weights[0].shape[0]
     weight = pl.BlockSpec((loads, CHUNK), lambda i: (0, i))
     out = (loads // 3, 3 * len(vectors) * cols)
@@ -570,29 +599,32 @@
         basis_kernel,
         grid=(rows // CHUNK,),
         out_shape=jax.ShapeDtypeStruct(out, F32),
-        in_specs=[pl.BlockSpec((CHUNK, cols), lambda i: (i, 0))] * len(vectors) + [weight, weight],
+        in_specs=[spec for _, spec in vectors] + [weight, weight],
         out_specs=pl.BlockSpec(out, lambda i: (0, 0)),
         compiler_params=pltpu.CompilerParams(vmem_limit_bytes=28 << 20),
         name="basis",
-    )(*vectors, *weights)
-
-
-def to_owner(rows, dipole_slot):
+    )(*[vector for vector, _ in vectors], *weights)
+
+
+def in_chunks(vector, n=None):
+    cols = vector.shape[-1]
+    if n is None:
+        return vector, pl.BlockSpec((CHUNK, cols), lambda i: (i, 0))
+    return vector, pl.BlockSpec((None, CHUNK, cols), lambda i: (n, i, 0))
+
+
+def to_owner(rows):
     slots, wide = rows.shape
     count = lax.axis_size(AXES)
-    received = lax.all_to_all(rows.reshape(count, slots // count, wide), AXES, 0, 0, tiled=True)
-    return received.reshape(slots, wide)[dipole_slot]
-
-
-def combine_kernel(k0_ref, k1_ref, k2_ref, c_ref, picked_ref, x_ref, out_ref, ch_ref, cl_ref):
+    return lax.all_to_all(rows.reshape(count, slots // count, wide), AXES, 0, 0, tiled=True)
+
+
+def combine_kernel(k0_ref, k1_ref, k2_ref, c_ref, x_ref, ch_ref, cl_ref):
     size = c_ref.shape[1]
 
     @pl.when(pl.program_id(0) == 0)
     def _():
         ch_ref[...], cl_ref[...] = halves(c_ref[...])
-        wide = c_ref.shape[0]
-        for k in range(3):
-            out_ref[k] = dot3(*halves(picked_ref[:, k * wide : (k + 1) * wide]), ch_ref[...], cl_ref[...])
 
     total = jnp.zeros(x_ref.shape, F32)
     for n, ref in enumerate((k0_ref, k1_ref, k2_ref)):
@@ -602,27 +634,55 @@
     x_ref[...] = total
 
 
-def combine(k0, k1, k2, coef, picked):
-    rows, cols = k0.shape
-    block = pl.BlockSpec((CHUNK, cols), lambda i: (i, 0))
-    whole = lambda shape: pl.BlockSpec(shape, lambda i: (0,) * len(shape))
-    out = (3, picked.shape[0], cols)
+def combine(vectors, coef):
+    rows, cols = vectors[0][0].shape[-2:]
     return pl.pallas_call(
         combine_kernel,
         grid=(rows // CHUNK,),
-        out_shape=(jax.ShapeDtypeStruct((rows, cols), F32), jax.ShapeDtypeStruct(out, F32)),
-        in_specs=[block] * 3 + [whole(coef.shape), whole(picked.shape)],
-        out_specs=(block, whole(out)),
+        out_shape=jax.ShapeDtypeStruct((rows, cols), F32),
+        in_specs=[spec for _, spec in vectors] + [pl.BlockSpec(coef.shape, lambda i: (0, 0))],
+        out_specs=pl.BlockSpec((CHUNK, cols), lambda i: (i, 0)),
         scratch_shapes=[pltpu.VMEM(coef.shape, BF16)] * 2,
-        compiler_params=pltpu.CompilerParams(vmem_limit_bytes=28 << 20),
+        compiler_params=pltpu.CompilerParams(vmem_limit_bytes=20 << 20),
         name="combine",
-    )(k0, k1, k2, coef, picked)
-
-
-def exact_path(right_side, valid, bands, weights, dipole_slot):
-    answer = plain_cg(right_side, valid, bands)
-    picked = to_owner(basis([answer], weights), dipole_slot)
-    return answer, picked.reshape(picked.shape[0], 3, -1).transpose(1, 0, 2)
+    )(*[vector for vector, _ in vectors], coef)
+
+
+def lead_kernel(slot_ref, received_ref, c_ref, out_ref, pick_ref):
+    _, places, wide = received_ref.shape
+    dipoles = out_ref.shape[1]
+    together = 8
+
+    def pick(i, carry):
+        for n in range(together):
+            slot = slot_ref[i * together + n]
+            pick_ref[pl.ds(i * together + n, 1), :] = received_ref[slot // places, pl.ds(slot % places, 1), :]
+        return carry
+
+    lax.fori_loop(0, dipoles // together, pick, 0)
+    ch, cl = halves(c_ref[...])
+    part = wide // 3
+    for k in range(3):
+        out_ref[k] = dot3(*halves(pick_ref[:, k * part : (k + 1) * part]), ch, cl)
+
+
+def lead(received, dipole_slot, coef):
+    out = (3, dipole_slot.shape[0], coef.shape[1])
+    return pl.pallas_call(
+        lead_kernel,
+        out_shape=jax.ShapeDtypeStruct(out, F32),
+        in_specs=[pl.BlockSpec(memory_space=pltpu.SMEM)] + in_vmem(2),
+        out_specs=in_vmem(1)[0],
+        scratch_shapes=[pltpu.VMEM((dipole_slot.shape[0], received.shape[2]), F32)],
+        compiler_params=pltpu.CompilerParams(vmem_limit_bytes=20 << 20),
+        name="lead",
+    )(dipole_slot, received, coef)
+
+
+def lead_exactly(answer, weights, dipole_slot):
+    received = to_owner(basis([in_chunks(answer)], weights))
+    picked = received.reshape(-1, received.shape[2])[dipole_slot]
+    return picked.reshape(picked.shape[0], 3, -1).transpose(1, 0, 2)
 
 
 def one_device(right_side, tile_stiff, tile_nodes, node_shift, slot_nodes, slot_load, dipole_slot):
@@ -631,20 +691,24 @@
     core = lax.axis_index("core")
     valid = jnp.stack([index > 0, index < count - 1, core]).astype(jnp.int32)
     left, right = halo_of(right_side)
-    band = assemble(tile_stiff, tile_nodes, node_shift)
-    to_right = jnp.concatenate([band[-2, 128:], band[-1, :192]], axis=0)
-    to_left = jnp.concatenate([band[0], band[1, :64]], axis=0)
+    band, to_right, to_left = assemble(tile_stiff, tile_nodes, node_shift)
     bands = (band, *both_ways(to_right, to_left))
     weights = load_matrix(slot_nodes, slot_load, right_side.shape[0])
-    k1, k2, mine, theirs = powers(right_side, left, right, valid, bands)
-    rows = basis([right_side, k1, k2], weights)
-    picked = to_owner(rows, dipole_slot)
-    coef, good = galerkin(core[None], *total_of(mine, theirs))
-    return lax.cond(
-        good[0] > 0,
-        lambda: combine(right_side, k1, k2, coef, picked),
-        lambda: exact_path(right_side, valid, bands, weights, dipole_slot),
-    )
+    images, mine, theirs = powers(right_side, left, right, valid, bands)
+    vectors = [in_chunks(right_side), in_chunks(images, 0), in_chunks(images, 1)]
+    rows = basis(vectors, weights)
+    received = to_owner(rows)
+    mine, theirs = total_of(mine, theirs)
+    coef, good = galerkin(core[None], mine, theirs)
+    answer = combine(vectors, coef)
+    leadfield = lead(received, dipole_slot, coef)
+
+    def exactly(_):
+        exact = plain_cg(right_side, valid, bands)
+        return jnp.ones((), jnp.int32), exact, lead_exactly(exact, weights, dipole_slot)
+
+    state = lax.while_loop(lambda state: state[0] == 0, exactly, (good[0], answer, leadfield))
+    return state[1:]
 
 
 def solution(mesh):

time: 736 us -> 742 us (level); the launches traced: 726 us -> 740 us
  local copies, waits for them, and re-layouts: 28.1 us -> 57.9 us
  waiting for transfers between devices: 78.4 us -> 70.1 us
    while x70 -> x87, local copies, waits for them, and re-layouts: 12.5 us -> 33.1 us
    unnamed x26 -> x25, local copies, waits for them, and re-layouts: 4.57 us -> 15.2 us
    all_to_all x2, waiting for transfers between devices: 24.1 us -> 16 us  [to_owner(): lax.all_to_all(rows.reshape(count, slots // count, wide), AXES, 0, 0, til...]
    pallas_call x7 -> x9, Pallas kernels: 124 us -> 123 us  [the longest x6 99.8 us: powers(): pl.pallas_call(powers_kernel, out_shape=(jax.ShapeDtypeStruct((ITERS - 1,...]
where the time goes in v2:
time: 742 us; the launch traced here: 740 us
  blocking collectives  258 us (35%)
  Pallas kernels  217 us (29%)
  starting transfers between devices  71.1 us (10%)
  waiting for transfers between devices  70.1 us (9%)
  local copies, waits for them, and re-layouts  57.9 us (8%)
  matrix products  48.6 us (7%)
  other arithmetic  15.1 us (2%)
    all_to_all x6, blocking collectives, total_of(): arrived = lax.all_to_all(pair, CHIPS, 0, 0, tiled=True)  166 us
    pallas_call x6, Pallas kernels, powers(): pl.pallas_call(powers_kernel, out_shape=(jax.ShapeDtypeStruct((ITERS - 1,...  99.8 us
    all_to_all x5, blocking collectives, total_of(): gathered = lax.all_to_all(own, CHIPS, 0, 0, tiled=True)  91.9 us
    pallas_call x5, Pallas kernels, solve(): pl.pallas_call(solve_kernel, out_shape=jax.ShapeDtypeStruct(target.shape,...  53.4 us
    dot_general x10, matrix products, times(): jnp.dot(a, b, preferred_element_type=F32, precision=lax.Precision.HIGHEST)  48.6 us
    while x86, local copies, waits for them, and re-layouts  32.2 us
    ppermute x7, waiting for transfers between devices, both_ways(): lax.ppermute(to_left, AXES, [(b, a) for a, b in up])  26.4 us
    pallas_call x1, Pallas kernels, galerkin(): pl.pallas_call(galerkin_kernel, out_shape=(jax.ShapeDtypeStruct((ITERS *...  20.5 us
  transfers between devices with their start and end apart: 29, of which 26 were waited for; matrix products, arithmetic and copies ran while one was open for 1% of the time, Pallas kernels for 5%

profile of v2, /device:TPU:1, one launch (start us, length us, event | category | flops | bytes accessed | tf_op | source)
XLA Modules:
  0.0 740.5 jit_solution(16555751768014124158)
XLA Ops:
  4.8 14.9 %assemble.1 = (f32[12,256,256]{2,1,0:T(8,128)}, f32[320,256]{1,0:T(8,128)S(1)}, f32[320,256]{1,0:T(8,128)S(1)}) custom-call(s32[256]{0:T(256)S(1)} %get-tuple-element.433.group_ref, s32[256]{0:T(256)S(1)} %multiply_minimum_fusion.first_ref, f32[32,32,256]{2,1,0:T(8,128)S(1)} %bitcast.57, s32[32,256]{1,0:T(8,128)S(1)} %reshape.128.place_ref, ...), custom_call_target="tpu_custom_call" | custom-call | tf_op jit(solution)/shard_map/assemble/pallas_call | solution.py:164
  19.7 4.9 collective-permute-start.6
  27.6 3.6 collective-permute-start.4
  33.9 4.4 collective-permute-done.5.right_ref
  38.3 18.4 %powers.9 = (f32[2,2048,256]{2,1,0:T(8,128)S(1)}, f32[3,2,256,128]{3,2,1,0:T(8,128)S(1)}, f32[3,2,256,128]{3,2,1,0:T(8,128)S(1)}) custom-call(s32[3]{0:T(128)S(1)} %pad_add_fusion.valid_ref, f32[2048,256]{1,0:T(8,128)} %refs_0_.1, f32[192,256]{1,0:T(8,128)S(1)} %collective-permute-done.4.left_ref, f32[192,256]{1,0:T(8,128)S(1)} %collective-permute-done.5.right_ref, ...), custom_call_target="tpu_custom_call" | custom-call | tf_op jit(solution)/shard_map/powers/pallas_call | solution.py:316
  61.0 32.3 %all_to_all.47 = f32[64,24,128]{2,1,0:T(8,128)S(1)} all-to-all(f32[64,24,128]{2,1,0:T(8,128)S(1)} %bitcast.61), channel_id=1, replica_groups=mesh['row'=4,'column'=4,'depth'=4,'core'=2] {'row','column','depth'}, dimensions={0} | all-to-all | bytes 1572864 | tf_op jit(solution)/shard_map/all_to_all | solution.py:465
  94.3 4.8 all-to-all-start.4
  99.9 4.5 loads.1
  109.3 9.5 %basis.3 = f32[256,2304]{1,0:T(8,128)S(1)} custom-call(f32[2048,256]{1,0:T(8,128)} %refs_0_.1, f32[2,2048,256]{2,1,0:T(8,128)S(1)} %copy-done.3, f32[2,2048,256]{2,1,0:T(8,128)S(1)} %copy-done.3, bf16[768,2048]{1,0:T(8,128)(2,1)S(1)} %get-tuple-element.598.refs_3_, bf16[768,2048]{1,0:T(8,128)(2,1)S(1)} %get-tuple-element.599.refs_4_), custom_call_target="tpu_custom_call" | custom-call | tf_op jit(solution)/shard_map/basis/pallas_call | solution.py:598
  118.8 2.5 reshape.137
  121.3 10.8 %all-to-all-start.5 = ((f32[128,2,2304]{2,1,0:T(2,128)}), f32[128,2,2304]{2,1,0:T(2,128)S(1)}, u32[]{:S(2)}, u32[]{:S(2)}) async-start(f32[128,2,2304]{2,1,0:T(2,128)} %reshape.137), calls=%async_computation.5 | async-start | bytes 4718592 | tf_op jit(solution)/shard_map/all_to_all | solution.py:619
  135.1 20.5 %galerkin.1 = (f32[768,256]{1,0:T(8,128)S(1)}, s32[1]{0:T(128)}) custom-call(s32[1]{0:T(128)} %bitcast.4.core_ref, f32[3,2,256,128]{3,2,1,0:T(8,128)S(1)} %bitcast.56, f32[3,2,256,128]{3,2,1,0:T(8,128)S(1)} %collective-permute-done.9.theirs_ref), custom_call_target="tpu_custom_call" | custom-call | tf_op jit(solution)/shard_map/galerkin/pallas_call | solution.py:430
  157.9 5.6 combine.1
  166.1 2.6 lead.1
  169.6 569.0 %while.31 = (s32[]{:T(128)}, f32[2048,256]{1,0:T(8,128)}, f32[3,128,256]{1,2,0:T(8,128)}, s32[]{:T(128)}, s32[3]{0:T(128)S(1)}, /*index=5*/f32[12,256,256]{2,1,0...) while((s32[]{:T(128)}, f32[2048,256]{1,0:T(8,128)}, ...), condition=%region_6.7_spmd, body=%region_2.6_spmd | while | flops 3228105216 | bytes 147095456 | solution.py:710
  170.3 3.2 copy.30
  174.9 533.4 %while.33 = (s32[]{:T(128)}, f32[2048,256]{1,0:T(8,128)}, f32[2048,256]{1,0:T(8,128)}, f32[2048,256]{1,0:T(8,128)}, f32[256,256]{1,0:T(8,128)S(1)}, /*index=5*/p...) while((s32[]{:T(128)}, f32[2048,256]{1,0:T(8,128)}, ...), condition=%wide.region_5.5_spmd.clone, body=%wide.region_3.4_spmd.clone.sunk | while | flops 3228103680 | bytes 121923144 | solution.py:510
  177.4 3.3 collective-permute-start
  183.3 4.4 collective-permute-done.1.right_ref
  187.7 16.3 %powers.10 = (f32[2,2048,256]{2,1,0:T(8,128)S(1)}, f32[3,2,256,128]{3,2,1,0:T(8,128)S(1)}, f32[3,2,256,128]{3,2,1,0:T(8,128)S(1)}) custom-call(s32[3]{0:T(128)S(1)} %get-tuple-element.581.valid_ref, f32[2048,256]{1,0:T(8,128)S(1)} %broadcast_select_fusion.5.own_ref, f32[192,256]{1,0:T(8,128)S(1)} %collective-permute-done.left_ref, ...), custom_call_target="tpu_custom_call" | custom-call | tf_op jit(solution)/shard_map/while/body/while/body/eval_jaxpr/powers/pallas_call | solution.py:316
  208.3 27.7 %all_to_all.48 = f32[64,24,128]{2,1,0:T(8,128)S(1)} all-to-all(f32[64,24,128]{2,1,0:T(8,128)S(1)} %bitcast.60), channel_id=1, replica_groups=mesh['row'=4,'column'=4,'depth'=4,'core'=2] {'row','column','depth'}, dimensions={0} | all-to-all | bytes 1572864 | tf_op jit(solution)/shard_map/while/body/while/body/eval_jaxpr/all_to_all | solution.py:465
  236.2 18.4 %all_to_all.49 = f32[64,24,128]{2,1,0:T(8,128)S(1)} all-to-all(f32[64,24,128]{2,1,0:T(8,128)S(1)} %broadcast_in_dim.45), channel_id=1, replica_groups=mesh['row'=4,'column'=4,'depth'=4,'core'=2] {'row','column','depth'}, dimensions={0} | all-to-all | bytes 1572864 | tf_op jit(solution)/shard_map/while/body/while/body/eval_jaxpr/all_to_all | solution.py:467
  254.5 3.1 collective-permute-start.3
  261.8 10.7 %solve.8 = f32[256,256]{1,0:T(8,128)} custom-call(f32[256,256]{1,0:T(8,128)} %get-tuple-element.542.matrix_ref, f32[256,256]{1,0:T(8,128)S(1)} %get-tuple-element.579.target_ref), custom_call_target="tpu_custom_call" | custom-call | tf_op jit(solution)/shard_map/while/body/while/body/eval_jaxpr/solve/pallas_call | solution.py:450
  272.4 6.0 add_select_fusion.3
  278.4 3.3 subtract_select_fusion.3
  287.6 2.4 collective-permute-start.1
  290.2 4.4 collective-permute-done.1.right_ref
  294.6 16.3 %powers.10 = (f32[2,2048,256]{2,1,0:T(8,128)S(1)}, f32[3,2,256,128]{3,2,1,0:T(8,128)S(1)}, f32[3,2,256,128]{3,2,1,0:T(8,128)S(1)}) custom-call(s32[3]{0:T(128)S(1)} %get-tuple-element.581.valid_ref, f32[2048,256]{1,0:T(8,128)S(1)} %broadcast_select_fusion.5.own_ref, f32[192,256]{1,0:T(8,128)S(1)} %collective-permute-done.left_ref, ...), custom_call_target="tpu_custom_call" | custom-call | tf_op jit(solution)/shard_map/while/body/while/body/eval_jaxpr/powers/pallas_call | solution.py:316
  315.2 26.4 %all_to_all.48 = f32[64,24,128]{2,1,0:T(8,128)S(1)} all-to-all(f32[64,24,128]{2,1,0:T(8,128)S(1)} %bitcast.60), channel_id=1, replica_groups=mesh['row'=4,'column'=4,'depth'=4,'core'=2] {'row','column','depth'}, dimensions={0} | all-to-all | bytes 1572864 | tf_op jit(solution)/shard_map/while/body/while/body/eval_jaxpr/all_to_all | solution.py:465
  341.8 18.4 %all_to_all.49 = f32[64,24,128]{2,1,0:T(8,128)S(1)} all-to-all(f32[64,24,128]{2,1,0:T(8,128)S(1)} %broadcast_in_dim.45), channel_id=1, replica_groups=mesh['row'=4,'column'=4,'depth'=4,'core'=2] {'row','column','depth'}, dimensions={0} | all-to-all | bytes 1572864 | tf_op jit(solution)/shard_map/while/body/while/body/eval_jaxpr/all_to_all | solution.py:467
  360.2 3.1 collective-permute-start.3
  367.5 10.7 %solve.8 = f32[256,256]{1,0:T(8,128)} custom-call(f32[256,256]{1,0:T(8,128)} %get-tuple-element.542.matrix_ref, f32[256,256]{1,0:T(8,128)S(1)} %get-tuple-element.579.target_ref), custom_call_target="tpu_custom_call" | custom-call | tf_op jit(solution)/shard_map/while/body/while/body/eval_jaxpr/solve/pallas_call | solution.py:450
  378.1 6.6 add_select_fusion.3
  384.7 3.3 subtract_select_fusion.3
  393.9 2.4 collective-permute-start.1
  396.5 4.4 collective-permute-done.1.right_ref
  400.9 16.3 %powers.10 = (f32[2,2048,256]{2,1,0:T(8,128)S(1)}, f32[3,2,256,128]{3,2,1,0:T(8,128)S(1)}, f32[3,2,256,128]{3,2,1,0:T(8,128)S(1)}) custom-call(s32[3]{0:T(128)S(1)} %get-tuple-element.581.valid_ref, f32[2048,256]{1,0:T(8,128)S(1)} %broadcast_select_fusion.5.own_ref, f32[192,256]{1,0:T(8,128)S(1)} %collective-permute-done.left_ref, ...), custom_call_target="tpu_custom_call" | custom-call | tf_op jit(solution)/shard_map/while/body/while/body/eval_jaxpr/powers/pallas_call | solution.py:316
  421.5 26.5 %all_to_all.48 = f32[64,24,128]{2,1,0:T(8,128)S(1)} all-to-all(f32[64,24,128]{2,1,0:T(8,128)S(1)} %bitcast.60), channel_id=1, replica_groups=mesh['row'=4,'column'=4,'depth'=4,'core'=2] {'row','column','depth'}, dimensions={0} | all-to-all | bytes 1572864 | tf_op jit(solution)/shard_map/while/body/while/body/eval_jaxpr/all_to_all | solution.py:465
  448.2 18.4 %all_to_all.49 = f32[64,24,128]{2,1,0:T(8,128)S(1)} all-to-all(f32[64,24,128]{2,1,0:T(8,128)S(1)} %broadcast_in_dim.45), channel_id=1, replica_groups=mesh['row'=4,'column'=4,'depth'=4,'core'=2] {'row','column','depth'}, dimensions={0} | all-to-all | bytes 1572864 | tf_op jit(solution)/shard_map/while/body/while/body/eval_jaxpr/all_to_all | solution.py:467
  466.5 3.1 collective-permute-start.3
  473.8 10.7 %solve.8 = f32[256,256]{1,0:T(8,128)} custom-call(f32[256,256]{1,0:T(8,128)} %get-tuple-element.542.matrix_ref, f32[256,256]{1,0:T(8,128)S(1)} %get-tuple-element.579.target_ref), custom_call_target="tpu_custom_call" | custom-call | tf_op jit(solution)/shard_map/while/body/while/body/eval_jaxpr/solve/pallas_call | solution.py:450
  484.4 6.6 add_select_fusion.3
  491.0 3.3 subtract_select_fusion.3
  500.2 2.4 collective-permute-start.1
  502.8 4.4 collective-permute-done.1.right_ref
  507.2 16.3 %powers.10 = (f32[2,2048,256]{2,1,0:T(8,128)S(1)}, f32[3,2,256,128]{3,2,1,0:T(8,128)S(1)}, f32[3,2,256,128]{3,2,1,0:T(8,128)S(1)}) custom-call(s32[3]{0:T(128)S(1)} %get-tuple-element.581.valid_ref, f32[2048,256]{1,0:T(8,128)S(1)} %broadcast_select_fusion.5.own_ref, f32[192,256]{1,0:T(8,128)S(1)} %collective-permute-done.left_ref, ...), custom_call_target="tpu_custom_call" | custom-call | tf_op jit(solution)/shard_map/while/body/while/body/eval_jaxpr/powers/pallas_call | solution.py:316
  527.9 26.5 %all_to_all.48 = f32[64,24,128]{2,1,0:T(8,128)S(1)} all-to-all(f32[64,24,128]{2,1,0:T(8,128)S(1)} %bitcast.60), channel_id=1, replica_groups=mesh['row'=4,'column'=4,'depth'=4,'core'=2] {'row','column','depth'}, dimensions={0} | all-to-all | bytes 1572864 | tf_op jit(solution)/shard_map/while/body/while/body/eval_jaxpr/all_to_all | solution.py:465
  554.5 18.4 %all_to_all.49 = f32[64,24,128]{2,1,0:T(8,128)S(1)} all-to-all(f32[64,24,128]{2,1,0:T(8,128)S(1)} %broadcast_in_dim.45), channel_id=1, replica_groups=mesh['row'=4,'column'=4,'depth'=4,'core'=2] {'row','column','depth'}, dimensions={0} | all-to-all | bytes 1572864 | tf_op jit(solution)/shard_map/while/body/while/body/eval_jaxpr/all_to_all | solution.py:467
  572.9 3.1 collective-permute-start.3
  580.1 10.7 %solve.8 = f32[256,256]{1,0:T(8,128)} custom-call(f32[256,256]{1,0:T(8,128)} %get-tuple-element.542.matrix_ref, f32[256,256]{1,0:T(8,128)S(1)} %get-tuple-element.579.target_ref), custom_call_target="tpu_custom_call" | custom-call | tf_op jit(solution)/shard_map/while/body/while/body/eval_jaxpr/solve/pallas_call | solution.py:450
  590.8 6.6 add_select_fusion.3
  597.4 3.3 subtract_select_fusion.3
  609.1 4.4 collective-permute-done.1.right_ref
  613.5 16.3 %powers.10 = (f32[2,2048,256]{2,1,0:T(8,128)S(1)}, f32[3,2,256,128]{3,2,1,0:T(8,128)S(1)}, f32[3,2,256,128]{3,2,1,0:T(8,128)S(1)}) custom-call(s32[3]{0:T(128)S(1)} %get-tuple-element.581.valid_ref, f32[2048,256]{1,0:T(8,128)S(1)} %broadcast_select_fusion.5.own_ref, f32[192,256]{1,0:T(8,128)S(1)} %collective-permute-done.left_ref, ...), custom_call_target="tpu_custom_call" | custom-call | tf_op jit(solution)/shard_map/while/body/while/body/eval_jaxpr/powers/pallas_call | solution.py:316
  634.2 26.5 %all_to_all.48 = f32[64,24,128]{2,1,0:T(8,128)S(1)} all-to-all(f32[64,24,128]{2,1,0:T(8,128)S(1)} %bitcast.60), channel_id=1, replica_groups=mesh['row'=4,'column'=4,'depth'=4,'core'=2] {'row','column','depth'}, dimensions={0} | all-to-all | bytes 1572864 | tf_op jit(solution)/shard_map/while/body/while/body/eval_jaxpr/all_to_all | solution.py:465
  660.8 18.4 %all_to_all.49 = f32[64,24,128]{2,1,0:T(8,128)S(1)} all-to-all(f32[64,24,128]{2,1,0:T(8,128)S(1)} %broadcast_in_dim.45), channel_id=1, replica_groups=mesh['row'=4,'column'=4,'depth'=4,'core'=2] {'row','column','depth'}, dimensions={0} | all-to-all | bytes 1572864 | tf_op jit(solution)/shard_map/while/body/while/body/eval_jaxpr/all_to_all | solution.py:467
  679.2 3.1 collective-permute-start.3
  686.4 10.7 %solve.8 = f32[256,256]{1,0:T(8,128)} custom-call(f32[256,256]{1,0:T(8,128)} %get-tuple-element.542.matrix_ref, f32[256,256]{1,0:T(8,128)S(1)} %get-tuple-element.579.target_ref), custom_call_target="tpu_custom_call" | custom-call | tf_op jit(solution)/shard_map/while/body/while/body/eval_jaxpr/solve/pallas_call | solution.py:450
  697.1 6.6 add_select_fusion.3
  703.7 3.3 subtract_select_fusion.3
  708.3 5.7 basis.2
  715.3 3.6 all-to-all-start.2
  719.5 15.4 %all-to-all-done.2 = f32[128,2,768]{2,1,0:T(2,128)S(1)} async-done(((f32[128,2,768]{2,1,0:T(2,128)}), f32[128,2,768]{2,1,0:T(2,128)S(1)}, u32[]{:S(2)}, u32[]{:S(2)}) %all-to-all-start.2) | async-done | bytes 786464 | tf_op jit(solution)/shard_map/while/body/all_to_all | solution.py:619
  (217 shorter events, 113.1 us)
Async XLA Ops:
  19.7 18.5 %collective-permute-start.6 = (f32[320,256]{1,0:T(8,128)S(1)}, f32[320,256]{1,0:T(8,128)S(1)}, u32[]{:S(2)}, u32[]{:S(2)}) collective-permute-start(f32[320,256]{1,0:T(8,128)S(1)} %get-tuple-element.313), channel_id=1, source_target_pairs={{0,1},{1,2},{2,3},{3,4},{4,5},{5,6},{6,7},{7,8},{8,9},{9,10},{10,1... | collective-permute-start | bytes 983048 | tf_op jit(solution)/shard_map/ppermute | solution.py:475
  24.6 13.6 %collective-permute-start.7 = (f32[320,256]{1,0:T(8,128)S(1)}, f32[320,256]{1,0:T(8,128)S(1)}, u32[]{:S(2)}, u32[]{:S(2)}) collective-permute-start(f32[320,256]{1,0:T(8,128)S(1)} %get-tuple-element.314), channel_id=1, source_target_pairs={{1,0},{2,1},{3,2},{4,3},{5,4},{6,5},{7,6},{8,7},{9,8},{10,9},{11,1... | collective-permute-start | bytes 983048 | tf_op jit(solution)/shard_map/ppermute | solution.py:475
  27.6 6.2 collective-permute-start.4
  31.3 7.0 collective-permute-start.5
  38.3 18.4 %copy-start.13 = (f32[320,256]{1,0:T(8,128)}, f32[320,256]{1,0:T(8,128)S(1)}, u32[]{:S(2)}) copy-start(f32[320,256]{1,0:T(8,128)S(1)} %collective-permute-done.7.rband_ref) | copy-start | bytes 983044
  56.7 2.0 copy-start.2
  58.7 2.3 collective-permute-start.8
  61.0 38.2 %copy-start.18 = (f32[16,768]{1,0:T(8,128)S(1)}, f32[16,768]{1,0:T(8,128)}, u32[]{:S(2)}) copy-start(f32[16,768]{1,0:T(8,128)} %param.16) | copy-start | bytes 147460
  94.3 5.4 copy-start.19
  94.3 26.9 %all-to-all-start.4 = ((f32[64,24,128]{2,1,0:T(8,128)}), f32[64,24,128]{2,1,0:T(8,128)S(1)}, u32[]{:S(2)}, u32[]{:S(2)}) async-start(f32[64,24,128]{2,1,0:T(8,128)} %broadcast_in_dim.38), calls=%async_computation.4 | async-start | bytes 1572864 | tf_op jit(solution)/shard_map/all_to_all | solution.py:467
  104.4 2.7 copy-start.17
  107.1 2.2 copy-start.3
  121.3 43.6 %all-to-all-start.5 = ((f32[128,2,2304]{2,1,0:T(2,128)}), f32[128,2,2304]{2,1,0:T(2,128)S(1)}, u32[]{:S(2)}, u32[]{:S(2)}) async-start(f32[128,2,2304]{2,1,0:T(2,128)} %reshape.137), calls=%async_computation.5 | async-start | bytes 4718592 | tf_op jit(solution)/shard_map/all_to_all | solution.py:619
  132.1 3.1 collective-permute-start.9
  155.7 2.2 copy-start.4
  170.3 3.2 copy-start.12
  174.9 2.2 copy-start.8
  177.1 10.6 %copy-start.10 = (f32[12,256,256]{2,1,0:T(8,128)S(1)}, f32[12,256,256]{2,1,0:T(8,128)}, u32[]{:S(2)}) copy-start(f32[12,256,256]{2,1,0:T(8,128)} %get-tuple-element.582.band_ref) | copy-start | bytes 9437188 | tf_op jit(solution)/shard_map/while/body/while
  177.4 5.9 collective-permute-start
  180.7 7.0 collective-permute-start.1
  204.0 2.0 copy-start
  205.9 2.3 collective-permute-start.2
  254.5 5.1 collective-permute-start.3
  272.4 6.0 copy-start.1
  272.4 6.0 copy-start.9
  272.4 6.0 copy-start.11
  283.0 2.2 copy-start.8
  285.2 9.4 %copy-start.10 = (f32[12,256,256]{2,1,0:T(8,128)S(1)}, f32[12,256,256]{2,1,0:T(8,128)}, u32[]{:S(2)}) copy-start(f32[12,256,256]{2,1,0:T(8,128)} %get-tuple-element.582.band_ref) | copy-start | bytes 9437188 | tf_op jit(solution)/shard_map/while/body/while
  285.5 4.7 collective-permute-start
  287.6 7.0 collective-permute-start.1
  312.9 2.3 collective-permute-start.2
  360.2 5.1 collective-permute-start.3
  378.1 6.6 copy-start.1
  378.1 6.6 copy-start.9
  378.1 6.6 copy-start.11
  389.3 2.2 copy-start.8
  391.5 9.4 %copy-start.10 = (f32[12,256,256]{2,1,0:T(8,128)S(1)}, f32[12,256,256]{2,1,0:T(8,128)}, u32[]{:S(2)}) copy-start(f32[12,256,256]{2,1,0:T(8,128)} %get-tuple-element.582.band_ref) | copy-start | bytes 9437188 | tf_op jit(solution)/shard_map/while/body/while
  391.9 4.7 collective-permute-start
  393.9 7.0 collective-permute-start.1
  417.2 2.0 copy-start
  419.2 2.3 collective-permute-start.2
  466.5 5.1 collective-permute-start.3
  484.4 6.6 copy-start.1
  484.4 6.6 copy-start.9
  484.4 6.6 copy-start.11
  495.6 2.2 copy-start.8
  497.9 9.4 %copy-start.10 = (f32[12,256,256]{2,1,0:T(8,128)S(1)}, f32[12,256,256]{2,1,0:T(8,128)}, u32[]{:S(2)}) copy-start(f32[12,256,256]{2,1,0:T(8,128)} %get-tuple-element.582.band_ref) | copy-start | bytes 9437188 | tf_op jit(solution)/shard_map/while/body/while
  498.2 4.7 collective-permute-start
  500.2 7.0 collective-permute-start.1
  525.5 2.3 collective-permute-start.2
  572.9 5.1 collective-permute-start.3
  590.8 6.6 copy-start.1
  590.8 6.6 copy-start.9
  590.8 6.6 copy-start.11
  602.0 2.2 copy-start.8
  604.2 9.4 %copy-start.10 = (f32[12,256,256]{2,1,0:T(8,128)S(1)}, f32[12,256,256]{2,1,0:T(8,128)}, u32[]{:S(2)}) copy-start(f32[12,256,256]{2,1,0:T(8,128)} %get-tuple-element.582.band_ref) | copy-start | bytes 9437188 | tf_op jit(solution)/shard_map/while/body/while
  604.5 4.7 collective-permute-start
  606.5 7.0 collective-permute-start.1
  631.8 2.3 collective-permute-start.2
  679.2 5.1 collective-permute-start.3
  697.1 6.6 copy-start.1
  697.1 6.6 copy-start.9
  697.1 6.6 copy-start.11
  715.3 19.7 %all-to-all-start.2 = ((f32[128,2,768]{2,1,0:T(2,128)}), f32[128,2,768]{2,1,0:T(2,128)S(1)}, u32[]{:S(2)}, u32[]{:S(2)}) async-start(f32[128,2,768]{2,1,0:T(2,128)} %reshape.114), calls=%async_computation.2 | async-start | bytes 1572864 | tf_op jit(solution)/shard_map/while/body/all_to_all | solution.py:619
  (13 other events, 18.9 us)

commit v3 on v2

--- a/solution.py
+++ b/solution.py
@@ -18,7 +18,7 @@
 STEP = WIN - REACH
 SHIFT = 4.5
 ROUNDS = 8
-CLOSE = 1e-7
+CLOSE = 1e-6
 GUARD = 0.01
 SMALL = 128
 SPAN = 80
@@ -55,8 +55,8 @@
 
 
 def assemble_kernel(
-    group_ref, first_ref, stiff_ref, place_ref, offset_ref, diag_ref,
-    out_ref, up_ref, down_ref,
+    core_ref, group_ref, first_ref, stiff_ref, place_ref, offset_ref, diag_ref,
+    out_ref, inner_ref, outer_ref,
     rows_ref, small_ref, block_ref, lane_ref, wait_ref,
 ):
     slots, _, tiles = stiff_ref.shape
@@ -140,13 +140,18 @@
         return carry
 
     lax.fori_loop(0, windows, gather, 0)
-    up_ref[:128] = out_ref[windows - 2, 128:]
-    up_ref[128:] = out_ref[windows - 1, :192]
-    down_ref[:WIN] = out_ref[0]
-    down_ref[WIN:] = out_ref[1, :64]
-
-
-def assemble(tile_stiff, tile_nodes, node_shift):
+
+    def edges(up_ref, down_ref):
+        up_ref[:128] = out_ref[windows - 2, 128:]
+        up_ref[128:] = out_ref[windows - 1, :192]
+        down_ref[:WIN] = out_ref[0]
+        down_ref[WIN:] = out_ref[1, :64]
+
+    pl.when(core_ref[0] == 0)(lambda: edges(inner_ref, outer_ref))
+    pl.when(core_ref[0] != 0)(lambda: edges(outer_ref, inner_ref))
+
+
+def assemble(core, tile_stiff, tile_nodes, node_shift):
     tiles, slots = tile_nodes.shape
     ext = node_shift.shape[0] + 2 * HALO
     windows = ext // STEP
@@ -164,7 +169,7 @@
     return pl.pallas_call(
         assemble_kernel,
         out_shape=(jax.ShapeDtypeStruct((windows, WIN, WIN), F32), edge, edge),
-        in_specs=[smem, smem] + in_vmem(4),
+        in_specs=[smem] * 3 + in_vmem(4),
         out_specs=tuple(in_vmem(3)),
         scratch_shapes=[
             pltpu.VMEM((slots, tiles, 128), F32),
@@ -176,6 +181,7 @@
         compiler_params=pltpu.CompilerParams(vmem_limit_bytes=28 << 20),
         name="assemble",
     )(
+        core,
         group,
         first,
         jnp.transpose(tile_stiff, (1, 2, 0)),
@@ -189,9 +195,9 @@
 
 
 def powers_kernel(
-    valid_ref, own_ref, left_ref, right_ref, band_ref, lband_ref, rband_ref,
+    valid_ref, own_ref, inner_ref, outer_ref, band_ref, iband_ref, oband_ref,
     image_ref, mine_ref, theirs_ref,
-    bh_ref, bl_ref, lh_ref, ll_ref, rh_ref, rl_ref, vh_ref, vl_ref, y_ref,
+    bh_ref, bl_ref, lh_ref, ll_ref, rh_ref, rl_ref, vh_ref, vl_ref, y_ref, sem,
 ):
     own, cols = own_ref.shape
     windows = band_ref.shape[0]
@@ -204,8 +210,6 @@
         return carry
 
     lax.fori_loop(0, windows, split_band, 0)
-    lh_ref[...], ll_ref[...] = halves(lband_ref[...])
-    rh_ref[...], rl_ref[...] = halves(rband_ref[...])
     for ref in (vh_ref, vl_ref):
         for n, width in enumerate((EDGE, HALO)):
             ref[n, : LOW - width] = jnp.zeros((LOW - width, cols), BF16)
@@ -214,8 +218,14 @@
     def put(n, at, value):
         vh_ref[n, at, :], vl_ref[n, at, :] = halves(value)
 
-    put(0, pl.ds(LOW - EDGE, EDGE), left_ref[...])
-    put(0, pl.ds(high, EDGE), right_ref[...])
+    def sides(left_ref, right_ref, lband_ref, rband_ref):
+        put(0, pl.ds(LOW - EDGE, EDGE), left_ref[...])
+        put(0, pl.ds(high, EDGE), right_ref[...])
+        lh_ref[...], ll_ref[...] = halves(lband_ref[...])
+        rh_ref[...], rl_ref[...] = halves(rband_ref[...])
+
+    pl.when(valid_ref[2] == 0)(lambda: sides(outer_ref, inner_ref, oband_ref, iband_ref))
+    pl.when(valid_ref[2] != 0)(lambda: sides(inner_ref, outer_ref, iband_ref, oband_ref))
 
     def split_own(i, carry):
         at = pl.multiple_of(i * chunk, chunk)
@@ -278,13 +288,12 @@
             at = pl.multiple_of(i * chunk, chunk)
             value = y_ref[pl.ds(LOW + at, chunk), :]
             put(then, pl.ds(LOW + at, chunk), value)
-
-            @pl.when(n + 1 < ITERS)
-            def _():
-                image_ref[jnp.minimum(n, ITERS - 2), pl.ds(at, chunk), :] = value
-
             return carry
 
+        copy = pltpu.make_async_copy(
+            y_ref.at[pl.ds(LOW, own)], image_ref.at[jnp.minimum(n, ITERS - 2)], sem
+        )
+        pl.when(n + 1 < ITERS)(copy.start)
         lax.fori_loop(0, own // chunk, split, 0)
 
         xh, xl = vh_ref[now, LOW:high], vl_ref[now, LOW:high]
@@ -295,6 +304,8 @@
         keep_moment(2 * n, by_high[:, :cols] + (cross + cross.T))
         keep_moment(2 * n + 1, by_high[:, 2 * cols : 3 * cols] + (by_high[:, 3 * cols :] + by_low))
 
+        pl.when(n + 1 < ITERS)(copy.wait)
+
         @pl.when(n == 0)
         def _():
             for ref in (vh_ref, vl_ref):
@@ -306,23 +317,23 @@
     lax.fori_loop(0, ITERS, power, 0)
 
 
-def powers(vector, left, right, valid, bands):
-    band, lband, rband = bands
+def powers(vector, inner, outer, valid, bands):
+    band, inner_band, outer_band = bands
     own, cols = vector.shape
     frame = own + 2 * LOW + 64
     half = jax.ShapeDtypeStruct((ITERS, cols // 128, cols, 128), F32)
     wide = pltpu.VMEM((2, frame, cols), BF16)
-    edge = pltpu.VMEM(lband.shape, BF16)
+    edge = pltpu.VMEM(inner_band.shape, BF16)
     return pl.pallas_call(
         powers_kernel,
-        out_shape=(jax.ShapeDtypeStruct((ITERS - 1, own, cols), F32), half, half),
+        out_shape=(pltpu.HBM((ITERS - 1, own, cols), F32), half, half),
         in_specs=[pl.BlockSpec(memory_space=pltpu.SMEM)] + in_vmem(6),
-        out_specs=tuple(in_vmem(3)),
+        out_specs=(pl.BlockSpec(memory_space=pltpu.HBM), *in_vmem(2)),
         compiler_params=pltpu.CompilerParams(vmem_limit_bytes=32 << 20),
         scratch_shapes=[pltpu.VMEM(band.shape, BF16)] * 2 + [edge] * 4 + [wide] * 2
-        + [pltpu.VMEM((frame, cols), F32)],
+        + [pltpu.VMEM((frame, cols), F32), pltpu.SemaphoreType.DMA],
         name="powers",
-    )(valid, vector, left, right, band, lband, rband)
+    )(valid, vector, inner, outer, band, inner_band, outer_band)
 
 
 def diagonals(matrix):
@@ -347,7 +358,7 @@
 
     def going(state):
         k, worst, _, _ = state
-        return (k < 40) & (worst > limit)
+        return (k < 40) & (size * worst * worst > limit)
 
     def step(state):
         k, _, total, power = state
@@ -358,9 +369,11 @@
 
     total = factor * (unit + rest)
     power = mul(rest, rest)
-    rounds, worst, total, _ = lax.while_loop(
+    rounds, worst, total, power = lax.while_loop(
         going, step, (1, jnp.max(jnp.abs(power)), total, power)
     )
+    worst = size * worst * worst
+    total = total + mul(total, power)
     return total * scale, worst, rounds
 
 
@@ -368,7 +381,7 @@
     return jnp.min(diagonals(left)[0] / diagonals(whole)[0])
 
 
-def galerkin_kernel(core_ref, mine_ref, theirs_ref, out_ref, good_ref, mom_ref):
+def galerkin_kernel(core_ref, mine_ref, theirs_ref, basis_ref, out_ref, rows_ref, good_ref, mom_ref):
     parts = mine_ref.shape[1]
 
     def unpack(source_ref, start):
@@ -396,14 +409,13 @@
 
     s0, w0, k0 = inverse_spd(h[0], split_dot, CLOSE)
     z01, z02, z0m = right_of(s0, h[1], h[2], m[0])
-    lower = split_dot(
-        jnp.concatenate([h[1], h[2]], axis=0), jnp.concatenate([z01, z02, z0m], axis=1)
-    )
-    first = h[2] - lower[:size, :size]
-    cross = h[3] - lower[:size, size : 2 * size]
-    m1 = m[1] - lower[:size, 2 * size :]
-    last = h[4] - lower[size:, size : 2 * size]
-    m2 = m[2] - lower[size:, 2 * size :]
+    upper = split_dot(h[1], jnp.concatenate([z01, z02, z0m], axis=1))
+    lower = split_dot(h[2], jnp.concatenate([z02, z0m], axis=1))
+    first = h[2] - upper[:, :size]
+    cross = h[3] - upper[:, size : 2 * size]
+    m1 = m[1] - upper[:, 2 * size :]
+    last = h[4] - lower[:, :size]
+    m2 = m[2] - lower[:, size:]
     first = 0.5 * (first + first.T)
     s1, w1, k1 = inverse_spd(first, split_dot, CLOSE)
     z12, z1m = right_of(s1, cross, m1)
@@ -418,24 +430,34 @@
     out_ref[:size] = y0
     out_ref[size : 2 * size] = y1
     out_ref[2 * size :] = y2
+    wide = out_ref.shape[0]
+    yh, yl = halves(out_ref[...])
+    for k in range(3):
+        part = dot3(*halves(basis_ref[:, k * wide : (k + 1) * wide]), yh, yl)
+        rows_ref[:, k * size : (k + 1) * size] = part
     share = jnp.minimum(ratio(first, h[2]), ratio(rest, h[4]))
     rounds = jnp.maximum(k0, jnp.maximum(k1, k2))
     worst = jnp.maximum(w0, jnp.maximum(w1, w2))
     good_ref[0] = jnp.where((share > GUARD) & (worst <= CLOSE) & (rounds <= ROUNDS), 1, 0)
 
 
-def galerkin(core, mine, theirs):
+def galerkin(core, mine, theirs, basis_rows):
     size = mine.shape[2]
+    slots, wide = basis_rows.shape
     smem = pl.BlockSpec(memory_space=pltpu.SMEM)
     return pl.pallas_call(
         galerkin_kernel,
-        out_shape=(jax.ShapeDtypeStruct((ITERS * size, size), F32), jax.ShapeDtypeStruct((1,), jnp.int32)),
-        in_specs=[smem] + in_vmem(2),
-        out_specs=(pl.BlockSpec(memory_space=pltpu.VMEM), smem),
+        out_shape=(
+            jax.ShapeDtypeStruct((ITERS * size, size), F32),
+            jax.ShapeDtypeStruct((slots, wide // ITERS), F32),
+            jax.ShapeDtypeStruct((1,), jnp.int32),
+        ),
+        in_specs=[smem] + in_vmem(3),
+        out_specs=(*in_vmem(2), smem),
         scratch_shapes=[pltpu.VMEM((2 * ITERS, size, size), F32)],
         compiler_params=pltpu.CompilerParams(vmem_limit_bytes=32 << 20),
         name="galerkin",
-    )(core, mine, theirs)
+    )(core, mine, theirs, basis_rows)
 
 
 def solve_kernel(matrix_ref, target_ref, out_ref):
@@ -469,14 +491,19 @@
     return gathered, lax.ppermute(gathered, "core", other)
 
 
-def both_ways(to_right, to_left):
+def swap_sides(inner, outer):
     count = lax.axis_size(AXES)
-    up = [(i, i + 1) for i in range(count - 1)]
-    return lax.ppermute(to_right, AXES, up), lax.ppermute(to_left, AXES, [(b, a) for a, b in up])
+    across = [(i, i + 1) for i in range(1, count - 1, 2)]
+    return (
+        lax.ppermute(inner, "core", [(0, 1), (1, 0)]),
+        lax.ppermute(outer, AXES, across + [(b, a) for a, b in across]),
+    )
 
 
 def halo_of(vector):
-    return both_ways(vector[-EDGE:], vector[:EDGE])
+    first = lax.axis_index("core") == 0
+    head, tail = vector[:EDGE], vector[-EDGE:]
+    return swap_sides(jnp.where(first, tail, head), jnp.where(first, head, tail))
 
 
 def plain_cg(right_side, valid, bands):
@@ -610,7 +637,8 @@
     cols = vector.shape[-1]
     if n is None:
         return vector, pl.BlockSpec((CHUNK, cols), lambda i: (i, 0))
-    return vector, pl.BlockSpec((None, CHUNK, cols), lambda i: (n, i, 0))
+    placed = pltpu.with_memory_space_constraint(vector, pltpu.HBM)
+    return placed, pl.BlockSpec((None, CHUNK, cols), lambda i: (n, i, 0))
 
 
 def to_owner(rows):
@@ -648,41 +676,32 @@
     )(*[vector for vector, _ in vectors], coef)
 
 
-def lead_kernel(slot_ref, received_ref, c_ref, out_ref, pick_ref):
+def lead_kernel(slot_ref, received_ref, out_ref):
     _, places, wide = received_ref.shape
-    dipoles = out_ref.shape[1]
+    _, dipoles, cols = out_ref.shape
     together = 8
 
     def pick(i, carry):
         for n in range(together):
             slot = slot_ref[i * together + n]
-            pick_ref[pl.ds(i * together + n, 1), :] = received_ref[slot // places, pl.ds(slot % places, 1), :]
+            row = received_ref[slot // places, pl.ds(slot % places, 1), :]
+            for k in range(wide // cols):
+                out_ref[k, pl.ds(i * together + n, 1), :] = row[:, k * cols : (k + 1) * cols]
         return carry
 
     lax.fori_loop(0, dipoles // together, pick, 0)
-    ch, cl = halves(c_ref[...])
-    part = wide // 3
-    for k in range(3):
-        out_ref[k] = dot3(*halves(pick_ref[:, k * part : (k + 1) * part]), ch, cl)
-
-
-def lead(received, dipole_slot, coef):
-    out = (3, dipole_slot.shape[0], coef.shape[1])
+
+
+def lead(received, dipole_slot):
+    out = (3, dipole_slot.shape[0], received.shape[2] // 3)
     return pl.pallas_call(
         lead_kernel,
         out_shape=jax.ShapeDtypeStruct(out, F32),
-        in_specs=[pl.BlockSpec(memory_space=pltpu.SMEM)] + in_vmem(2),
+        in_specs=[pl.BlockSpec(memory_space=pltpu.SMEM)] + in_vmem(1),
         out_specs=in_vmem(1)[0],
-        scratch_shapes=[pltpu.VMEM((dipole_slot.shape[0], received.shape[2]), F32)],
         compiler_params=pltpu.CompilerParams(vmem_limit_bytes=20 << 20),
         name="lead",
-    )(dipole_slot, received, coef)
-
-
-def lead_exactly(answer, weights, dipole_slot):
-    received = to_owner(basis([in_chunks(answer)], weights))
-    picked = received.reshape(-1, received.shape[2])[dipole_slot]
-    return picked.reshape(picked.shape[0], 3, -1).transpose(1, 0, 2)
+    )(dipole_slot, received)
 
 
 def one_device(right_side, tile_stiff, tile_nodes, node_shift, slot_nodes, slot_load, dipole_slot):
@@ -690,22 +709,23 @@
     index = lax.axis_index(AXES)
     core = lax.axis_index("core")
     valid = jnp.stack([index > 0, index < count - 1, core]).astype(jnp.int32)
-    left, right = halo_of(right_side)
-    band, to_right, to_left = assemble(tile_stiff, tile_nodes, node_shift)
-    bands = (band, *both_ways(to_right, to_left))
+    inner, outer = halo_of(right_side)
+    band, inner_band, outer_band = assemble(core[None], tile_stiff, tile_nodes, node_shift)
+    bands = (band, *swap_sides(inner_band, outer_band))
     weights = load_matrix(slot_nodes, slot_load, right_side.shape[0])
-    images, mine, theirs = powers(right_side, left, right, valid, bands)
+    images, mine, theirs = powers(right_side, inner, outer, valid, bands)
     vectors = [in_chunks(right_side), in_chunks(images, 0), in_chunks(images, 1)]
-    rows = basis(vectors, weights)
+    basis_rows = basis(vectors, weights)
+    mine, theirs = total_of(mine, theirs)
+    coef, rows, good = galerkin(core[None], mine, theirs, basis_rows)
     received = to_owner(rows)
-    mine, theirs = total_of(mine, theirs)
-    coef, good = galerkin(core[None], mine, theirs)
     answer = combine(vectors, coef)
-    leadfield = lead(received, dipole_slot, coef)
+    leadfield = lead(received, dipole_slot)
 
     def exactly(_):
         exact = plain_cg(right_side, valid, bands)
-        return jnp.ones((), jnp.int32), exact, lead_exactly(exact, weights, dipole_slot)
+        received = to_owner(basis([in_chunks(exact)], weights))
+        return jnp.ones((), jnp.int32), exact, lead(received, dipole_slot)
 
     state = lax.while_loop(lambda state: state[0] == 0, exactly, (good[0], answer, leadfield))
     return state[1:]

time: 742 us -> 697 us (0.939)
  local copies, waits for them, and re-layouts: 57.9 us -> 27.9 us
  starting transfers between devices: 71.1 us -> 43.9 us
  blocking collectives: 258 us -> 275 us
  waiting for transfers between devices: 70.1 us -> 61.1 us
    all_to_all x6, blocking collectives: 166 us -> 145 us  [total_of(): arrived = lax.all_to_all(pair, CHIPS, 0, 0, tiled=True)]
    all_to_all x0 -> x1, blocking collectives: none -> 19.5 us  [to_owner(): lax.all_to_all(rows.reshape(count, slots // count, wide), AXES, 0, 0, til...]
    all_to_all x5 -> x6, blocking collectives: 91.9 us -> 110 us  [total_of(): gathered = lax.all_to_all(own, CHIPS, 0, 0, tiled=True)]
    ppermute x14, starting transfers between devices: 35.5 us -> 21.4 us  [the longest x7 18.3 us: swap_sides(): lax.ppermute(outer, AXES, across + [(b, a) for a, b in across])]
    unnamed x25 -> x18, local copies, waits for them, and re-layouts: 15.2 us -> 2.27 us
    all_to_all x2 -> x1, starting transfers between devices: 14.3 us -> 3.55 us  [to_owner(): lax.all_to_all(rows.reshape(count, slots // count, wide), AXES, 0, 0, til...]
    while x87 -> x76, local copies, waits for them, and re-layouts: 33.1 us -> 22.4 us
    all_to_all x2 -> x1, waiting for transfers between devices: 16 us -> 9.81 us  [to_owner(): lax.all_to_all(rows.reshape(count, slots // count, wide), AXES, 0, 0, til...]
  transfers between devices with their start and end apart: 29 -> 27, of which waited for: 26 -> 18; matrix products, arithmetic and copies ran while one was open for 1% -> 0% of each run, Pallas kernels for 5% -> 3%
where the time goes in v3:
time: 697 us; the launch traced here: 696 us
  blocking collectives  275 us (39%)
  Pallas kernels  220 us (32%)
  waiting for transfers between devices  61.1 us (9%)
  matrix products  48.6 us (7%)
  starting transfers between devices  43.9 us (6%)
  local copies, waits for them, and re-layouts  27.9 us (4%)
  other arithmetic  15.6 us (2%)
    all_to_all x6, blocking collectives, total_of(): arrived = lax.all_to_all(pair, CHIPS, 0, 0, tiled=True)  145 us
    all_to_all x6, blocking collectives, total_of(): gathered = lax.all_to_all(own, CHIPS, 0, 0, tiled=True)  110 us
    pallas_call x6, Pallas kernels, powers(): pl.pallas_call(powers_kernel, out_shape=(pltpu.HBM((ITERS - 1, own, cols)...  97.3 us
    pallas_call x5, Pallas kernels, solve(): pl.pallas_call(solve_kernel, out_shape=jax.ShapeDtypeStruct(target.shape,...  53.3 us
    dot_general x10, matrix products, times(): jnp.dot(a, b, preferred_element_type=F32, precision=lax.Precision.HIGHEST)  48.6 us
    ppermute x7, waiting for transfers between devices, swap_sides(): lax.ppermute(outer, AXES, across + [(b, a) for a, b in across])  27.4 us
    while x76, local copies, waits for them, and re-layouts  22.4 us
    pallas_call x1, Pallas kernels, galerkin(): pl.pallas_call(galerkin_kernel, out_shape=(jax.ShapeDtypeStruct((ITERS *...  21.8 us
  transfers between devices with their start and end apart: 27, of which 18 were waited for; matrix products, arithmetic and copies ran while one was open for 0% of the time, Pallas kernels for 3%

profile of v3, /device:TPU:1, one launch (start us, length us, event | category | flops | bytes accessed | tf_op | source)
XLA Modules:
  0.0 695.6 jit_solution(7687784462687099396)
XLA Ops:
  4.8 15.0 %assemble.1 = (f32[12,256,256]{2,1,0:T(8,128)}, f32[320,256]{1,0:T(8,128)S(1)}, f32[320,256]{1,0:T(8,128)S(1)}) custom-call(s32[1]{0:T(128)} %bitcast.core_ref, s32[256]{0:T(256)S(1)} %get-tuple-element.407.group_ref, s32[256]{0:T(256)S(1)} %multiply_minimum_fusion.first_ref, f32[32,32,256]{2,1,0:T(8,128)S(1)} %bitcast.50, ...), custom_call_target="tpu_custom_call" | custom-call | tf_op jit(solution)/shard_map/assemble/pallas_call | solution.py:169
  21.2 3.5 collective-permute-start.7
  28.0 4.8 collective-permute-done.5.outer_ref
  32.8 18.0 %powers.9 = (f32[2,2048,256]{2,1,0:T(8,128)}, f32[3,2,256,128]{3,2,1,0:T(8,128)S(1)}, f32[3,2,256,128]{3,2,1,0:T(8,128)S(1)}) custom-call(s32[3]{0:T(128)S(1)} %pad_add_fusion.valid_ref, f32[2048,256]{1,0:T(8,128)} %k0_ref.1, f32[192,256]{1,0:T(8,128)S(1)} %collective-permute-done.4.inner_ref, f32[192,256]{1,0:T(8,128)S(1)} %collective-permute-done.5.outer_ref, ...), custom_call_target="tpu_custom_call" | custom-call | tf_op jit(solution)/shard_map/powers/pallas_call | solution.py:327
  53.2 29.0 %all_to_all.48 = f32[64,24,128]{2,1,0:T(8,128)S(1)} all-to-all(f32[64,24,128]{2,1,0:T(8,128)S(1)} %bitcast.54), channel_id=1, replica_groups=mesh['row'=4,'column'=4,'depth'=4,'core'=2] {'row','column','depth'}, dimensions={0} | all-to-all | bytes 1572864 | tf_op jit(solution)/shard_map/all_to_all | solution.py:487
  82.4 18.4 %all_to_all.49 = f32[64,24,128]{2,1,0:T(8,128)S(1)} all-to-all(f32[64,24,128]{2,1,0:T(8,128)S(1)} %broadcast_in_dim.38), channel_id=1, replica_groups=mesh['row'=4,'column'=4,'depth'=4,'core'=2] {'row','column','depth'}, dimensions={0} | all-to-all | bytes 1572864 | tf_op jit(solution)/shard_map/all_to_all | solution.py:489
  100.8 3.1 collective-permute-start.9
  104.6 4.5 loads.1
  109.1 11.0 %basis.3.basis_ref = f32[256,2304]{1,0:T(8,128)S(1)} custom-call(f32[2048,256]{1,0:T(8,128)} %k0_ref.1, f32[2,2048,256]{2,1,0:T(8,128)} %get-tuple-element.318.refs_1_.refs_2_.k1_ref.k2_ref, f32[2,2048,256]{2,1,0:T(8,128)} %get-tuple-element.318.refs_1_.refs_2_.k1_ref.k2_ref, bf16[768,2048]{1,0:T(8,128)(2,1)S(1)} %get-tuple-element.575.refs_3_, ...), custom_call_target="tpu_custom_call" | custom-call | tf_op jit(solution)/shard_map/basis/pallas_call | solution.py:625
  120.2 21.8 %galerkin.1 = (f32[768,256]{1,0:T(8,128)S(1)}, f32[256,768]{1,0:T(8,128)S(1)}, s32[1]{0:T(128)}) custom-call(s32[1]{0:T(128)} %bitcast.core_ref, f32[3,2,256,128]{3,2,1,0:T(8,128)S(1)} %bitcast.49, f32[3,2,256,128]{3,2,1,0:T(8,128)S(1)} %collective-permute-done.9.theirs_ref, f32[256,2304]{1,0:T(8,128)S(1)} %basis.3.basis_ref), custom_call_target="tpu_custom_call" | custom-call | tf_op jit(solution)/shard_map/galerkin/pallas_call | solution.py:448
  143.3 3.6 all-to-all-start.5
  146.9 6.4 combine.1
  153.3 9.8 %all-to-all-done.5.received_ref = f32[128,2,768]{2,1,0:T(2,128)S(1)} async-done(((f32[128,2,768]{2,1,0:T(2,128)}), f32[128,2,768]{2,1,0:T(2,128)S(1)}, u32[]{:S(2)}, u32[]{:S(2)}) %all-to-all-start.5) | async-done | bytes 786464 | tf_op jit(solution)/shard_map/all_to_all | solution.py:647
  163.1 2.6 lead.3
  165.7 529.8 %while.31 = (s32[]{:T(128)}, f32[2048,256]{1,0:T(8,128)}, f32[3,128,256]{2,1,0:T(8,128)}, s32[]{:T(128)}, s32[3]{0:T(128)S(1)}, /*index=5*/f32[12,256,256]{2,1,0...) while((s32[]{:T(128)}, f32[2048,256]{1,0:T(8,128)}, ...), condition=%region_6.7_spmd, body=%region_2.6_spmd | while | flops 3228201984 | bytes 125071248 | solution.py:730
  166.4 3.2 copy.26
  170.9 495.1 %while.33 = (s32[]{:T(128)}, f32[2048,256]{1,0:T(8,128)}, f32[2048,256]{1,0:T(8,128)}, f32[2048,256]{1,0:T(8,128)}, f32[256,256]{1,0:T(8,128)S(1)}, /*index=5*/p...) while((s32[]{:T(128)}, f32[2048,256]{1,0:T(8,128)}, ...), condition=%wide.region_5.5_spmd.clone, body=%wide.region_3.4_spmd.clone.sunk | while | flops 3228201984 | bytes 105145936 | solution.py:537
  176.8 5.0 collective-permute-done.1.outer_ref
  181.8 15.9 %powers.10 = (f32[2,2048,256]{2,1,0:T(8,128)}, f32[3,2,256,128]{3,2,1,0:T(8,128)S(1)}, f32[3,2,256,128]{3,2,1,0:T(8,128)S(1)}) custom-call(s32[3]{0:T(128)S(1)} %get-tuple-element.557.valid_ref, f32[2048,256]{1,0:T(8,128)S(1)} %broadcast_select_fusion.5.own_ref, f32[192,256]{1,0:T(8,128)S(1)} %collective-permute-done.inner_ref, ...), custom_call_target="tpu_custom_call" | custom-call | tf_op jit(solution)/shard_map/while/body/while/body/eval_jaxpr/powers/pallas_call | solution.py:327
  200.1 22.4 %all_to_all.50 = f32[64,24,128]{2,1,0:T(8,128)S(1)} all-to-all(f32[64,24,128]{2,1,0:T(8,128)S(1)} %bitcast.53), channel_id=1, replica_groups=mesh['row'=4,'column'=4,'depth'=4,'core'=2] {'row','column','depth'}, dimensions={0} | all-to-all | bytes 1572864 | tf_op jit(solution)/shard_map/while/body/while/body/eval_jaxpr/all_to_all | solution.py:487
  222.7 18.4 %all_to_all.51 = f32[64,24,128]{2,1,0:T(8,128)S(1)} all-to-all(f32[64,24,128]{2,1,0:T(8,128)S(1)} %broadcast_in_dim.45), channel_id=1, replica_groups=mesh['row'=4,'column'=4,'depth'=4,'core'=2] {'row','column','depth'}, dimensions={0} | all-to-all | bytes 1572864 | tf_op jit(solution)/shard_map/while/body/while/body/eval_jaxpr/all_to_all | solution.py:489
  241.1 3.1 collective-permute-start.3
  248.3 10.7 %solve.8 = f32[256,256]{1,0:T(8,128)} custom-call(f32[256,256]{1,0:T(8,128)} %get-tuple-element.516.matrix_ref, f32[256,256]{1,0:T(8,128)S(1)} %get-tuple-element.555.target_ref), custom_call_target="tpu_custom_call" | custom-call | tf_op jit(solution)/shard_map/while/body/while/body/eval_jaxpr/solve/pallas_call | solution.py:472
  259.0 6.0 add_select_fusion.3
  264.9 3.3 subtract_select_fusion.3
  272.2 2.7 collective-permute-start.1
  274.9 4.4 collective-permute-done.1.outer_ref
  279.3 15.9 %powers.10 = (f32[2,2048,256]{2,1,0:T(8,128)}, f32[3,2,256,128]{3,2,1,0:T(8,128)S(1)}, f32[3,2,256,128]{3,2,1,0:T(8,128)S(1)}) custom-call(s32[3]{0:T(128)S(1)} %get-tuple-element.557.valid_ref, f32[2048,256]{1,0:T(8,128)S(1)} %broadcast_select_fusion.5.own_ref, f32[192,256]{1,0:T(8,128)S(1)} %collective-permute-done.inner_ref, ...), custom_call_target="tpu_custom_call" | custom-call | tf_op jit(solution)/shard_map/while/body/while/body/eval_jaxpr/powers/pallas_call | solution.py:327
  297.6 23.5 %all_to_all.50 = f32[64,24,128]{2,1,0:T(8,128)S(1)} all-to-all(f32[64,24,128]{2,1,0:T(8,128)S(1)} %bitcast.53), channel_id=1, replica_groups=mesh['row'=4,'column'=4,'depth'=4,'core'=2] {'row','column','depth'}, dimensions={0} | all-to-all | bytes 1572864 | tf_op jit(solution)/shard_map/while/body/while/body/eval_jaxpr/all_to_all | solution.py:487
  321.2 18.4 %all_to_all.51 = f32[64,24,128]{2,1,0:T(8,128)S(1)} all-to-all(f32[64,24,128]{2,1,0:T(8,128)S(1)} %broadcast_in_dim.45), channel_id=1, replica_groups=mesh['row'=4,'column'=4,'depth'=4,'core'=2] {'row','column','depth'}, dimensions={0} | all-to-all | bytes 1572864 | tf_op jit(solution)/shard_map/while/body/while/body/eval_jaxpr/all_to_all | solution.py:489
  339.6 3.1 collective-permute-start.3
  346.8 10.7 %solve.8 = f32[256,256]{1,0:T(8,128)} custom-call(f32[256,256]{1,0:T(8,128)} %get-tuple-element.516.matrix_ref, f32[256,256]{1,0:T(8,128)S(1)} %get-tuple-element.555.target_ref), custom_call_target="tpu_custom_call" | custom-call | tf_op jit(solution)/shard_map/while/body/while/body/eval_jaxpr/solve/pallas_call | solution.py:472
  357.5 6.6 add_select_fusion.3
  364.1 3.3 subtract_select_fusion.3
  371.3 2.7 collective-permute-start.1
  374.0 4.4 collective-permute-done.1.outer_ref
  378.4 15.9 %powers.10 = (f32[2,2048,256]{2,1,0:T(8,128)}, f32[3,2,256,128]{3,2,1,0:T(8,128)S(1)}, f32[3,2,256,128]{3,2,1,0:T(8,128)S(1)}) custom-call(s32[3]{0:T(128)S(1)} %get-tuple-element.557.valid_ref, f32[2048,256]{1,0:T(8,128)S(1)} %broadcast_select_fusion.5.own_ref, f32[192,256]{1,0:T(8,128)S(1)} %collective-permute-done.inner_ref, ...), custom_call_target="tpu_custom_call" | custom-call | tf_op jit(solution)/shard_map/while/body/while/body/eval_jaxpr/powers/pallas_call | solution.py:327
  396.7 23.5 %all_to_all.50 = f32[64,24,128]{2,1,0:T(8,128)S(1)} all-to-all(f32[64,24,128]{2,1,0:T(8,128)S(1)} %bitcast.53), channel_id=1, replica_groups=mesh['row'=4,'column'=4,'depth'=4,'core'=2] {'row','column','depth'}, dimensions={0} | all-to-all | bytes 1572864 | tf_op jit(solution)/shard_map/while/body/while/body/eval_jaxpr/all_to_all | solution.py:487
  420.3 18.4 %all_to_all.51 = f32[64,24,128]{2,1,0:T(8,128)S(1)} all-to-all(f32[64,24,128]{2,1,0:T(8,128)S(1)} %broadcast_in_dim.45), channel_id=1, replica_groups=mesh['row'=4,'column'=4,'depth'=4,'core'=2] {'row','column','depth'}, dimensions={0} | all-to-all | bytes 1572864 | tf_op jit(solution)/shard_map/while/body/while/body/eval_jaxpr/all_to_all | solution.py:489
  438.7 3.1 collective-permute-start.3
  445.9 10.7 %solve.8 = f32[256,256]{1,0:T(8,128)} custom-call(f32[256,256]{1,0:T(8,128)} %get-tuple-element.516.matrix_ref, f32[256,256]{1,0:T(8,128)S(1)} %get-tuple-element.555.target_ref), custom_call_target="tpu_custom_call" | custom-call | tf_op jit(solution)/shard_map/while/body/while/body/eval_jaxpr/solve/pallas_call | solution.py:472
  456.6 6.6 add_select_fusion.3
  463.2 3.3 subtract_select_fusion.3
  470.4 2.7 collective-permute-start.1
  473.1 4.4 collective-permute-done.1.outer_ref
  477.5 15.9 %powers.10 = (f32[2,2048,256]{2,1,0:T(8,128)}, f32[3,2,256,128]{3,2,1,0:T(8,128)S(1)}, f32[3,2,256,128]{3,2,1,0:T(8,128)S(1)}) custom-call(s32[3]{0:T(128)S(1)} %get-tuple-element.557.valid_ref, f32[2048,256]{1,0:T(8,128)S(1)} %broadcast_select_fusion.5.own_ref, f32[192,256]{1,0:T(8,128)S(1)} %collective-permute-done.inner_ref, ...), custom_call_target="tpu_custom_call" | custom-call | tf_op jit(solution)/shard_map/while/body/while/body/eval_jaxpr/powers/pallas_call | solution.py:327
  495.9 23.5 %all_to_all.50 = f32[64,24,128]{2,1,0:T(8,128)S(1)} all-to-all(f32[64,24,128]{2,1,0:T(8,128)S(1)} %bitcast.53), channel_id=1, replica_groups=mesh['row'=4,'column'=4,'depth'=4,'core'=2] {'row','column','depth'}, dimensions={0} | all-to-all | bytes 1572864 | tf_op jit(solution)/shard_map/while/body/while/body/eval_jaxpr/all_to_all | solution.py:487
  519.5 18.4 %all_to_all.51 = f32[64,24,128]{2,1,0:T(8,128)S(1)} all-to-all(f32[64,24,128]{2,1,0:T(8,128)S(1)} %broadcast_in_dim.45), channel_id=1, replica_groups=mesh['row'=4,'column'=4,'depth'=4,'core'=2] {'row','column','depth'}, dimensions={0} | all-to-all | bytes 1572864 | tf_op jit(solution)/shard_map/while/body/while/body/eval_jaxpr/all_to_all | solution.py:489
  537.8 3.1 collective-permute-start.3
  545.1 10.7 %solve.8 = f32[256,256]{1,0:T(8,128)} custom-call(f32[256,256]{1,0:T(8,128)} %get-tuple-element.516.matrix_ref, f32[256,256]{1,0:T(8,128)S(1)} %get-tuple-element.555.target_ref), custom_call_target="tpu_custom_call" | custom-call | tf_op jit(solution)/shard_map/while/body/while/body/eval_jaxpr/solve/pallas_call | solution.py:472
  555.7 6.6 add_select_fusion.3
  562.3 3.3 subtract_select_fusion.3
  569.6 2.7 collective-permute-start.1
  572.3 4.4 collective-permute-done.1.outer_ref
  576.7 15.9 %powers.10 = (f32[2,2048,256]{2,1,0:T(8,128)}, f32[3,2,256,128]{3,2,1,0:T(8,128)S(1)}, f32[3,2,256,128]{3,2,1,0:T(8,128)S(1)}) custom-call(s32[3]{0:T(128)S(1)} %get-tuple-element.557.valid_ref, f32[2048,256]{1,0:T(8,128)S(1)} %broadcast_select_fusion.5.own_ref, f32[192,256]{1,0:T(8,128)S(1)} %collective-permute-done.inner_ref, ...), custom_call_target="tpu_custom_call" | custom-call | tf_op jit(solution)/shard_map/while/body/while/body/eval_jaxpr/powers/pallas_call | solution.py:327
  595.0 23.5 %all_to_all.50 = f32[64,24,128]{2,1,0:T(8,128)S(1)} all-to-all(f32[64,24,128]{2,1,0:T(8,128)S(1)} %bitcast.53), channel_id=1, replica_groups=mesh['row'=4,'column'=4,'depth'=4,'core'=2] {'row','column','depth'}, dimensions={0} | all-to-all | bytes 1572864 | tf_op jit(solution)/shard_map/while/body/while/body/eval_jaxpr/all_to_all | solution.py:487
  618.6 18.4 %all_to_all.51 = f32[64,24,128]{2,1,0:T(8,128)S(1)} all-to-all(f32[64,24,128]{2,1,0:T(8,128)S(1)} %broadcast_in_dim.45), channel_id=1, replica_groups=mesh['row'=4,'column'=4,'depth'=4,'core'=2] {'row','column','depth'}, dimensions={0} | all-to-all | bytes 1572864 | tf_op jit(solution)/shard_map/while/body/while/body/eval_jaxpr/all_to_all | solution.py:489
  637.0 3.1 collective-permute-start.3
  644.2 10.7 %solve.8 = f32[256,256]{1,0:T(8,128)} custom-call(f32[256,256]{1,0:T(8,128)} %get-tuple-element.516.matrix_ref, f32[256,256]{1,0:T(8,128)S(1)} %get-tuple-element.555.target_ref), custom_call_target="tpu_custom_call" | custom-call | tf_op jit(solution)/shard_map/while/body/while/body/eval_jaxpr/solve/pallas_call | solution.py:472
  654.9 6.6 add_select_fusion.3
  661.5 3.3 subtract_select_fusion.3
  666.1 5.7 basis.2
  672.2 19.5 %all_to_all.47.received_ref = f32[128,2,768]{2,1,0:T(2,128)S(1)} all-to-all(f32[128,2,768]{2,1,0:T(2,128)S(1)} %reshape.96), channel_id=1, replica_groups=mesh['row'=4,'column'=4,'depth'=4,'core'=2] {'row','column','depth','core'}, dimensions={0} | all-to-all | bytes 1572864 | tf_op jit(solution)/shard_map/while/body/all_to_all | solution.py:647
  691.7 2.6 lead.2
  (193 shorter events, 71.8 us)
Async XLA Ops:
  19.8 13.0 %collective-permute-start.6 = (f32[320,256]{1,0:T(8,128)S(1)}, f32[320,256]{1,0:T(8,128)S(1)}, u32[]{:S(2)}, u32[]{:S(2)}) collective-permute-start(f32[320,256]{1,0:T(8,128)S(1)} %get-tuple-element.314), channel_id=1, source_target_pairs={{0,1},{1,0},{2,3},{3,2},{4,5},{5,4},{6,7},{7,6},{8,9},{9,8},{10,11... | collective-permute-start | bytes 983048 | tf_op jit(solution)/shard_map/ppermute | solution.py:498
  21.2 11.6 %collective-permute-start.7 = (f32[320,256]{1,0:T(8,128)S(1)}, f32[320,256]{1,0:T(8,128)S(1)}, u32[]{:S(2)}, u32[]{:S(2)}) collective-permute-start(f32[320,256]{1,0:T(8,128)S(1)} %get-tuple-element.315), channel_id=1, source_target_pairs={{1,2},{3,4},{5,6},{7,8},{9,10},{11,12},{13,14},{15,16},{17,18},{19... | collective-permute-start | bytes 983048 | tf_op jit(solution)/shard_map/ppermute | solution.py:499
  25.8 7.0 %collective-permute-start.5 = (f32[192,256]{1,0:T(8,128)S(1)}, f32[192,256]{1,0:T(8,128)S(1)}, u32[]{:S(2)}, u32[]{:S(2)}) collective-permute-start(f32[192,256]{1,0:T(8,128)S(1)} %get-tuple-element.418), channel_id=1, source_target_pairs={{1,2},{3,4},{5,6},{7,8},{9,10},{11,12},{13,14},{15,16},{17,18},{19... | collective-permute-start | bytes 589832 | tf_op jit(solution)/shard_map/ppermute | solution.py:499
  27.8 5.0 collective-permute-start.4
  32.8 18.0 %copy-start.7 = (f32[320,256]{1,0:T(8,128)}, f32[320,256]{1,0:T(8,128)S(1)}, u32[]{:S(2)}) copy-start(f32[320,256]{1,0:T(8,128)S(1)} %collective-permute-done.7.oband_ref) | copy-start | bytes 983044
  50.8 2.4 collective-permute-start.8
  53.2 50.6 %copy-start.15 = (s32[16,256]{1,0:T(8,128)S(1)}, s32[16,256]{1,0:T(8,128)}, u32[]{:S(2)}) copy-start(s32[16,256]{1,0:T(8,128)} %param.15) | copy-start | bytes 49156
  82.2 21.8 %copy-start.12 = (f32[16,768]{1,0:T(8,128)S(1)}, f32[16,768]{1,0:T(8,128)}, u32[]{:S(2)}) copy-start(f32[16,768]{1,0:T(8,128)} %param.16) | copy-start | bytes 147460
  100.8 19.3 %collective-permute-start.9 = (f32[3,2,256,128]{3,2,1,0:T(8,128)S(1)}, f32[3,2,256,128]{3,2,1,0:T(8,128)S(1)}, u32[]{:S(2)}, u32[]{:S(2)}) collective-permute-start(f32[3,2,256,128]{3,2,1,0:T(8,128)S(1)} %bitcast.48), channel_id=1, source_target_pairs={{0,1},{1,0},{2,3},{3,2},{4,5},{5,4},{6,7},{7,6},{8,9},{9,8},{10,11... | collective-permute-start | bytes 2359304 | tf_op jit(solution)/shard_map/ppermute | solution.py:491
  109.1 11.0 %copy-start.10 = (bf16[768,2048]{1,0:T(8,128)(2,1)}, bf16[768,2048]{1,0:T(8,128)(2,1)S(1)}, u32[]{:S(2)}) copy-start(bf16[768,2048]{1,0:T(8,128)(2,1)S(1)} %get-tuple-element.575.refs_3_) | copy-start | bytes 9437188
  109.1 11.0 %copy-start.11 = (bf16[768,2048]{1,0:T(8,128)(2,1)}, bf16[768,2048]{1,0:T(8,128)(2,1)S(1)}, u32[]{:S(2)}) copy-start(bf16[768,2048]{1,0:T(8,128)(2,1)S(1)} %get-tuple-element.576.refs_4_) | copy-start | bytes 9437188
  143.3 19.8 %all-to-all-start.5 = ((f32[128,2,768]{2,1,0:T(2,128)}), f32[128,2,768]{2,1,0:T(2,128)S(1)}, u32[]{:S(2)}, u32[]{:S(2)}) async-start(f32[128,2,768]{2,1,0:T(2,128)} %reshape.116), calls=%async_computation.5 | async-start | bytes 1572864 | tf_op jit(solution)/shard_map/all_to_all | solution.py:647
  146.9 16.2 %copy-start.13 = (s32[128]{0:T(128)S(1)}, s32[128]{0:T(128)}, u32[]{:S(2)}) copy-start(s32[128]{0:T(128)} %slot_ref.1) | copy-start | bytes 1540
  146.9 18.8 %copy-start.8 = (f32[320,256]{1,0:T(8,128)S(1)}, f32[320,256]{1,0:T(8,128)}, u32[]{:S(2)}) copy-start(f32[320,256]{1,0:T(8,128)} %copy-done.7) | copy-start | bytes 983044
  166.3 3.2 copy-start.6
  170.9 2.2 copy-start.1
  173.1 8.7 %copy-start.3 = (f32[12,256,256]{2,1,0:T(8,128)S(1)}, f32[12,256,256]{2,1,0:T(8,128)}, u32[]{:S(2)}) copy-start(f32[12,256,256]{2,1,0:T(8,128)} %get-tuple-element.558.band_ref) | copy-start | bytes 9437188 | tf_op jit(solution)/shard_map/while/body/while
  173.5 3.3 collective-permute-start
  174.8 7.0 %collective-permute-start.1 = (f32[192,256]{1,0:T(8,128)S(1)}, f32[192,256]{1,0:T(8,128)S(1)}, u32[]{:S(2)}, u32[]{:S(2)}) collective-permute-start(f32[192,256]{1,0:T(8,128)S(1)} %get-tuple-element.509), channel_id=1, source_target_pairs={{1,2},{3,4},{5,6},{7,8},{9,10},{11,12},{13,14},{15,16},{17,18},{19... | collective-permute-start | bytes 589832 | tf_op jit(solution)/shard_map/while/body/while/body/eval_jaxpr/ppermute | solution.py:499
  197.7 2.4 collective-permute-start.2
  241.1 5.1 collective-permute-start.3
  258.9 6.0 copy-start.2
  258.9 6.0 copy-start.4
  259.0 6.0 copy-start.5
  268.2 1.3 copy-start.9
  269.5 2.2 copy-start.1
  271.7 7.5 %copy-start.3 = (f32[12,256,256]{2,1,0:T(8,128)S(1)}, f32[12,256,256]{2,1,0:T(8,128)}, u32[]{:S(2)}) copy-start(f32[12,256,256]{2,1,0:T(8,128)} %get-tuple-element.558.band_ref) | copy-start | bytes 9437188 | tf_op jit(solution)/shard_map/while/body/while
  272.1 2.8 collective-permute-start
  272.2 7.1 %collective-permute-start.1 = (f32[192,256]{1,0:T(8,128)S(1)}, f32[192,256]{1,0:T(8,128)S(1)}, u32[]{:S(2)}, u32[]{:S(2)}) collective-permute-start(f32[192,256]{1,0:T(8,128)S(1)} %get-tuple-element.509), channel_id=1, source_target_pairs={{1,2},{3,4},{5,6},{7,8},{9,10},{11,12},{13,14},{15,16},{17,18},{19... | collective-permute-start | bytes 589832 | tf_op jit(solution)/shard_map/while/body/while/body/eval_jaxpr/ppermute | solution.py:499
  295.1 2.4 collective-permute-start.2
  339.6 5.1 collective-permute-start.3
  357.5 6.6 copy-start.2
  357.5 6.6 copy-start.4
  357.5 6.6 copy-start.5
  367.3 1.3 copy-start.9
  368.7 2.2 copy-start.1
  370.9 7.5 %copy-start.3 = (f32[12,256,256]{2,1,0:T(8,128)S(1)}, f32[12,256,256]{2,1,0:T(8,128)}, u32[]{:S(2)}) copy-start(f32[12,256,256]{2,1,0:T(8,128)} %get-tuple-element.558.band_ref) | copy-start | bytes 9437188 | tf_op jit(solution)/shard_map/while/body/while
  371.2 2.8 collective-permute-start
  371.3 7.1 %collective-permute-start.1 = (f32[192,256]{1,0:T(8,128)S(1)}, f32[192,256]{1,0:T(8,128)S(1)}, u32[]{:S(2)}, u32[]{:S(2)}) collective-permute-start(f32[192,256]{1,0:T(8,128)S(1)} %get-tuple-element.509), channel_id=1, source_target_pairs={{1,2},{3,4},{5,6},{7,8},{9,10},{11,12},{13,14},{15,16},{17,18},{19... | collective-permute-start | bytes 589832 | tf_op jit(solution)/shard_map/while/body/while/body/eval_jaxpr/ppermute | solution.py:499
  394.3 2.4 collective-permute-start.2
  438.7 5.1 collective-permute-start.3
  456.6 6.6 copy-start.2
  456.6 6.6 copy-start.4
  456.6 6.6 copy-start.5
  466.5 1.3 copy-start.9
  467.8 2.2 copy-start.1
  470.0 7.5 %copy-start.3 = (f32[12,256,256]{2,1,0:T(8,128)S(1)}, f32[12,256,256]{2,1,0:T(8,128)}, u32[]{:S(2)}) copy-start(f32[12,256,256]{2,1,0:T(8,128)} %get-tuple-element.558.band_ref) | copy-start | bytes 9437188 | tf_op jit(solution)/shard_map/while/body/while
  470.3 2.8 collective-permute-start
  470.4 7.1 %collective-permute-start.1 = (f32[192,256]{1,0:T(8,128)S(1)}, f32[192,256]{1,0:T(8,128)S(1)}, u32[]{:S(2)}, u32[]{:S(2)}) collective-permute-start(f32[192,256]{1,0:T(8,128)S(1)} %get-tuple-element.509), channel_id=1, source_target_pairs={{1,2},{3,4},{5,6},{7,8},{9,10},{11,12},{13,14},{15,16},{17,18},{19... | collective-permute-start | bytes 589832 | tf_op jit(solution)/shard_map/while/body/while/body/eval_jaxpr/ppermute | solution.py:499
  493.4 2.4 collective-permute-start.2
  537.8 5.1 collective-permute-start.3
  555.7 6.6 copy-start.2
  555.7 6.6 copy-start.4
  555.7 6.6 copy-start.5
  566.9 2.2 copy-start.1
  569.1 7.5 %copy-start.3 = (f32[12,256,256]{2,1,0:T(8,128)S(1)}, f32[12,256,256]{2,1,0:T(8,128)}, u32[]{:S(2)}) copy-start(f32[12,256,256]{2,1,0:T(8,128)} %get-tuple-element.558.band_ref) | copy-start | bytes 9437188 | tf_op jit(solution)/shard_map/while/body/while
  569.5 2.8 collective-permute-start
  569.6 7.1 %collective-permute-start.1 = (f32[192,256]{1,0:T(8,128)S(1)}, f32[192,256]{1,0:T(8,128)S(1)}, u32[]{:S(2)}, u32[]{:S(2)}) collective-permute-start(f32[192,256]{1,0:T(8,128)S(1)} %get-tuple-element.509), channel_id=1, source_target_pairs={{1,2},{3,4},{5,6},{7,8},{9,10},{11,12},{13,14},{15,16},{17,18},{19... | collective-permute-start | bytes 589832 | tf_op jit(solution)/shard_map/while/body/while/body/eval_jaxpr/ppermute | solution.py:499
  592.5 2.4 collective-permute-start.2
  637.0 5.1 collective-permute-start.3
  654.9 6.6 copy-start.2
  654.9 6.6 copy-start.4
  654.9 6.6 copy-start.5
  671.7 20.0 %copy-start.14 = (s32[128]{0:T(128)S(1)}, s32[128]{0:T(128)}, u32[]{:S(2)}) copy-start(s32[128]{0:T(128)} %get-tuple-element.666) | copy-start | bytes 1540 | tf_op jit(solution)/shard_map/while
  (3 other events, 3.9 us)

commit v4 on v3

--- a/solution.py
+++ b/solution.py
@@ -192,6 +192,7 @@
 
 
 LOW = 2 * HALO
+PACK = 320
 
 
 def powers_kernel(
@@ -242,11 +243,20 @@
 
     def keep_moment(j, value):
         here = valid_ref[2] == j // ITERS
+        low, up = value[:, :128], value[:, 128:]
+        mixed = jnp.where(
+            iota((64, 128), 1) < 64, pltpu.roll(low[64:128], 64, 1), up[192:]
+        )
         for ref, chosen in ((mine_ref, here), (theirs_ref, jnp.logical_not(here))):
             @pl.when(chosen)
             def _(ref=ref):
-                for c in range(cols // 128):
-                    ref[j % ITERS, c] = value[:, c * 128 : (c + 1) * 128]
+                at = pl.multiple_of(j % ITERS * PACK, 64)
+                ref[pl.ds(at, 64), :] = low[:64]
+                ref[pl.ds(at + 64, 192), :] = up[:192]
+                ref[pl.ds(at + 256, 64), :] = mixed
+
+    for ref in (mine_ref, theirs_ref):
+        ref[ITERS * PACK :] = jnp.zeros((ref.shape[0] - ITERS * PACK, 128), F32)
 
     def power(n, carry):
         now = n % 2
@@ -321,7 +331,7 @@
     band, inner_band, outer_band = bands
     own, cols = vector.shape
     frame = own + 2 * LOW + 64
-    half = jax.ShapeDtypeStruct((ITERS, cols // 128, cols, 128), F32)
+    half = jax.ShapeDtypeStruct((1024, 128), F32)
     wide = pltpu.VMEM((2, frame, cols), BF16)
     edge = pltpu.VMEM(inner_band.shape, BF16)
     return pl.pallas_call(
@@ -382,11 +392,21 @@
 
 
 def galerkin_kernel(core_ref, mine_ref, theirs_ref, basis_ref, out_ref, rows_ref, good_ref, mom_ref):
-    parts = mine_ref.shape[1]
+    size = out_ref.shape[1]
+    gap = jnp.zeros((64, 128), F32)
+    right = iota((64, 128), 1) < 64
+    upper = iota((size, size), 0) // 64 <= iota((size, size), 1) // 64
 
     def unpack(source_ref, start):
         for n in range(ITERS):
-            mom_ref[start + n] = jnp.concatenate([source_ref[n, c] for c in range(parts)], axis=1)
+            at = n * PACK
+            mixed = source_ref[at + 256 : at + 320]
+            low = [source_ref[at : at + 64], jnp.where(right, 0.0, pltpu.roll(mixed, 64, 1)), gap, gap]
+            up = [source_ref[at + 64 : at + 256], jnp.where(right, 0.0, mixed)]
+            half = jnp.concatenate(
+                [jnp.concatenate(low, axis=0), jnp.concatenate(up, axis=0)], axis=1
+            )
+            mom_ref[start + n] = jnp.where(upper, half, half.T)
 
     @pl.when(core_ref[0] == 0)
     def _():
@@ -399,9 +419,7 @@
         unpack(mine_ref, ITERS)
 
     m = [mom_ref[n] for n in range(2 * ITERS)]
-    m = [x if n % 2 == 0 else 0.5 * (x + x.T) for n, x in enumerate(m)]
     h = [m[n + 1] + SHIFT * m[n] for n in range(2 * ITERS - 1)]
-    size = m[0].shape[0]
 
     def right_of(inverse, *targets):
         wide = split_dot(inverse, jnp.concatenate(targets, axis=1))
@@ -434,22 +452,22 @@
     yh, yl = halves(out_ref[...])
     for k in range(3):
         part = dot3(*halves(basis_ref[:, k * wide : (k + 1) * wide]), yh, yl)
-        rows_ref[:, k * size : (k + 1) * size] = part
+        rows_ref[:, :, k * size : (k + 1) * size] = part.reshape(rows_ref.shape[0], -1, size)
     share = jnp.minimum(ratio(first, h[2]), ratio(rest, h[4]))
     rounds = jnp.maximum(k0, jnp.maximum(k1, k2))
     worst = jnp.maximum(w0, jnp.maximum(w1, w2))
     good_ref[0] = jnp.where((share > GUARD) & (worst <= CLOSE) & (rounds <= ROUNDS), 1, 0)
 
 
-def galerkin(core, mine, theirs, basis_rows):
-    size = mine.shape[2]
+def galerkin(core, mine, theirs, basis_rows, peers):
     slots, wide = basis_rows.shape
+    size = wide // (3 * ITERS)
     smem = pl.BlockSpec(memory_space=pltpu.SMEM)
     return pl.pallas_call(
         galerkin_kernel,
         out_shape=(
             jax.ShapeDtypeStruct((ITERS * size, size), F32),
-            jax.ShapeDtypeStruct((slots, wide // ITERS), F32),
+            jax.ShapeDtypeStruct((peers, slots // peers, wide // ITERS), F32),
             jax.ShapeDtypeStruct((1,), jnp.int32),
         ),
         in_specs=[smem] + in_vmem(3),
@@ -510,8 +528,18 @@
     def times(a, b):
         return jnp.dot(a, b, preferred_element_type=F32, precision=lax.Precision.HIGHEST)
 
-    def gram_of(parts):
-        return jnp.concatenate([parts[0], parts[1]], axis=1)
+    def gram_of(lines, n):
+        part = lines[n * PACK : (n + 1) * PACK]
+        mixed = part[256:]
+        gap = jnp.zeros((64, 64), F32)
+        low = jnp.concatenate([gap, mixed[:, :64]], axis=1)
+        up = jnp.concatenate([gap, mixed[:, 64:]], axis=1)
+        empty = jnp.zeros((128, 128), F32)
+        half = jnp.concatenate(
+            [jnp.concatenate([part[:64], low, empty]), jnp.concatenate([part[64:256], up])], axis=1
+        )
+        block = jnp.arange(half.shape[0]) // 64
+        return jnp.where(block[:, None] <= block[None, :], half, half.T)
 
     def step(k, state):
         answer, residual, direction, gram = state
@@ -520,9 +548,9 @@
         image, mine, theirs = powers(vector, *halo_of(vector), valid, bands)
         low, high = total_of(mine, theirs)
         low = jnp.where(valid[2] == 0, low, high)
-        square = gram_of(low[0])
+        square = gram_of(low, 0)
         gram = jnp.where(k == 0, square, gram)
-        dir_gram = gram_of(low[1]) + SHIFT * square
+        dir_gram = gram_of(low, 1) + SHIFT * square
         factor = solve(
             jnp.where(on_direction, dir_gram, gram), jnp.where(on_direction, gram, square)
         )
@@ -537,23 +565,42 @@
     return lax.fori_loop(0, 2 * ITERS - 1, step, state)[0]
 
 
-def loads_kernel(nodes_ref, load_ref, high_ref, low_ref):
-    groups, pairs = nodes_ref.shape
-    slots = 8
-    support = pairs // slots
+def loads_kernel(nodes_ref, load_ref, high_ref, low_ref, line_ref):
+    support, slots = nodes_ref.shape
+    unit = 8
+    groups = slots // unit
+    pairs = unit * support
     blocks = high_ref.shape[1] // 128
-    own_lane = iota((slots, pairs), 1) // support == iota((slots, pairs), 0)
+    wide = 3 * slots
+    one = lambda mask: jnp.where(mask, 1.0, 0.0).astype(BF16)
+
+    source = iota((wide, wide), 0)
+    target = iota((wide, wide), 1)
+    apart = one(source == target % slots * 3 + target // slots)
+    parts = dot(jnp.concatenate(halves(load_ref[...]), axis=0), apart)
+
+    owner = iota((groups, slots), 1) // unit == iota((groups, slots), 0)
+    place = iota((slots, pairs), 0) % unit == iota((slots, pairs), 1) % unit
+    turn = iota((slots, pairs), 1) // unit
+    nodes = nodes_ref[...]
+    fields = [parts[h * support : (h + 1) * support, k * slots : (k + 1) * slots] for k in range(3) for h in range(2)]
+    fields += [(nodes // 128).astype(F32), (nodes % 128).astype(F32)]
+    total = jnp.zeros((len(fields) * groups, pairs), F32)
+    for s in range(support):
+        spread = [jnp.where(owner, field[s : s + 1, :], 0.0) for field in fields]
+        total = total + dot(jnp.concatenate(spread, axis=0).astype(BF16), one(place & (turn == s)))
+    line_ref[...] = total
+
+    own_lane = iota((unit, pairs), 1) % unit == iota((unit, pairs), 0)
     row = iota((128, pairs), 0)
 
+    def line(n, g):
+        return line_ref[pl.ds(n * groups + g, 1), :]
+
     def half_group(g):
-        nodes = nodes_ref[pl.ds(g, 1), :]
-        hot = jnp.where(row == nodes % 128, 1.0, 0.0).astype(BF16)
-        block = jnp.broadcast_to(nodes // 128, (slots, pairs))
-        terms = []
-        for k in range(3):
-            spread = jnp.where(own_lane, load_ref[k, pl.ds(g, 1), :], 0.0)
-            high = spread.astype(BF16).astype(F32)
-            terms.append((high, spread - high))
+        hot = one(row == line(7, g).astype(jnp.int32))
+        block = jnp.broadcast_to(line(6, g).astype(jnp.int32), (unit, pairs))
+        terms = [[jnp.where(own_lane, line(2 * k + h, g), 0.0) for h in range(2)] for k in range(3)]
         rows = []
         for c in range(blocks):
             hit = block == c
@@ -567,15 +614,14 @@
     def group(g, carry):
         first = half_group(2 * g)
         second = half_group(2 * g + 1)
-        total = groups * slots
         for c in range(blocks):
             for k in range(3):
-                at = (c * 3 + k) * slots
-                value = jnp.concatenate([first[at : at + slots], second[at : at + slots]], axis=0)
+                at = (c * 3 + k) * unit
+                value = jnp.concatenate([first[at : at + unit], second[at : at + unit]], axis=0)
                 high, low = halves(value)
-                to = pl.multiple_of(k * total + g * 2 * slots, 16)
-                high_ref[pl.ds(to, 2 * slots), c * 128 : (c + 1) * 128] = high
-                low_ref[pl.ds(to, 2 * slots), c * 128 : (c + 1) * 128] = low
+                to = pl.multiple_of(k * slots + g * 2 * unit, 16)
+                high_ref[pl.ds(to, 2 * unit), c * 128 : (c + 1) * 128] = high
+                low_ref[pl.ds(to, 2 * unit), c * 128 : (c + 1) * 128] = low
         return carry
 
     lax.fori_loop(0, groups // 2, group, 0)
@@ -583,18 +629,16 @@
 
 def load_matrix(slot_nodes, slot_load, rows):
     support, slots = slot_nodes.shape
-    groups = slots * support // 128
-    nodes = slot_nodes.T.reshape(groups, 128)
-    loads = slot_load.reshape(support, slots, 3).transpose(2, 1, 0).reshape(3, groups, 128)
     out = jax.ShapeDtypeStruct((3 * slots, rows), BF16)
     return pl.pallas_call(
         loads_kernel,
         out_shape=(out, out),
         in_specs=in_vmem(2),
         out_specs=tuple(in_vmem(2)),
-        compiler_params=pltpu.CompilerParams(vmem_limit_bytes=20 << 20),
+        scratch_shapes=[pltpu.VMEM((slots, 8 * support), F32)],
+        compiler_params=pltpu.CompilerParams(vmem_limit_bytes=24 << 20),
         name="loads",
-    )(nodes, loads)
+    )(slot_nodes, slot_load)
 
 
 CHUNK = 512
@@ -642,9 +686,7 @@
 
 
 def to_owner(rows):
-    slots, wide = rows.shape
-    count = lax.axis_size(AXES)
-    return lax.all_to_all(rows.reshape(count, slots // count, wide), AXES, 0, 0, tiled=True)
+    return lax.all_to_all(rows, AXES, 0, 0, tiled=True)
 
 
 def combine_kernel(k0_ref, k1_ref, k2_ref, c_ref, x_ref, ch_ref, cl_ref):
@@ -717,14 +759,15 @@
     vectors = [in_chunks(right_side), in_chunks(images, 0), in_chunks(images, 1)]
     basis_rows = basis(vectors, weights)
     mine, theirs = total_of(mine, theirs)
-    coef, rows, good = galerkin(core[None], mine, theirs, basis_rows)
+    coef, rows, good = galerkin(core[None], mine, theirs, basis_rows, count)
     received = to_owner(rows)
     answer = combine(vectors, coef)
     leadfield = lead(received, dipole_slot)
 
     def exactly(_):
         exact = plain_cg(right_side, valid, bands)
-        received = to_owner(basis([in_chunks(exact)], weights))
+        own_rows = basis([in_chunks(exact)], weights)
+        received = to_owner(own_rows.reshape(count, -1, own_rows.shape[1]))
         return jnp.ones((), jnp.int32), exact, lead(received, dipole_slot)
 
     state = lax.while_loop(lambda state: state[0] == 0, exactly, (good[0], answer, leadfield))

time: 697 us -> 674 us (0.967)
  blocking collectives: 275 us -> 244 us
    all_to_all x6, blocking collectives: 145 us -> 129 us  [total_of(): arrived = lax.all_to_all(pair, CHIPS, 0, 0, tiled=True)]
    all_to_all x6, blocking collectives: 110 us -> 94.9 us  [total_of(): gathered = lax.all_to_all(own, CHIPS, 0, 0, tiled=True)]
    select_n x0 -> x10, other arithmetic: none -> 8.72 us  [the longest x5 8.7 us: step(): jnp.where(on_direction, dir_gram, gram)]
    while x76 -> x156, local copies, waits for them, and re-layouts: 22.4 us -> 26.6 us
where the time goes in v4:
time: 674 us; the launch traced here: 672 us
  blocking collectives  244 us (36%)
  Pallas kernels  222 us (33%)
  waiting for transfers between devices  57.3 us (9%)
  matrix products  48.7 us (7%)
  starting transfers between devices  43.8 us (6%)
  local copies, waits for them, and re-layouts  33.3 us (5%)
  other arithmetic  19.1 us (3%)
    all_to_all x6, blocking collectives, total_of(): arrived = lax.all_to_all(pair, CHIPS, 0, 0, tiled=True)  129 us
    pallas_call x6, Pallas kernels, powers(): pl.pallas_call(powers_kernel, out_shape=(pltpu.HBM((ITERS - 1, own, cols)...  97.7 us
    all_to_all x6, blocking collectives, total_of(): gathered = lax.all_to_all(own, CHIPS, 0, 0, tiled=True)  94.9 us
    pallas_call x5, Pallas kernels, solve(): pl.pallas_call(solve_kernel, out_shape=jax.ShapeDtypeStruct(target.shape,...  53.3 us
    dot_general x10, matrix products, times(): jnp.dot(a, b, preferred_element_type=F32, precision=lax.Precision.HIGHEST)  48.7 us
    ppermute x7, waiting for transfers between devices, swap_sides(): lax.ppermute(outer, AXES, across + [(b, a) for a, b in across])  28.5 us
    while x156, local copies, waits for them, and re-layouts  26.6 us
    pallas_call x1, Pallas kernels, galerkin(): pl.pallas_call(galerkin_kernel, out_shape=(jax.ShapeDtypeStruct((ITERS *...  22.5 us
  transfers between devices with their start and end apart: 27, of which 18 were waited for; matrix products, arithmetic and copies ran while one was open for 0% of the time, Pallas kernels for 3%

profile of v4, /device:TPU:1, one launch (start us, length us, event | category | flops | bytes accessed | tf_op | source)
XLA Modules:
  0.0 671.6 jit_solution(7333061944449146382)
XLA Ops:
  4.8 15.0 %assemble.1 = (f32[12,256,256]{2,1,0:T(8,128)}, f32[320,256]{1,0:T(8,128)S(1)}, f32[320,256]{1,0:T(8,128)S(1)}) custom-call(s32[1]{0:T(128)} %bitcast.core_ref, s32[256]{0:T(256)S(1)} %get-tuple-element.409.group_ref, s32[256]{0:T(256)S(1)} %multiply_minimum_fusion.first_ref, f32[32,32,256]{2,1,0:T(8,128)S(1)} %bitcast.50, ...), custom_call_target="tpu_custom_call" | custom-call | tf_op jit(solution)/shard_map/assemble/pallas_call | solution.py:169
  21.1 3.5 collective-permute-start.7
  28.0 4.8 collective-permute-done.5.outer_ref
  32.8 17.9 %powers.9 = (f32[2,2048,256]{2,1,0:T(8,128)}, f32[1024,128]{1,0:T(8,128)S(1)}, f32[1024,128]{1,0:T(8,128)S(1)}) custom-call(s32[3]{0:T(128)S(1)} %pad_add_fusion.valid_ref, f32[2048,256]{1,0:T(8,128)} %k0_ref.1, f32[192,256]{1,0:T(8,128)S(1)} %collective-permute-done.4.inner_ref, f32[192,256]{1,0:T(8,128)S(1)} %collective-permute-done.5.outer_ref, ...), custom_call_target="tpu_custom_call" | custom-call | tf_op jit(solution)/shard_map/powers/pallas_call | solution.py:337
  52.8 26.5 %all_to_all.48 = f32[64,16,128]{2,1,0:T(8,128)S(1)} all-to-all(f32[64,16,128]{2,1,0:T(8,128)S(1)} %bitcast.53), channel_id=1, replica_groups=mesh['row'=4,'column'=4,'depth'=4,'core'=2] {'row','column','depth'}, dimensions={0} | all-to-all | bytes 1048576 | tf_op jit(solution)/shard_map/all_to_all | solution.py:505
  79.4 15.8 %all_to_all.49 = f32[64,16,128]{2,1,0:T(8,128)S(1)} all-to-all(f32[64,16,128]{2,1,0:T(8,128)S(1)} %broadcast_in_dim.46), channel_id=1, replica_groups=mesh['row'=4,'column'=4,'depth'=4,'core'=2] {'row','column','depth'}, dimensions={0} | all-to-all | bytes 1048576 | tf_op jit(solution)/shard_map/all_to_all | solution.py:507
  95.2 2.9 collective-permute-start.9
  98.1 5.5 loads.1
  103.7 10.5 %basis.3.basis_ref = f32[256,2304]{1,0:T(8,128)S(1)} custom-call(f32[2048,256]{1,0:T(8,128)S(1)} %copy-done.9, f32[2,2048,256]{2,1,0:T(8,128)} %get-tuple-element.320.refs_1_.refs_2_.k1_ref.k2_ref, f32[2,2048,256]{2,1,0:T(8,128)} %get-tuple-element.320.refs_1_.refs_2_.k1_ref.k2_ref, bf16[768,2048]{1,0:T(8,128)(2,1)S(1)} %get-tuple-element.589.refs_3_, ...), custom_call_target="tpu_custom_call" | custom-call | tf_op jit(solution)/shard_map/basis/pallas_call | solution.py:669
  114.2 22.5 %galerkin.1 = (f32[768,256]{1,0:T(8,128)S(1)}, f32[128,2,768]{2,1,0:T(2,128)}, s32[1]{0:T(128)}) custom-call(s32[1]{0:T(128)} %bitcast.core_ref, f32[1024,128]{1,0:T(8,128)S(1)} %bitcast.49, f32[1024,128]{1,0:T(8,128)S(1)} %collective-permute-done.9.theirs_ref, f32[256,2304]{1,0:T(8,128)S(1)} %basis.3.basis_ref), custom_call_target="tpu_custom_call" | custom-call | tf_op jit(solution)/shard_map/galerkin/pallas_call | solution.py:466
  136.7 3.6 all-to-all-start.5
  140.3 6.4 combine.1
  146.6 9.8 %all-to-all-done.5.received_ref = f32[128,2,768]{2,1,0:T(2,128)S(1)} async-done(((f32[128,2,768]{2,1,0:T(2,128)}), f32[128,2,768]{2,1,0:T(2,128)S(1)}, u32[]{:S(2)}, u32[]{:S(2)}) %all-to-all-start.5) | async-done | bytes 786464 | tf_op jit(solution)/shard_map/all_to_all | solution.py:689
  156.4 2.6 lead.3
  159.0 512.5 %while.31 = (s32[]{:T(128)}, f32[2048,256]{1,0:T(8,128)}, f32[3,128,256]{2,1,0:T(8,128)}, s32[]{:T(128)}, s32[3]{0:T(128)S(1)}, /*index=5*/f32[12,256,256]{2,1,0...) while((s32[]{:T(128)}, f32[2048,256]{1,0:T(8,128)}, ...), condition=%region_6.7_spmd, body=%region_2.6_spmd | while | flops 3232530432 | bytes 127982696 | solution.py:773
  159.7 3.2 copy.33
  164.3 477.3 %while.33 = (s32[]{:T(128)}, f32[2048,256]{1,0:T(8,128)}, f32[2048,256]{1,0:T(8,128)}, f32[2048,256]{1,0:T(8,128)}, f32[256,256]{1,0:T(8,128)S(1)}, /*index=5*/p...) while((s32[]{:T(128)}, f32[2048,256]{1,0:T(8,128)}, ...), condition=%wide.region_5.5_spmd.clone, body=%wide.region_3.4_spmd.clone.sunk | while | flops 3232530432 | bytes 108057400 | solution.py:565
  170.4 5.0 collective-permute-done.1.outer_ref
  175.5 16.0 %powers.10 = (f32[2,2048,256]{2,1,0:T(8,128)}, f32[1024,128]{1,0:T(8,128)S(1)}, f32[1024,128]{1,0:T(8,128)S(1)}) custom-call(s32[3]{0:T(128)S(1)} %get-tuple-element.571.valid_ref, f32[2048,256]{1,0:T(8,128)S(1)} %broadcast_select_fusion.5.own_ref, f32[192,256]{1,0:T(8,128)S(1)} %collective-permute-done.inner_ref, ...), custom_call_target="tpu_custom_call" | custom-call | tf_op jit(solution)/shard_map/while/body/while/body/eval_jaxpr/powers/pallas_call | solution.py:337
  193.5 19.8 %all_to_all.50 = f32[64,16,128]{2,1,0:T(8,128)S(1)} all-to-all(f32[64,16,128]{2,1,0:T(8,128)S(1)} %bitcast.51), channel_id=1, replica_groups=mesh['row'=4,'column'=4,'depth'=4,'core'=2] {'row','column','depth'}, dimensions={0} | all-to-all | bytes 1048576 | tf_op jit(solution)/shard_map/while/body/while/body/eval_jaxpr/all_to_all | solution.py:505
  213.3 15.8 %all_to_all.51 = f32[64,16,128]{2,1,0:T(8,128)S(1)} all-to-all(f32[64,16,128]{2,1,0:T(8,128)S(1)} %broadcast_in_dim.53), channel_id=1, replica_groups=mesh['row'=4,'column'=4,'depth'=4,'core'=2] {'row','column','depth'}, dimensions={0} | all-to-all | bytes 1048576 | tf_op jit(solution)/shard_map/while/body/while/body/eval_jaxpr/all_to_all | solution.py:507
  229.4 3.0 collective-permute-start.3
  237.7 10.7 %solve.8 = f32[256,256]{1,0:T(8,128)} custom-call(f32[256,256]{1,0:T(8,128)} %fusion.36.matrix_ref, f32[256,256]{1,0:T(8,128)S(1)} %fusion.37.target_ref), custom_call_target="tpu_custom_call" | custom-call | tf_op jit(solution)/shard_map/while/body/while/body/eval_jaxpr/solve/pallas_call | solution.py:490
  248.4 6.0 add_select_fusion.3
  254.3 3.3 subtract_select_fusion.3
  262.4 2.4 collective-permute-start.1
  264.8 4.7 collective-permute-done.1.outer_ref
  269.5 16.0 %powers.10 = (f32[2,2048,256]{2,1,0:T(8,128)}, f32[1024,128]{1,0:T(8,128)S(1)}, f32[1024,128]{1,0:T(8,128)S(1)}) custom-call(s32[3]{0:T(128)S(1)} %get-tuple-element.571.valid_ref, f32[2048,256]{1,0:T(8,128)S(1)} %broadcast_select_fusion.5.own_ref, f32[192,256]{1,0:T(8,128)S(1)} %collective-permute-done.inner_ref, ...), custom_call_target="tpu_custom_call" | custom-call | tf_op jit(solution)/shard_map/while/body/while/body/eval_jaxpr/powers/pallas_call | solution.py:337
  287.5 20.7 %all_to_all.50 = f32[64,16,128]{2,1,0:T(8,128)S(1)} all-to-all(f32[64,16,128]{2,1,0:T(8,128)S(1)} %bitcast.51), channel_id=1, replica_groups=mesh['row'=4,'column'=4,'depth'=4,'core'=2] {'row','column','depth'}, dimensions={0} | all-to-all | bytes 1048576 | tf_op jit(solution)/shard_map/while/body/while/body/eval_jaxpr/all_to_all | solution.py:505
  308.3 15.8 %all_to_all.51 = f32[64,16,128]{2,1,0:T(8,128)S(1)} all-to-all(f32[64,16,128]{2,1,0:T(8,128)S(1)} %broadcast_in_dim.53), channel_id=1, replica_groups=mesh['row'=4,'column'=4,'depth'=4,'core'=2] {'row','column','depth'}, dimensions={0} | all-to-all | bytes 1048576 | tf_op jit(solution)/shard_map/while/body/while/body/eval_jaxpr/all_to_all | solution.py:507
  324.4 3.0 collective-permute-start.3
  332.7 10.7 %solve.8 = f32[256,256]{1,0:T(8,128)} custom-call(f32[256,256]{1,0:T(8,128)} %fusion.36.matrix_ref, f32[256,256]{1,0:T(8,128)S(1)} %fusion.37.target_ref), custom_call_target="tpu_custom_call" | custom-call | tf_op jit(solution)/shard_map/while/body/while/body/eval_jaxpr/solve/pallas_call | solution.py:490
  343.3 6.6 add_select_fusion.3
  349.9 3.3 subtract_select_fusion.3
  358.0 2.4 collective-permute-start.1
  360.4 4.7 collective-permute-done.1.outer_ref
  365.1 15.9 %powers.10 = (f32[2,2048,256]{2,1,0:T(8,128)}, f32[1024,128]{1,0:T(8,128)S(1)}, f32[1024,128]{1,0:T(8,128)S(1)}) custom-call(s32[3]{0:T(128)S(1)} %get-tuple-element.571.valid_ref, f32[2048,256]{1,0:T(8,128)S(1)} %broadcast_select_fusion.5.own_ref, f32[192,256]{1,0:T(8,128)S(1)} %collective-permute-done.inner_ref, ...), custom_call_target="tpu_custom_call" | custom-call | tf_op jit(solution)/shard_map/while/body/while/body/eval_jaxpr/powers/pallas_call | solution.py:337
  383.1 20.7 %all_to_all.50 = f32[64,16,128]{2,1,0:T(8,128)S(1)} all-to-all(f32[64,16,128]{2,1,0:T(8,128)S(1)} %bitcast.51), channel_id=1, replica_groups=mesh['row'=4,'column'=4,'depth'=4,'core'=2] {'row','column','depth'}, dimensions={0} | all-to-all | bytes 1048576 | tf_op jit(solution)/shard_map/while/body/while/body/eval_jaxpr/all_to_all | solution.py:505
  404.0 15.8 %all_to_all.51 = f32[64,16,128]{2,1,0:T(8,128)S(1)} all-to-all(f32[64,16,128]{2,1,0:T(8,128)S(1)} %broadcast_in_dim.53), channel_id=1, replica_groups=mesh['row'=4,'column'=4,'depth'=4,'core'=2] {'row','column','depth'}, dimensions={0} | all-to-all | bytes 1048576 | tf_op jit(solution)/shard_map/while/body/while/body/eval_jaxpr/all_to_all | solution.py:507
  420.0 3.0 collective-permute-start.3
  428.3 10.7 %solve.8 = f32[256,256]{1,0:T(8,128)} custom-call(f32[256,256]{1,0:T(8,128)} %fusion.36.matrix_ref, f32[256,256]{1,0:T(8,128)S(1)} %fusion.37.target_ref), custom_call_target="tpu_custom_call" | custom-call | tf_op jit(solution)/shard_map/while/body/while/body/eval_jaxpr/solve/pallas_call | solution.py:490
  439.0 6.6 add_select_fusion.3
  445.6 3.3 subtract_select_fusion.3
  453.6 2.4 collective-permute-start.1
  456.1 4.7 collective-permute-done.1.outer_ref
  460.7 15.9 %powers.10 = (f32[2,2048,256]{2,1,0:T(8,128)}, f32[1024,128]{1,0:T(8,128)S(1)}, f32[1024,128]{1,0:T(8,128)S(1)}) custom-call(s32[3]{0:T(128)S(1)} %get-tuple-element.571.valid_ref, f32[2048,256]{1,0:T(8,128)S(1)} %broadcast_select_fusion.5.own_ref, f32[192,256]{1,0:T(8,128)S(1)} %collective-permute-done.inner_ref, ...), custom_call_target="tpu_custom_call" | custom-call | tf_op jit(solution)/shard_map/while/body/while/body/eval_jaxpr/powers/pallas_call | solution.py:337
  478.7 20.7 %all_to_all.50 = f32[64,16,128]{2,1,0:T(8,128)S(1)} all-to-all(f32[64,16,128]{2,1,0:T(8,128)S(1)} %bitcast.51), channel_id=1, replica_groups=mesh['row'=4,'column'=4,'depth'=4,'core'=2] {'row','column','depth'}, dimensions={0} | all-to-all | bytes 1048576 | tf_op jit(solution)/shard_map/while/body/while/body/eval_jaxpr/all_to_all | solution.py:505
  499.6 15.8 %all_to_all.51 = f32[64,16,128]{2,1,0:T(8,128)S(1)} all-to-all(f32[64,16,128]{2,1,0:T(8,128)S(1)} %broadcast_in_dim.53), channel_id=1, replica_groups=mesh['row'=4,'column'=4,'depth'=4,'core'=2] {'row','column','depth'}, dimensions={0} | all-to-all | bytes 1048576 | tf_op jit(solution)/shard_map/while/body/while/body/eval_jaxpr/all_to_all | solution.py:507
  515.6 3.0 collective-permute-start.3
  523.9 10.7 %solve.8 = f32[256,256]{1,0:T(8,128)} custom-call(f32[256,256]{1,0:T(8,128)} %fusion.36.matrix_ref, f32[256,256]{1,0:T(8,128)S(1)} %fusion.37.target_ref), custom_call_target="tpu_custom_call" | custom-call | tf_op jit(solution)/shard_map/while/body/while/body/eval_jaxpr/solve/pallas_call | solution.py:490
  534.6 6.6 add_select_fusion.3
  541.2 3.3 subtract_select_fusion.3
  549.2 2.4 collective-permute-start.1
  551.7 4.7 collective-permute-done.1.outer_ref
  556.3 15.9 %powers.10 = (f32[2,2048,256]{2,1,0:T(8,128)}, f32[1024,128]{1,0:T(8,128)S(1)}, f32[1024,128]{1,0:T(8,128)S(1)}) custom-call(s32[3]{0:T(128)S(1)} %get-tuple-element.571.valid_ref, f32[2048,256]{1,0:T(8,128)S(1)} %broadcast_select_fusion.5.own_ref, f32[192,256]{1,0:T(8,128)S(1)} %collective-permute-done.inner_ref, ...), custom_call_target="tpu_custom_call" | custom-call | tf_op jit(solution)/shard_map/while/body/while/body/eval_jaxpr/powers/pallas_call | solution.py:337
  574.3 20.7 %all_to_all.50 = f32[64,16,128]{2,1,0:T(8,128)S(1)} all-to-all(f32[64,16,128]{2,1,0:T(8,128)S(1)} %bitcast.51), channel_id=1, replica_groups=mesh['row'=4,'column'=4,'depth'=4,'core'=2] {'row','column','depth'}, dimensions={0} | all-to-all | bytes 1048576 | tf_op jit(solution)/shard_map/while/body/while/body/eval_jaxpr/all_to_all | solution.py:505
  595.2 15.8 %all_to_all.51 = f32[64,16,128]{2,1,0:T(8,128)S(1)} all-to-all(f32[64,16,128]{2,1,0:T(8,128)S(1)} %broadcast_in_dim.53), channel_id=1, replica_groups=mesh['row'=4,'column'=4,'depth'=4,'core'=2] {'row','column','depth'}, dimensions={0} | all-to-all | bytes 1048576 | tf_op jit(solution)/shard_map/while/body/while/body/eval_jaxpr/all_to_all | solution.py:507
  611.2 3.0 collective-permute-start.3
  619.5 10.7 %solve.8 = f32[256,256]{1,0:T(8,128)} custom-call(f32[256,256]{1,0:T(8,128)} %fusion.36.matrix_ref, f32[256,256]{1,0:T(8,128)S(1)} %fusion.37.target_ref), custom_call_target="tpu_custom_call" | custom-call | tf_op jit(solution)/shard_map/while/body/while/body/eval_jaxpr/solve/pallas_call | solution.py:490
  630.2 6.6 add_select_fusion.3
  636.8 3.3 subtract_select_fusion.3
  641.6 5.7 basis.2
  647.8 19.8 %all_to_all.47.received_ref = f32[128,2,768]{2,1,0:T(2,128)S(1)} all-to-all(f32[128,2,768]{2,1,0:T(2,128)S(1)} %reshape.106), channel_id=1, replica_groups=mesh['row'=4,'column'=4,'depth'=4,'core'=2] {'row','column','depth','core'}, dimensions={0} | all-to-all | bytes 1572864 | tf_op jit(solution)/shard_map/while/body/all_to_all | solution.py:689
  667.6 2.6 lead.2
  (309 shorter events, 77.4 us)
Async XLA Ops:
  19.8 13.0 %collective-permute-start.6 = (f32[320,256]{1,0:T(8,128)S(1)}, f32[320,256]{1,0:T(8,128)S(1)}, u32[]{:S(2)}, u32[]{:S(2)}) collective-permute-start(f32[320,256]{1,0:T(8,128)S(1)} %get-tuple-element.316), channel_id=1, source_target_pairs={{0,1},{1,0},{2,3},{3,2},{4,5},{5,4},{6,7},{7,6},{8,9},{9,8},{10,11... | collective-permute-start | bytes 983048 | tf_op jit(solution)/shard_map/ppermute | solution.py:516
  21.1 11.6 %collective-permute-start.7 = (f32[320,256]{1,0:T(8,128)S(1)}, f32[320,256]{1,0:T(8,128)S(1)}, u32[]{:S(2)}, u32[]{:S(2)}) collective-permute-start(f32[320,256]{1,0:T(8,128)S(1)} %get-tuple-element.317), channel_id=1, source_target_pairs={{1,2},{3,4},{5,6},{7,8},{9,10},{11,12},{13,14},{15,16},{17,18},{19... | collective-permute-start | bytes 983048 | tf_op jit(solution)/shard_map/ppermute | solution.py:517
  25.8 7.0 %collective-permute-start.5 = (f32[192,256]{1,0:T(8,128)S(1)}, f32[192,256]{1,0:T(8,128)S(1)}, u32[]{:S(2)}, u32[]{:S(2)}) collective-permute-start(f32[192,256]{1,0:T(8,128)S(1)} %get-tuple-element.424), channel_id=1, source_target_pairs={{1,2},{3,4},{5,6},{7,8},{9,10},{11,12},{13,14},{15,16},{17,18},{19... | collective-permute-start | bytes 589832 | tf_op jit(solution)/shard_map/ppermute | solution.py:517
  27.8 5.0 collective-permute-start.4
  50.7 2.0 collective-permute-start.8
  52.7 45.4 %copy-start.1 = (f32[16,768]{1,0:T(8,128)S(1)}, f32[16,768]{1,0:T(8,128)}, u32[]{:S(2)}) copy-start(f32[16,768]{1,0:T(8,128)} %load_ref.1) | copy-start | bytes 147460
  52.7 45.4 %copy-start.2 = (s32[16,256]{1,0:T(8,128)S(1)}, s32[16,256]{1,0:T(8,128)}, u32[]{:S(2)}) copy-start(s32[16,256]{1,0:T(8,128)} %nodes_ref.1) | copy-start | bytes 49156
  52.7 51.0 %copy-start.9 = (f32[2048,256]{1,0:T(8,128)S(1)}, f32[2048,256]{1,0:T(8,128)}, u32[]{:S(2)}) copy-start(f32[2048,256]{1,0:T(8,128)} %k0_ref.1) | copy-start | bytes 6291460
  95.2 18.9 %collective-permute-start.9 = (f32[1024,128]{1,0:T(8,128)S(1)}, f32[1024,128]{1,0:T(8,128)S(1)}, u32[]{:S(2)}, u32[]{:S(2)}) collective-permute-start(f32[1024,128]{1,0:T(8,128)S(1)} %bitcast.48), channel_id=1, source_target_pairs={{0,1},{1,0},{2,3},{3,2},{4,5},{5,4},{6,7},{7,6},{8,9},{9,8},{10,11... | collective-permute-start | bytes 1572872 | tf_op jit(solution)/shard_map/ppermute | solution.py:509
  103.7 10.5 %copy-start.19 = (bf16[768,2048]{1,0:T(8,128)(2,1)}, bf16[768,2048]{1,0:T(8,128)(2,1)S(1)}, u32[]{:S(2)}) copy-start(bf16[768,2048]{1,0:T(8,128)(2,1)S(1)} %get-tuple-element.589.refs_3_) | copy-start | bytes 9437188
  103.7 10.5 %copy-start.20 = (bf16[768,2048]{1,0:T(8,128)(2,1)}, bf16[768,2048]{1,0:T(8,128)(2,1)S(1)}, u32[]{:S(2)}) copy-start(bf16[768,2048]{1,0:T(8,128)(2,1)S(1)} %get-tuple-element.590.refs_4_) | copy-start | bytes 9437188
  136.7 19.8 %all-to-all-start.5 = ((f32[128,2,768]{2,1,0:T(2,128)}), f32[128,2,768]{2,1,0:T(2,128)S(1)}, u32[]{:S(2)}, u32[]{:S(2)}) async-start(f32[128,2,768]{2,1,0:T(2,128)} %get-tuple-element.325), calls=%async_computation.5 | async-start | bytes 1572864 | tf_op jit(solution)/shard_map/all_to_all | solution.py:689
  140.2 16.2 %copy-start.21 = (s32[128]{0:T(128)S(1)}, s32[128]{0:T(128)}, u32[]{:S(2)}) copy-start(s32[128]{0:T(128)} %slot_ref.1) | copy-start | bytes 1540
  164.3 11.1 %copy-start.13 = (f32[320,256]{1,0:T(8,128)}, f32[320,256]{1,0:T(8,128)S(1)}, u32[]{:S(2)}) copy-start(f32[320,256]{1,0:T(8,128)S(1)} %get-tuple-element.573.iband_ref) | copy-start | bytes 983044 | tf_op jit(solution)/shard_map/while/body/while
  164.3 11.1 %copy-start.15 = (f32[320,256]{1,0:T(8,128)}, f32[320,256]{1,0:T(8,128)S(1)}, u32[]{:S(2)}) copy-start(f32[320,256]{1,0:T(8,128)S(1)} %get-tuple-element.574.oband_ref) | copy-start | bytes 983044 | tf_op jit(solution)/shard_map/while/body/while
  166.8 8.7 %copy-start.5 = (f32[12,256,256]{2,1,0:T(8,128)S(1)}, f32[12,256,256]{2,1,0:T(8,128)}, u32[]{:S(2)}) copy-start(f32[12,256,256]{2,1,0:T(8,128)} %get-tuple-element.572.band_ref) | copy-start | bytes 9437188 | tf_op jit(solution)/shard_map/while/body/while
  167.1 3.3 collective-permute-start
  168.5 7.0 %collective-permute-start.1 = (f32[192,256]{1,0:T(8,128)S(1)}, f32[192,256]{1,0:T(8,128)S(1)}, u32[]{:S(2)}, u32[]{:S(2)}) collective-permute-start(f32[192,256]{1,0:T(8,128)S(1)} %get-tuple-element.519), channel_id=1, source_target_pairs={{1,2},{3,4},{5,6},{7,8},{9,10},{11,12},{13,14},{15,16},{17,18},{19... | collective-permute-start | bytes 589832 | tf_op jit(solution)/shard_map/while/body/while/body/eval_jaxpr/ppermute | solution.py:517
  191.4 2.0 collective-permute-start.2
  229.4 4.5 collective-permute-start.3
  248.3 6.0 copy-start.4
  248.4 6.0 copy-start.6
  248.4 6.0 copy-start.7
  259.1 10.3 %copy-start.13 = (f32[320,256]{1,0:T(8,128)}, f32[320,256]{1,0:T(8,128)S(1)}, u32[]{:S(2)}) copy-start(f32[320,256]{1,0:T(8,128)S(1)} %get-tuple-element.573.iband_ref) | copy-start | bytes 983044 | tf_op jit(solution)/shard_map/while/body/while
  259.1 10.3 %copy-start.15 = (f32[320,256]{1,0:T(8,128)}, f32[320,256]{1,0:T(8,128)S(1)}, u32[]{:S(2)}) copy-start(f32[320,256]{1,0:T(8,128)S(1)} %get-tuple-element.574.oband_ref) | copy-start | bytes 983044 | tf_op jit(solution)/shard_map/while/body/while
  261.6 7.9 %copy-start.5 = (f32[12,256,256]{2,1,0:T(8,128)S(1)}, f32[12,256,256]{2,1,0:T(8,128)}, u32[]{:S(2)}) copy-start(f32[12,256,256]{2,1,0:T(8,128)} %get-tuple-element.572.band_ref) | copy-start | bytes 9437188 | tf_op jit(solution)/shard_map/while/body/while
  261.9 2.9 collective-permute-start
  262.4 7.1 %collective-permute-start.1 = (f32[192,256]{1,0:T(8,128)S(1)}, f32[192,256]{1,0:T(8,128)S(1)}, u32[]{:S(2)}, u32[]{:S(2)}) collective-permute-start(f32[192,256]{1,0:T(8,128)S(1)} %get-tuple-element.519), channel_id=1, source_target_pairs={{1,2},{3,4},{5,6},{7,8},{9,10},{11,12},{13,14},{15,16},{17,18},{19... | collective-permute-start | bytes 589832 | tf_op jit(solution)/shard_map/while/body/while/body/eval_jaxpr/ppermute | solution.py:517
  285.4 2.0 collective-permute-start.2
  324.4 4.5 collective-permute-start.3
  343.3 6.6 copy-start.4
  343.3 6.6 copy-start.6
  343.3 6.6 copy-start.7
  354.7 10.3 %copy-start.13 = (f32[320,256]{1,0:T(8,128)}, f32[320,256]{1,0:T(8,128)S(1)}, u32[]{:S(2)}) copy-start(f32[320,256]{1,0:T(8,128)S(1)} %get-tuple-element.573.iband_ref) | copy-start | bytes 983044 | tf_op jit(solution)/shard_map/while/body/while
  354.7 10.3 %copy-start.15 = (f32[320,256]{1,0:T(8,128)}, f32[320,256]{1,0:T(8,128)S(1)}, u32[]{:S(2)}) copy-start(f32[320,256]{1,0:T(8,128)S(1)} %get-tuple-element.574.oband_ref) | copy-start | bytes 983044 | tf_op jit(solution)/shard_map/while/body/while
  357.2 7.9 %copy-start.5 = (f32[12,256,256]{2,1,0:T(8,128)S(1)}, f32[12,256,256]{2,1,0:T(8,128)}, u32[]{:S(2)}) copy-start(f32[12,256,256]{2,1,0:T(8,128)} %get-tuple-element.572.band_ref) | copy-start | bytes 9437188 | tf_op jit(solution)/shard_map/while/body/while
  357.5 2.9 collective-permute-start
  358.0 7.1 %collective-permute-start.1 = (f32[192,256]{1,0:T(8,128)S(1)}, f32[192,256]{1,0:T(8,128)S(1)}, u32[]{:S(2)}, u32[]{:S(2)}) collective-permute-start(f32[192,256]{1,0:T(8,128)S(1)} %get-tuple-element.519), channel_id=1, source_target_pairs={{1,2},{3,4},{5,6},{7,8},{9,10},{11,12},{13,14},{15,16},{17,18},{19... | collective-permute-start | bytes 589832 | tf_op jit(solution)/shard_map/while/body/while/body/eval_jaxpr/ppermute | solution.py:517
  381.1 2.0 collective-permute-start.2
  420.0 4.5 collective-permute-start.3
  439.0 6.6 copy-start.4
  439.0 6.6 copy-start.6
  439.0 6.6 copy-start.7
  450.4 10.3 %copy-start.13 = (f32[320,256]{1,0:T(8,128)}, f32[320,256]{1,0:T(8,128)S(1)}, u32[]{:S(2)}) copy-start(f32[320,256]{1,0:T(8,128)S(1)} %get-tuple-element.573.iband_ref) | copy-start | bytes 983044 | tf_op jit(solution)/shard_map/while/body/while
  450.4 10.3 %copy-start.15 = (f32[320,256]{1,0:T(8,128)}, f32[320,256]{1,0:T(8,128)S(1)}, u32[]{:S(2)}) copy-start(f32[320,256]{1,0:T(8,128)S(1)} %get-tuple-element.574.oband_ref) | copy-start | bytes 983044 | tf_op jit(solution)/shard_map/while/body/while
  452.8 7.9 %copy-start.5 = (f32[12,256,256]{2,1,0:T(8,128)S(1)}, f32[12,256,256]{2,1,0:T(8,128)}, u32[]{:S(2)}) copy-start(f32[12,256,256]{2,1,0:T(8,128)} %get-tuple-element.572.band_ref) | copy-start | bytes 9437188 | tf_op jit(solution)/shard_map/while/body/while
  453.1 2.9 collective-permute-start
  453.6 7.1 %collective-permute-start.1 = (f32[192,256]{1,0:T(8,128)S(1)}, f32[192,256]{1,0:T(8,128)S(1)}, u32[]{:S(2)}, u32[]{:S(2)}) collective-permute-start(f32[192,256]{1,0:T(8,128)S(1)} %get-tuple-element.519), channel_id=1, source_target_pairs={{1,2},{3,4},{5,6},{7,8},{9,10},{11,12},{13,14},{15,16},{17,18},{19... | collective-permute-start | bytes 589832 | tf_op jit(solution)/shard_map/while/body/while/body/eval_jaxpr/ppermute | solution.py:517
  476.7 2.0 collective-permute-start.2
  515.6 4.5 collective-permute-start.3
  534.6 6.6 copy-start.4
  534.6 6.6 copy-start.6
  534.6 6.6 copy-start.7
  546.0 10.3 %copy-start.13 = (f32[320,256]{1,0:T(8,128)}, f32[320,256]{1,0:T(8,128)S(1)}, u32[]{:S(2)}) copy-start(f32[320,256]{1,0:T(8,128)S(1)} %get-tuple-element.573.iband_ref) | copy-start | bytes 983044 | tf_op jit(solution)/shard_map/while/body/while
  546.0 10.3 %copy-start.15 = (f32[320,256]{1,0:T(8,128)}, f32[320,256]{1,0:T(8,128)S(1)}, u32[]{:S(2)}) copy-start(f32[320,256]{1,0:T(8,128)S(1)} %get-tuple-element.574.oband_ref) | copy-start | bytes 983044 | tf_op jit(solution)/shard_map/while/body/while
  548.4 7.9 %copy-start.5 = (f32[12,256,256]{2,1,0:T(8,128)S(1)}, f32[12,256,256]{2,1,0:T(8,128)}, u32[]{:S(2)}) copy-start(f32[12,256,256]{2,1,0:T(8,128)} %get-tuple-element.572.band_ref) | copy-start | bytes 9437188 | tf_op jit(solution)/shard_map/while/body/while
  548.8 2.9 collective-permute-start
  549.2 7.1 %collective-permute-start.1 = (f32[192,256]{1,0:T(8,128)S(1)}, f32[192,256]{1,0:T(8,128)S(1)}, u32[]{:S(2)}, u32[]{:S(2)}) collective-permute-start(f32[192,256]{1,0:T(8,128)S(1)} %get-tuple-element.519), channel_id=1, source_target_pairs={{1,2},{3,4},{5,6},{7,8},{9,10},{11,12},{13,14},{15,16},{17,18},{19... | collective-permute-start | bytes 589832 | tf_op jit(solution)/shard_map/while/body/while/body/eval_jaxpr/ppermute | solution.py:517
  572.3 2.0 collective-permute-start.2
  611.2 4.5 collective-permute-start.3
  630.2 6.6 copy-start.4
  630.2 6.6 copy-start.6
  630.2 6.6 copy-start.7
  647.3 20.3 %copy-start.22 = (s32[128]{0:T(128)S(1)}, s32[128]{0:T(128)}, u32[]{:S(2)}) copy-start(s32[128]{0:T(128)} %get-tuple-element.653) | copy-start | bytes 1540 | tf_op jit(solution)/shard_map/while
  (42 other events, 46.8 us)

commit v5 on v4

--- a/solution.py
+++ b/solution.py
@@ -23,7 +23,7 @@
 SMALL = 128
 SPAN = 80
 BATCH = 8
-TOGETHER = 2
+TOGETHER = 4
 EDGE = 192
 
 
@@ -356,7 +356,7 @@
     return dot3(*halves(a), *halves(b))
 
 
-def inverse_spd(matrix, mul, limit):
+def inverse_spd(matrix):
     size = matrix.shape[0]
     unit = (iota((size, size), 0) == iota((size, size), 1)).astype(F32)
     along, down = diagonals(matrix)
@@ -368,30 +368,70 @@
 
     def going(state):
         k, worst, _, _ = state
-        return (k < 40) & (size * worst * worst > limit)
+        return (k < 40) & (size * worst * worst > 1e-9)
 
     def step(state):
         k, _, total, power = state
-        both = mul(jnp.concatenate([total, power], axis=0), power)
+        both = full_dot(jnp.concatenate([total, power], axis=0), power)
         total = total + both[:size]
         power = both[size:]
         return k + 1, jnp.max(jnp.abs(power)), total, power
 
     total = factor * (unit + rest)
-    power = mul(rest, rest)
+    power = full_dot(rest, rest)
     rounds, worst, total, power = lax.while_loop(
         going, step, (1, jnp.max(jnp.abs(power)), total, power)
     )
     worst = size * worst * worst
-    total = total + mul(total, power)
+    total = total + full_dot(total, power)
     return total * scale, worst, rounds
+
+
+def solve_fast(matrix, target):
+    size = matrix.shape[0]
+    direct = target.shape[1] == size
+    unit = jnp.where(iota((size, size), 0) == iota((size, size), 1), 1.0, 0.0)
+    along, down = diagonals(matrix)
+    along, down = lax.rsqrt(along), lax.rsqrt(down)
+    scaled = matrix * (along * down)
+    norm = jnp.max(jnp.sum(jnp.abs(scaled), axis=1, keepdims=True), axis=0, keepdims=True)
+    factor = jnp.where(norm < 1.9, 1.0, 1.9 / norm)
+    power = unit - factor * scaled
+
+    def twice(power, total):
+        both = split_dot(power, jnp.concatenate([power, total], axis=1))
+        return both[:, :size], total + both[:, size:]
+
+    if direct:
+        power, total = twice(power, target * (down * factor))
+    else:
+        total = factor * (unit + power)
+        power = split_dot(power, power)
+    power, total = twice(power, total)
+
+    def going(state):
+        k, worst, _, _ = state
+        return (k < 40) & (size * worst * worst > CLOSE)
+
+    def step(state):
+        k, _, power, total = state
+        power, total = twice(power, total)
+        return k + 1, jnp.max(jnp.abs(power)), power, total
+
+    rounds, worst, power, total = lax.while_loop(
+        going, step, (2, jnp.max(jnp.abs(power)), power, total)
+    )
+    total = total + split_dot(power, total)
+    if not direct:
+        total = split_dot(total * along, target)
+    return total * down, size * worst * worst, rounds
 
 
 def ratio(left, whole):
     return jnp.min(diagonals(left)[0] / diagonals(whole)[0])
 
 
-def galerkin_kernel(core_ref, mine_ref, theirs_ref, basis_ref, out_ref, rows_ref, good_ref, mom_ref):
+def galerkin_kernel(core_ref, mine_ref, theirs_ref, basis_ref, out_ref, rows_ref, good_ref, mom_ref, coef_ref, stage_ref, sems):
     size = out_ref.shape[1]
     gap = jnp.zeros((64, 128), F32)
     right = iota((64, 128), 1) < 64
@@ -421,12 +461,11 @@
     m = [mom_ref[n] for n in range(2 * ITERS)]
     h = [m[n + 1] + SHIFT * m[n] for n in range(2 * ITERS - 1)]
 
-    def right_of(inverse, *targets):
-        wide = split_dot(inverse, jnp.concatenate(targets, axis=1))
-        return [wide[:, n * size : (n + 1) * size] for n in range(len(targets))]
-
-    s0, w0, k0 = inverse_spd(h[0], split_dot, CLOSE)
-    z01, z02, z0m = right_of(s0, h[1], h[2], m[0])
+    def solved(matrix, *targets):
+        wide, worst, rounds = solve_fast(matrix, jnp.concatenate(targets, axis=1))
+        return [wide[:, n * size : (n + 1) * size] for n in range(len(targets))], worst, rounds
+
+    (z01, z02, z0m), w0, k0 = solved(h[0], h[1], h[2], m[0])
     upper = split_dot(h[1], jnp.concatenate([z01, z02, z0m], axis=1))
     lower = split_dot(h[2], jnp.concatenate([z02, z0m], axis=1))
     first = h[2] - upper[:, :size]
@@ -435,27 +474,33 @@
     last = h[4] - lower[:, :size]
     m2 = m[2] - lower[:, size:]
     first = 0.5 * (first + first.T)
-    s1, w1, k1 = inverse_spd(first, split_dot, CLOSE)
-    z12, z1m = right_of(s1, cross, m1)
+    (z12, z1m), w1, k1 = solved(first, cross, m1)
     lower = split_dot(cross.T, jnp.concatenate([z12, z1m], axis=1))
     rest = last - lower[:, :size]
     rest = 0.5 * (rest + rest.T)
     m2 = m2 - lower[:, size:]
-    s2, w2, k2 = inverse_spd(rest, split_dot, CLOSE)
-    y2 = split_dot(s2, m2)
+    (y2,), w2, k2 = solved(rest, m2)
     y1 = z1m - split_dot(z12, y2)
     y0 = z0m - split_dot(jnp.concatenate([z01, z02], axis=1), jnp.concatenate([y1, y2], axis=0))
-    out_ref[:size] = y0
-    out_ref[size : 2 * size] = y1
-    out_ref[2 * size :] = y2
-    wide = out_ref.shape[0]
-    yh, yl = halves(out_ref[...])
+    for n, y in enumerate((y0, y1, y2)):
+        coef_ref[n * size : (n + 1) * size] = y
+    keep = pltpu.make_async_copy(coef_ref, out_ref, sems.at[0])
+    keep.start()
+    wide = coef_ref.shape[0]
+    yh, yl = halves(coef_ref[...])
+    sends = []
     for k in range(3):
         part = dot3(*halves(basis_ref[:, k * wide : (k + 1) * wide]), yh, yl)
-        rows_ref[:, :, k * size : (k + 1) * size] = part.reshape(rows_ref.shape[0], -1, size)
+        stage_ref[k] = part.reshape(rows_ref.shape[0], -1, size)
+        sends.append(
+            pltpu.make_async_copy(stage_ref.at[k], rows_ref.at[:, :, pl.ds(k * size, size)], sems.at[k + 1])
+        )
+        sends[-1].start()
     share = jnp.minimum(ratio(first, h[2]), ratio(rest, h[4]))
     rounds = jnp.maximum(k0, jnp.maximum(k1, k2))
     worst = jnp.maximum(w0, jnp.maximum(w1, w2))
+    for copy in [keep, *sends]:
+        copy.wait()
     good_ref[0] = jnp.where((share > GUARD) & (worst <= CLOSE) & (rounds <= ROUNDS), 1, 0)
 
 
@@ -466,13 +511,18 @@
     return pl.pallas_call(
         galerkin_kernel,
         out_shape=(
-            jax.ShapeDtypeStruct((ITERS * size, size), F32),
-            jax.ShapeDtypeStruct((peers, slots // peers, wide // ITERS), F32),
+            pltpu.HBM((ITERS * size, size), F32),
+            pltpu.HBM((peers, slots // peers, wide // ITERS), F32),
             jax.ShapeDtypeStruct((1,), jnp.int32),
         ),
         in_specs=[smem] + in_vmem(3),
-        out_specs=(*in_vmem(2), smem),
-        scratch_shapes=[pltpu.VMEM((2 * ITERS, size, size), F32)],
+        out_specs=(*[pl.BlockSpec(memory_space=pltpu.HBM)] * 2, smem),
+        scratch_shapes=[
+            pltpu.VMEM((2 * ITERS, size, size), F32),
+            pltpu.VMEM((ITERS * size, size), F32),
+            pltpu.VMEM((3, peers, slots // peers, size), F32),
+            pltpu.SemaphoreType.DMA((4,)),
+        ],
         compiler_params=pltpu.CompilerParams(vmem_limit_bytes=32 << 20),
         name="galerkin",
     )(core, mine, theirs, basis_rows)
@@ -481,7 +531,7 @@
 def solve_kernel(matrix_ref, target_ref, out_ref):
     matrix = matrix_ref[...]
     matrix = 0.5 * (matrix + matrix.T)
-    inverse, _, _ = inverse_spd(matrix, full_dot, 1e-9)
+    inverse, _, _ = inverse_spd(matrix)
     guess = full_dot(inverse, target_ref[...])
     out_ref[...] = guess + full_dot(inverse, target_ref[...] - full_dot(matrix, guess))
 
@@ -715,23 +765,21 @@
         scratch_shapes=[pltpu.VMEM(coef.shape, BF16)] * 2,
         compiler_params=pltpu.CompilerParams(vmem_limit_bytes=20 << 20),
         name="combine",
-    )(*[vector for vector, _ in vectors], coef)
+    )(*[vector for vector, _ in vectors], pltpu.with_memory_space_constraint(coef, pltpu.HBM))
 
 
 def lead_kernel(slot_ref, received_ref, out_ref):
-    _, places, wide = received_ref.shape
+    peers, places, wide = received_ref.shape
     _, dipoles, cols = out_ref.shape
-    together = 8
-
-    def pick(i, carry):
-        for n in range(together):
-            slot = slot_ref[i * together + n]
-            row = received_ref[slot // places, pl.ds(slot % places, 1), :]
-            for k in range(wide // cols):
-                out_ref[k, pl.ds(i * together + n, 1), :] = row[:, k * cols : (k + 1) * cols]
-        return carry
-
-    lax.fori_loop(0, dipoles // together, pick, 0)
+    left = received_ref[...].reshape(peers * places, wide)
+    hot = jnp.where(iota((peers * places, dipoles), 0) == slot_ref[...], 1.0, 0.0).astype(BF16)
+    picked = jnp.zeros((dipoles, wide), F32)
+    for _ in range(3):
+        part = left.astype(BF16)
+        left = left - part.astype(F32)
+        picked = picked + dot(hot, part, ((0,), (0,)))
+    for k in range(3):
+        out_ref[k] = picked[:, k * cols : (k + 1) * cols]
 
 
 def lead(received, dipole_slot):
@@ -739,11 +787,11 @@
     return pl.pallas_call(
         lead_kernel,
         out_shape=jax.ShapeDtypeStruct(out, F32),
-        in_specs=[pl.BlockSpec(memory_space=pltpu.SMEM)] + in_vmem(1),
+        in_specs=in_vmem(2),
         out_specs=in_vmem(1)[0],
         compiler_params=pltpu.CompilerParams(vmem_limit_bytes=20 << 20),
         name="lead",
-    )(dipole_slot, received)
+    )(dipole_slot[None], received)
 
 
 def one_device(right_side, tile_stiff, tile_nodes, node_shift, slot_nodes, slot_load, dipole_slot):

time: 674 us -> 681 us (1.010); the launches traced: 672 us -> 670 us
  no operation moved by 1% of the time
where the time goes in v5:
time: 681 us; the launch traced here: 670 us
  blocking collectives  244 us (36%)
  Pallas kernels  216 us (32%)
  waiting for transfers between devices  57.6 us (8%)
  matrix products  48.7 us (7%)
  starting transfers between devices  43.9 us (6%)
  local copies, waits for them, and re-layouts  35.8 us (5%)
  other arithmetic  19.1 us (3%)
    all_to_all x6, blocking collectives, total_of(): arrived = lax.all_to_all(pair, CHIPS, 0, 0, tiled=True)  129 us
    pallas_call x6, Pallas kernels, powers(): pl.pallas_call(powers_kernel, out_shape=(pltpu.HBM((ITERS - 1, own, cols)...  97.7 us
    all_to_all x6, blocking collectives, total_of(): gathered = lax.all_to_all(own, CHIPS, 0, 0, tiled=True)  94.8 us
    pallas_call x5, Pallas kernels, solve(): pl.pallas_call(solve_kernel, out_shape=jax.ShapeDtypeStruct(target.shape,...  53.3 us
    dot_general x10, matrix products, times(): jnp.dot(a, b, preferred_element_type=F32, precision=lax.Precision.HIGHEST)  48.7 us
    ppermute x7, waiting for transfers between devices, swap_sides(): lax.ppermute(outer, AXES, across + [(b, a) for a, b in across])  28.5 us
    while x156, local copies, waits for them, and re-layouts  28.1 us
    pallas_call x1, Pallas kernels, galerkin(): pl.pallas_call(galerkin_kernel, out_shape=(pltpu.HBM((ITERS * size, size)...  22 us
  transfers between devices with their start and end apart: 27, of which 18 were waited for; matrix products, arithmetic and copies ran while one was open for 0% of the time, Pallas kernels for 3%

profile of v5, /device:TPU:1, one launch (start us, length us, event | category | flops | bytes accessed | tf_op | source)
XLA Modules:
  0.0 670.5 jit_solution(13226116141383257371)
XLA Ops:
  4.8 11.7 %assemble.1 = (f32[12,256,256]{2,1,0:T(8,128)}, f32[320,256]{1,0:T(8,128)S(1)}, f32[320,256]{1,0:T(8,128)S(1)}) custom-call(s32[1]{0:T(128)} %bitcast.1.core_ref, s32[256]{0:T(256)S(1)} %get-tuple-element.409.group_ref, s32[256]{0:T(256)S(1)} %multiply_minimum_fusion.first_ref, f32[32,32,256]{2,1,0:T(8,128)S(1)} %bitcast.52, ...), custom_call_target="tpu_custom_call" | custom-call | tf_op jit(solution)/shard_map/assemble/pallas_call | solution.py:169
  17.9 3.6 collective-permute-start.7
  22.5 2.0 collective-permute-start.5
  24.7 4.8 collective-permute-done.5.outer_ref
  29.5 17.9 %powers.9 = (f32[2,2048,256]{2,1,0:T(8,128)}, f32[1024,128]{1,0:T(8,128)S(1)}, f32[1024,128]{1,0:T(8,128)S(1)}) custom-call(s32[3]{0:T(128)S(1)} %pad_add_fusion.valid_ref, f32[2048,256]{1,0:T(8,128)} %k0_ref.1, f32[192,256]{1,0:T(8,128)S(1)} %collective-permute-done.4.inner_ref, f32[192,256]{1,0:T(8,128)S(1)} %collective-permute-done.5.outer_ref, ...), custom_call_target="tpu_custom_call" | custom-call | tf_op jit(solution)/shard_map/powers/pallas_call | solution.py:337
  49.5 26.5 %all_to_all.48 = f32[64,16,128]{2,1,0:T(8,128)S(1)} all-to-all(f32[64,16,128]{2,1,0:T(8,128)S(1)} %bitcast.55), channel_id=1, replica_groups=mesh['row'=4,'column'=4,'depth'=4,'core'=2] {'row','column','depth'}, dimensions={0} | all-to-all | bytes 1048576 | tf_op jit(solution)/shard_map/all_to_all | solution.py:555
  76.1 15.7 %all_to_all.49 = f32[64,16,128]{2,1,0:T(8,128)S(1)} all-to-all(f32[64,16,128]{2,1,0:T(8,128)S(1)} %broadcast_in_dim.52), channel_id=1, replica_groups=mesh['row'=4,'column'=4,'depth'=4,'core'=2] {'row','column','depth'}, dimensions={0} | all-to-all | bytes 1048576 | tf_op jit(solution)/shard_map/all_to_all | solution.py:557
  91.8 3.0 collective-permute-start.9
  94.8 5.4 loads.1
  100.3 10.5 %basis.3.basis_ref = f32[256,2304]{1,0:T(8,128)S(1)} custom-call(f32[2048,256]{1,0:T(8,128)S(1)} %copy-done.9, f32[2,2048,256]{2,1,0:T(8,128)} %get-tuple-element.320.refs_1_.refs_2_.k1_ref.k2_ref, f32[2,2048,256]{2,1,0:T(8,128)} %get-tuple-element.320.refs_1_.refs_2_.k1_ref.k2_ref, bf16[768,2048]{1,0:T(8,128)(2,1)S(1)} %get-tuple-element.590.refs_3_, ...), custom_call_target="tpu_custom_call" | custom-call | tf_op jit(solution)/shard_map/basis/pallas_call | solution.py:719
  110.8 22.0 %galerkin.1 = (f32[768,256]{1,0:T(8,128)}, f32[128,2,768]{2,1,0:T(2,128)}, s32[1]{0:T(128)}) custom-call(s32[1]{0:T(128)} %bitcast.1.core_ref, f32[1024,128]{1,0:T(8,128)S(1)} %bitcast.51, f32[1024,128]{1,0:T(8,128)S(1)} %collective-permute-done.9.theirs_ref, f32[256,2304]{1,0:T(8,128)S(1)} %basis.3.basis_ref), custom_call_target="tpu_custom_call" | custom-call | tf_op jit(solution)/shard_map/galerkin/pallas_call | solution.py:511
  132.8 3.6 all-to-all-start.5
  136.4 6.3 combine.1
  142.7 10.0 %all-to-all-done.5.received_ref = f32[128,2,768]{2,1,0:T(2,128)S(1)} async-done(((f32[128,2,768]{2,1,0:T(2,128)}), f32[128,2,768]{2,1,0:T(2,128)S(1)}, u32[]{:S(2)}, u32[]{:S(2)}) %all-to-all-start.5) | async-done | bytes 786464 | tf_op jit(solution)/shard_map/all_to_all | solution.py:739
  154.3 514.9 %while.31 = (s32[]{:T(128)}, f32[2048,256]{1,0:T(8,128)}, f32[3,128,256]{2,1,0:T(8,128)}, s32[]{:T(128)}, s32[3]{0:T(128)S(1)}, /*index=5*/f32[12,256,256]{2,1,0...) while((s32[]{:T(128)}, f32[2048,256]{1,0:T(8,128)}, ...), condition=%region_6.7_spmd, body=%region_2.6_spmd | while | flops 3232530432 | bytes 127982720 | solution.py:821
  155.2 3.0 copy.33
  158.2 3.1 copy.32
  161.3 477.3 %while.33 = (s32[]{:T(128)}, f32[2048,256]{1,0:T(8,128)}, f32[2048,256]{1,0:T(8,128)}, f32[2048,256]{1,0:T(8,128)}, f32[256,256]{1,0:T(8,128)S(1)}, /*index=5*/p...) while((s32[]{:T(128)}, f32[2048,256]{1,0:T(8,128)}, ...), condition=%wide.region_5.5_spmd.clone, body=%wide.region_3.4_spmd.clone.sunk | while | flops 3232530432 | bytes 108057400 | solution.py:615
  167.4 5.0 collective-permute-done.1.outer_ref
  172.5 15.9 %powers.10 = (f32[2,2048,256]{2,1,0:T(8,128)}, f32[1024,128]{1,0:T(8,128)S(1)}, f32[1024,128]{1,0:T(8,128)S(1)}) custom-call(s32[3]{0:T(128)S(1)} %get-tuple-element.571.valid_ref, f32[2048,256]{1,0:T(8,128)S(1)} %broadcast_select_fusion.5.own_ref, f32[192,256]{1,0:T(8,128)S(1)} %collective-permute-done.inner_ref, ...), custom_call_target="tpu_custom_call" | custom-call | tf_op jit(solution)/shard_map/while/body/while/body/eval_jaxpr/powers/pallas_call | solution.py:337
  190.5 19.8 %all_to_all.50 = f32[64,16,128]{2,1,0:T(8,128)S(1)} all-to-all(f32[64,16,128]{2,1,0:T(8,128)S(1)} %bitcast.53), channel_id=1, replica_groups=mesh['row'=4,'column'=4,'depth'=4,'core'=2] {'row','column','depth'}, dimensions={0} | all-to-all | bytes 1048576 | tf_op jit(solution)/shard_map/while/body/while/body/eval_jaxpr/all_to_all | solution.py:555
  210.4 15.8 %all_to_all.51 = f32[64,16,128]{2,1,0:T(8,128)S(1)} all-to-all(f32[64,16,128]{2,1,0:T(8,128)S(1)} %broadcast_in_dim.60), channel_id=1, replica_groups=mesh['row'=4,'column'=4,'depth'=4,'core'=2] {'row','column','depth'}, dimensions={0} | all-to-all | bytes 1048576 | tf_op jit(solution)/shard_map/while/body/while/body/eval_jaxpr/all_to_all | solution.py:557
  226.4 3.0 collective-permute-start.3
  234.7 10.7 %solve.8 = f32[256,256]{1,0:T(8,128)} custom-call(f32[256,256]{1,0:T(8,128)} %fusion.36.matrix_ref, f32[256,256]{1,0:T(8,128)S(1)} %fusion.37.target_ref), custom_call_target="tpu_custom_call" | custom-call | tf_op jit(solution)/shard_map/while/body/while/body/eval_jaxpr/solve/pallas_call | solution.py:540
  245.4 6.0 add_select_fusion.3
  251.3 3.3 subtract_select_fusion.3
  259.4 2.4 collective-permute-start.1
  261.8 4.7 collective-permute-done.1.outer_ref
  266.5 16.0 %powers.10 = (f32[2,2048,256]{2,1,0:T(8,128)}, f32[1024,128]{1,0:T(8,128)S(1)}, f32[1024,128]{1,0:T(8,128)S(1)}) custom-call(s32[3]{0:T(128)S(1)} %get-tuple-element.571.valid_ref, f32[2048,256]{1,0:T(8,128)S(1)} %broadcast_select_fusion.5.own_ref, f32[192,256]{1,0:T(8,128)S(1)} %collective-permute-done.inner_ref, ...), custom_call_target="tpu_custom_call" | custom-call | tf_op jit(solution)/shard_map/while/body/while/body/eval_jaxpr/powers/pallas_call | solution.py:337
  284.5 20.7 %all_to_all.50 = f32[64,16,128]{2,1,0:T(8,128)S(1)} all-to-all(f32[64,16,128]{2,1,0:T(8,128)S(1)} %bitcast.53), channel_id=1, replica_groups=mesh['row'=4,'column'=4,'depth'=4,'core'=2] {'row','column','depth'}, dimensions={0} | all-to-all | bytes 1048576 | tf_op jit(solution)/shard_map/while/body/while/body/eval_jaxpr/all_to_all | solution.py:555
  305.3 15.8 %all_to_all.51 = f32[64,16,128]{2,1,0:T(8,128)S(1)} all-to-all(f32[64,16,128]{2,1,0:T(8,128)S(1)} %broadcast_in_dim.60), channel_id=1, replica_groups=mesh['row'=4,'column'=4,'depth'=4,'core'=2] {'row','column','depth'}, dimensions={0} | all-to-all | bytes 1048576 | tf_op jit(solution)/shard_map/while/body/while/body/eval_jaxpr/all_to_all | solution.py:557
  321.4 3.0 collective-permute-start.3
  329.7 10.7 %solve.8 = f32[256,256]{1,0:T(8,128)} custom-call(f32[256,256]{1,0:T(8,128)} %fusion.36.matrix_ref, f32[256,256]{1,0:T(8,128)S(1)} %fusion.37.target_ref), custom_call_target="tpu_custom_call" | custom-call | tf_op jit(solution)/shard_map/while/body/while/body/eval_jaxpr/solve/pallas_call | solution.py:540
  340.4 6.6 add_select_fusion.3
  346.9 3.3 subtract_select_fusion.3
  355.0 2.4 collective-permute-start.1
  357.4 4.7 collective-permute-done.1.outer_ref
  362.1 15.9 %powers.10 = (f32[2,2048,256]{2,1,0:T(8,128)}, f32[1024,128]{1,0:T(8,128)S(1)}, f32[1024,128]{1,0:T(8,128)S(1)}) custom-call(s32[3]{0:T(128)S(1)} %get-tuple-element.571.valid_ref, f32[2048,256]{1,0:T(8,128)S(1)} %broadcast_select_fusion.5.own_ref, f32[192,256]{1,0:T(8,128)S(1)} %collective-permute-done.inner_ref, ...), custom_call_target="tpu_custom_call" | custom-call | tf_op jit(solution)/shard_map/while/body/while/body/eval_jaxpr/powers/pallas_call | solution.py:337
  380.1 20.7 %all_to_all.50 = f32[64,16,128]{2,1,0:T(8,128)S(1)} all-to-all(f32[64,16,128]{2,1,0:T(8,128)S(1)} %bitcast.53), channel_id=1, replica_groups=mesh['row'=4,'column'=4,'depth'=4,'core'=2] {'row','column','depth'}, dimensions={0} | all-to-all | bytes 1048576 | tf_op jit(solution)/shard_map/while/body/while/body/eval_jaxpr/all_to_all | solution.py:555
  401.0 15.8 %all_to_all.51 = f32[64,16,128]{2,1,0:T(8,128)S(1)} all-to-all(f32[64,16,128]{2,1,0:T(8,128)S(1)} %broadcast_in_dim.60), channel_id=1, replica_groups=mesh['row'=4,'column'=4,'depth'=4,'core'=2] {'row','column','depth'}, dimensions={0} | all-to-all | bytes 1048576 | tf_op jit(solution)/shard_map/while/body/while/body/eval_jaxpr/all_to_all | solution.py:557
  417.0 3.0 collective-permute-start.3
  425.3 10.7 %solve.8 = f32[256,256]{1,0:T(8,128)} custom-call(f32[256,256]{1,0:T(8,128)} %fusion.36.matrix_ref, f32[256,256]{1,0:T(8,128)S(1)} %fusion.37.target_ref), custom_call_target="tpu_custom_call" | custom-call | tf_op jit(solution)/shard_map/while/body/while/body/eval_jaxpr/solve/pallas_call | solution.py:540
  436.0 6.6 add_select_fusion.3
  442.6 3.3 subtract_select_fusion.3
  450.6 2.4 collective-permute-start.1
  453.1 4.7 collective-permute-done.1.outer_ref
  457.7 15.9 %powers.10 = (f32[2,2048,256]{2,1,0:T(8,128)}, f32[1024,128]{1,0:T(8,128)S(1)}, f32[1024,128]{1,0:T(8,128)S(1)}) custom-call(s32[3]{0:T(128)S(1)} %get-tuple-element.571.valid_ref, f32[2048,256]{1,0:T(8,128)S(1)} %broadcast_select_fusion.5.own_ref, f32[192,256]{1,0:T(8,128)S(1)} %collective-permute-done.inner_ref, ...), custom_call_target="tpu_custom_call" | custom-call | tf_op jit(solution)/shard_map/while/body/while/body/eval_jaxpr/powers/pallas_call | solution.py:337
  475.7 20.7 %all_to_all.50 = f32[64,16,128]{2,1,0:T(8,128)S(1)} all-to-all(f32[64,16,128]{2,1,0:T(8,128)S(1)} %bitcast.53), channel_id=1, replica_groups=mesh['row'=4,'column'=4,'depth'=4,'core'=2] {'row','column','depth'}, dimensions={0} | all-to-all | bytes 1048576 | tf_op jit(solution)/shard_map/while/body/while/body/eval_jaxpr/all_to_all | solution.py:555
  496.6 15.8 %all_to_all.51 = f32[64,16,128]{2,1,0:T(8,128)S(1)} all-to-all(f32[64,16,128]{2,1,0:T(8,128)S(1)} %broadcast_in_dim.60), channel_id=1, replica_groups=mesh['row'=4,'column'=4,'depth'=4,'core'=2] {'row','column','depth'}, dimensions={0} | all-to-all | bytes 1048576 | tf_op jit(solution)/shard_map/while/body/while/body/eval_jaxpr/all_to_all | solution.py:557
  512.6 3.0 collective-permute-start.3
  520.9 10.7 %solve.8 = f32[256,256]{1,0:T(8,128)} custom-call(f32[256,256]{1,0:T(8,128)} %fusion.36.matrix_ref, f32[256,256]{1,0:T(8,128)S(1)} %fusion.37.target_ref), custom_call_target="tpu_custom_call" | custom-call | tf_op jit(solution)/shard_map/while/body/while/body/eval_jaxpr/solve/pallas_call | solution.py:540
  531.6 6.6 add_select_fusion.3
  538.2 3.3 subtract_select_fusion.3
  546.2 2.4 collective-permute-start.1
  548.7 4.7 collective-permute-done.1.outer_ref
  553.4 15.9 %powers.10 = (f32[2,2048,256]{2,1,0:T(8,128)}, f32[1024,128]{1,0:T(8,128)S(1)}, f32[1024,128]{1,0:T(8,128)S(1)}) custom-call(s32[3]{0:T(128)S(1)} %get-tuple-element.571.valid_ref, f32[2048,256]{1,0:T(8,128)S(1)} %broadcast_select_fusion.5.own_ref, f32[192,256]{1,0:T(8,128)S(1)} %collective-permute-done.inner_ref, ...), custom_call_target="tpu_custom_call" | custom-call | tf_op jit(solution)/shard_map/while/body/while/body/eval_jaxpr/powers/pallas_call | solution.py:337
  571.4 20.7 %all_to_all.50 = f32[64,16,128]{2,1,0:T(8,128)S(1)} all-to-all(f32[64,16,128]{2,1,0:T(8,128)S(1)} %bitcast.53), channel_id=1, replica_groups=mesh['row'=4,'column'=4,'depth'=4,'core'=2] {'row','column','depth'}, dimensions={0} | all-to-all | bytes 1048576 | tf_op jit(solution)/shard_map/while/body/while/body/eval_jaxpr/all_to_all | solution.py:555
  592.2 15.8 %all_to_all.51 = f32[64,16,128]{2,1,0:T(8,128)S(1)} all-to-all(f32[64,16,128]{2,1,0:T(8,128)S(1)} %broadcast_in_dim.60), channel_id=1, replica_groups=mesh['row'=4,'column'=4,'depth'=4,'core'=2] {'row','column','depth'}, dimensions={0} | all-to-all | bytes 1048576 | tf_op jit(solution)/shard_map/while/body/while/body/eval_jaxpr/all_to_all | solution.py:557
  608.2 3.0 collective-permute-start.3
  616.6 10.7 %solve.8 = f32[256,256]{1,0:T(8,128)} custom-call(f32[256,256]{1,0:T(8,128)} %fusion.36.matrix_ref, f32[256,256]{1,0:T(8,128)S(1)} %fusion.37.target_ref), custom_call_target="tpu_custom_call" | custom-call | tf_op jit(solution)/shard_map/while/body/while/body/eval_jaxpr/solve/pallas_call | solution.py:540
  627.2 6.6 add_select_fusion.3
  633.8 3.3 subtract_select_fusion.3
  638.6 5.7 basis.2
  645.7 20.4 %all_to_all.47.received_ref = f32[128,2,768]{2,1,0:T(2,128)S(1)} all-to-all(f32[128,2,768]{2,1,0:T(2,128)} %reshape.106), channel_id=1, replica_groups=mesh['row'=4,'column'=4,'depth'=4,'core'=2] {'row','column','depth','core'}, dimensions={0} | all-to-all | bytes 1572864 | tf_op jit(solution)/shard_map/while/body/all_to_all | solution.py:739
  (309 shorter events, 78.0 us)
Async XLA Ops:
  16.5 13.0 %collective-permute-start.6 = (f32[320,256]{1,0:T(8,128)S(1)}, f32[320,256]{1,0:T(8,128)S(1)}, u32[]{:S(2)}, u32[]{:S(2)}) collective-permute-start(f32[320,256]{1,0:T(8,128)S(1)} %get-tuple-element.316), channel_id=1, source_target_pairs={{0,1},{1,0},{2,3},{3,2},{4,5},{5,4},{6,7},{7,6},{8,9},{9,8},{10,11... | collective-permute-start | bytes 983048 | tf_op jit(solution)/shard_map/ppermute | solution.py:566
  17.9 11.6 %collective-permute-start.7 = (f32[320,256]{1,0:T(8,128)S(1)}, f32[320,256]{1,0:T(8,128)S(1)}, u32[]{:S(2)}, u32[]{:S(2)}) collective-permute-start(f32[320,256]{1,0:T(8,128)S(1)} %get-tuple-element.317), channel_id=1, source_target_pairs={{1,2},{3,4},{5,6},{7,8},{9,10},{11,12},{13,14},{15,16},{17,18},{19... | collective-permute-start | bytes 983048 | tf_op jit(solution)/shard_map/ppermute | solution.py:567
  22.5 7.0 %collective-permute-start.5 = (f32[192,256]{1,0:T(8,128)S(1)}, f32[192,256]{1,0:T(8,128)S(1)}, u32[]{:S(2)}, u32[]{:S(2)}) collective-permute-start(f32[192,256]{1,0:T(8,128)S(1)} %get-tuple-element.424), channel_id=1, source_target_pairs={{1,2},{3,4},{5,6},{7,8},{9,10},{11,12},{13,14},{15,16},{17,18},{19... | collective-permute-start | bytes 589832 | tf_op jit(solution)/shard_map/ppermute | solution.py:567
  24.5 5.0 collective-permute-start.4
  47.4 2.0 collective-permute-start.8
  49.4 45.4 %copy-start.1 = (f32[16,768]{1,0:T(8,128)S(1)}, f32[16,768]{1,0:T(8,128)}, u32[]{:S(2)}) copy-start(f32[16,768]{1,0:T(8,128)} %load_ref.1) | copy-start | bytes 147460
  49.4 45.4 %copy-start.2 = (s32[16,256]{1,0:T(8,128)S(1)}, s32[16,256]{1,0:T(8,128)}, u32[]{:S(2)}) copy-start(s32[16,256]{1,0:T(8,128)} %nodes_ref.1) | copy-start | bytes 49156
  49.4 50.9 %copy-start.9 = (f32[2048,256]{1,0:T(8,128)S(1)}, f32[2048,256]{1,0:T(8,128)}, u32[]{:S(2)}) copy-start(f32[2048,256]{1,0:T(8,128)} %k0_ref.1) | copy-start | bytes 6291460
  91.8 19.0 %collective-permute-start.9 = (f32[1024,128]{1,0:T(8,128)S(1)}, f32[1024,128]{1,0:T(8,128)S(1)}, u32[]{:S(2)}, u32[]{:S(2)}) collective-permute-start(f32[1024,128]{1,0:T(8,128)S(1)} %bitcast.50), channel_id=1, source_target_pairs={{0,1},{1,0},{2,3},{3,2},{4,5},{5,4},{6,7},{7,6},{8,9},{9,8},{10,11... | collective-permute-start | bytes 1572872 | tf_op jit(solution)/shard_map/ppermute | solution.py:559
  100.2 10.5 %copy-start.19 = (bf16[768,2048]{1,0:T(8,128)(2,1)}, bf16[768,2048]{1,0:T(8,128)(2,1)S(1)}, u32[]{:S(2)}) copy-start(bf16[768,2048]{1,0:T(8,128)(2,1)S(1)} %get-tuple-element.590.refs_3_) | copy-start | bytes 9437188
  100.3 10.5 %copy-start.20 = (bf16[768,2048]{1,0:T(8,128)(2,1)}, bf16[768,2048]{1,0:T(8,128)(2,1)S(1)}, u32[]{:S(2)}) copy-start(bf16[768,2048]{1,0:T(8,128)(2,1)S(1)} %get-tuple-element.591.refs_4_) | copy-start | bytes 9437188
  132.8 19.9 %all-to-all-start.5 = ((f32[128,2,768]{2,1,0:T(2,128)}), f32[128,2,768]{2,1,0:T(2,128)S(1)}, u32[]{:S(2)}, u32[]{:S(2)}) async-start(f32[128,2,768]{2,1,0:T(2,128)} %get-tuple-element.325), calls=%async_computation.5 | async-start | bytes 1572864 | tf_op jit(solution)/shard_map/all_to_all | solution.py:739
  136.4 16.3 %copy-start.21 = (s32[128]{0:T(128)S(1)}, s32[128]{0:T(128)}, u32[]{:S(2)}) copy-start(s32[128]{0:T(128)} %param.17) | copy-start | bytes 1540
  161.3 11.1 %copy-start.13 = (f32[320,256]{1,0:T(8,128)}, f32[320,256]{1,0:T(8,128)S(1)}, u32[]{:S(2)}) copy-start(f32[320,256]{1,0:T(8,128)S(1)} %get-tuple-element.573.iband_ref) | copy-start | bytes 983044 | tf_op jit(solution)/shard_map/while/body/while
  161.3 11.1 %copy-start.15 = (f32[320,256]{1,0:T(8,128)}, f32[320,256]{1,0:T(8,128)S(1)}, u32[]{:S(2)}) copy-start(f32[320,256]{1,0:T(8,128)S(1)} %get-tuple-element.574.oband_ref) | copy-start | bytes 983044 | tf_op jit(solution)/shard_map/while/body/while
  163.8 8.7 %copy-start.5 = (f32[12,256,256]{2,1,0:T(8,128)S(1)}, f32[12,256,256]{2,1,0:T(8,128)}, u32[]{:S(2)}) copy-start(f32[12,256,256]{2,1,0:T(8,128)} %get-tuple-element.572.band_ref) | copy-start | bytes 9437188 | tf_op jit(solution)/shard_map/while/body/while
  164.1 3.3 collective-permute-start
  165.5 7.0 %collective-permute-start.1 = (f32[192,256]{1,0:T(8,128)S(1)}, f32[192,256]{1,0:T(8,128)S(1)}, u32[]{:S(2)}, u32[]{:S(2)}) collective-permute-start(f32[192,256]{1,0:T(8,128)S(1)} %get-tuple-element.519), channel_id=1, source_target_pairs={{1,2},{3,4},{5,6},{7,8},{9,10},{11,12},{13,14},{15,16},{17,18},{19... | collective-permute-start | bytes 589832 | tf_op jit(solution)/shard_map/while/body/while/body/eval_jaxpr/ppermute | solution.py:567
  188.4 2.0 collective-permute-start.2
  226.4 4.5 collective-permute-start.3
  245.4 6.0 copy-start.6
  245.4 6.0 copy-start.7
  256.1 10.3 %copy-start.13 = (f32[320,256]{1,0:T(8,128)}, f32[320,256]{1,0:T(8,128)S(1)}, u32[]{:S(2)}) copy-start(f32[320,256]{1,0:T(8,128)S(1)} %get-tuple-element.573.iband_ref) | copy-start | bytes 983044 | tf_op jit(solution)/shard_map/while/body/while
  256.1 10.3 %copy-start.15 = (f32[320,256]{1,0:T(8,128)}, f32[320,256]{1,0:T(8,128)S(1)}, u32[]{:S(2)}) copy-start(f32[320,256]{1,0:T(8,128)S(1)} %get-tuple-element.574.oband_ref) | copy-start | bytes 983044 | tf_op jit(solution)/shard_map/while/body/while
  258.6 7.9 %copy-start.5 = (f32[12,256,256]{2,1,0:T(8,128)S(1)}, f32[12,256,256]{2,1,0:T(8,128)}, u32[]{:S(2)}) copy-start(f32[12,256,256]{2,1,0:T(8,128)} %get-tuple-element.572.band_ref) | copy-start | bytes 9437188 | tf_op jit(solution)/shard_map/while/body/while
  258.9 2.9 collective-permute-start
  259.4 7.1 %collective-permute-start.1 = (f32[192,256]{1,0:T(8,128)S(1)}, f32[192,256]{1,0:T(8,128)S(1)}, u32[]{:S(2)}, u32[]{:S(2)}) collective-permute-start(f32[192,256]{1,0:T(8,128)S(1)} %get-tuple-element.519), channel_id=1, source_target_pairs={{1,2},{3,4},{5,6},{7,8},{9,10},{11,12},{13,14},{15,16},{17,18},{19... | collective-permute-start | bytes 589832 | tf_op jit(solution)/shard_map/while/body/while/body/eval_jaxpr/ppermute | solution.py:567
  282.4 2.0 collective-permute-start.2
  321.4 4.5 collective-permute-start.3
  340.3 6.6 copy-start.4
  340.4 6.6 copy-start.6
  340.4 6.6 copy-start.7
  351.8 10.3 %copy-start.13 = (f32[320,256]{1,0:T(8,128)}, f32[320,256]{1,0:T(8,128)S(1)}, u32[]{:S(2)}) copy-start(f32[320,256]{1,0:T(8,128)S(1)} %get-tuple-element.573.iband_ref) | copy-start | bytes 983044 | tf_op jit(solution)/shard_map/while/body/while
  351.8 10.3 %copy-start.15 = (f32[320,256]{1,0:T(8,128)}, f32[320,256]{1,0:T(8,128)S(1)}, u32[]{:S(2)}) copy-start(f32[320,256]{1,0:T(8,128)S(1)} %get-tuple-element.574.oband_ref) | copy-start | bytes 983044 | tf_op jit(solution)/shard_map/while/body/while
  354.2 7.9 %copy-start.5 = (f32[12,256,256]{2,1,0:T(8,128)S(1)}, f32[12,256,256]{2,1,0:T(8,128)}, u32[]{:S(2)}) copy-start(f32[12,256,256]{2,1,0:T(8,128)} %get-tuple-element.572.band_ref) | copy-start | bytes 9437188 | tf_op jit(solution)/shard_map/while/body/while
  354.5 2.9 collective-permute-start
  355.0 7.1 %collective-permute-start.1 = (f32[192,256]{1,0:T(8,128)S(1)}, f32[192,256]{1,0:T(8,128)S(1)}, u32[]{:S(2)}, u32[]{:S(2)}) collective-permute-start(f32[192,256]{1,0:T(8,128)S(1)} %get-tuple-element.519), channel_id=1, source_target_pairs={{1,2},{3,4},{5,6},{7,8},{9,10},{11,12},{13,14},{15,16},{17,18},{19... | collective-permute-start | bytes 589832 | tf_op jit(solution)/shard_map/while/body/while/body/eval_jaxpr/ppermute | solution.py:567
  378.1 2.0 collective-permute-start.2
  417.0 4.5 collective-permute-start.3
  436.0 6.6 copy-start.4
  436.0 6.6 copy-start.6
  436.0 6.6 copy-start.7
  447.4 10.3 %copy-start.13 = (f32[320,256]{1,0:T(8,128)}, f32[320,256]{1,0:T(8,128)S(1)}, u32[]{:S(2)}) copy-start(f32[320,256]{1,0:T(8,128)S(1)} %get-tuple-element.573.iband_ref) | copy-start | bytes 983044 | tf_op jit(solution)/shard_map/while/body/while
  447.4 10.3 %copy-start.15 = (f32[320,256]{1,0:T(8,128)}, f32[320,256]{1,0:T(8,128)S(1)}, u32[]{:S(2)}) copy-start(f32[320,256]{1,0:T(8,128)S(1)} %get-tuple-element.574.oband_ref) | copy-start | bytes 983044 | tf_op jit(solution)/shard_map/while/body/while
  449.8 7.9 %copy-start.5 = (f32[12,256,256]{2,1,0:T(8,128)S(1)}, f32[12,256,256]{2,1,0:T(8,128)}, u32[]{:S(2)}) copy-start(f32[12,256,256]{2,1,0:T(8,128)} %get-tuple-element.572.band_ref) | copy-start | bytes 9437188 | tf_op jit(solution)/shard_map/while/body/while
  450.1 2.9 collective-permute-start
  450.6 7.1 %collective-permute-start.1 = (f32[192,256]{1,0:T(8,128)S(1)}, f32[192,256]{1,0:T(8,128)S(1)}, u32[]{:S(2)}, u32[]{:S(2)}) collective-permute-start(f32[192,256]{1,0:T(8,128)S(1)} %get-tuple-element.519), channel_id=1, source_target_pairs={{1,2},{3,4},{5,6},{7,8},{9,10},{11,12},{13,14},{15,16},{17,18},{19... | collective-permute-start | bytes 589832 | tf_op jit(solution)/shard_map/while/body/while/body/eval_jaxpr/ppermute | solution.py:567
  473.7 2.0 collective-permute-start.2
  512.6 4.5 collective-permute-start.3
  531.6 6.6 copy-start.4
  531.6 6.6 copy-start.6
  531.6 6.6 copy-start.7
  543.0 10.3 %copy-start.13 = (f32[320,256]{1,0:T(8,128)}, f32[320,256]{1,0:T(8,128)S(1)}, u32[]{:S(2)}) copy-start(f32[320,256]{1,0:T(8,128)S(1)} %get-tuple-element.573.iband_ref) | copy-start | bytes 983044 | tf_op jit(solution)/shard_map/while/body/while
  543.0 10.3 %copy-start.15 = (f32[320,256]{1,0:T(8,128)}, f32[320,256]{1,0:T(8,128)S(1)}, u32[]{:S(2)}) copy-start(f32[320,256]{1,0:T(8,128)S(1)} %get-tuple-element.574.oband_ref) | copy-start | bytes 983044 | tf_op jit(solution)/shard_map/while/body/while
  545.5 7.9 %copy-start.5 = (f32[12,256,256]{2,1,0:T(8,128)S(1)}, f32[12,256,256]{2,1,0:T(8,128)}, u32[]{:S(2)}) copy-start(f32[12,256,256]{2,1,0:T(8,128)} %get-tuple-element.572.band_ref) | copy-start | bytes 9437188 | tf_op jit(solution)/shard_map/while/body/while
  545.8 2.9 collective-permute-start
  546.2 7.1 %collective-permute-start.1 = (f32[192,256]{1,0:T(8,128)S(1)}, f32[192,256]{1,0:T(8,128)S(1)}, u32[]{:S(2)}, u32[]{:S(2)}) collective-permute-start(f32[192,256]{1,0:T(8,128)S(1)} %get-tuple-element.519), channel_id=1, source_target_pairs={{1,2},{3,4},{5,6},{7,8},{9,10},{11,12},{13,14},{15,16},{17,18},{19... | collective-permute-start | bytes 589832 | tf_op jit(solution)/shard_map/while/body/while/body/eval_jaxpr/ppermute | solution.py:567
  569.3 2.0 collective-permute-start.2
  608.2 4.5 collective-permute-start.3
  627.2 6.6 copy-start.4
  627.2 6.6 copy-start.6
  627.2 6.6 copy-start.7
  644.3 21.8 %copy-start.22 = (s32[128]{0:T(128)S(1)}, s32[128]{0:T(128)}, u32[]{:S(2)}) copy-start(s32[128]{0:T(128)} %get-tuple-element.669) | copy-start | bytes 1540 | tf_op jit(solution)/shard_map/while
  644.3 23.3 %copy-start.10 = (f32[2048,256]{1,0:T(8,128)S(1)}, f32[2048,256]{1,0:T(8,128)}, u32[]{:S(2)}) copy-start(f32[2048,256]{1,0:T(8,128)} %get-tuple-element.641) | copy-start | bytes 6291460 | tf_op jit(solution)/shard_map/while
  (42 other events, 49.5 us)

commit v6 on v5

--- a/solution.py
+++ b/solution.py
@@ -195,14 +195,41 @@
 PACK = 320
 
 
-def powers_kernel(
-    valid_ref, own_ref, inner_ref, outer_ref, band_ref, iband_ref, oband_ref,
-    image_ref, mine_ref, theirs_ref,
-    bh_ref, bl_ref, lh_ref, ll_ref, rh_ref, rl_ref, vh_ref, vl_ref, y_ref, sem,
+def frame_put(high_ref, low_ref):
+    def put(at, value):
+        high_ref[at, :], low_ref[at, :] = halves(value)
+
+    return put
+
+
+def add_windows(y_ref, bh_ref, bl_ref, xh_ref, xl_ref):
+    def window(i, carry):
+        values = []
+        for m in range(3):
+            at = pl.multiple_of(HALO + (3 * i + m) * STEP, 64)
+            xh = xh_ref[pl.ds(at, WIN), :]
+            xl = xl_ref[pl.ds(at, WIN), :]
+            values.append((at, dot3(bh_ref[3 * i + m], bl_ref[3 * i + m], xh, xl)))
+        for at, value in values:
+            y_ref[pl.ds(at, WIN), :] += value
+        return carry
+
+    lax.fori_loop(0, bh_ref.shape[0] // 3, window, 0)
+
+
+def clear_rows(y_ref):
+    def clear(i, carry):
+        y_ref[pl.ds(pl.multiple_of(i * 64, 64), 64), :] = jnp.zeros((64, y_ref.shape[1]), F32)
+        return carry
+
+    lax.fori_loop(0, y_ref.shape[0] // 64, clear, 0)
+
+
+def first_kernel(
+    valid_ref, own_ref, inner_ref, outer_ref, band_ref,
+    bh_ref, bl_ref, xh_ref, xl_ref, y_ref,
 ):
     own, cols = own_ref.shape
-    windows = band_ref.shape[0]
-    frame = y_ref.shape[0]
     high = LOW + own
     chunk = 256
 
@@ -210,34 +237,51 @@
         bh_ref[g], bl_ref[g] = halves(band_ref[g])
         return carry
 
-    lax.fori_loop(0, windows, split_band, 0)
+    lax.fori_loop(0, band_ref.shape[0], split_band, 0)
+    put = frame_put(xh_ref, xl_ref)
+    for ref in (xh_ref, xl_ref):
+        ref[: LOW - EDGE] = jnp.zeros((LOW - EDGE, cols), BF16)
+        ref[high + EDGE :] = jnp.zeros((ref.shape[0] - high - EDGE, cols), BF16)
+
+    def sides(left_ref, right_ref):
+        put(pl.ds(LOW - EDGE, EDGE), left_ref[...])
+        put(pl.ds(high, EDGE), right_ref[...])
+
+    pl.when(valid_ref[2] == 0)(lambda: sides(outer_ref, inner_ref))
+    pl.when(valid_ref[2] != 0)(lambda: sides(inner_ref, outer_ref))
+
+    def split_own(i, carry):
+        at = pl.multiple_of(i * chunk, chunk)
+        put(pl.ds(LOW + at, chunk), own_ref[pl.ds(at, chunk), :])
+        return carry
+
+    lax.fori_loop(0, own // chunk, split_own, 0)
+    clear_rows(y_ref)
+    add_windows(y_ref, bh_ref, bl_ref, xh_ref, xl_ref)
+
+
+def powers_kernel(
+    valid_ref, bh_ref, bl_ref, xh_ref, xl_ref, begun_ref, iband_ref, oband_ref,
+    image_ref, mine_ref, theirs_ref,
+    lh_ref, ll_ref, rh_ref, rl_ref, vh_ref, vl_ref, y_ref, sem,
+):
+    frame, cols = y_ref.shape
+    own = image_ref.shape[1]
+    high = LOW + own
+    chunk = 256
+
     for ref in (vh_ref, vl_ref):
-        for n, width in enumerate((EDGE, HALO)):
-            ref[n, : LOW - width] = jnp.zeros((LOW - width, cols), BF16)
-            ref[n, high + width :] = jnp.zeros((frame - high - width, cols), BF16)
-
-    def put(n, at, value):
-        vh_ref[n, at, :], vl_ref[n, at, :] = halves(value)
-
-    def sides(left_ref, right_ref, lband_ref, rband_ref):
-        put(0, pl.ds(LOW - EDGE, EDGE), left_ref[...])
-        put(0, pl.ds(high, EDGE), right_ref[...])
+        for n in range(2):
+            ref[n, :HALO] = jnp.zeros((HALO, cols), BF16)
+            ref[n, high + HALO :] = jnp.zeros((frame - high - HALO, cols), BF16)
+    vh_ref[2], vl_ref[2] = xh_ref[...], xl_ref[...]
+
+    def sides(lband_ref, rband_ref):
         lh_ref[...], ll_ref[...] = halves(lband_ref[...])
         rh_ref[...], rl_ref[...] = halves(rband_ref[...])
 
-    pl.when(valid_ref[2] == 0)(lambda: sides(outer_ref, inner_ref, oband_ref, iband_ref))
-    pl.when(valid_ref[2] != 0)(lambda: sides(inner_ref, outer_ref, iband_ref, oband_ref))
-
-    def split_own(i, carry):
-        at = pl.multiple_of(i * chunk, chunk)
-        put(0, pl.ds(LOW + at, chunk), own_ref[pl.ds(at, chunk), :])
-        return carry
-
-    lax.fori_loop(0, own // chunk, split_own, 0)
-
-    def clear(i, carry):
-        y_ref[pl.ds(pl.multiple_of(i * 64, 64), 64), :] = jnp.zeros((64, cols), F32)
-        return carry
+    pl.when(valid_ref[2] == 0)(lambda: sides(oband_ref, iband_ref))
+    pl.when(valid_ref[2] != 0)(lambda: sides(iband_ref, oband_ref))
 
     tn = ((0,), (0,))
 
@@ -259,22 +303,19 @@
         ref[ITERS * PACK :] = jnp.zeros((ref.shape[0] - ITERS * PACK, 128), F32)
 
     def power(n, carry):
-        now = n % 2
-        then = 1 - now
-        lax.fori_loop(0, frame // 64, clear, 0)
-
-        def window(i, carry):
-            values = []
-            for m in range(3):
-                at = pl.multiple_of(HALO + (3 * i + m) * STEP, 64)
-                xh = vh_ref[now, pl.ds(at, WIN), :]
-                xl = vl_ref[now, pl.ds(at, WIN), :]
-                values.append((at, dot3(bh_ref[3 * i + m], bl_ref[3 * i + m], xh, xl)))
-            for at, value in values:
-                y_ref[pl.ds(at, WIN), :] += value
-            return carry
-
-        lax.fori_loop(0, windows // 3, window, 0)
+        now = (n + 2) % 3
+        then = n % 3
+        source = (vh_ref.at[now], vl_ref.at[now])
+        put = frame_put(vh_ref.at[then], vl_ref.at[then])
+
+        @pl.when(n == 0)
+        def _():
+            y_ref[...] = begun_ref[...]
+
+        @pl.when(n > 0)
+        def _():
+            clear_rows(y_ref)
+            add_windows(y_ref, bh_ref, bl_ref, *source)
 
         values = []
         for h_ref, l_ref, lo, rows, out, at in (
@@ -291,13 +332,12 @@
         for out, rows, value in values:
             y_ref[out : out + rows] += value
 
-        put(then, pl.ds(HALO, HALO), jnp.where(valid_ref[0] > 0, y_ref[HALO:LOW], 0.0))
-        put(then, pl.ds(high, HALO), jnp.where(valid_ref[1] > 0, y_ref[high : high + HALO], 0.0))
+        put(pl.ds(HALO, HALO), jnp.where(valid_ref[0] > 0, y_ref[HALO:LOW], 0.0))
+        put(pl.ds(high, HALO), jnp.where(valid_ref[1] > 0, y_ref[high : high + HALO], 0.0))
 
         def split(i, carry):
             at = pl.multiple_of(i * chunk, chunk)
-            value = y_ref[pl.ds(LOW + at, chunk), :]
-            put(then, pl.ds(LOW + at, chunk), value)
+            put(pl.ds(LOW + at, chunk), y_ref[pl.ds(LOW + at, chunk), :])
             return carry
 
         copy = pltpu.make_async_copy(
@@ -313,37 +353,41 @@
         cross = by_high[:, cols : 2 * cols]
         keep_moment(2 * n, by_high[:, :cols] + (cross + cross.T))
         keep_moment(2 * n + 1, by_high[:, 2 * cols : 3 * cols] + (by_high[:, 3 * cols :] + by_low))
-
         pl.when(n + 1 < ITERS)(copy.wait)
-
-        @pl.when(n == 0)
-        def _():
-            for ref in (vh_ref, vl_ref):
-                ref[0, : HALO] = jnp.zeros((HALO, cols), BF16)
-                ref[0, high + HALO :] = jnp.zeros((frame - high - HALO, cols), BF16)
-
         return carry
 
     lax.fori_loop(0, ITERS, power, 0)
 
 
-def powers(vector, inner, outer, valid, bands):
-    band, inner_band, outer_band = bands
+def begin(vector, inner, outer, valid, band):
     own, cols = vector.shape
     frame = own + 2 * LOW + 64
+    part = jax.ShapeDtypeStruct(band.shape, BF16)
+    wide = jax.ShapeDtypeStruct((frame, cols), BF16)
+    return pl.pallas_call(
+        first_kernel,
+        out_shape=(part, part, wide, wide, jax.ShapeDtypeStruct((frame, cols), F32)),
+        in_specs=[pl.BlockSpec(memory_space=pltpu.SMEM)] + in_vmem(4),
+        out_specs=tuple(in_vmem(5)),
+        compiler_params=pltpu.CompilerParams(vmem_limit_bytes=20 << 20),
+        name="begin",
+    )(valid, vector, inner, outer, band)
+
+
+def powers(own, begun, valid, edges):
+    frame, cols = begun[-1].shape
     half = jax.ShapeDtypeStruct((1024, 128), F32)
-    wide = pltpu.VMEM((2, frame, cols), BF16)
-    edge = pltpu.VMEM(inner_band.shape, BF16)
+    wide = pltpu.VMEM((3, frame, cols), BF16)
+    edge = pltpu.VMEM(edges[0].shape, BF16)
     return pl.pallas_call(
         powers_kernel,
         out_shape=(pltpu.HBM((ITERS - 1, own, cols), F32), half, half),
-        in_specs=[pl.BlockSpec(memory_space=pltpu.SMEM)] + in_vmem(6),
+        in_specs=[pl.BlockSpec(memory_space=pltpu.SMEM)] + in_vmem(7),
         out_specs=(pl.BlockSpec(memory_space=pltpu.HBM), *in_vmem(2)),
-        compiler_params=pltpu.CompilerParams(vmem_limit_bytes=32 << 20),
-        scratch_shapes=[pltpu.VMEM(band.shape, BF16)] * 2 + [edge] * 4 + [wide] * 2
-        + [pltpu.VMEM((frame, cols), F32), pltpu.SemaphoreType.DMA],
+        compiler_params=pltpu.CompilerParams(vmem_limit_bytes=28 << 20),
+        scratch_shapes=[edge] * 4 + [wide] * 2 + [pltpu.VMEM((frame, cols), F32), pltpu.SemaphoreType.DMA],
         name="powers",
-    )(valid, vector, inner, outer, band, inner_band, outer_band)
+    )(valid, *begun, *edges)
 
 
 def diagonals(matrix):
@@ -409,22 +453,25 @@
         power = split_dot(power, power)
     power, total = twice(power, total)
 
+    def left_out(power):
+        return jnp.max(jnp.sum(power * power, axis=0, keepdims=True))
+
     def going(state):
         k, worst, _, _ = state
-        return (k < 40) & (size * worst * worst > CLOSE)
+        return (k < 40) & (worst > CLOSE)
 
     def step(state):
         k, _, power, total = state
         power, total = twice(power, total)
-        return k + 1, jnp.max(jnp.abs(power)), power, total
+        return k + 1, left_out(power), power, total
 
     rounds, worst, power, total = lax.while_loop(
-        going, step, (2, jnp.max(jnp.abs(power)), power, total)
+        going, step, (2, left_out(power), power, total)
     )
     total = total + split_dot(power, total)
     if not direct:
         total = split_dot(total * along, target)
-    return total * down, size * worst * worst, rounds
+    return total * down, worst, rounds
 
 
 def ratio(left, whole):
@@ -595,7 +642,8 @@
         answer, residual, direction, gram = state
         on_direction = k % 2 == 0
         vector = jnp.where(on_direction, direction, residual)
-        image, mine, theirs = powers(vector, *halo_of(vector), valid, bands)
+        begun = begin(vector, *halo_of(vector), valid, bands[0])
+        image, mine, theirs = powers(vector.shape[0], begun, valid, bands[1:])
         low, high = total_of(mine, theirs)
         low = jnp.where(valid[2] == 0, low, high)
         square = gram_of(low, 0)
@@ -803,7 +851,8 @@
     band, inner_band, outer_band = assemble(core[None], tile_stiff, tile_nodes, node_shift)
     bands = (band, *swap_sides(inner_band, outer_band))
     weights = load_matrix(slot_nodes, slot_load, right_side.shape[0])
-    images, mine, theirs = powers(right_side, inner, outer, valid, bands)
+    begun = begin(right_side, inner, outer, valid, band)
+    images, mine, theirs = powers(right_side.shape[0], begun, valid, bands[1:])
     vectors = [in_chunks(right_side), in_chunks(images, 0), in_chunks(images, 1)]
     basis_rows = basis(vectors, weights)
     mine, theirs = total_of(mine, theirs)

time: 681 us -> 684 us (level)
    pallas_call x0 -> x6, Pallas kernels: none -> 24.5 us  [begin(): pl.pallas_call(first_kernel, out_shape=(part, part, wide, wide, jax.Shape...]
    pallas_call x6, Pallas kernels: 97.7 us -> 78.7 us  [powers(): pl.pallas_call(powers_kernel, out_shape=(pltpu.HBM((ITERS - 1, own, cols)...]
    while x156 -> x146, local copies, waits for them, and re-layouts: 28.1 us -> 22 us
  transfers between devices with their start and end apart: 27 -> 27, of which waited for: 18 -> 18; matrix products, arithmetic and copies ran while one was open for 0% -> 0% of each run, Pallas kernels for 3% -> 4%
where the time goes in v6:
time: 684 us; the launch traced here: 675 us
  blocking collectives  244 us (36%)
  Pallas kernels  220 us (32%)
  waiting for transfers between devices  56 us (8%)
  matrix products  48.7 us (7%)
  starting transfers between devices  45.6 us (7%)
  local copies, waits for them, and re-layouts  29.7 us (4%)
  other arithmetic  25.4 us (4%)
    all_to_all x6, blocking collectives, total_of(): arrived = lax.all_to_all(pair, CHIPS, 0, 0, tiled=True)  129 us
    all_to_all x6, blocking collectives, total_of(): gathered = lax.all_to_all(own, CHIPS, 0, 0, tiled=True)  94.8 us
    pallas_call x6, Pallas kernels, powers(): pl.pallas_call(powers_kernel, out_shape=(pltpu.HBM((ITERS - 1, own, cols)...  78.7 us
    pallas_call x5, Pallas kernels, solve(): pl.pallas_call(solve_kernel, out_shape=jax.ShapeDtypeStruct(target.shape,...  53.3 us
    dot_general x10, matrix products, times(): jnp.dot(a, b, preferred_element_type=F32, precision=lax.Precision.HIGHEST)  48.7 us
    ppermute x7, waiting for transfers between devices, swap_sides(): lax.ppermute(outer, AXES, across + [(b, a) for a, b in across])  27 us
    pallas_call x6, Pallas kernels, begin(): pl.pallas_call(first_kernel, out_shape=(part, part, wide, wide, jax.Shape...  24.5 us
    while x146, local copies, waits for them, and re-layouts  22 us
  transfers between devices with their start and end apart: 27, of which 18 were waited for; matrix products, arithmetic and copies ran while one was open for 0% of the time, Pallas kernels for 4%

profile of v6, /device:TPU:1, one launch (start us, length us, event | category | flops | bytes accessed | tf_op | source)
XLA Modules:
  0.0 674.7 jit_solution(8157468456491501616)
XLA Ops:
  4.8 11.7 %assemble.1 = (f32[12,256,256]{2,1,0:T(8,128)}, f32[320,256]{1,0:T(8,128)S(1)}, f32[320,256]{1,0:T(8,128)S(1)}) custom-call(s32[1]{0:T(128)} %bitcast.1.core_ref, s32[256]{0:T(256)S(1)} %get-tuple-element.429.group_ref, s32[256]{0:T(256)S(1)} %multiply_minimum_fusion.first_ref, f32[32,32,256]{2,1,0:T(8,128)S(1)} %bitcast.52, ...), custom_call_target="tpu_custom_call" | custom-call | tf_op jit(solution)/shard_map/assemble/pallas_call | solution.py:169
  17.8 3.6 collective-permute-start.7
  22.6 3.9 collective-permute-start.5
  26.6 3.2 collective-permute-done.5.outer_ref
  29.8 5.7 begin.9
  35.6 13.1 %powers.9 = (f32[2,2048,256]{2,1,0:T(8,128)}, f32[1024,128]{1,0:T(8,128)S(1)}, f32[1024,128]{1,0:T(8,128)S(1)}) custom-call(s32[3]{0:T(128)S(1)} %pad_add_fusion.valid_ref, bf16[12,256,256]{2,1,0:T(8,128)(2,1)S(1)} %get-tuple-element.326.bh_ref, bf16[12,256,256]{2,1,0:T(8,128)(2,1)S(1)} %get-tuple-element.327.bl_ref, ...), custom_call_target="tpu_custom_call" | custom-call | tf_op jit(solution)/shard_map/powers/pallas_call | solution.py:382
  50.7 26.3 %all_to_all.48 = f32[64,16,128]{2,1,0:T(8,128)} all-to-all(f32[64,16,128]{2,1,0:T(8,128)S(1)} %bitcast.55), channel_id=1, replica_groups=mesh['row'=4,'column'=4,'depth'=4,'core'=2] {'row','column','depth'}, dimensions={0} | all-to-all | bytes 1048576 | tf_op jit(solution)/shard_map/all_to_all | solution.py:602
  78.1 15.7 %all_to_all.49 = f32[64,16,128]{2,1,0:T(8,128)S(1)} all-to-all(f32[64,16,128]{2,1,0:T(8,128)S(1)} %broadcast_in_dim.52), channel_id=1, replica_groups=mesh['row'=4,'column'=4,'depth'=4,'core'=2] {'row','column','depth'}, dimensions={0} | all-to-all | bytes 1048576 | tf_op jit(solution)/shard_map/all_to_all | solution.py:604
  93.8 3.2 collective-permute-start.9
  97.0 5.5 loads.1
  102.6 10.5 %basis.3.basis_ref = f32[256,2304]{1,0:T(8,128)S(1)} custom-call(f32[2048,256]{1,0:T(8,128)S(1)} %copy-done.8, f32[2,2048,256]{2,1,0:T(8,128)} %get-tuple-element.335.refs_1_.refs_2_.k1_ref.k2_ref, f32[2,2048,256]{2,1,0:T(8,128)} %get-tuple-element.335.refs_1_.refs_2_.k1_ref.k2_ref, bf16[768,2048]{1,0:T(8,128)(2,1)S(1)} %get-tuple-element.620.refs_3_, ...), custom_call_target="tpu_custom_call" | custom-call | tf_op jit(solution)/shard_map/basis/pallas_call | solution.py:767
  113.1 20.7 %galerkin.1 = (f32[768,256]{1,0:T(8,128)}, f32[128,2,768]{2,1,0:T(2,128)}, s32[1]{0:T(128)}) custom-call(s32[1]{0:T(128)} %bitcast.1.core_ref, f32[1024,128]{1,0:T(8,128)S(1)} %bitcast.51, f32[1024,128]{1,0:T(8,128)S(1)} %collective-permute-done.9.theirs_ref, f32[256,2304]{1,0:T(8,128)S(1)} %basis.3.basis_ref), custom_call_target="tpu_custom_call" | custom-call | tf_op jit(solution)/shard_map/galerkin/pallas_call | solution.py:558
  133.8 3.6 all-to-all-start.5
  137.4 6.3 combine.1
  143.6 10.0 %all-to-all-done.5.received_ref = f32[128,2,768]{2,1,0:T(2,128)S(1)} async-done(((f32[128,2,768]{2,1,0:T(2,128)}), f32[128,2,768]{2,1,0:T(2,128)S(1)}, u32[]{:S(2)}, u32[]{:S(2)}) %all-to-all-start.5) | async-done | bytes 786464 | tf_op jit(solution)/shard_map/all_to_all | solution.py:787
  155.2 518.2 %while.31 = (s32[]{:T(128)}, f32[2048,256]{1,0:T(8,128)}, f32[3,128,256]{2,1,0:T(8,128)}, s32[]{:T(128)}, s32[3]{0:T(128)S(1)}, /*index=5*/f32[12,256,256]{2,1,0...) while((s32[]{:T(128)}, f32[2048,256]{1,0:T(8,128)}, ...), condition=%region_6.7_spmd, body=%region_2.6_spmd | while | flops 3232530432 | bytes 119594080 | solution.py:870
  158.7 484.2 %while.33 = (s32[]{:T(128)}, f32[2048,256]{1,0:T(8,128)}, f32[2048,256]{1,0:T(8,128)}, f32[2048,256]{1,0:T(8,128)}, f32[256,256]{1,0:T(8,128)S(1)}, /*index=5*/p...) while((s32[]{:T(128)}, f32[2048,256]{1,0:T(8,128)}, ...), condition=%wide.region_5.5_spmd.clone, body=%wide.region_3.4_spmd.clone.sunk | while | flops 3232530432 | bytes 99668760 | solution.py:663
  165.9 5.0 collective-permute-done.1.outer_ref
  171.0 3.7 begin.10
  174.7 13.1 %powers.10 = (f32[2,2048,256]{2,1,0:T(8,128)}, f32[1024,128]{1,0:T(8,128)S(1)}, f32[1024,128]{1,0:T(8,128)S(1)}) custom-call(s32[3]{0:T(128)S(1)} %get-tuple-element.601.valid_ref, bf16[12,256,256]{2,1,0:T(8,128)(2,1)S(1)} %get-tuple-element.545.bh_ref, bf16[12,256,256]{2,1,0:T(8,128)(2,1)S(1)} %get-tuple-element.546.bl_ref, ...), custom_call_target="tpu_custom_call" | custom-call | tf_op jit(solution)/shard_map/while/body/while/body/eval_jaxpr/powers/pallas_call | solution.py:382
  189.9 19.7 %all_to_all.50 = f32[64,16,128]{2,1,0:T(8,128)S(1)} all-to-all(f32[64,16,128]{2,1,0:T(8,128)S(1)} %bitcast.53), channel_id=1, replica_groups=mesh['row'=4,'column'=4,'depth'=4,'core'=2] {'row','column','depth'}, dimensions={0} | all-to-all | bytes 1048576 | tf_op jit(solution)/shard_map/while/body/while/body/eval_jaxpr/all_to_all | solution.py:602
  209.8 15.8 %all_to_all.51 = f32[64,16,128]{2,1,0:T(8,128)S(1)} all-to-all(f32[64,16,128]{2,1,0:T(8,128)S(1)} %broadcast_in_dim.60), channel_id=1, replica_groups=mesh['row'=4,'column'=4,'depth'=4,'core'=2] {'row','column','depth'}, dimensions={0} | all-to-all | bytes 1048576 | tf_op jit(solution)/shard_map/while/body/while/body/eval_jaxpr/all_to_all | solution.py:604
  225.8 3.0 collective-permute-start.3
  234.2 10.7 %solve.8 = f32[256,256]{1,0:T(8,128)} custom-call(f32[256,256]{1,0:T(8,128)} %fusion.36.matrix_ref, f32[256,256]{1,0:T(8,128)S(1)} %fusion.37.target_ref), custom_call_target="tpu_custom_call" | custom-call | tf_op jit(solution)/shard_map/while/body/while/body/eval_jaxpr/solve/pallas_call | solution.py:587
  244.9 6.0 add_select_fusion.3
  250.8 3.3 subtract_select_fusion.3
  260.7 4.7 collective-permute-done.1.outer_ref
  265.4 3.7 begin.10
  269.1 13.1 %powers.10 = (f32[2,2048,256]{2,1,0:T(8,128)}, f32[1024,128]{1,0:T(8,128)S(1)}, f32[1024,128]{1,0:T(8,128)S(1)}) custom-call(s32[3]{0:T(128)S(1)} %get-tuple-element.601.valid_ref, bf16[12,256,256]{2,1,0:T(8,128)(2,1)S(1)} %get-tuple-element.545.bh_ref, bf16[12,256,256]{2,1,0:T(8,128)(2,1)S(1)} %get-tuple-element.546.bl_ref, ...), custom_call_target="tpu_custom_call" | custom-call | tf_op jit(solution)/shard_map/while/body/while/body/eval_jaxpr/powers/pallas_call | solution.py:382
  284.3 20.7 %all_to_all.50 = f32[64,16,128]{2,1,0:T(8,128)S(1)} all-to-all(f32[64,16,128]{2,1,0:T(8,128)S(1)} %bitcast.53), channel_id=1, replica_groups=mesh['row'=4,'column'=4,'depth'=4,'core'=2] {'row','column','depth'}, dimensions={0} | all-to-all | bytes 1048576 | tf_op jit(solution)/shard_map/while/body/while/body/eval_jaxpr/all_to_all | solution.py:602
  305.2 15.8 %all_to_all.51 = f32[64,16,128]{2,1,0:T(8,128)S(1)} all-to-all(f32[64,16,128]{2,1,0:T(8,128)S(1)} %broadcast_in_dim.60), channel_id=1, replica_groups=mesh['row'=4,'column'=4,'depth'=4,'core'=2] {'row','column','depth'}, dimensions={0} | all-to-all | bytes 1048576 | tf_op jit(solution)/shard_map/while/body/while/body/eval_jaxpr/all_to_all | solution.py:604
  321.2 3.0 collective-permute-start.3
  329.6 10.7 %solve.8 = f32[256,256]{1,0:T(8,128)} custom-call(f32[256,256]{1,0:T(8,128)} %fusion.36.matrix_ref, f32[256,256]{1,0:T(8,128)S(1)} %fusion.37.target_ref), custom_call_target="tpu_custom_call" | custom-call | tf_op jit(solution)/shard_map/while/body/while/body/eval_jaxpr/solve/pallas_call | solution.py:587
  340.3 6.6 add_select_fusion.3
  346.9 3.3 subtract_select_fusion.3
  358.3 4.7 collective-permute-done.1.outer_ref
  363.0 3.7 begin.10
  366.8 13.1 %powers.10 = (f32[2,2048,256]{2,1,0:T(8,128)}, f32[1024,128]{1,0:T(8,128)S(1)}, f32[1024,128]{1,0:T(8,128)S(1)}) custom-call(s32[3]{0:T(128)S(1)} %get-tuple-element.601.valid_ref, bf16[12,256,256]{2,1,0:T(8,128)(2,1)S(1)} %get-tuple-element.545.bh_ref, bf16[12,256,256]{2,1,0:T(8,128)(2,1)S(1)} %get-tuple-element.546.bl_ref, ...), custom_call_target="tpu_custom_call" | custom-call | tf_op jit(solution)/shard_map/while/body/while/body/eval_jaxpr/powers/pallas_call | solution.py:382
  381.9 20.7 %all_to_all.50 = f32[64,16,128]{2,1,0:T(8,128)S(1)} all-to-all(f32[64,16,128]{2,1,0:T(8,128)S(1)} %bitcast.53), channel_id=1, replica_groups=mesh['row'=4,'column'=4,'depth'=4,'core'=2] {'row','column','depth'}, dimensions={0} | all-to-all | bytes 1048576 | tf_op jit(solution)/shard_map/while/body/while/body/eval_jaxpr/all_to_all | solution.py:602
  402.8 15.8 %all_to_all.51 = f32[64,16,128]{2,1,0:T(8,128)S(1)} all-to-all(f32[64,16,128]{2,1,0:T(8,128)S(1)} %broadcast_in_dim.60), channel_id=1, replica_groups=mesh['row'=4,'column'=4,'depth'=4,'core'=2] {'row','column','depth'}, dimensions={0} | all-to-all | bytes 1048576 | tf_op jit(solution)/shard_map/while/body/while/body/eval_jaxpr/all_to_all | solution.py:604
  418.8 3.0 collective-permute-start.3
  427.2 10.7 %solve.8 = f32[256,256]{1,0:T(8,128)} custom-call(f32[256,256]{1,0:T(8,128)} %fusion.36.matrix_ref, f32[256,256]{1,0:T(8,128)S(1)} %fusion.37.target_ref), custom_call_target="tpu_custom_call" | custom-call | tf_op jit(solution)/shard_map/while/body/while/body/eval_jaxpr/solve/pallas_call | solution.py:587
  437.9 6.6 add_select_fusion.3
  444.5 3.3 subtract_select_fusion.3
  454.3 4.7 collective-permute-done.1.outer_ref
  459.0 3.7 begin.10
  462.8 13.1 %powers.10 = (f32[2,2048,256]{2,1,0:T(8,128)}, f32[1024,128]{1,0:T(8,128)S(1)}, f32[1024,128]{1,0:T(8,128)S(1)}) custom-call(s32[3]{0:T(128)S(1)} %get-tuple-element.601.valid_ref, bf16[12,256,256]{2,1,0:T(8,128)(2,1)S(1)} %get-tuple-element.545.bh_ref, bf16[12,256,256]{2,1,0:T(8,128)(2,1)S(1)} %get-tuple-element.546.bl_ref, ...), custom_call_target="tpu_custom_call" | custom-call | tf_op jit(solution)/shard_map/while/body/while/body/eval_jaxpr/powers/pallas_call | solution.py:382
  477.9 20.7 %all_to_all.50 = f32[64,16,128]{2,1,0:T(8,128)S(1)} all-to-all(f32[64,16,128]{2,1,0:T(8,128)S(1)} %bitcast.53), channel_id=1, replica_groups=mesh['row'=4,'column'=4,'depth'=4,'core'=2] {'row','column','depth'}, dimensions={0} | all-to-all | bytes 1048576 | tf_op jit(solution)/shard_map/while/body/while/body/eval_jaxpr/all_to_all | solution.py:602
  498.8 15.8 %all_to_all.51 = f32[64,16,128]{2,1,0:T(8,128)S(1)} all-to-all(f32[64,16,128]{2,1,0:T(8,128)S(1)} %broadcast_in_dim.60), channel_id=1, replica_groups=mesh['row'=4,'column'=4,'depth'=4,'core'=2] {'row','column','depth'}, dimensions={0} | all-to-all | bytes 1048576 | tf_op jit(solution)/shard_map/while/body/while/body/eval_jaxpr/all_to_all | solution.py:604
  514.8 3.0 collective-permute-start.3
  523.2 10.7 %solve.8 = f32[256,256]{1,0:T(8,128)} custom-call(f32[256,256]{1,0:T(8,128)} %fusion.36.matrix_ref, f32[256,256]{1,0:T(8,128)S(1)} %fusion.37.target_ref), custom_call_target="tpu_custom_call" | custom-call | tf_op jit(solution)/shard_map/while/body/while/body/eval_jaxpr/solve/pallas_call | solution.py:587
  533.9 6.6 add_select_fusion.3
  540.5 3.3 subtract_select_fusion.3
  551.9 4.7 collective-permute-done.1.outer_ref
  556.6 3.7 begin.10
  560.4 13.1 %powers.10 = (f32[2,2048,256]{2,1,0:T(8,128)}, f32[1024,128]{1,0:T(8,128)S(1)}, f32[1024,128]{1,0:T(8,128)S(1)}) custom-call(s32[3]{0:T(128)S(1)} %get-tuple-element.601.valid_ref, bf16[12,256,256]{2,1,0:T(8,128)(2,1)S(1)} %get-tuple-element.545.bh_ref, bf16[12,256,256]{2,1,0:T(8,128)(2,1)S(1)} %get-tuple-element.546.bl_ref, ...), custom_call_target="tpu_custom_call" | custom-call | tf_op jit(solution)/shard_map/while/body/while/body/eval_jaxpr/powers/pallas_call | solution.py:382
  575.6 20.7 %all_to_all.50 = f32[64,16,128]{2,1,0:T(8,128)S(1)} all-to-all(f32[64,16,128]{2,1,0:T(8,128)S(1)} %bitcast.53), channel_id=1, replica_groups=mesh['row'=4,'column'=4,'depth'=4,'core'=2] {'row','column','depth'}, dimensions={0} | all-to-all | bytes 1048576 | tf_op jit(solution)/shard_map/while/body/while/body/eval_jaxpr/all_to_all | solution.py:602
  596.4 15.8 %all_to_all.51 = f32[64,16,128]{2,1,0:T(8,128)S(1)} all-to-all(f32[64,16,128]{2,1,0:T(8,128)S(1)} %broadcast_in_dim.60), channel_id=1, replica_groups=mesh['row'=4,'column'=4,'depth'=4,'core'=2] {'row','column','depth'}, dimensions={0} | all-to-all | bytes 1048576 | tf_op jit(solution)/shard_map/while/body/while/body/eval_jaxpr/all_to_all | solution.py:604
  612.4 3.0 collective-permute-start.3
  620.8 10.7 %solve.8 = f32[256,256]{1,0:T(8,128)} custom-call(f32[256,256]{1,0:T(8,128)} %fusion.36.matrix_ref, f32[256,256]{1,0:T(8,128)S(1)} %fusion.37.target_ref), custom_call_target="tpu_custom_call" | custom-call | tf_op jit(solution)/shard_map/while/body/while/body/eval_jaxpr/solve/pallas_call | solution.py:587
  631.5 6.6 add_select_fusion.3
  638.1 3.3 subtract_select_fusion.3
  642.9 5.7 basis.2
  650.0 20.4 %all_to_all.47.received_ref = f32[128,2,768]{2,1,0:T(2,128)S(1)} all-to-all(f32[128,2,768]{2,1,0:T(2,128)} %reshape.106), channel_id=1, replica_groups=mesh['row'=4,'column'=4,'depth'=4,'core'=2] {'row','column','depth','core'}, dimensions={0} | all-to-all | bytes 1572864 | tf_op jit(solution)/shard_map/while/body/all_to_all | solution.py:787
  (305 shorter events, 93.6 us)
Async XLA Ops:
  16.5 19.1 %collective-permute-start.6 = (f32[320,256]{1,0:T(8,128)S(1)}, f32[320,256]{1,0:T(8,128)S(1)}, u32[]{:S(2)}, u32[]{:S(2)}) collective-permute-start(f32[320,256]{1,0:T(8,128)S(1)} %get-tuple-element.331), channel_id=1, source_target_pairs={{0,1},{1,0},{2,3},{3,2},{4,5},{5,4},{6,7},{7,6},{8,9},{9,8},{10,11... | collective-permute-start | bytes 983048 | tf_op jit(solution)/shard_map/ppermute | solution.py:613
  17.8 17.7 %collective-permute-start.7 = (f32[320,256]{1,0:T(8,128)S(1)}, f32[320,256]{1,0:T(8,128)S(1)}, u32[]{:S(2)}, u32[]{:S(2)}) collective-permute-start(f32[320,256]{1,0:T(8,128)S(1)} %get-tuple-element.332), channel_id=1, source_target_pairs={{1,2},{3,4},{5,6},{7,8},{9,10},{11,12},{13,14},{15,16},{17,18},{19... | collective-permute-start | bytes 983048 | tf_op jit(solution)/shard_map/ppermute | solution.py:614
  22.5 4.1 collective-permute-start.4
  22.6 7.2 %collective-permute-start.5 = (f32[192,256]{1,0:T(8,128)S(1)}, f32[192,256]{1,0:T(8,128)S(1)}, u32[]{:S(2)}, u32[]{:S(2)}) collective-permute-start(f32[192,256]{1,0:T(8,128)S(1)} %get-tuple-element.444), channel_id=1, source_target_pairs={{1,2},{3,4},{5,6},{7,8},{9,10},{11,12},{13,14},{15,16},{17,18},{19... | collective-permute-start | bytes 589832 | tf_op jit(solution)/shard_map/ppermute | solution.py:614
  48.7 2.0 collective-permute-start.8
  50.7 46.3 %copy-start.1 = (f32[16,768]{1,0:T(8,128)S(1)}, f32[16,768]{1,0:T(8,128)}, u32[]{:S(2)}) copy-start(f32[16,768]{1,0:T(8,128)} %load_ref.1) | copy-start | bytes 147460
  50.7 46.3 %copy-start.2 = (s32[16,256]{1,0:T(8,128)S(1)}, s32[16,256]{1,0:T(8,128)}, u32[]{:S(2)}) copy-start(s32[16,256]{1,0:T(8,128)} %nodes_ref.1) | copy-start | bytes 49156
  50.7 51.9 %copy-start.8 = (f32[2048,256]{1,0:T(8,128)S(1)}, f32[2048,256]{1,0:T(8,128)}, u32[]{:S(2)}) copy-start(f32[2048,256]{1,0:T(8,128)} %k0_ref.1) | copy-start | bytes 6291460
  93.8 19.2 %collective-permute-start.9 = (f32[1024,128]{1,0:T(8,128)S(1)}, f32[1024,128]{1,0:T(8,128)S(1)}, u32[]{:S(2)}, u32[]{:S(2)}) collective-permute-start(f32[1024,128]{1,0:T(8,128)S(1)} %bitcast.50), channel_id=1, source_target_pairs={{0,1},{1,0},{2,3},{3,2},{4,5},{5,4},{6,7},{7,6},{8,9},{9,8},{10,11... | collective-permute-start | bytes 1572872 | tf_op jit(solution)/shard_map/ppermute | solution.py:606
  102.5 10.5 %copy-start.18 = (bf16[768,2048]{1,0:T(8,128)(2,1)}, bf16[768,2048]{1,0:T(8,128)(2,1)S(1)}, u32[]{:S(2)}) copy-start(bf16[768,2048]{1,0:T(8,128)(2,1)S(1)} %get-tuple-element.620.refs_3_) | copy-start | bytes 9437188
  102.5 10.5 %copy-start.19 = (bf16[768,2048]{1,0:T(8,128)(2,1)}, bf16[768,2048]{1,0:T(8,128)(2,1)S(1)}, u32[]{:S(2)}) copy-start(bf16[768,2048]{1,0:T(8,128)(2,1)S(1)} %get-tuple-element.621.refs_4_) | copy-start | bytes 9437188
  133.8 19.8 %all-to-all-start.5 = ((f32[128,2,768]{2,1,0:T(2,128)}), f32[128,2,768]{2,1,0:T(2,128)S(1)}, u32[]{:S(2)}, u32[]{:S(2)}) async-start(f32[128,2,768]{2,1,0:T(2,128)} %get-tuple-element.340), calls=%async_computation.5 | async-start | bytes 1572864 | tf_op jit(solution)/shard_map/all_to_all | solution.py:787
  137.4 16.3 %copy-start.20 = (s32[128]{0:T(128)S(1)}, s32[128]{0:T(128)}, u32[]{:S(2)}) copy-start(s32[128]{0:T(128)} %param.17) | copy-start | bytes 1540
  158.7 16.0 %copy-start.12 = (f32[320,256]{1,0:T(8,128)}, f32[320,256]{1,0:T(8,128)S(1)}, u32[]{:S(2)}) copy-start(f32[320,256]{1,0:T(8,128)S(1)} %get-tuple-element.603.iband_ref) | copy-start | bytes 983044 | tf_op jit(solution)/shard_map/while/body/while
  158.7 16.0 %copy-start.14 = (f32[320,256]{1,0:T(8,128)}, f32[320,256]{1,0:T(8,128)S(1)}, u32[]{:S(2)}) copy-start(f32[320,256]{1,0:T(8,128)S(1)} %get-tuple-element.604.oband_ref) | copy-start | bytes 983044 | tf_op jit(solution)/shard_map/while/body/while
  160.5 10.4 %copy-start.4 = (f32[12,256,256]{2,1,0:T(8,128)S(1)}, f32[12,256,256]{2,1,0:T(8,128)}, u32[]{:S(2)}) copy-start(f32[12,256,256]{2,1,0:T(8,128)} %get-tuple-element.602.band_ref) | copy-start | bytes 9437188 | tf_op jit(solution)/shard_map/while/body/while
  162.6 3.3 collective-permute-start
  164.0 7.0 %collective-permute-start.1 = (f32[192,256]{1,0:T(8,128)S(1)}, f32[192,256]{1,0:T(8,128)S(1)}, u32[]{:S(2)}, u32[]{:S(2)}) collective-permute-start(f32[192,256]{1,0:T(8,128)S(1)} %get-tuple-element.544), channel_id=1, source_target_pairs={{1,2},{3,4},{5,6},{7,8},{9,10},{11,12},{13,14},{15,16},{17,18},{19... | collective-permute-start | bytes 589832 | tf_op jit(solution)/shard_map/while/body/while/body/eval_jaxpr/ppermute | solution.py:614
  187.9 2.0 collective-permute-start.2
  225.8 4.5 collective-permute-start.3
  244.9 6.0 copy-start.5
  244.9 6.0 copy-start.6
  255.6 13.5 %copy-start.12 = (f32[320,256]{1,0:T(8,128)}, f32[320,256]{1,0:T(8,128)S(1)}, u32[]{:S(2)}) copy-start(f32[320,256]{1,0:T(8,128)S(1)} %get-tuple-element.603.iband_ref) | copy-start | bytes 983044 | tf_op jit(solution)/shard_map/while/body/while
  255.6 13.5 %copy-start.14 = (f32[320,256]{1,0:T(8,128)}, f32[320,256]{1,0:T(8,128)S(1)}, u32[]{:S(2)}) copy-start(f32[320,256]{1,0:T(8,128)S(1)} %get-tuple-element.604.oband_ref) | copy-start | bytes 983044 | tf_op jit(solution)/shard_map/while/body/while
  257.5 7.9 %copy-start.4 = (f32[12,256,256]{2,1,0:T(8,128)S(1)}, f32[12,256,256]{2,1,0:T(8,128)}, u32[]{:S(2)}) copy-start(f32[12,256,256]{2,1,0:T(8,128)} %get-tuple-element.602.band_ref) | copy-start | bytes 9437188 | tf_op jit(solution)/shard_map/while/body/while
  257.8 2.9 collective-permute-start
  258.3 7.1 %collective-permute-start.1 = (f32[192,256]{1,0:T(8,128)S(1)}, f32[192,256]{1,0:T(8,128)S(1)}, u32[]{:S(2)}, u32[]{:S(2)}) collective-permute-start(f32[192,256]{1,0:T(8,128)S(1)} %get-tuple-element.544), channel_id=1, source_target_pairs={{1,2},{3,4},{5,6},{7,8},{9,10},{11,12},{13,14},{15,16},{17,18},{19... | collective-permute-start | bytes 589832 | tf_op jit(solution)/shard_map/while/body/while/body/eval_jaxpr/ppermute | solution.py:614
  282.3 2.0 collective-permute-start.2
  321.2 4.5 collective-permute-start.3
  340.3 6.6 copy-start.3
  340.3 6.6 copy-start.5
  340.3 6.6 copy-start.6
  351.7 15.1 %copy-start.12 = (f32[320,256]{1,0:T(8,128)}, f32[320,256]{1,0:T(8,128)S(1)}, u32[]{:S(2)}) copy-start(f32[320,256]{1,0:T(8,128)S(1)} %get-tuple-element.603.iband_ref) | copy-start | bytes 983044 | tf_op jit(solution)/shard_map/while/body/while
  351.7 15.1 %copy-start.14 = (f32[320,256]{1,0:T(8,128)}, f32[320,256]{1,0:T(8,128)S(1)}, u32[]{:S(2)}) copy-start(f32[320,256]{1,0:T(8,128)S(1)} %get-tuple-element.604.oband_ref) | copy-start | bytes 983044 | tf_op jit(solution)/shard_map/while/body/while
  353.5 9.5 %copy-start.4 = (f32[12,256,256]{2,1,0:T(8,128)S(1)}, f32[12,256,256]{2,1,0:T(8,128)}, u32[]{:S(2)}) copy-start(f32[12,256,256]{2,1,0:T(8,128)} %get-tuple-element.602.band_ref) | copy-start | bytes 9437188 | tf_op jit(solution)/shard_map/while/body/while
  355.6 2.7 collective-permute-start
  356.0 7.0 %collective-permute-start.1 = (f32[192,256]{1,0:T(8,128)S(1)}, f32[192,256]{1,0:T(8,128)S(1)}, u32[]{:S(2)}, u32[]{:S(2)}) collective-permute-start(f32[192,256]{1,0:T(8,128)S(1)} %get-tuple-element.544), channel_id=1, source_target_pairs={{1,2},{3,4},{5,6},{7,8},{9,10},{11,12},{13,14},{15,16},{17,18},{19... | collective-permute-start | bytes 589832 | tf_op jit(solution)/shard_map/while/body/while/body/eval_jaxpr/ppermute | solution.py:614
  379.9 2.0 collective-permute-start.2
  418.8 4.5 collective-permute-start.3
  437.9 6.6 copy-start.3
  437.9 6.6 copy-start.5
  437.9 6.6 copy-start.6
  449.3 13.5 %copy-start.12 = (f32[320,256]{1,0:T(8,128)}, f32[320,256]{1,0:T(8,128)S(1)}, u32[]{:S(2)}) copy-start(f32[320,256]{1,0:T(8,128)S(1)} %get-tuple-element.603.iband_ref) | copy-start | bytes 983044 | tf_op jit(solution)/shard_map/while/body/while
  449.3 13.5 %copy-start.14 = (f32[320,256]{1,0:T(8,128)}, f32[320,256]{1,0:T(8,128)S(1)}, u32[]{:S(2)}) copy-start(f32[320,256]{1,0:T(8,128)S(1)} %get-tuple-element.604.oband_ref) | copy-start | bytes 983044 | tf_op jit(solution)/shard_map/while/body/while
  451.1 7.9 %copy-start.4 = (f32[12,256,256]{2,1,0:T(8,128)S(1)}, f32[12,256,256]{2,1,0:T(8,128)}, u32[]{:S(2)}) copy-start(f32[12,256,256]{2,1,0:T(8,128)} %get-tuple-element.602.band_ref) | copy-start | bytes 9437188 | tf_op jit(solution)/shard_map/while/body/while
  451.4 2.9 collective-permute-start
  451.9 7.1 %collective-permute-start.1 = (f32[192,256]{1,0:T(8,128)S(1)}, f32[192,256]{1,0:T(8,128)S(1)}, u32[]{:S(2)}, u32[]{:S(2)}) collective-permute-start(f32[192,256]{1,0:T(8,128)S(1)} %get-tuple-element.544), channel_id=1, source_target_pairs={{1,2},{3,4},{5,6},{7,8},{9,10},{11,12},{13,14},{15,16},{17,18},{19... | collective-permute-start | bytes 589832 | tf_op jit(solution)/shard_map/while/body/while/body/eval_jaxpr/ppermute | solution.py:614
  475.9 2.0 collective-permute-start.2
  514.8 4.5 collective-permute-start.3
  533.9 6.6 copy-start.3
  533.9 6.6 copy-start.5
  533.9 6.6 copy-start.6
  545.3 15.1 %copy-start.12 = (f32[320,256]{1,0:T(8,128)}, f32[320,256]{1,0:T(8,128)S(1)}, u32[]{:S(2)}) copy-start(f32[320,256]{1,0:T(8,128)S(1)} %get-tuple-element.603.iband_ref) | copy-start | bytes 983044 | tf_op jit(solution)/shard_map/while/body/while
  545.3 15.1 %copy-start.14 = (f32[320,256]{1,0:T(8,128)}, f32[320,256]{1,0:T(8,128)S(1)}, u32[]{:S(2)}) copy-start(f32[320,256]{1,0:T(8,128)S(1)} %get-tuple-element.604.oband_ref) | copy-start | bytes 983044 | tf_op jit(solution)/shard_map/while/body/while
  547.1 9.5 %copy-start.4 = (f32[12,256,256]{2,1,0:T(8,128)S(1)}, f32[12,256,256]{2,1,0:T(8,128)}, u32[]{:S(2)}) copy-start(f32[12,256,256]{2,1,0:T(8,128)} %get-tuple-element.602.band_ref) | copy-start | bytes 9437188 | tf_op jit(solution)/shard_map/while/body/while
  549.2 2.7 collective-permute-start
  549.6 7.0 %collective-permute-start.1 = (f32[192,256]{1,0:T(8,128)S(1)}, f32[192,256]{1,0:T(8,128)S(1)}, u32[]{:S(2)}, u32[]{:S(2)}) collective-permute-start(f32[192,256]{1,0:T(8,128)S(1)} %get-tuple-element.544), channel_id=1, source_target_pairs={{1,2},{3,4},{5,6},{7,8},{9,10},{11,12},{13,14},{15,16},{17,18},{19... | collective-permute-start | bytes 589832 | tf_op jit(solution)/shard_map/while/body/while/body/eval_jaxpr/ppermute | solution.py:614
  573.5 2.0 collective-permute-start.2
  612.4 4.5 collective-permute-start.3
  631.5 6.6 copy-start.3
  631.5 6.6 copy-start.5
  631.5 6.6 copy-start.6
  648.6 21.8 %copy-start.21 = (s32[128]{0:T(128)S(1)}, s32[128]{0:T(128)}, u32[]{:S(2)}) copy-start(s32[128]{0:T(128)} %get-tuple-element.699) | copy-start | bytes 1540 | tf_op jit(solution)/shard_map/while
  648.6 23.3 %copy-start.9 = (f32[2048,256]{1,0:T(8,128)S(1)}, f32[2048,256]{1,0:T(8,128)}, u32[]{:S(2)}) copy-start(f32[2048,256]{1,0:T(8,128)} %get-tuple-element.671) | copy-start | bytes 6291460 | tf_op jit(solution)/shard_map/while
  (37 other events, 37.1 us)

commit v7 on v6

--- a/solution.py
+++ b/solution.py
@@ -227,9 +227,10 @@
 
 def first_kernel(
     valid_ref, own_ref, inner_ref, outer_ref, band_ref,
-    bh_ref, bl_ref, xh_ref, xl_ref, y_ref,
+    bh_ref, bl_ref, vh_ref, vl_ref, y_ref,
 ):
     own, cols = own_ref.shape
+    xh_ref, xl_ref = vh_ref.at[2], vl_ref.at[2]
     high = LOW + own
     chunk = 256
 
@@ -261,9 +262,9 @@
 
 
 def powers_kernel(
-    valid_ref, bh_ref, bl_ref, xh_ref, xl_ref, begun_ref, iband_ref, oband_ref,
-    image_ref, mine_ref, theirs_ref,
-    lh_ref, ll_ref, rh_ref, rl_ref, vh_ref, vl_ref, y_ref, sem,
+    valid_ref, bh_ref, bl_ref, _high_ref, _low_ref, _begun_ref, iband_ref, oband_ref,
+    image_ref, mine_ref, theirs_ref, vh_ref, vl_ref, y_ref,
+    lh_ref, ll_ref, rh_ref, rl_ref, sem,
 ):
     frame, cols = y_ref.shape
     own = image_ref.shape[1]
@@ -274,7 +275,6 @@
         for n in range(2):
             ref[n, :HALO] = jnp.zeros((HALO, cols), BF16)
             ref[n, high + HALO :] = jnp.zeros((frame - high - HALO, cols), BF16)
-    vh_ref[2], vl_ref[2] = xh_ref[...], xl_ref[...]
 
     def sides(lband_ref, rband_ref):
         lh_ref[...], ll_ref[...] = halves(lband_ref[...])
@@ -307,10 +307,6 @@
         then = n % 3
         source = (vh_ref.at[now], vl_ref.at[now])
         put = frame_put(vh_ref.at[then], vl_ref.at[then])
-
-        @pl.when(n == 0)
-        def _():
-            y_ref[...] = begun_ref[...]
 
         @pl.when(n > 0)
         def _():
@@ -363,7 +359,7 @@
     own, cols = vector.shape
     frame = own + 2 * LOW + 64
     part = jax.ShapeDtypeStruct(band.shape, BF16)
-    wide = jax.ShapeDtypeStruct((frame, cols), BF16)
+    wide = jax.ShapeDtypeStruct((3, frame, cols), BF16)
     return pl.pallas_call(
         first_kernel,
         out_shape=(part, part, wide, wide, jax.ShapeDtypeStruct((frame, cols), F32)),
@@ -375,19 +371,24 @@
 
 
 def powers(own, begun, valid, edges):
-    frame, cols = begun[-1].shape
+    _, cols = begun[-1].shape
     half = jax.ShapeDtypeStruct((1024, 128), F32)
-    wide = pltpu.VMEM((3, frame, cols), BF16)
     edge = pltpu.VMEM(edges[0].shape, BF16)
     return pl.pallas_call(
         powers_kernel,
-        out_shape=(pltpu.HBM((ITERS - 1, own, cols), F32), half, half),
+        out_shape=(
+            pltpu.HBM((ITERS - 1, own, cols), F32),
+            half,
+            half,
+            *[jax.ShapeDtypeStruct(part.shape, part.dtype) for part in begun[2:]],
+        ),
         in_specs=[pl.BlockSpec(memory_space=pltpu.SMEM)] + in_vmem(7),
-        out_specs=(pl.BlockSpec(memory_space=pltpu.HBM), *in_vmem(2)),
+        out_specs=(pl.BlockSpec(memory_space=pltpu.HBM), *in_vmem(5)),
+        input_output_aliases={3: 3, 4: 4, 5: 5},
         compiler_params=pltpu.CompilerParams(vmem_limit_bytes=28 << 20),
-        scratch_shapes=[edge] * 4 + [wide] * 2 + [pltpu.VMEM((frame, cols), F32), pltpu.SemaphoreType.DMA],
+        scratch_shapes=[edge] * 4 + [pltpu.SemaphoreType.DMA],
         name="powers",
-    )(valid, *begun, *edges)
+    )(valid, *begun, *edges)[:3]
 
 
 def diagonals(matrix):
@@ -570,7 +571,8 @@
             pltpu.VMEM((3, peers, slots // peers, size), F32),
             pltpu.SemaphoreType.DMA((4,)),
         ],
-        compiler_params=pltpu.CompilerParams(vmem_limit_bytes=32 << 20),
+        compiler_params=pltpu.CompilerParams(
+            vmem_limit_bytes=32 << 20),
         name="galerkin",
     )(core, mine, theirs, basis_rows)
 

time: 684 us -> 683 us (level)
  no operation moved by 1% of the time
where the time goes in v7:
time: 683 us; the launch traced here: 673 us
  blocking collectives  244 us (36%)
  Pallas kernels  218 us (32%)
  waiting for transfers between devices  56.1 us (8%)
  matrix products  48.7 us (7%)
  starting transfers between devices  45.4 us (7%)
  local copies, waits for them, and re-layouts  29.7 us (4%)
  other arithmetic  25.4 us (4%)
    all_to_all x6, blocking collectives, total_of(): arrived = lax.all_to_all(pair, CHIPS, 0, 0, tiled=True)  129 us
    all_to_all x6, blocking collectives, total_of(): gathered = lax.all_to_all(own, CHIPS, 0, 0, tiled=True)  94.8 us
    pallas_call x6, Pallas kernels, powers(): pl.pallas_call(powers_kernel, out_shape=(pltpu.HBM((ITERS - 1, own, cols)...  76.5 us
    pallas_call x5, Pallas kernels, solve(): pl.pallas_call(solve_kernel, out_shape=jax.ShapeDtypeStruct(target.shape,...  53.3 us
    dot_general x10, matrix products, times(): jnp.dot(a, b, preferred_element_type=F32, precision=lax.Precision.HIGHEST)  48.7 us
    ppermute x7, waiting for transfers between devices, swap_sides(): lax.ppermute(outer, AXES, across + [(b, a) for a, b in across])  27 us
    pallas_call x6, Pallas kernels, begin(): pl.pallas_call(first_kernel, out_shape=(part, part, wide, wide, jax.Shape...  24.5 us
    while x146, local copies, waits for them, and re-layouts  22 us
  transfers between devices with their start and end apart: 27, of which 18 were waited for; matrix products, arithmetic and copies ran while one was open for 0% of the time, Pallas kernels for 4%

profile of v7, /device:TPU:1, one launch (start us, length us, event | category | flops | bytes accessed | tf_op | source)
XLA Modules:
  0.0 672.5 jit_solution(1495557332178364984)
XLA Ops:
  4.8 11.7 %assemble.1 = (f32[12,256,256]{2,1,0:T(8,128)}, f32[320,256]{1,0:T(8,128)S(1)}, f32[320,256]{1,0:T(8,128)S(1)}) custom-call(s32[1]{0:T(128)} %bitcast.1.core_ref, s32[256]{0:T(256)S(1)} %get-tuple-element.429.group_ref, s32[256]{0:T(256)S(1)} %multiply_minimum_fusion.first_ref, f32[32,32,256]{2,1,0:T(8,128)S(1)} %bitcast.52, ...), custom_call_target="tpu_custom_call" | custom-call | tf_op jit(solution)/shard_map/assemble/pallas_call | solution.py:169
  17.8 3.6 collective-permute-start.7
  22.6 3.9 collective-permute-start.5
  26.6 3.2 collective-permute-done.5.outer_ref
  29.8 5.7 begin.9
  35.6 12.8 %powers.9 = (f32[2,2048,256]{2,1,0:T(8,128)}, f32[1024,128]{1,0:T(8,128)S(1)}, f32[1024,128]{1,0:T(8,128)S(1)}, bf16[3,2624,256]{2,1,0:T(8,128)(2,1)S(1)}, bf16[...) custom-call(s32[3]{0:T(128)S(1)} %pad_add_fusion.valid_ref, ...), custom_call_target="tpu_custom_call", output_to_operand_aliasing={{3}: (3, {}), {4}: (4, {}), {5}: (5, {})} | custom-call | tf_op jit(solution)/shard_map/powers/pallas_call | solution.py:377
  50.4 26.3 %all_to_all.48 = f32[64,16,128]{2,1,0:T(8,128)} all-to-all(f32[64,16,128]{2,1,0:T(8,128)S(1)} %bitcast.55), channel_id=1, replica_groups=mesh['row'=4,'column'=4,'depth'=4,'core'=2] {'row','column','depth'}, dimensions={0} | all-to-all | bytes 1048576 | tf_op jit(solution)/shard_map/all_to_all | solution.py:604
  77.8 15.7 %all_to_all.49 = f32[64,16,128]{2,1,0:T(8,128)S(1)} all-to-all(f32[64,16,128]{2,1,0:T(8,128)S(1)} %broadcast_in_dim.52), channel_id=1, replica_groups=mesh['row'=4,'column'=4,'depth'=4,'core'=2] {'row','column','depth'}, dimensions={0} | all-to-all | bytes 1048576 | tf_op jit(solution)/shard_map/all_to_all | solution.py:606
  93.5 3.0 collective-permute-start.9
  96.5 5.4 loads.1
  102.0 10.5 %basis.3.basis_ref = f32[256,2304]{1,0:T(8,128)S(1)} custom-call(f32[2048,256]{1,0:T(8,128)S(1)} %copy-done.8, f32[2,2048,256]{2,1,0:T(8,128)} %get-tuple-element.335.refs_1_.refs_2_.k1_ref.k2_ref, f32[2,2048,256]{2,1,0:T(8,128)} %get-tuple-element.335.refs_1_.refs_2_.k1_ref.k2_ref, bf16[768,2048]{1,0:T(8,128)(2,1)S(1)} %get-tuple-element.620.refs_3_, ...), custom_call_target="tpu_custom_call" | custom-call | tf_op jit(solution)/shard_map/basis/pallas_call | solution.py:769
  112.5 20.9 %galerkin.1 = (f32[768,256]{1,0:T(8,128)}, f32[128,2,768]{2,1,0:T(2,128)}, s32[1]{0:T(128)}) custom-call(s32[1]{0:T(128)} %bitcast.1.core_ref, f32[1024,128]{1,0:T(8,128)S(1)} %bitcast.51, f32[1024,128]{1,0:T(8,128)S(1)} %collective-permute-done.9.theirs_ref, f32[256,2304]{1,0:T(8,128)S(1)} %basis.3.basis_ref), custom_call_target="tpu_custom_call" | custom-call | tf_op jit(solution)/shard_map/galerkin/pallas_call | solution.py:559
  133.4 3.6 all-to-all-start.5
  137.0 6.3 combine.1
  143.3 10.0 %all-to-all-done.5.received_ref = f32[128,2,768]{2,1,0:T(2,128)S(1)} async-done(((f32[128,2,768]{2,1,0:T(2,128)}), f32[128,2,768]{2,1,0:T(2,128)S(1)}, u32[]{:S(2)}, u32[]{:S(2)}) %all-to-all-start.5) | async-done | bytes 786464 | tf_op jit(solution)/shard_map/all_to_all | solution.py:789
  154.8 516.4 %while.31 = (s32[]{:T(128)}, f32[2048,256]{1,0:T(8,128)}, f32[3,128,256]{2,1,0:T(8,128)}, s32[]{:T(128)}, s32[3]{0:T(128)S(1)}, /*index=5*/f32[12,256,256]{2,1,0...) while((s32[]{:T(128)}, f32[2048,256]{1,0:T(8,128)}, ...), condition=%region_6.7_spmd, body=%region_2.6_spmd | while | flops 3232530432 | bytes 119594080 | solution.py:872
  158.4 482.4 %while.33 = (s32[]{:T(128)}, f32[2048,256]{1,0:T(8,128)}, f32[2048,256]{1,0:T(8,128)}, f32[2048,256]{1,0:T(8,128)}, f32[256,256]{1,0:T(8,128)S(1)}, /*index=5*/p...) while((s32[]{:T(128)}, f32[2048,256]{1,0:T(8,128)}, ...), condition=%wide.region_5.5_spmd.clone, body=%wide.region_3.4_spmd.clone.sunk | while | flops 3232530432 | bytes 99668760 | solution.py:665
  165.6 5.0 collective-permute-done.1.outer_ref
  170.6 3.7 begin.10
  174.4 12.8 %powers.10 = (f32[2,2048,256]{2,1,0:T(8,128)}, f32[1024,128]{1,0:T(8,128)S(1)}, f32[1024,128]{1,0:T(8,128)S(1)}, bf16[3,2624,256]{2,1,0:T(8,128)(2,1)S(1)}, bf16...) custom-call(s32[3]{0:T(128)S(1)} %get-tuple-element.601.valid_ref, ...), custom_call_target="tpu_custom_call", output_to_operand_aliasing={{3}: (3, {}), {4}: (4, {}), {5}: (5, {})} | custom-call | tf_op jit(solution)/shard_map/while/body/while/body/eval_jaxpr/powers/pallas_call | solution.py:377
  189.2 19.7 %all_to_all.50 = f32[64,16,128]{2,1,0:T(8,128)S(1)} all-to-all(f32[64,16,128]{2,1,0:T(8,128)S(1)} %bitcast.53), channel_id=1, replica_groups=mesh['row'=4,'column'=4,'depth'=4,'core'=2] {'row','column','depth'}, dimensions={0} | all-to-all | bytes 1048576 | tf_op jit(solution)/shard_map/while/body/while/body/eval_jaxpr/all_to_all | solution.py:604
  209.1 15.8 %all_to_all.51 = f32[64,16,128]{2,1,0:T(8,128)S(1)} all-to-all(f32[64,16,128]{2,1,0:T(8,128)S(1)} %broadcast_in_dim.60), channel_id=1, replica_groups=mesh['row'=4,'column'=4,'depth'=4,'core'=2] {'row','column','depth'}, dimensions={0} | all-to-all | bytes 1048576 | tf_op jit(solution)/shard_map/while/body/while/body/eval_jaxpr/all_to_all | solution.py:606
  225.1 3.0 collective-permute-start.3
  233.5 10.7 %solve.8 = f32[256,256]{1,0:T(8,128)} custom-call(f32[256,256]{1,0:T(8,128)} %fusion.36.matrix_ref, f32[256,256]{1,0:T(8,128)S(1)} %fusion.37.target_ref), custom_call_target="tpu_custom_call" | custom-call | tf_op jit(solution)/shard_map/while/body/while/body/eval_jaxpr/solve/pallas_call | solution.py:589
  244.2 6.0 add_select_fusion.3
  250.2 3.3 subtract_select_fusion.3
  260.0 4.7 collective-permute-done.1.outer_ref
  264.7 3.7 begin.10
  268.5 12.7 %powers.10 = (f32[2,2048,256]{2,1,0:T(8,128)}, f32[1024,128]{1,0:T(8,128)S(1)}, f32[1024,128]{1,0:T(8,128)S(1)}, bf16[3,2624,256]{2,1,0:T(8,128)(2,1)S(1)}, bf16...) custom-call(s32[3]{0:T(128)S(1)} %get-tuple-element.601.valid_ref, ...), custom_call_target="tpu_custom_call", output_to_operand_aliasing={{3}: (3, {}), {4}: (4, {}), {5}: (5, {})} | custom-call | tf_op jit(solution)/shard_map/while/body/while/body/eval_jaxpr/powers/pallas_call | solution.py:377
  283.3 20.7 %all_to_all.50 = f32[64,16,128]{2,1,0:T(8,128)S(1)} all-to-all(f32[64,16,128]{2,1,0:T(8,128)S(1)} %bitcast.53), channel_id=1, replica_groups=mesh['row'=4,'column'=4,'depth'=4,'core'=2] {'row','column','depth'}, dimensions={0} | all-to-all | bytes 1048576 | tf_op jit(solution)/shard_map/while/body/while/body/eval_jaxpr/all_to_all | solution.py:604
  304.1 15.8 %all_to_all.51 = f32[64,16,128]{2,1,0:T(8,128)S(1)} all-to-all(f32[64,16,128]{2,1,0:T(8,128)S(1)} %broadcast_in_dim.60), channel_id=1, replica_groups=mesh['row'=4,'column'=4,'depth'=4,'core'=2] {'row','column','depth'}, dimensions={0} | all-to-all | bytes 1048576 | tf_op jit(solution)/shard_map/while/body/while/body/eval_jaxpr/all_to_all | solution.py:606
  320.1 3.0 collective-permute-start.3
  328.5 10.7 %solve.8 = f32[256,256]{1,0:T(8,128)} custom-call(f32[256,256]{1,0:T(8,128)} %fusion.36.matrix_ref, f32[256,256]{1,0:T(8,128)S(1)} %fusion.37.target_ref), custom_call_target="tpu_custom_call" | custom-call | tf_op jit(solution)/shard_map/while/body/while/body/eval_jaxpr/solve/pallas_call | solution.py:589
  339.2 6.6 add_select_fusion.3
  345.8 3.3 subtract_select_fusion.3
  357.2 4.7 collective-permute-done.1.outer_ref
  361.9 3.7 begin.10
  365.7 12.7 %powers.10 = (f32[2,2048,256]{2,1,0:T(8,128)}, f32[1024,128]{1,0:T(8,128)S(1)}, f32[1024,128]{1,0:T(8,128)S(1)}, bf16[3,2624,256]{2,1,0:T(8,128)(2,1)S(1)}, bf16...) custom-call(s32[3]{0:T(128)S(1)} %get-tuple-element.601.valid_ref, ...), custom_call_target="tpu_custom_call", output_to_operand_aliasing={{3}: (3, {}), {4}: (4, {}), {5}: (5, {})} | custom-call | tf_op jit(solution)/shard_map/while/body/while/body/eval_jaxpr/powers/pallas_call | solution.py:377
  380.5 20.7 %all_to_all.50 = f32[64,16,128]{2,1,0:T(8,128)S(1)} all-to-all(f32[64,16,128]{2,1,0:T(8,128)S(1)} %bitcast.53), channel_id=1, replica_groups=mesh['row'=4,'column'=4,'depth'=4,'core'=2] {'row','column','depth'}, dimensions={0} | all-to-all | bytes 1048576 | tf_op jit(solution)/shard_map/while/body/while/body/eval_jaxpr/all_to_all | solution.py:604
  401.4 15.8 %all_to_all.51 = f32[64,16,128]{2,1,0:T(8,128)S(1)} all-to-all(f32[64,16,128]{2,1,0:T(8,128)S(1)} %broadcast_in_dim.60), channel_id=1, replica_groups=mesh['row'=4,'column'=4,'depth'=4,'core'=2] {'row','column','depth'}, dimensions={0} | all-to-all | bytes 1048576 | tf_op jit(solution)/shard_map/while/body/while/body/eval_jaxpr/all_to_all | solution.py:606
  417.4 3.0 collective-permute-start.3
  425.8 10.7 %solve.8 = f32[256,256]{1,0:T(8,128)} custom-call(f32[256,256]{1,0:T(8,128)} %fusion.36.matrix_ref, f32[256,256]{1,0:T(8,128)S(1)} %fusion.37.target_ref), custom_call_target="tpu_custom_call" | custom-call | tf_op jit(solution)/shard_map/while/body/while/body/eval_jaxpr/solve/pallas_call | solution.py:589
  436.5 6.6 add_select_fusion.3
  443.1 3.3 subtract_select_fusion.3
  452.9 4.7 collective-permute-done.1.outer_ref
  457.6 3.7 begin.10
  461.3 12.7 %powers.10 = (f32[2,2048,256]{2,1,0:T(8,128)}, f32[1024,128]{1,0:T(8,128)S(1)}, f32[1024,128]{1,0:T(8,128)S(1)}, bf16[3,2624,256]{2,1,0:T(8,128)(2,1)S(1)}, bf16...) custom-call(s32[3]{0:T(128)S(1)} %get-tuple-element.601.valid_ref, ...), custom_call_target="tpu_custom_call", output_to_operand_aliasing={{3}: (3, {}), {4}: (4, {}), {5}: (5, {})} | custom-call | tf_op jit(solution)/shard_map/while/body/while/body/eval_jaxpr/powers/pallas_call | solution.py:377
  476.1 20.7 %all_to_all.50 = f32[64,16,128]{2,1,0:T(8,128)S(1)} all-to-all(f32[64,16,128]{2,1,0:T(8,128)S(1)} %bitcast.53), channel_id=1, replica_groups=mesh['row'=4,'column'=4,'depth'=4,'core'=2] {'row','column','depth'}, dimensions={0} | all-to-all | bytes 1048576 | tf_op jit(solution)/shard_map/while/body/while/body/eval_jaxpr/all_to_all | solution.py:604
  497.0 15.8 %all_to_all.51 = f32[64,16,128]{2,1,0:T(8,128)S(1)} all-to-all(f32[64,16,128]{2,1,0:T(8,128)S(1)} %broadcast_in_dim.60), channel_id=1, replica_groups=mesh['row'=4,'column'=4,'depth'=4,'core'=2] {'row','column','depth'}, dimensions={0} | all-to-all | bytes 1048576 | tf_op jit(solution)/shard_map/while/body/while/body/eval_jaxpr/all_to_all | solution.py:606
  513.0 3.0 collective-permute-start.3
  521.5 10.7 %solve.8 = f32[256,256]{1,0:T(8,128)} custom-call(f32[256,256]{1,0:T(8,128)} %fusion.36.matrix_ref, f32[256,256]{1,0:T(8,128)S(1)} %fusion.37.target_ref), custom_call_target="tpu_custom_call" | custom-call | tf_op jit(solution)/shard_map/while/body/while/body/eval_jaxpr/solve/pallas_call | solution.py:589
  532.1 6.6 add_select_fusion.3
  538.7 3.3 subtract_select_fusion.3
  550.2 4.7 collective-permute-done.1.outer_ref
  554.8 3.8 begin.10
  558.6 12.7 %powers.10 = (f32[2,2048,256]{2,1,0:T(8,128)}, f32[1024,128]{1,0:T(8,128)S(1)}, f32[1024,128]{1,0:T(8,128)S(1)}, bf16[3,2624,256]{2,1,0:T(8,128)(2,1)S(1)}, bf16...) custom-call(s32[3]{0:T(128)S(1)} %get-tuple-element.601.valid_ref, ...), custom_call_target="tpu_custom_call", output_to_operand_aliasing={{3}: (3, {}), {4}: (4, {}), {5}: (5, {})} | custom-call | tf_op jit(solution)/shard_map/while/body/while/body/eval_jaxpr/powers/pallas_call | solution.py:377
  573.4 20.7 %all_to_all.50 = f32[64,16,128]{2,1,0:T(8,128)S(1)} all-to-all(f32[64,16,128]{2,1,0:T(8,128)S(1)} %bitcast.53), channel_id=1, replica_groups=mesh['row'=4,'column'=4,'depth'=4,'core'=2] {'row','column','depth'}, dimensions={0} | all-to-all | bytes 1048576 | tf_op jit(solution)/shard_map/while/body/while/body/eval_jaxpr/all_to_all | solution.py:604
  594.3 15.8 %all_to_all.51 = f32[64,16,128]{2,1,0:T(8,128)S(1)} all-to-all(f32[64,16,128]{2,1,0:T(8,128)S(1)} %broadcast_in_dim.60), channel_id=1, replica_groups=mesh['row'=4,'column'=4,'depth'=4,'core'=2] {'row','column','depth'}, dimensions={0} | all-to-all | bytes 1048576 | tf_op jit(solution)/shard_map/while/body/while/body/eval_jaxpr/all_to_all | solution.py:606
  610.3 3.0 collective-permute-start.3
  618.7 10.7 %solve.8 = f32[256,256]{1,0:T(8,128)} custom-call(f32[256,256]{1,0:T(8,128)} %fusion.36.matrix_ref, f32[256,256]{1,0:T(8,128)S(1)} %fusion.37.target_ref), custom_call_target="tpu_custom_call" | custom-call | tf_op jit(solution)/shard_map/while/body/while/body/eval_jaxpr/solve/pallas_call | solution.py:589
  629.4 6.6 add_select_fusion.3
  636.0 3.3 subtract_select_fusion.3
  640.8 5.7 basis.2
  647.8 20.4 %all_to_all.47.received_ref = f32[128,2,768]{2,1,0:T(2,128)S(1)} all-to-all(f32[128,2,768]{2,1,0:T(2,128)} %reshape.106), channel_id=1, replica_groups=mesh['row'=4,'column'=4,'depth'=4,'core'=2] {'row','column','depth','core'}, dimensions={0} | all-to-all | bytes 1572864 | tf_op jit(solution)/shard_map/while/body/all_to_all | solution.py:789
  (305 shorter events, 93.7 us)
Async XLA Ops:
  16.5 19.1 %collective-permute-start.6 = (f32[320,256]{1,0:T(8,128)S(1)}, f32[320,256]{1,0:T(8,128)S(1)}, u32[]{:S(2)}, u32[]{:S(2)}) collective-permute-start(f32[320,256]{1,0:T(8,128)S(1)} %get-tuple-element.331), channel_id=1, source_target_pairs={{0,1},{1,0},{2,3},{3,2},{4,5},{5,4},{6,7},{7,6},{8,9},{9,8},{10,11... | collective-permute-start | bytes 983048 | tf_op jit(solution)/shard_map/ppermute | solution.py:615
  17.8 17.7 %collective-permute-start.7 = (f32[320,256]{1,0:T(8,128)S(1)}, f32[320,256]{1,0:T(8,128)S(1)}, u32[]{:S(2)}, u32[]{:S(2)}) collective-permute-start(f32[320,256]{1,0:T(8,128)S(1)} %get-tuple-element.332), channel_id=1, source_target_pairs={{1,2},{3,4},{5,6},{7,8},{9,10},{11,12},{13,14},{15,16},{17,18},{19... | collective-permute-start | bytes 983048 | tf_op jit(solution)/shard_map/ppermute | solution.py:616
  22.5 4.1 collective-permute-start.4
  22.6 7.2 %collective-permute-start.5 = (f32[192,256]{1,0:T(8,128)S(1)}, f32[192,256]{1,0:T(8,128)S(1)}, u32[]{:S(2)}, u32[]{:S(2)}) collective-permute-start(f32[192,256]{1,0:T(8,128)S(1)} %get-tuple-element.444), channel_id=1, source_target_pairs={{1,2},{3,4},{5,6},{7,8},{9,10},{11,12},{13,14},{15,16},{17,18},{19... | collective-permute-start | bytes 589832 | tf_op jit(solution)/shard_map/ppermute | solution.py:616
  48.3 2.0 collective-permute-start.8
  50.3 46.2 %copy-start.1 = (f32[16,768]{1,0:T(8,128)S(1)}, f32[16,768]{1,0:T(8,128)}, u32[]{:S(2)}) copy-start(f32[16,768]{1,0:T(8,128)} %load_ref.1) | copy-start | bytes 147460
  50.3 46.2 %copy-start.2 = (s32[16,256]{1,0:T(8,128)S(1)}, s32[16,256]{1,0:T(8,128)}, u32[]{:S(2)}) copy-start(s32[16,256]{1,0:T(8,128)} %nodes_ref.1) | copy-start | bytes 49156
  50.3 51.7 %copy-start.8 = (f32[2048,256]{1,0:T(8,128)S(1)}, f32[2048,256]{1,0:T(8,128)}, u32[]{:S(2)}) copy-start(f32[2048,256]{1,0:T(8,128)} %k0_ref.1) | copy-start | bytes 6291460
  93.5 19.0 %collective-permute-start.9 = (f32[1024,128]{1,0:T(8,128)S(1)}, f32[1024,128]{1,0:T(8,128)S(1)}, u32[]{:S(2)}, u32[]{:S(2)}) collective-permute-start(f32[1024,128]{1,0:T(8,128)S(1)} %bitcast.50), channel_id=1, source_target_pairs={{0,1},{1,0},{2,3},{3,2},{4,5},{5,4},{6,7},{7,6},{8,9},{9,8},{10,11... | collective-permute-start | bytes 1572872 | tf_op jit(solution)/shard_map/ppermute | solution.py:608
  102.0 10.5 %copy-start.18 = (bf16[768,2048]{1,0:T(8,128)(2,1)}, bf16[768,2048]{1,0:T(8,128)(2,1)S(1)}, u32[]{:S(2)}) copy-start(bf16[768,2048]{1,0:T(8,128)(2,1)S(1)} %get-tuple-element.620.refs_3_) | copy-start | bytes 9437188
  102.0 10.5 %copy-start.19 = (bf16[768,2048]{1,0:T(8,128)(2,1)}, bf16[768,2048]{1,0:T(8,128)(2,1)S(1)}, u32[]{:S(2)}) copy-start(bf16[768,2048]{1,0:T(8,128)(2,1)S(1)} %get-tuple-element.621.refs_4_) | copy-start | bytes 9437188
  133.4 19.9 %all-to-all-start.5 = ((f32[128,2,768]{2,1,0:T(2,128)}), f32[128,2,768]{2,1,0:T(2,128)S(1)}, u32[]{:S(2)}, u32[]{:S(2)}) async-start(f32[128,2,768]{2,1,0:T(2,128)} %get-tuple-element.340), calls=%async_computation.5 | async-start | bytes 1572864 | tf_op jit(solution)/shard_map/all_to_all | solution.py:789
  137.0 16.3 %copy-start.20 = (s32[128]{0:T(128)S(1)}, s32[128]{0:T(128)}, u32[]{:S(2)}) copy-start(s32[128]{0:T(128)} %param.17) | copy-start | bytes 1540
  158.4 16.0 %copy-start.12 = (f32[320,256]{1,0:T(8,128)}, f32[320,256]{1,0:T(8,128)S(1)}, u32[]{:S(2)}) copy-start(f32[320,256]{1,0:T(8,128)S(1)} %get-tuple-element.603.iband_ref) | copy-start | bytes 983044 | tf_op jit(solution)/shard_map/while/body/while
  158.4 16.0 %copy-start.14 = (f32[320,256]{1,0:T(8,128)}, f32[320,256]{1,0:T(8,128)S(1)}, u32[]{:S(2)}) copy-start(f32[320,256]{1,0:T(8,128)S(1)} %get-tuple-element.604.oband_ref) | copy-start | bytes 983044 | tf_op jit(solution)/shard_map/while/body/while
  160.2 10.4 %copy-start.4 = (f32[12,256,256]{2,1,0:T(8,128)S(1)}, f32[12,256,256]{2,1,0:T(8,128)}, u32[]{:S(2)}) copy-start(f32[12,256,256]{2,1,0:T(8,128)} %get-tuple-element.602.band_ref) | copy-start | bytes 9437188 | tf_op jit(solution)/shard_map/while/body/while
  162.3 3.3 collective-permute-start
  163.7 7.0 %collective-permute-start.1 = (f32[192,256]{1,0:T(8,128)S(1)}, f32[192,256]{1,0:T(8,128)S(1)}, u32[]{:S(2)}, u32[]{:S(2)}) collective-permute-start(f32[192,256]{1,0:T(8,128)S(1)} %get-tuple-element.544), channel_id=1, source_target_pairs={{1,2},{3,4},{5,6},{7,8},{9,10},{11,12},{13,14},{15,16},{17,18},{19... | collective-permute-start | bytes 589832 | tf_op jit(solution)/shard_map/while/body/while/body/eval_jaxpr/ppermute | solution.py:616
  187.2 2.0 collective-permute-start.2
  225.1 4.5 collective-permute-start.3
  244.2 6.0 copy-start.5
  244.2 6.0 copy-start.6
  255.0 13.5 %copy-start.12 = (f32[320,256]{1,0:T(8,128)}, f32[320,256]{1,0:T(8,128)S(1)}, u32[]{:S(2)}) copy-start(f32[320,256]{1,0:T(8,128)S(1)} %get-tuple-element.603.iband_ref) | copy-start | bytes 983044 | tf_op jit(solution)/shard_map/while/body/while
  255.0 13.5 %copy-start.14 = (f32[320,256]{1,0:T(8,128)}, f32[320,256]{1,0:T(8,128)S(1)}, u32[]{:S(2)}) copy-start(f32[320,256]{1,0:T(8,128)S(1)} %get-tuple-element.604.oband_ref) | copy-start | bytes 983044 | tf_op jit(solution)/shard_map/while/body/while
  256.8 7.9 %copy-start.4 = (f32[12,256,256]{2,1,0:T(8,128)S(1)}, f32[12,256,256]{2,1,0:T(8,128)}, u32[]{:S(2)}) copy-start(f32[12,256,256]{2,1,0:T(8,128)} %get-tuple-element.602.band_ref) | copy-start | bytes 9437188 | tf_op jit(solution)/shard_map/while/body/while
  257.1 2.9 collective-permute-start
  257.6 7.1 %collective-permute-start.1 = (f32[192,256]{1,0:T(8,128)S(1)}, f32[192,256]{1,0:T(8,128)S(1)}, u32[]{:S(2)}, u32[]{:S(2)}) collective-permute-start(f32[192,256]{1,0:T(8,128)S(1)} %get-tuple-element.544), channel_id=1, source_target_pairs={{1,2},{3,4},{5,6},{7,8},{9,10},{11,12},{13,14},{15,16},{17,18},{19... | collective-permute-start | bytes 589832 | tf_op jit(solution)/shard_map/while/body/while/body/eval_jaxpr/ppermute | solution.py:616
  281.2 2.0 collective-permute-start.2
  320.1 4.5 collective-permute-start.3
  339.2 6.6 copy-start.3
  339.2 6.6 copy-start.5
  339.2 6.6 copy-start.6
  350.6 15.1 %copy-start.12 = (f32[320,256]{1,0:T(8,128)}, f32[320,256]{1,0:T(8,128)S(1)}, u32[]{:S(2)}) copy-start(f32[320,256]{1,0:T(8,128)S(1)} %get-tuple-element.603.iband_ref) | copy-start | bytes 983044 | tf_op jit(solution)/shard_map/while/body/while
  350.6 15.1 %copy-start.14 = (f32[320,256]{1,0:T(8,128)}, f32[320,256]{1,0:T(8,128)S(1)}, u32[]{:S(2)}) copy-start(f32[320,256]{1,0:T(8,128)S(1)} %get-tuple-element.604.oband_ref) | copy-start | bytes 983044 | tf_op jit(solution)/shard_map/while/body/while
  352.4 9.5 %copy-start.4 = (f32[12,256,256]{2,1,0:T(8,128)S(1)}, f32[12,256,256]{2,1,0:T(8,128)}, u32[]{:S(2)}) copy-start(f32[12,256,256]{2,1,0:T(8,128)} %get-tuple-element.602.band_ref) | copy-start | bytes 9437188 | tf_op jit(solution)/shard_map/while/body/while
  354.5 2.7 collective-permute-start
  354.9 7.0 %collective-permute-start.1 = (f32[192,256]{1,0:T(8,128)S(1)}, f32[192,256]{1,0:T(8,128)S(1)}, u32[]{:S(2)}, u32[]{:S(2)}) collective-permute-start(f32[192,256]{1,0:T(8,128)S(1)} %get-tuple-element.544), channel_id=1, source_target_pairs={{1,2},{3,4},{5,6},{7,8},{9,10},{11,12},{13,14},{15,16},{17,18},{19... | collective-permute-start | bytes 589832 | tf_op jit(solution)/shard_map/while/body/while/body/eval_jaxpr/ppermute | solution.py:616
  378.5 2.0 collective-permute-start.2
  417.4 4.5 collective-permute-start.3
  436.5 6.6 copy-start.3
  436.5 6.6 copy-start.5
  436.5 6.6 copy-start.6
  447.9 13.5 %copy-start.12 = (f32[320,256]{1,0:T(8,128)}, f32[320,256]{1,0:T(8,128)S(1)}, u32[]{:S(2)}) copy-start(f32[320,256]{1,0:T(8,128)S(1)} %get-tuple-element.603.iband_ref) | copy-start | bytes 983044 | tf_op jit(solution)/shard_map/while/body/while
  447.9 13.5 %copy-start.14 = (f32[320,256]{1,0:T(8,128)}, f32[320,256]{1,0:T(8,128)S(1)}, u32[]{:S(2)}) copy-start(f32[320,256]{1,0:T(8,128)S(1)} %get-tuple-element.604.oband_ref) | copy-start | bytes 983044 | tf_op jit(solution)/shard_map/while/body/while
  449.7 7.9 %copy-start.4 = (f32[12,256,256]{2,1,0:T(8,128)S(1)}, f32[12,256,256]{2,1,0:T(8,128)}, u32[]{:S(2)}) copy-start(f32[12,256,256]{2,1,0:T(8,128)} %get-tuple-element.602.band_ref) | copy-start | bytes 9437188 | tf_op jit(solution)/shard_map/while/body/while
  450.0 2.9 collective-permute-start
  450.5 7.1 %collective-permute-start.1 = (f32[192,256]{1,0:T(8,128)S(1)}, f32[192,256]{1,0:T(8,128)S(1)}, u32[]{:S(2)}, u32[]{:S(2)}) collective-permute-start(f32[192,256]{1,0:T(8,128)S(1)} %get-tuple-element.544), channel_id=1, source_target_pairs={{1,2},{3,4},{5,6},{7,8},{9,10},{11,12},{13,14},{15,16},{17,18},{19... | collective-permute-start | bytes 589832 | tf_op jit(solution)/shard_map/while/body/while/body/eval_jaxpr/ppermute | solution.py:616
  474.1 2.0 collective-permute-start.2
  513.0 4.5 collective-permute-start.3
  532.1 6.6 copy-start.3
  532.1 6.6 copy-start.5
  532.1 6.6 copy-start.6
  543.5 15.1 %copy-start.12 = (f32[320,256]{1,0:T(8,128)}, f32[320,256]{1,0:T(8,128)S(1)}, u32[]{:S(2)}) copy-start(f32[320,256]{1,0:T(8,128)S(1)} %get-tuple-element.603.iband_ref) | copy-start | bytes 983044 | tf_op jit(solution)/shard_map/while/body/while
  543.5 15.1 %copy-start.14 = (f32[320,256]{1,0:T(8,128)}, f32[320,256]{1,0:T(8,128)S(1)}, u32[]{:S(2)}) copy-start(f32[320,256]{1,0:T(8,128)S(1)} %get-tuple-element.604.oband_ref) | copy-start | bytes 983044 | tf_op jit(solution)/shard_map/while/body/while
  545.3 9.5 %copy-start.4 = (f32[12,256,256]{2,1,0:T(8,128)S(1)}, f32[12,256,256]{2,1,0:T(8,128)}, u32[]{:S(2)}) copy-start(f32[12,256,256]{2,1,0:T(8,128)} %get-tuple-element.602.band_ref) | copy-start | bytes 9437188 | tf_op jit(solution)/shard_map/while/body/while
  547.4 2.8 collective-permute-start
  547.9 7.0 %collective-permute-start.1 = (f32[192,256]{1,0:T(8,128)S(1)}, f32[192,256]{1,0:T(8,128)S(1)}, u32[]{:S(2)}, u32[]{:S(2)}) collective-permute-start(f32[192,256]{1,0:T(8,128)S(1)} %get-tuple-element.544), channel_id=1, source_target_pairs={{1,2},{3,4},{5,6},{7,8},{9,10},{11,12},{13,14},{15,16},{17,18},{19... | collective-permute-start | bytes 589832 | tf_op jit(solution)/shard_map/while/body/while/body/eval_jaxpr/ppermute | solution.py:616
  571.4 2.0 collective-permute-start.2
  610.3 4.5 collective-permute-start.3
  629.4 6.6 copy-start.3
  629.4 6.6 copy-start.5
  629.4 6.6 copy-start.6
  646.5 21.8 %copy-start.21 = (s32[128]{0:T(128)S(1)}, s32[128]{0:T(128)}, u32[]{:S(2)}) copy-start(s32[128]{0:T(128)} %get-tuple-element.699) | copy-start | bytes 1540 | tf_op jit(solution)/shard_map/while
  646.5 23.3 %copy-start.9 = (f32[2048,256]{1,0:T(8,128)S(1)}, f32[2048,256]{1,0:T(8,128)}, u32[]{:S(2)}) copy-start(f32[2048,256]{1,0:T(8,128)} %get-tuple-element.671) | copy-start | bytes 6291460 | tf_op jit(solution)/shard_map/while
  (37 other events, 37.1 us)

commit v8 on v7

--- a/solution.py
+++ b/solution.py
@@ -764,11 +764,11 @@
 def basis(vectors, weights):
     rows, cols = vectors[0][0].shape[-2:]
     loads = weights[0].shape[0]
-    weight = pl.BlockSpec((loads, CHUNK), lambda i: (0, i))
+    weight = pl.BlockSpec((loads, 2 * CHUNK), lambda i: (0, i))
     out = (loads // 3, 3 * len(vectors) * cols)
     return pl.pallas_call(
         basis_kernel,
-        grid=(rows // CHUNK,),
+        grid=(rows // (2 * CHUNK),),
         out_shape=jax.ShapeDtypeStruct(out, F32),
         in_specs=[spec for _, spec in vectors] + [weight, weight],
         out_specs=pl.BlockSpec(out, lambda i: (0, 0)),
@@ -777,12 +777,12 @@
     )(*[vector for vector, _ in vectors], *weights)
 
 
-def in_chunks(vector, n=None):
+def in_chunks(vector, n=None, step=CHUNK):
     cols = vector.shape[-1]
     if n is None:
-        return vector, pl.BlockSpec((CHUNK, cols), lambda i: (i, 0))
+        return vector, pl.BlockSpec((step, cols), lambda i: (i, 0))
     placed = pltpu.with_memory_space_constraint(vector, pltpu.HBM)
-    return placed, pl.BlockSpec((None, CHUNK, cols), lambda i: (n, i, 0))
+    return placed, pl.BlockSpec((None, step, cols), lambda i: (n, i, 0))
 
 
 def to_owner(rows):
@@ -856,7 +856,11 @@
     begun = begin(right_side, inner, outer, valid, band)
     images, mine, theirs = powers(right_side.shape[0], begun, valid, bands[1:])
     vectors = [in_chunks(right_side), in_chunks(images, 0), in_chunks(images, 1)]
-    basis_rows = basis(vectors, weights)
+    basis_rows = basis(
+        [in_chunks(right_side, None, 2 * CHUNK)]
+        + [in_chunks(images, n, 2 * CHUNK) for n in range(2)],
+        weights,
+    )
     mine, theirs = total_of(mine, theirs)
     coef, rows, good = galerkin(core[None], mine, theirs, basis_rows, count)
     received = to_owner(rows)
@@ -865,7 +869,7 @@
 
     def exactly(_):
         exact = plain_cg(right_side, valid, bands)
-        own_rows = basis([in_chunks(exact)], weights)
+        own_rows = basis([in_chunks(exact, None, 2 * CHUNK)], weights)
         received = to_owner(own_rows.reshape(count, -1, own_rows.shape[1]))
         return jnp.ones((), jnp.int32), exact, lead(received, dipole_slot)
 

time: 683 us -> 680 us (level)
  no operation moved by 1% of the time
where the time goes in v8:
time: 680 us; the launch traced here: 671 us
  blocking collectives  244 us (36%)
  Pallas kernels  218 us (32%)
  waiting for transfers between devices  55.9 us (8%)
  matrix products  48.7 us (7%)
  starting transfers between devices  45.6 us (7%)
  local copies, waits for them, and re-layouts  29.7 us (4%)
  other arithmetic  25.4 us (4%)
    all_to_all x6, blocking collectives, total_of(): arrived = lax.all_to_all(pair, CHIPS, 0, 0, tiled=True)  129 us
    all_to_all x6, blocking collectives, total_of(): gathered = lax.all_to_all(own, CHIPS, 0, 0, tiled=True)  94.8 us
    pallas_call x6, Pallas kernels, powers(): pl.pallas_call(powers_kernel, out_shape=(pltpu.HBM((ITERS - 1, own, cols)...  76.5 us
    pallas_call x5, Pallas kernels, solve(): pl.pallas_call(solve_kernel, out_shape=jax.ShapeDtypeStruct(target.shape,...  53.3 us
    dot_general x10, matrix products, times(): jnp.dot(a, b, preferred_element_type=F32, precision=lax.Precision.HIGHEST)  48.7 us
    ppermute x7, waiting for transfers between devices, swap_sides(): lax.ppermute(outer, AXES, across + [(b, a) for a, b in across])  27 us
    pallas_call x6, Pallas kernels, begin(): pl.pallas_call(first_kernel, out_shape=(part, part, wide, wide, jax.Shape...  24.5 us
    while x146, local copies, waits for them, and re-layouts  22 us
  transfers between devices with their start and end apart: 27, of which 18 were waited for; matrix products, arithmetic and copies ran while one was open for 0% of the time, Pallas kernels for 4%

profile of v8, /device:TPU:1, one launch (start us, length us, event | category | flops | bytes accessed | tf_op | source)
XLA Modules:
  0.0 671.2 jit_solution(14123163912737895760)
XLA Ops:
  4.8 11.7 %assemble.1 = (f32[12,256,256]{2,1,0:T(8,128)}, f32[320,256]{1,0:T(8,128)S(1)}, f32[320,256]{1,0:T(8,128)S(1)}) custom-call(s32[1]{0:T(128)} %bitcast.1.core_ref, s32[256]{0:T(256)S(1)} %get-tuple-element.429.group_ref, s32[256]{0:T(256)S(1)} %multiply_minimum_fusion.first_ref, f32[32,32,256]{2,1,0:T(8,128)S(1)} %bitcast.52, ...), custom_call_target="tpu_custom_call" | custom-call | tf_op jit(solution)/shard_map/assemble/pallas_call | solution.py:169
  17.8 3.5 collective-permute-start.7
  22.5 3.9 collective-permute-start.5
  26.6 3.2 collective-permute-done.5.outer_ref
  29.8 5.7 begin.9
  35.6 12.8 %powers.9 = (f32[2,2048,256]{2,1,0:T(8,128)}, f32[1024,128]{1,0:T(8,128)S(1)}, f32[1024,128]{1,0:T(8,128)S(1)}, bf16[3,2624,256]{2,1,0:T(8,128)(2,1)S(1)}, bf16[...) custom-call(s32[3]{0:T(128)S(1)} %pad_add_fusion.valid_ref, ...), custom_call_target="tpu_custom_call", output_to_operand_aliasing={{3}: (3, {}), {4}: (4, {}), {5}: (5, {})} | custom-call | tf_op jit(solution)/shard_map/powers/pallas_call | solution.py:377
  50.4 26.3 %all_to_all.48 = f32[64,16,128]{2,1,0:T(8,128)} all-to-all(f32[64,16,128]{2,1,0:T(8,128)S(1)} %bitcast.55), channel_id=1, replica_groups=mesh['row'=4,'column'=4,'depth'=4,'core'=2] {'row','column','depth'}, dimensions={0} | all-to-all | bytes 1048576 | tf_op jit(solution)/shard_map/all_to_all | solution.py:604
  77.8 15.7 %all_to_all.49 = f32[64,16,128]{2,1,0:T(8,128)S(1)} all-to-all(f32[64,16,128]{2,1,0:T(8,128)S(1)} %broadcast_in_dim.52), channel_id=1, replica_groups=mesh['row'=4,'column'=4,'depth'=4,'core'=2] {'row','column','depth'}, dimensions={0} | all-to-all | bytes 1048576 | tf_op jit(solution)/shard_map/all_to_all | solution.py:606
  93.5 3.2 collective-permute-start.9
  96.7 5.5 loads.1
  102.2 10.9 %basis.3.basis_ref = f32[256,2304]{1,0:T(8,128)S(1)} custom-call(f32[2048,256]{1,0:T(8,128)S(1)} %copy-done.8, f32[2,2048,256]{2,1,0:T(8,128)} %get-tuple-element.335.refs_1_.refs_2_.k1_ref.k2_ref, f32[2,2048,256]{2,1,0:T(8,128)} %get-tuple-element.335.refs_1_.refs_2_.k1_ref.k2_ref, bf16[768,2048]{1,0:T(8,128)(2,1)S(1)} %get-tuple-element.620.refs_3_, ...), custom_call_target="tpu_custom_call" | custom-call | tf_op jit(solution)/shard_map/basis/pallas_call | solution.py:769
  113.2 20.9 %galerkin.1 = (f32[768,256]{1,0:T(8,128)}, f32[128,2,768]{2,1,0:T(2,128)}, s32[1]{0:T(128)}) custom-call(s32[1]{0:T(128)} %bitcast.1.core_ref, f32[1024,128]{1,0:T(8,128)S(1)} %bitcast.51, f32[1024,128]{1,0:T(8,128)S(1)} %collective-permute-done.9.theirs_ref, f32[256,2304]{1,0:T(8,128)S(1)} %basis.3.basis_ref), custom_call_target="tpu_custom_call" | custom-call | tf_op jit(solution)/shard_map/galerkin/pallas_call | solution.py:559
  134.2 3.6 all-to-all-start.5
  137.7 6.3 combine.1
  144.0 9.9 %all-to-all-done.5.received_ref = f32[128,2,768]{2,1,0:T(2,128)S(1)} async-done(((f32[128,2,768]{2,1,0:T(2,128)}), f32[128,2,768]{2,1,0:T(2,128)S(1)}, u32[]{:S(2)}, u32[]{:S(2)}) %all-to-all-start.5) | async-done | bytes 786464 | tf_op jit(solution)/shard_map/all_to_all | solution.py:789
  155.5 515.3 %while.31 = (s32[]{:T(128)}, f32[2048,256]{1,0:T(8,128)}, f32[3,128,256]{2,1,0:T(8,128)}, s32[]{:T(128)}, s32[3]{0:T(128)S(1)}, /*index=5*/f32[12,256,256]{2,1,0...) while((s32[]{:T(128)}, f32[2048,256]{1,0:T(8,128)}, ...), condition=%region_6.7_spmd, body=%region_2.6_spmd | while | flops 3232530432 | bytes 119594080 | solution.py:876
  158.8 482.4 %while.33 = (s32[]{:T(128)}, f32[2048,256]{1,0:T(8,128)}, f32[2048,256]{1,0:T(8,128)}, f32[2048,256]{1,0:T(8,128)}, f32[256,256]{1,0:T(8,128)S(1)}, /*index=5*/p...) while((s32[]{:T(128)}, f32[2048,256]{1,0:T(8,128)}, ...), condition=%wide.region_5.5_spmd.clone, body=%wide.region_3.4_spmd.clone.sunk | while | flops 3232530432 | bytes 99668760 | solution.py:665
  166.0 5.0 collective-permute-done.1.outer_ref
  171.1 3.7 begin.10
  174.8 12.8 %powers.10 = (f32[2,2048,256]{2,1,0:T(8,128)}, f32[1024,128]{1,0:T(8,128)S(1)}, f32[1024,128]{1,0:T(8,128)S(1)}, bf16[3,2624,256]{2,1,0:T(8,128)(2,1)S(1)}, bf16...) custom-call(s32[3]{0:T(128)S(1)} %get-tuple-element.601.valid_ref, ...), custom_call_target="tpu_custom_call", output_to_operand_aliasing={{3}: (3, {}), {4}: (4, {}), {5}: (5, {})} | custom-call | tf_op jit(solution)/shard_map/while/body/while/body/eval_jaxpr/powers/pallas_call | solution.py:377
  189.6 19.7 %all_to_all.50 = f32[64,16,128]{2,1,0:T(8,128)S(1)} all-to-all(f32[64,16,128]{2,1,0:T(8,128)S(1)} %bitcast.53), channel_id=1, replica_groups=mesh['row'=4,'column'=4,'depth'=4,'core'=2] {'row','column','depth'}, dimensions={0} | all-to-all | bytes 1048576 | tf_op jit(solution)/shard_map/while/body/while/body/eval_jaxpr/all_to_all | solution.py:604
  209.5 15.8 %all_to_all.51 = f32[64,16,128]{2,1,0:T(8,128)S(1)} all-to-all(f32[64,16,128]{2,1,0:T(8,128)S(1)} %broadcast_in_dim.60), channel_id=1, replica_groups=mesh['row'=4,'column'=4,'depth'=4,'core'=2] {'row','column','depth'}, dimensions={0} | all-to-all | bytes 1048576 | tf_op jit(solution)/shard_map/while/body/while/body/eval_jaxpr/all_to_all | solution.py:606
  225.5 3.0 collective-permute-start.3
  233.9 10.7 %solve.8 = f32[256,256]{1,0:T(8,128)} custom-call(f32[256,256]{1,0:T(8,128)} %fusion.36.matrix_ref, f32[256,256]{1,0:T(8,128)S(1)} %fusion.37.target_ref), custom_call_target="tpu_custom_call" | custom-call | tf_op jit(solution)/shard_map/while/body/while/body/eval_jaxpr/solve/pallas_call | solution.py:589
  244.6 6.0 add_select_fusion.3
  250.6 3.3 subtract_select_fusion.3
  260.4 4.7 collective-permute-done.1.outer_ref
  265.1 3.7 begin.10
  268.9 12.7 %powers.10 = (f32[2,2048,256]{2,1,0:T(8,128)}, f32[1024,128]{1,0:T(8,128)S(1)}, f32[1024,128]{1,0:T(8,128)S(1)}, bf16[3,2624,256]{2,1,0:T(8,128)(2,1)S(1)}, bf16...) custom-call(s32[3]{0:T(128)S(1)} %get-tuple-element.601.valid_ref, ...), custom_call_target="tpu_custom_call", output_to_operand_aliasing={{3}: (3, {}), {4}: (4, {}), {5}: (5, {})} | custom-call | tf_op jit(solution)/shard_map/while/body/while/body/eval_jaxpr/powers/pallas_call | solution.py:377
  283.7 20.7 %all_to_all.50 = f32[64,16,128]{2,1,0:T(8,128)S(1)} all-to-all(f32[64,16,128]{2,1,0:T(8,128)S(1)} %bitcast.53), channel_id=1, replica_groups=mesh['row'=4,'column'=4,'depth'=4,'core'=2] {'row','column','depth'}, dimensions={0} | all-to-all | bytes 1048576 | tf_op jit(solution)/shard_map/while/body/while/body/eval_jaxpr/all_to_all | solution.py:604
  304.5 15.8 %all_to_all.51 = f32[64,16,128]{2,1,0:T(8,128)S(1)} all-to-all(f32[64,16,128]{2,1,0:T(8,128)S(1)} %broadcast_in_dim.60), channel_id=1, replica_groups=mesh['row'=4,'column'=4,'depth'=4,'core'=2] {'row','column','depth'}, dimensions={0} | all-to-all | bytes 1048576 | tf_op jit(solution)/shard_map/while/body/while/body/eval_jaxpr/all_to_all | solution.py:606
  320.5 3.0 collective-permute-start.3
  328.9 10.7 %solve.8 = f32[256,256]{1,0:T(8,128)} custom-call(f32[256,256]{1,0:T(8,128)} %fusion.36.matrix_ref, f32[256,256]{1,0:T(8,128)S(1)} %fusion.37.target_ref), custom_call_target="tpu_custom_call" | custom-call | tf_op jit(solution)/shard_map/while/body/while/body/eval_jaxpr/solve/pallas_call | solution.py:589
  339.6 6.6 add_select_fusion.3
  346.2 3.3 subtract_select_fusion.3
  357.7 4.7 collective-permute-done.1.outer_ref
  362.3 3.7 begin.10
  366.1 12.7 %powers.10 = (f32[2,2048,256]{2,1,0:T(8,128)}, f32[1024,128]{1,0:T(8,128)S(1)}, f32[1024,128]{1,0:T(8,128)S(1)}, bf16[3,2624,256]{2,1,0:T(8,128)(2,1)S(1)}, bf16...) custom-call(s32[3]{0:T(128)S(1)} %get-tuple-element.601.valid_ref, ...), custom_call_target="tpu_custom_call", output_to_operand_aliasing={{3}: (3, {}), {4}: (4, {}), {5}: (5, {})} | custom-call | tf_op jit(solution)/shard_map/while/body/while/body/eval_jaxpr/powers/pallas_call | solution.py:377
  380.9 20.7 %all_to_all.50 = f32[64,16,128]{2,1,0:T(8,128)S(1)} all-to-all(f32[64,16,128]{2,1,0:T(8,128)S(1)} %bitcast.53), channel_id=1, replica_groups=mesh['row'=4,'column'=4,'depth'=4,'core'=2] {'row','column','depth'}, dimensions={0} | all-to-all | bytes 1048576 | tf_op jit(solution)/shard_map/while/body/while/body/eval_jaxpr/all_to_all | solution.py:604
  401.8 15.8 %all_to_all.51 = f32[64,16,128]{2,1,0:T(8,128)S(1)} all-to-all(f32[64,16,128]{2,1,0:T(8,128)S(1)} %broadcast_in_dim.60), channel_id=1, replica_groups=mesh['row'=4,'column'=4,'depth'=4,'core'=2] {'row','column','depth'}, dimensions={0} | all-to-all | bytes 1048576 | tf_op jit(solution)/shard_map/while/body/while/body/eval_jaxpr/all_to_all | solution.py:606
  417.8 3.0 collective-permute-start.3
  426.2 10.7 %solve.8 = f32[256,256]{1,0:T(8,128)} custom-call(f32[256,256]{1,0:T(8,128)} %fusion.36.matrix_ref, f32[256,256]{1,0:T(8,128)S(1)} %fusion.37.target_ref), custom_call_target="tpu_custom_call" | custom-call | tf_op jit(solution)/shard_map/while/body/while/body/eval_jaxpr/solve/pallas_call | solution.py:589
  436.9 6.6 add_select_fusion.3
  443.5 3.3 subtract_select_fusion.3
  453.3 4.7 collective-permute-done.1.outer_ref
  458.0 3.7 begin.10
  461.7 12.7 %powers.10 = (f32[2,2048,256]{2,1,0:T(8,128)}, f32[1024,128]{1,0:T(8,128)S(1)}, f32[1024,128]{1,0:T(8,128)S(1)}, bf16[3,2624,256]{2,1,0:T(8,128)(2,1)S(1)}, bf16...) custom-call(s32[3]{0:T(128)S(1)} %get-tuple-element.601.valid_ref, ...), custom_call_target="tpu_custom_call", output_to_operand_aliasing={{3}: (3, {}), {4}: (4, {}), {5}: (5, {})} | custom-call | tf_op jit(solution)/shard_map/while/body/while/body/eval_jaxpr/powers/pallas_call | solution.py:377
  476.6 20.7 %all_to_all.50 = f32[64,16,128]{2,1,0:T(8,128)S(1)} all-to-all(f32[64,16,128]{2,1,0:T(8,128)S(1)} %bitcast.53), channel_id=1, replica_groups=mesh['row'=4,'column'=4,'depth'=4,'core'=2] {'row','column','depth'}, dimensions={0} | all-to-all | bytes 1048576 | tf_op jit(solution)/shard_map/while/body/while/body/eval_jaxpr/all_to_all | solution.py:604
  497.4 15.8 %all_to_all.51 = f32[64,16,128]{2,1,0:T(8,128)S(1)} all-to-all(f32[64,16,128]{2,1,0:T(8,128)S(1)} %broadcast_in_dim.60), channel_id=1, replica_groups=mesh['row'=4,'column'=4,'depth'=4,'core'=2] {'row','column','depth'}, dimensions={0} | all-to-all | bytes 1048576 | tf_op jit(solution)/shard_map/while/body/while/body/eval_jaxpr/all_to_all | solution.py:606
  513.4 3.0 collective-permute-start.3
  521.9 10.7 %solve.8 = f32[256,256]{1,0:T(8,128)} custom-call(f32[256,256]{1,0:T(8,128)} %fusion.36.matrix_ref, f32[256,256]{1,0:T(8,128)S(1)} %fusion.37.target_ref), custom_call_target="tpu_custom_call" | custom-call | tf_op jit(solution)/shard_map/while/body/while/body/eval_jaxpr/solve/pallas_call | solution.py:589
  532.5 6.6 add_select_fusion.3
  539.1 3.3 subtract_select_fusion.3
  550.6 4.7 collective-permute-done.1.outer_ref
  555.2 3.8 begin.10
  559.0 12.7 %powers.10 = (f32[2,2048,256]{2,1,0:T(8,128)}, f32[1024,128]{1,0:T(8,128)S(1)}, f32[1024,128]{1,0:T(8,128)S(1)}, bf16[3,2624,256]{2,1,0:T(8,128)(2,1)S(1)}, bf16...) custom-call(s32[3]{0:T(128)S(1)} %get-tuple-element.601.valid_ref, ...), custom_call_target="tpu_custom_call", output_to_operand_aliasing={{3}: (3, {}), {4}: (4, {}), {5}: (5, {})} | custom-call | tf_op jit(solution)/shard_map/while/body/while/body/eval_jaxpr/powers/pallas_call | solution.py:377
  573.8 20.7 %all_to_all.50 = f32[64,16,128]{2,1,0:T(8,128)S(1)} all-to-all(f32[64,16,128]{2,1,0:T(8,128)S(1)} %bitcast.53), channel_id=1, replica_groups=mesh['row'=4,'column'=4,'depth'=4,'core'=2] {'row','column','depth'}, dimensions={0} | all-to-all | bytes 1048576 | tf_op jit(solution)/shard_map/while/body/while/body/eval_jaxpr/all_to_all | solution.py:604
  594.7 15.8 %all_to_all.51 = f32[64,16,128]{2,1,0:T(8,128)S(1)} all-to-all(f32[64,16,128]{2,1,0:T(8,128)S(1)} %broadcast_in_dim.60), channel_id=1, replica_groups=mesh['row'=4,'column'=4,'depth'=4,'core'=2] {'row','column','depth'}, dimensions={0} | all-to-all | bytes 1048576 | tf_op jit(solution)/shard_map/while/body/while/body/eval_jaxpr/all_to_all | solution.py:606
  610.7 3.0 collective-permute-start.3
  619.1 10.7 %solve.8 = f32[256,256]{1,0:T(8,128)} custom-call(f32[256,256]{1,0:T(8,128)} %fusion.36.matrix_ref, f32[256,256]{1,0:T(8,128)S(1)} %fusion.37.target_ref), custom_call_target="tpu_custom_call" | custom-call | tf_op jit(solution)/shard_map/while/body/while/body/eval_jaxpr/solve/pallas_call | solution.py:589
  629.8 6.6 add_select_fusion.3
  636.4 3.3 subtract_select_fusion.3
  641.2 5.1 basis.2
  647.7 20.4 %all_to_all.47.received_ref = f32[128,2,768]{2,1,0:T(2,128)S(1)} all-to-all(f32[128,2,768]{2,1,0:T(2,128)} %reshape.106), channel_id=1, replica_groups=mesh['row'=4,'column'=4,'depth'=4,'core'=2] {'row','column','depth','core'}, dimensions={0} | all-to-all | bytes 1572864 | tf_op jit(solution)/shard_map/while/body/all_to_all | solution.py:789
  (305 shorter events, 93.7 us)
Async XLA Ops:
  16.5 19.1 %collective-permute-start.6 = (f32[320,256]{1,0:T(8,128)S(1)}, f32[320,256]{1,0:T(8,128)S(1)}, u32[]{:S(2)}, u32[]{:S(2)}) collective-permute-start(f32[320,256]{1,0:T(8,128)S(1)} %get-tuple-element.331), channel_id=1, source_target_pairs={{0,1},{1,0},{2,3},{3,2},{4,5},{5,4},{6,7},{7,6},{8,9},{9,8},{10,11... | collective-permute-start | bytes 983048 | tf_op jit(solution)/shard_map/ppermute | solution.py:615
  17.8 17.7 %collective-permute-start.7 = (f32[320,256]{1,0:T(8,128)S(1)}, f32[320,256]{1,0:T(8,128)S(1)}, u32[]{:S(2)}, u32[]{:S(2)}) collective-permute-start(f32[320,256]{1,0:T(8,128)S(1)} %get-tuple-element.332), channel_id=1, source_target_pairs={{1,2},{3,4},{5,6},{7,8},{9,10},{11,12},{13,14},{15,16},{17,18},{19... | collective-permute-start | bytes 983048 | tf_op jit(solution)/shard_map/ppermute | solution.py:616
  22.5 4.1 collective-permute-start.4
  22.5 7.2 %collective-permute-start.5 = (f32[192,256]{1,0:T(8,128)S(1)}, f32[192,256]{1,0:T(8,128)S(1)}, u32[]{:S(2)}, u32[]{:S(2)}) collective-permute-start(f32[192,256]{1,0:T(8,128)S(1)} %get-tuple-element.444), channel_id=1, source_target_pairs={{1,2},{3,4},{5,6},{7,8},{9,10},{11,12},{13,14},{15,16},{17,18},{19... | collective-permute-start | bytes 589832 | tf_op jit(solution)/shard_map/ppermute | solution.py:616
  48.3 2.0 collective-permute-start.8
  50.3 46.4 %copy-start.1 = (f32[16,768]{1,0:T(8,128)S(1)}, f32[16,768]{1,0:T(8,128)}, u32[]{:S(2)}) copy-start(f32[16,768]{1,0:T(8,128)} %load_ref.1) | copy-start | bytes 147460
  50.3 46.4 %copy-start.2 = (s32[16,256]{1,0:T(8,128)S(1)}, s32[16,256]{1,0:T(8,128)}, u32[]{:S(2)}) copy-start(s32[16,256]{1,0:T(8,128)} %nodes_ref.1) | copy-start | bytes 49156
  50.3 51.9 %copy-start.8 = (f32[2048,256]{1,0:T(8,128)S(1)}, f32[2048,256]{1,0:T(8,128)}, u32[]{:S(2)}) copy-start(f32[2048,256]{1,0:T(8,128)} %k0_ref.1) | copy-start | bytes 6291460
  93.5 19.7 %collective-permute-start.9 = (f32[1024,128]{1,0:T(8,128)S(1)}, f32[1024,128]{1,0:T(8,128)S(1)}, u32[]{:S(2)}, u32[]{:S(2)}) collective-permute-start(f32[1024,128]{1,0:T(8,128)S(1)} %bitcast.50), channel_id=1, source_target_pairs={{0,1},{1,0},{2,3},{3,2},{4,5},{5,4},{6,7},{7,6},{8,9},{9,8},{10,11... | collective-permute-start | bytes 1572872 | tf_op jit(solution)/shard_map/ppermute | solution.py:608
  102.2 11.0 %copy-start.18 = (bf16[768,2048]{1,0:T(8,128)(2,1)}, bf16[768,2048]{1,0:T(8,128)(2,1)S(1)}, u32[]{:S(2)}) copy-start(bf16[768,2048]{1,0:T(8,128)(2,1)S(1)} %get-tuple-element.620.refs_3_) | copy-start | bytes 9437188
  102.2 11.0 %copy-start.19 = (bf16[768,2048]{1,0:T(8,128)(2,1)}, bf16[768,2048]{1,0:T(8,128)(2,1)S(1)}, u32[]{:S(2)}) copy-start(bf16[768,2048]{1,0:T(8,128)(2,1)S(1)} %get-tuple-element.621.refs_4_) | copy-start | bytes 9437188
  134.2 19.8 %all-to-all-start.5 = ((f32[128,2,768]{2,1,0:T(2,128)}), f32[128,2,768]{2,1,0:T(2,128)S(1)}, u32[]{:S(2)}, u32[]{:S(2)}) async-start(f32[128,2,768]{2,1,0:T(2,128)} %get-tuple-element.340), calls=%async_computation.5 | async-start | bytes 1572864 | tf_op jit(solution)/shard_map/all_to_all | solution.py:789
  137.7 16.2 %copy-start.20 = (s32[128]{0:T(128)S(1)}, s32[128]{0:T(128)}, u32[]{:S(2)}) copy-start(s32[128]{0:T(128)} %param.17) | copy-start | bytes 1540
  158.8 16.0 %copy-start.12 = (f32[320,256]{1,0:T(8,128)}, f32[320,256]{1,0:T(8,128)S(1)}, u32[]{:S(2)}) copy-start(f32[320,256]{1,0:T(8,128)S(1)} %get-tuple-element.603.iband_ref) | copy-start | bytes 983044 | tf_op jit(solution)/shard_map/while/body/while
  158.8 16.0 %copy-start.14 = (f32[320,256]{1,0:T(8,128)}, f32[320,256]{1,0:T(8,128)S(1)}, u32[]{:S(2)}) copy-start(f32[320,256]{1,0:T(8,128)S(1)} %get-tuple-element.604.oband_ref) | copy-start | bytes 983044 | tf_op jit(solution)/shard_map/while/body/while
  160.6 10.4 %copy-start.4 = (f32[12,256,256]{2,1,0:T(8,128)S(1)}, f32[12,256,256]{2,1,0:T(8,128)}, u32[]{:S(2)}) copy-start(f32[12,256,256]{2,1,0:T(8,128)} %get-tuple-element.602.band_ref) | copy-start | bytes 9437188 | tf_op jit(solution)/shard_map/while/body/while
  162.7 3.3 collective-permute-start
  164.1 7.0 %collective-permute-start.1 = (f32[192,256]{1,0:T(8,128)S(1)}, f32[192,256]{1,0:T(8,128)S(1)}, u32[]{:S(2)}, u32[]{:S(2)}) collective-permute-start(f32[192,256]{1,0:T(8,128)S(1)} %get-tuple-element.544), channel_id=1, source_target_pairs={{1,2},{3,4},{5,6},{7,8},{9,10},{11,12},{13,14},{15,16},{17,18},{19... | collective-permute-start | bytes 589832 | tf_op jit(solution)/shard_map/while/body/while/body/eval_jaxpr/ppermute | solution.py:616
  187.6 2.0 collective-permute-start.2
  225.5 4.5 collective-permute-start.3
  244.6 6.0 copy-start.5
  244.6 6.0 copy-start.6
  255.4 13.5 %copy-start.12 = (f32[320,256]{1,0:T(8,128)}, f32[320,256]{1,0:T(8,128)S(1)}, u32[]{:S(2)}) copy-start(f32[320,256]{1,0:T(8,128)S(1)} %get-tuple-element.603.iband_ref) | copy-start | bytes 983044 | tf_op jit(solution)/shard_map/while/body/while
  255.4 13.5 %copy-start.14 = (f32[320,256]{1,0:T(8,128)}, f32[320,256]{1,0:T(8,128)S(1)}, u32[]{:S(2)}) copy-start(f32[320,256]{1,0:T(8,128)S(1)} %get-tuple-element.604.oband_ref) | copy-start | bytes 983044 | tf_op jit(solution)/shard_map/while/body/while
  257.2 7.9 %copy-start.4 = (f32[12,256,256]{2,1,0:T(8,128)S(1)}, f32[12,256,256]{2,1,0:T(8,128)}, u32[]{:S(2)}) copy-start(f32[12,256,256]{2,1,0:T(8,128)} %get-tuple-element.602.band_ref) | copy-start | bytes 9437188 | tf_op jit(solution)/shard_map/while/body/while
  257.5 2.9 collective-permute-start
  258.0 7.1 %collective-permute-start.1 = (f32[192,256]{1,0:T(8,128)S(1)}, f32[192,256]{1,0:T(8,128)S(1)}, u32[]{:S(2)}, u32[]{:S(2)}) collective-permute-start(f32[192,256]{1,0:T(8,128)S(1)} %get-tuple-element.544), channel_id=1, source_target_pairs={{1,2},{3,4},{5,6},{7,8},{9,10},{11,12},{13,14},{15,16},{17,18},{19... | collective-permute-start | bytes 589832 | tf_op jit(solution)/shard_map/while/body/while/body/eval_jaxpr/ppermute | solution.py:616
  281.6 2.0 collective-permute-start.2
  320.5 4.5 collective-permute-start.3
  339.6 6.6 copy-start.3
  339.6 6.6 copy-start.5
  339.6 6.6 copy-start.6
  351.0 15.1 %copy-start.12 = (f32[320,256]{1,0:T(8,128)}, f32[320,256]{1,0:T(8,128)S(1)}, u32[]{:S(2)}) copy-start(f32[320,256]{1,0:T(8,128)S(1)} %get-tuple-element.603.iband_ref) | copy-start | bytes 983044 | tf_op jit(solution)/shard_map/while/body/while
  351.0 15.1 %copy-start.14 = (f32[320,256]{1,0:T(8,128)}, f32[320,256]{1,0:T(8,128)S(1)}, u32[]{:S(2)}) copy-start(f32[320,256]{1,0:T(8,128)S(1)} %get-tuple-element.604.oband_ref) | copy-start | bytes 983044 | tf_op jit(solution)/shard_map/while/body/while
  352.8 9.5 %copy-start.4 = (f32[12,256,256]{2,1,0:T(8,128)S(1)}, f32[12,256,256]{2,1,0:T(8,128)}, u32[]{:S(2)}) copy-start(f32[12,256,256]{2,1,0:T(8,128)} %get-tuple-element.602.band_ref) | copy-start | bytes 9437188 | tf_op jit(solution)/shard_map/while/body/while
  354.9 2.7 collective-permute-start
  355.4 7.0 %collective-permute-start.1 = (f32[192,256]{1,0:T(8,128)S(1)}, f32[192,256]{1,0:T(8,128)S(1)}, u32[]{:S(2)}, u32[]{:S(2)}) collective-permute-start(f32[192,256]{1,0:T(8,128)S(1)} %get-tuple-element.544), channel_id=1, source_target_pairs={{1,2},{3,4},{5,6},{7,8},{9,10},{11,12},{13,14},{15,16},{17,18},{19... | collective-permute-start | bytes 589832 | tf_op jit(solution)/shard_map/while/body/while/body/eval_jaxpr/ppermute | solution.py:616
  378.9 2.0 collective-permute-start.2
  417.8 4.5 collective-permute-start.3
  436.9 6.6 copy-start.3
  436.9 6.6 copy-start.5
  436.9 6.6 copy-start.6
  448.3 13.5 %copy-start.12 = (f32[320,256]{1,0:T(8,128)}, f32[320,256]{1,0:T(8,128)S(1)}, u32[]{:S(2)}) copy-start(f32[320,256]{1,0:T(8,128)S(1)} %get-tuple-element.603.iband_ref) | copy-start | bytes 983044 | tf_op jit(solution)/shard_map/while/body/while
  448.3 13.5 %copy-start.14 = (f32[320,256]{1,0:T(8,128)}, f32[320,256]{1,0:T(8,128)S(1)}, u32[]{:S(2)}) copy-start(f32[320,256]{1,0:T(8,128)S(1)} %get-tuple-element.604.oband_ref) | copy-start | bytes 983044 | tf_op jit(solution)/shard_map/while/body/while
  450.1 7.9 %copy-start.4 = (f32[12,256,256]{2,1,0:T(8,128)S(1)}, f32[12,256,256]{2,1,0:T(8,128)}, u32[]{:S(2)}) copy-start(f32[12,256,256]{2,1,0:T(8,128)} %get-tuple-element.602.band_ref) | copy-start | bytes 9437188 | tf_op jit(solution)/shard_map/while/body/while
  450.4 2.9 collective-permute-start
  450.9 7.1 %collective-permute-start.1 = (f32[192,256]{1,0:T(8,128)S(1)}, f32[192,256]{1,0:T(8,128)S(1)}, u32[]{:S(2)}, u32[]{:S(2)}) collective-permute-start(f32[192,256]{1,0:T(8,128)S(1)} %get-tuple-element.544), channel_id=1, source_target_pairs={{1,2},{3,4},{5,6},{7,8},{9,10},{11,12},{13,14},{15,16},{17,18},{19... | collective-permute-start | bytes 589832 | tf_op jit(solution)/shard_map/while/body/while/body/eval_jaxpr/ppermute | solution.py:616
  474.5 2.0 collective-permute-start.2
  513.4 4.5 collective-permute-start.3
  532.5 6.6 copy-start.3
  532.5 6.6 copy-start.5
  532.5 6.6 copy-start.6
  543.9 15.1 %copy-start.12 = (f32[320,256]{1,0:T(8,128)}, f32[320,256]{1,0:T(8,128)S(1)}, u32[]{:S(2)}) copy-start(f32[320,256]{1,0:T(8,128)S(1)} %get-tuple-element.603.iband_ref) | copy-start | bytes 983044 | tf_op jit(solution)/shard_map/while/body/while
  543.9 15.1 %copy-start.14 = (f32[320,256]{1,0:T(8,128)}, f32[320,256]{1,0:T(8,128)S(1)}, u32[]{:S(2)}) copy-start(f32[320,256]{1,0:T(8,128)S(1)} %get-tuple-element.604.oband_ref) | copy-start | bytes 983044 | tf_op jit(solution)/shard_map/while/body/while
  545.7 9.5 %copy-start.4 = (f32[12,256,256]{2,1,0:T(8,128)S(1)}, f32[12,256,256]{2,1,0:T(8,128)}, u32[]{:S(2)}) copy-start(f32[12,256,256]{2,1,0:T(8,128)} %get-tuple-element.602.band_ref) | copy-start | bytes 9437188 | tf_op jit(solution)/shard_map/while/body/while
  547.8 2.8 collective-permute-start
  548.3 7.0 %collective-permute-start.1 = (f32[192,256]{1,0:T(8,128)S(1)}, f32[192,256]{1,0:T(8,128)S(1)}, u32[]{:S(2)}, u32[]{:S(2)}) collective-permute-start(f32[192,256]{1,0:T(8,128)S(1)} %get-tuple-element.544), channel_id=1, source_target_pairs={{1,2},{3,4},{5,6},{7,8},{9,10},{11,12},{13,14},{15,16},{17,18},{19... | collective-permute-start | bytes 589832 | tf_op jit(solution)/shard_map/while/body/while/body/eval_jaxpr/ppermute | solution.py:616
  571.8 2.0 collective-permute-start.2
  610.7 4.5 collective-permute-start.3
  629.8 6.6 copy-start.3
  629.8 6.6 copy-start.5
  629.8 6.6 copy-start.6
  646.3 21.8 %copy-start.21 = (s32[128]{0:T(128)S(1)}, s32[128]{0:T(128)}, u32[]{:S(2)}) copy-start(s32[128]{0:T(128)} %get-tuple-element.699) | copy-start | bytes 1540 | tf_op jit(solution)/shard_map/while
  646.3 23.3 %copy-start.9 = (f32[2048,256]{1,0:T(8,128)S(1)}, f32[2048,256]{1,0:T(8,128)}, u32[]{:S(2)}) copy-start(f32[2048,256]{1,0:T(8,128)} %get-tuple-element.671) | copy-start | bytes 6291460 | tf_op jit(solution)/shard_map/while
  (37 other events, 37.1 us)
